TPU v7x, 32 devices: a whole 2x2x4 slice. The times are simulated.
32 devices in a mesh: fsdp: 2 (over x), ctx: 4 (over z), tp: 4 (over y, core).
Axes of the slice: x: 2, y: 2, z: 4, core: 2. Of those that a mesh axis runs over, the one named last changes fastest.
Arguments:
- inputs: bfloat16 [2, 1024, 2048], P('fsdp', 'ctx'), may hold values from -6 to 6
- cotangent: bfloat16 [2, 1024, 2048], P('fsdp', 'ctx'), may hold values from -6 to 6
- prefix: int32 [2], P('fsdp'), may hold values from 102 to 512
- attn_gain: bfloat16 [2048], P('fsdp'), may hold values from 0.099609375 to 1.8984375
- w_query: bfloat16 [2048, 2048], P('fsdp', 'tp'), may hold values from -0.125 to 0.125
- key_projection: bfloat16 [2048, 512], P('fsdp', 'tp'), may hold values from -0.125 to 0.125
- value_projection: bfloat16 [2048, 512], P('fsdp', 'tp'), may hold values from -0.125 to 0.125
- w_out: bfloat16 [2048, 2048], P('fsdp', 'tp'), may hold values from -1 to 1
- ffn_gain: bfloat16 [2048], P('fsdp'), may hold values from 0.099609375 to 1.8984375
- w_gate: bfloat16 [2048, 8192], P('fsdp', 'tp'), may hold values from -0.125 to 0.125
- w_up: bfloat16 [2048, 8192], P('fsdp', 'tp'), may hold values from -0.125 to 0.125
- w_down: bfloat16 [2048, 8192], P('fsdp', 'tp'), may hold values from -0.0625 to 0.0625
Outputs:
- output: bfloat16 [2, 1024, 2048], P('fsdp', 'ctx')
- grad_input: bfloat16 [2, 1024, 2048], P('fsdp', 'ctx')
- grad_attn_gain: float32 [2048], P('fsdp')
- grad_query: float32 [2048, 2048], P('fsdp', 'tp')
- grad_key: float32 [2048, 512], P('fsdp', 'tp')
- grad_value: float32 [2048, 512], P('fsdp', 'tp')
- grad_out: float32 [2048, 2048], P('fsdp', 'tp')
- grad_ffn_gain: float32 [2048], P('fsdp')
- grad_gate: float32 [2048, 8192], P('fsdp', 'tp')
- grad_up: float32 [2048, 8192], P('fsdp', 'tp')
- grad_down: float32 [2048, 8192], P('fsdp', 'tp')
Inputs may be any that keep to these rules, and one draw needn't show every extreme that they name: prefix holds, for each sequence, how many of its leading positions every position of that sequence may attend.
All inputs are finite; a program needn't handle non-finite values.
Results may differ from a plain program's by a relative error of at most 0.024.
Values may be sent and summed in bfloat16 or wider, within the bound.
A program may use at most 192 MiB of HBM per device.

v0:
```python
import math

import jax
import jax.numpy as jnp
from jax import lax
from jax.sharding import PartitionSpec as P

HEAD_SIZE = 64


EPSILON = 1e-05
THETA = 500000.0
MASKED = -1e30


def contract(left, right, left_dim, right_dim):
    return lax.dot_general(
        left, right, (((left_dim,), (right_dim,)), ((), ())), preferred_element_type=jnp.float32
    )


def rope_tables(row_start, row_count):
    position = (row_start + jnp.arange(row_count, dtype=jnp.int32)).astype(jnp.float32)
    exponent = jnp.arange(HEAD_SIZE // 2, dtype=jnp.int32).astype(jnp.float32) * (2.0 / HEAD_SIZE)
    angles = position[:, None] * jnp.power(THETA, -exponent)[None, :]
    return (jnp.cos(angles), jnp.sin(angles))


def apply_rotary(values, cosine_lookup, sine_lookup, direction):
    half_width = values.shape[-1] // 2
    leading = values[..., :half_width]
    trailing = values[..., half_width:]
    cos_wide = cosine_lookup[:, None, :]
    sin_wide = direction * sine_lookup[:, None, :]
    return jnp.concatenate(
        [leading * cos_wide - trailing * sin_wide, trailing * cos_wide + leading * sin_wide],
        axis=-1,
    )


def masked_scores(query_block, key_block, prefix_one, row_start):
    row_count = query_block.shape[0]
    length_total = key_block.shape[0]
    scores = jnp.einsum(
        "qkgd,pkd->kgqp", query_block, key_block, preferred_element_type=jnp.float32
    ) * (1.0 / math.sqrt(HEAD_SIZE))
    query_place = row_start + jnp.arange(row_count, dtype=jnp.int32)
    key_place = jnp.arange(length_total, dtype=jnp.int32)
    allowed = (key_place[None, :] <= query_place[:, None]) | (key_place[None, :] < prefix_one)
    return jnp.where(allowed, scores, MASKED)


def attend(query_block, key_block, value_block, prefix_one, row_start):
    scores = masked_scores(query_block, key_block, prefix_one, row_start)
    row_peak = jnp.max(scores, axis=-1, keepdims=True)
    weights = jnp.exp(scores - row_peak)
    row_total = jnp.sum(weights, axis=-1, keepdims=True)
    probabilities = (weights / row_total).astype(jnp.bfloat16)
    attended = jnp.einsum(
        "kgqp,pkd->qkgd", probabilities, value_block, preferred_element_type=jnp.float32
    )
    return (attended.astype(jnp.bfloat16), row_peak + jnp.log(row_total))


def attend_back(query_block, key_block, value_block, grad_block, log_total, prefix_one, row_start):
    scores = masked_scores(query_block, key_block, prefix_one, row_start)
    probabilities = jnp.exp(scores - log_total)
    rounded = probabilities.astype(jnp.bfloat16)
    grad_probs = jnp.einsum(
        "qkgd,pkd->kgqp", grad_block, value_block, preferred_element_type=jnp.float32
    )
    delta_rows = jnp.sum(probabilities * grad_probs, axis=-1, keepdims=True)
    grad_scores = (probabilities * (grad_probs - delta_rows)).astype(jnp.bfloat16)
    score_scale = 1.0 / math.sqrt(HEAD_SIZE)
    grad_queries = (
        jnp.einsum("kgqp,pkd->qkgd", grad_scores, key_block, preferred_element_type=jnp.float32)
        * score_scale
    )
    grad_keys = (
        jnp.einsum("kgqp,qkgd->pkd", grad_scores, query_block, preferred_element_type=jnp.float32)
        * score_scale
    )
    grad_values = jnp.einsum(
        "kgqp,qkgd->pkd", rounded, grad_block, preferred_element_type=jnp.float32
    )
    return (grad_queries, grad_keys, grad_values)


def local(
    inputs,
    cotangent,
    prefix,
    attn_gain,
    w_query,
    key_projection,
    value_projection,
    w_out,
    ffn_gain,
    w_gate,
    w_up,
    w_down,
):
    gathered = (
        lax.all_gather(attn_gain, "fsdp", axis=0, tiled=True),
        lax.all_gather(w_query, "fsdp", axis=0, tiled=True),
        lax.all_gather(key_projection, "fsdp", axis=0, tiled=True),
        lax.all_gather(value_projection, "fsdp", axis=0, tiled=True),
        lax.all_gather(w_out, "fsdp", axis=0, tiled=True),
        lax.all_gather(ffn_gain, "fsdp", axis=0, tiled=True),
        lax.all_gather(w_gate, "fsdp", axis=0, tiled=True),
        lax.all_gather(w_up, "fsdp", axis=0, tiled=True),
        lax.all_gather(w_down, "fsdp", axis=0, tiled=True),
    )
    gain_first = gathered[0].astype(jnp.float32)
    query_weight = gathered[1]
    key_weight = gathered[2]
    value_weight = gathered[3]
    out_weight = gathered[4]
    gain_second = gathered[5].astype(jnp.float32)
    gate_weight = gathered[6]
    up_weight = gathered[7]
    down_weight = gathered[8]
    seq_count, row_count, model_width = inputs.shape
    token_count = seq_count * row_count
    query_heads = query_weight.shape[1] // HEAD_SIZE
    kv_heads = key_weight.shape[1] // HEAD_SIZE
    heads_per_group = query_heads // kv_heads
    row_start = lax.axis_index("ctx") * row_count
    cosine_lookup, sine_lookup = rope_tables(row_start, row_count)
    residual = inputs.reshape(token_count, model_width).astype(jnp.float32)
    rms_first = lax.rsqrt(jnp.mean(residual * residual, axis=-1, keepdims=True) + EPSILON)
    normalized_rows = (residual * rms_first * gain_first).astype(jnp.bfloat16)
    query_unrotated = jnp.dot(normalized_rows, query_weight, preferred_element_type=jnp.float32)
    key_unrotated = jnp.dot(normalized_rows, key_weight, preferred_element_type=jnp.float32)
    query_rot = apply_rotary(
        query_unrotated.reshape(seq_count, row_count, query_heads, HEAD_SIZE),
        cosine_lookup,
        sine_lookup,
        1.0,
    ).astype(jnp.bfloat16)
    key_rot = apply_rotary(
        key_unrotated.reshape(seq_count, row_count, kv_heads, HEAD_SIZE),
        cosine_lookup,
        sine_lookup,
        1.0,
    ).astype(jnp.bfloat16)
    key_rot = key_rot.reshape(seq_count, row_count, kv_heads * HEAD_SIZE)
    value_matrix = jnp.dot(
        normalized_rows, value_weight, preferred_element_type=jnp.float32
    ).astype(jnp.bfloat16)
    value_matrix = value_matrix.reshape(seq_count, row_count, kv_heads * HEAD_SIZE)
    key_whole, value_whole = (
        lax.all_gather(key_rot, "ctx", axis=1, tiled=True),
        lax.all_gather(value_matrix, "ctx", axis=1, tiled=True),
    )
    length_total = key_whole.shape[1]
    query_groups = query_rot.reshape(seq_count, row_count, kv_heads, heads_per_group, HEAD_SIZE)

    def forward_one(operands):
        query_block, key_block, value_block, prefix_one = operands
        return attend(
            query_block,
            key_block.reshape(length_total, kv_heads, HEAD_SIZE),
            value_block.reshape(length_total, kv_heads, HEAD_SIZE),
            prefix_one,
            row_start,
        )

    attended, log_total = lax.map(forward_one, (query_groups, key_whole, value_whole, prefix))
    attended_flat = attended.reshape(token_count, query_heads * HEAD_SIZE)
    attn_term = contract(attended_flat, out_weight, 1, 1)
    cot_rows = cotangent.reshape(token_count, model_width)
    middle = residual + lax.psum(attn_term.astype(jnp.bfloat16), "tp").astype(jnp.float32)
    rms_second = lax.rsqrt(jnp.mean(middle * middle, axis=-1, keepdims=True) + EPSILON)
    normed_local = (middle * rms_second * gain_second).astype(jnp.bfloat16)
    gating = jnp.dot(normed_local, gate_weight, preferred_element_type=jnp.float32)
    upward = jnp.dot(normed_local, up_weight, preferred_element_type=jnp.float32)
    hidden = (jax.nn.silu(gating) * upward).astype(jnp.bfloat16)
    ffn_term = contract(hidden, down_weight, 1, 1)
    ffn_branch = lax.psum(ffn_term.astype(jnp.bfloat16), "tp").astype(jnp.float32)
    output_rows = (middle + ffn_branch).astype(jnp.bfloat16)
    grad_rows = cotangent.reshape(token_count, model_width)
    grad_down = contract(grad_rows, hidden, 0, 0)
    grad_hidden = jnp.dot(grad_rows, down_weight, preferred_element_type=jnp.float32)
    sigmoid_gate = jax.nn.sigmoid(gating)
    grad_gating = (
        grad_hidden * upward * sigmoid_gate * (1.0 + gating * (1.0 - sigmoid_gate))
    ).astype(jnp.bfloat16)
    grad_upward = (grad_hidden * gating * sigmoid_gate).astype(jnp.bfloat16)
    grad_gate = contract(normed_local, grad_gating, 0, 0)
    grad_up = contract(normed_local, grad_upward, 0, 0)
    mid_term = contract(grad_gating, gate_weight, 1, 1) + contract(grad_upward, up_weight, 1, 1)
    grad_mid_norm = lax.psum(mid_term.astype(jnp.bfloat16), "tp").astype(jnp.float32)
    scaled_mid = grad_mid_norm * gain_second
    grad_gain_second = jnp.sum(grad_mid_norm * middle * rms_second, axis=0)
    cube_second = rms_second * rms_second * rms_second
    grad_middle = (
        cot_rows.astype(jnp.float32)
        + rms_second * scaled_mid
        - middle * cube_second * jnp.mean(scaled_mid * middle, axis=-1, keepdims=True)
    )
    branch_local = grad_middle.astype(jnp.bfloat16)
    grad_out = contract(branch_local, attended_flat, 0, 0)
    grad_attended = jnp.dot(branch_local, out_weight, preferred_element_type=jnp.float32).astype(
        jnp.bfloat16
    )
    grad_attended = grad_attended.reshape(
        seq_count, row_count, kv_heads, heads_per_group, HEAD_SIZE
    )
    key_back, value_back = (key_whole, value_whole)

    def backward_one(operands):
        query_block, key_block, value_block, grad_block, total_block, prefix_one = operands
        return attend_back(
            query_block,
            key_block.reshape(length_total, kv_heads, HEAD_SIZE),
            value_block.reshape(length_total, kv_heads, HEAD_SIZE),
            grad_block,
            total_block,
            prefix_one,
            row_start,
        )

    grad_query_rot, grad_key_all, grad_value_all = lax.map(
        backward_one, (query_groups, key_back, value_back, grad_attended, log_total, prefix)
    )
    grad_key_all = grad_key_all.reshape(seq_count, length_total, kv_heads * HEAD_SIZE)
    grad_value_all = grad_value_all.reshape(seq_count, length_total, kv_heads * HEAD_SIZE)
    grad_key_rows, grad_value_rows = (
        lax.psum_scatter(
            grad_key_all.astype(jnp.bfloat16), "ctx", scatter_dimension=1, tiled=True
        ).astype(jnp.float32),
        lax.psum_scatter(
            grad_value_all.astype(jnp.bfloat16), "ctx", scatter_dimension=1, tiled=True
        ).astype(jnp.float32),
    )
    grad_query_pre = apply_rotary(
        grad_query_rot.reshape(seq_count, row_count, query_heads, HEAD_SIZE),
        cosine_lookup,
        sine_lookup,
        -1.0,
    ).astype(jnp.bfloat16)
    grad_query_pre = grad_query_pre.reshape(token_count, query_heads * HEAD_SIZE)
    grad_key_pre = apply_rotary(
        grad_key_rows.reshape(seq_count, row_count, kv_heads, HEAD_SIZE),
        cosine_lookup,
        sine_lookup,
        -1.0,
    ).astype(jnp.bfloat16)
    grad_key_pre = grad_key_pre.reshape(token_count, kv_heads * HEAD_SIZE)
    grad_value_pre = grad_value_rows.astype(jnp.bfloat16).reshape(token_count, kv_heads * HEAD_SIZE)
    grad_query = contract(normalized_rows, grad_query_pre, 0, 0)
    grad_key = contract(normalized_rows, grad_key_pre, 0, 0)
    grad_value = contract(normalized_rows, grad_value_pre, 0, 0)
    grad_normed_part = (
        contract(grad_query_pre, query_weight, 1, 1)
        + contract(grad_key_pre, key_weight, 1, 1)
        + contract(grad_value_pre, value_weight, 1, 1)
    )
    grad_normed = lax.psum(grad_normed_part.astype(jnp.bfloat16), "tp").astype(jnp.float32)
    scaled_first = grad_normed * gain_first
    grad_gain_first = jnp.sum(grad_normed * residual * rms_first, axis=0)
    cube_first = rms_first * rms_first * rms_first
    grad_full = (
        grad_middle
        + rms_first * scaled_first
        - residual * cube_first * jnp.mean(scaled_first * residual, axis=-1, keepdims=True)
    )
    input_rows = grad_full.astype(jnp.bfloat16)
    output_whole, input_whole = (output_rows, input_rows)
    output = output_whole.reshape(seq_count, row_count, model_width)
    grad_input = input_whole.reshape(seq_count, row_count, model_width)
    spread = (
        lax.psum_scatter(
            grad_gain_first.astype(jnp.bfloat16), ("fsdp", "ctx"), scatter_dimension=0, tiled=True
        ).astype(jnp.float32),
        lax.psum_scatter(
            grad_query.astype(jnp.bfloat16), ("fsdp", "ctx"), scatter_dimension=0, tiled=True
        ).astype(jnp.float32),
        lax.psum_scatter(
            grad_key.astype(jnp.bfloat16), ("fsdp", "ctx"), scatter_dimension=0, tiled=True
        ).astype(jnp.float32),
        lax.psum_scatter(
            grad_value.astype(jnp.bfloat16), ("fsdp", "ctx"), scatter_dimension=0, tiled=True
        ).astype(jnp.float32),
        lax.psum_scatter(
            grad_out.astype(jnp.bfloat16), ("fsdp", "ctx"), scatter_dimension=0, tiled=True
        ).astype(jnp.float32),
        lax.psum_scatter(
            grad_gain_second.astype(jnp.bfloat16), ("fsdp", "ctx"), scatter_dimension=0, tiled=True
        ).astype(jnp.float32),
        lax.psum_scatter(
            grad_gate.astype(jnp.bfloat16), ("fsdp", "ctx"), scatter_dimension=0, tiled=True
        ).astype(jnp.float32),
        lax.psum_scatter(
            grad_up.astype(jnp.bfloat16), ("fsdp", "ctx"), scatter_dimension=0, tiled=True
        ).astype(jnp.float32),
        lax.psum_scatter(
            grad_down.astype(jnp.bfloat16), ("fsdp", "ctx"), scatter_dimension=0, tiled=True
        ).astype(jnp.float32),
    )
    reduced = (
        lax.all_gather(spread[0].astype(jnp.bfloat16), "ctx", axis=0, tiled=True).astype(
            jnp.float32
        ),
        lax.all_gather(spread[1].astype(jnp.bfloat16), "ctx", axis=0, tiled=True).astype(
            jnp.float32
        ),
        lax.all_gather(spread[2].astype(jnp.bfloat16), "ctx", axis=0, tiled=True).astype(
            jnp.float32
        ),
        lax.all_gather(spread[3].astype(jnp.bfloat16), "ctx", axis=0, tiled=True).astype(
            jnp.float32
        ),
        lax.all_gather(spread[4].astype(jnp.bfloat16), "ctx", axis=0, tiled=True).astype(
            jnp.float32
        ),
        lax.all_gather(spread[5].astype(jnp.bfloat16), "ctx", axis=0, tiled=True).astype(
            jnp.float32
        ),
        lax.all_gather(spread[6].astype(jnp.bfloat16), "ctx", axis=0, tiled=True).astype(
            jnp.float32
        ),
        lax.all_gather(spread[7].astype(jnp.bfloat16), "ctx", axis=0, tiled=True).astype(
            jnp.float32
        ),
        lax.all_gather(spread[8].astype(jnp.bfloat16), "ctx", axis=0, tiled=True).astype(
            jnp.float32
        ),
    )
    return (
        output,
        grad_input,
        reduced[0],
        reduced[1],
        reduced[2],
        reduced[3],
        reduced[4],
        reduced[5],
        reduced[6],
        reduced[7],
        reduced[8],
    )


def solution(mesh):
    return jax.shard_map(
        local,
        mesh=mesh,
        in_specs=(
            P("fsdp", "ctx", None),
            P("fsdp", "ctx", None),
            P("fsdp"),
            P("fsdp"),
            P("fsdp", "tp"),
            P("fsdp", "tp"),
            P("fsdp", "tp"),
            P("fsdp", "tp"),
            P("fsdp"),
            P("fsdp", "tp"),
            P("fsdp", "tp"),
            P("fsdp", "tp"),
        ),
        out_specs=(
            P("fsdp", "ctx", None),
            P("fsdp", "ctx", None),
            P("fsdp"),
            P("fsdp", "tp"),
            P("fsdp", "tp"),
            P("fsdp", "tp"),
            P("fsdp", "tp"),
            P("fsdp"),
            P("fsdp", "tp"),
            P("fsdp", "tp"),
            P("fsdp", "tp"),
        ),
        check_vma=False,
    )
```

profile of v0, /device:TPU:0, one launch (start us, length us, event | category | flops | bytes accessed | tf_op | source)
XLA Modules:
  0.0 1649.7 jit_solution(9051051704497028200)
XLA Ops:
  8.8 9.9 all_gather.61
  18.7 4.4 all_gather.60
  24.4 14.9 all-gather
  39.5 11.3 all_gather.63
  52.4 14.3 all_gather.64
  67.7 3.9 copy.45
  71.6 2.4 convolution_bitcast_fusion.1
  74.1 1.4 fusion.76
  76.7 2.3 copy-done
  79.0 1.5 fusion.46
  80.5 4.3 all-gather.16.cloned.1.call-done
  84.8 3.3 convolution_convert_fusion.4
  90.1 4.5 all_gather.67
  94.6 30.1 %all-reduce.8.cloned.1.call-done = bf16[256,2048]{1,0:T(8,128)(2,1)} async-done(((bf16[256,2048]{1,0:T(8,128)(2,1)}), bf16[256,2048]{1,0:T(8,128)(2,1)}) %all-reduce.8.cloned.1.call-update) | async-done | bytes 1048592 | tf_op jit(solution)/shard_map/psum | solution.py:173
  124.6 1.7 multiply_reduce_fusion
  126.9 103.6 %all-gather.18.cloned.1.call-done = bf16[2048,2048]{1,0:T(8,128)(2,1)} async-done(((bf16[1024,2048]{1,0:T(8,128)(2,1)}), bf16[2048,2048]{1,0:T(8,128)(2,1)}) %all-gather.18.cloned.1.call-update) | async-done | bytes 8388624 | tf_op jit(solution)/shard_map/all_gather | solution.py:110
  230.5 7.0 fusion.77
  237.6 98.4 %all-gather.20.cloned.1.call-done = bf16[2048,2048]{1,0:T(8,128)(2,1)} async-done(((bf16[1024,2048]{1,0:T(8,128)(2,1)}), bf16[2048,2048]{1,0:T(8,128)(2,1)}) %all-gather.20.cloned.1.call-update) | async-done | bytes 8388624 | tf_op jit(solution)/shard_map/all_gather | solution.py:111
  335.9 7.0 fusion.78
  343.0 98.4 %all-gather.22.cloned.1.call-done = bf16[2048,2048]{1,0:T(8,128)(2,1)} async-done(((bf16[1024,2048]{1,0:T(8,128)(2,1)}), bf16[2048,2048]{1,0:T(8,128)(2,1)}) %all-gather.22.cloned.1.call-update) | async-done | bytes 8388624 | tf_op jit(solution)/shard_map/all_gather | solution.py:112
  441.3 8.9 multiply_convert_fusion
  450.2 6.6 fusion.79
  456.8 3.3 fusion.16
  460.4 36.2 %all-reduce.10.cloned.1.call-done = bf16[256,2048]{1,0:T(8,128)(2,1)} async-done(((bf16[256,2048]{1,0:T(8,128)(2,1)}), bf16[256,2048]{1,0:T(8,128)(2,1)}) %all-reduce.10.cloned.1.call-update) | async-done | bytes 1048592 | tf_op jit(solution)/shard_map/psum | solution.py:193
  496.6 2.7 fusion.28
  499.8 3.3 convolution_convert_fusion.8
  504.3 5.4 fusion
  510.2 1.8 fusion.2
  512.0 2.1 fusion.45
  514.2 3.9 convolution_multiply_fusion
  518.1 5.6 fusion.42
  524.9 2.2 convolution_convert_fusion.3
  527.2 4.4 convolution_convert_fusion.2
  531.7 7.0 convolution_convert_fusion.1
  539.2 7.0 convolution_convert_fusion
  547.5 7.0 convert_bitcast_fusion
  554.6 7.1 convolution_convert_fusion.5
  562.6 1.8 fusion.80
  564.4 1.4 fusion.64
  566.1 3.4 fusion.17
  573.1 52.6 %reduce-scatter.14.cloned.1.call-done = bf16[256,512]{1,0:T(8,128)(2,1)} async-done(((bf16[2048,512]{1,0:T(8,128)(2,1)}), bf16[256,512]{1,0:T(8,128)(2,1)}) %reduce-scatter.14.cloned.1.call-update) | async-done | bytes 262160 | tf_op jit(solution)/shard_map/reduce_scatter | solution.py:277
  625.8 70.8 %reduce-scatter.20.cloned.1.call-done = bf16[256,512]{1,0:T(8,128)(2,1)} async-done(((bf16[2048,512]{1,0:T(8,128)(2,1)}), bf16[256,512]{1,0:T(8,128)(2,1)}) %reduce-scatter.20.cloned.1.call-update) | async-done | bytes 262160 | tf_op jit(solution)/shard_map/reduce_scatter | solution.py:286
  696.7 150.5 %reduce-scatter.22.cloned.1.call-done = bf16[256,2048]{1,0:T(8,128)(2,1)} async-done(((bf16[2048,2048]{1,0:T(8,128)(2,1)}), bf16[256,2048]{1,0:T(8,128)(2,1)}) %reduce-scatter.22.cloned.1.call-update) | async-done | bytes 1048592 | tf_op jit(solution)/shard_map/reduce_scatter | solution.py:292
  847.3 150.7 %reduce-scatter.24.cloned.1.call-done = bf16[256,2048]{1,0:T(8,128)(2,1)} async-done(((bf16[2048,2048]{1,0:T(8,128)(2,1)}), bf16[256,2048]{1,0:T(8,128)(2,1)}) %reduce-scatter.24.cloned.1.call-update) | async-done | bytes 1048592 | tf_op jit(solution)/shard_map/reduce_scatter | solution.py:295
  998.1 151.0 %reduce-scatter.26.cloned.1.call-done = bf16[256,2048]{0,1:T(8,128)(2,1)} async-done(((bf16[2048,2048]{0,1:T(8,128)(2,1)}), bf16[256,2048]{0,1:T(8,128)(2,1)}) %reduce-scatter.26.cloned.1.call-update) | async-done | bytes 1048592 | tf_op jit(solution)/shard_map/reduce_scatter | solution.py:298
  1150.3 52.1 %all-reduce.12.cloned.1.call-done = (bf16[256,2048]{1,0:T(8,128)(2,1)}, bf16[256,2048]{1,0:T(8,128)(2,1)}) async-done(((bf16[256,2048]{1,0:T(8,128)(2,1)}, bf16[256,2048]{1,0:T(8,128)(2,1)}), (bf16[256,2048]{1,0:T(8,128)(2,1)}, bf16[256,2048]{1,0:T(8,128)(2,1)})) %all-reduce.12.cloned.1.call-update) | async-done | bytes 2097168 | tf_op jit(solution)/shard_map/psum | solution.py:180
  1202.5 2.0 fusion.35
  1204.5 21.9 %all-reduce.2 = (bf16[2048]{0:T(1024)(128)(2,1)S(1)}, bf16[2048]{0:T(1024)(128)(2,1)S(1)}) all-reduce(bf16[2048]{0:T(1024)(128)(2,1)S(1)} %get-tuple-element.103, bf16[2048]{0:T(1024)(128)(2,1)S(1)} %copy-done.34), channel_id=5, replica_groups=mesh['fsdp'=2,'ctx'=4,'tp'=4] {'fsdp','ctx'}, use_global_device_ids=true, to_apply=%region_14.15.clone | all-reduce | flops 4096 | bytes 16384
  1226.5 7.6 all-gather.1
  1234.6 34.4 %reduce-scatter.16.cloned.1.call-done = bf16[256,128]{1,0:T(8,128)(2,1)} async-done(((bf16[2048,128]{1,0:T(8,128)(2,1)}), bf16[256,128]{1,0:T(8,128)(2,1)}) %reduce-scatter.16.cloned.1.call-update) | async-done | bytes 65552 | tf_op jit(solution)/shard_map/reduce_scatter | solution.py:280
  1269.0 14.9 all_gather.73
  1284.7 49.7 %reduce-scatter.18.cloned.1.call-done = bf16[256,128]{1,0:T(8,128)(2,1)} async-done(((bf16[2048,128]{1,0:T(8,128)(2,1)}), bf16[256,128]{1,0:T(8,128)(2,1)}) %reduce-scatter.18.cloned.1.call-update) | async-done | bytes 65552 | tf_op jit(solution)/shard_map/reduce_scatter | solution.py:283
  1334.4 15.2 all_gather.74
  1350.4 10.9 all-gather.2
  1362.0 4.2 fusion.49
  1366.2 2.8 convert_element_type.335
  1369.0 23.5 %all-gather.26.cloned.1.call-done = bf16[1024,512]{1,0:T(8,128)(2,1)} async-done(((bf16[256,512]{1,0:T(8,128)(2,1)}), bf16[1024,512]{1,0:T(8,128)(2,1)}) %all-gather.26.cloned.1.call-update) | async-done | bytes 1048592 | tf_op jit(solution)/shard_map/all_gather | solution.py:315
  1392.5 2.8 convert_element_type.341
  1395.4 78.7 %all-gather.28.cloned.1.call-done = bf16[1024,2048]{1,0:T(8,128)(2,1)} async-done(((bf16[256,2048]{1,0:T(8,128)(2,1)}), bf16[1024,2048]{1,0:T(8,128)(2,1)}) %all-gather.28.cloned.1.call-update) | async-done | bytes 4194320 | tf_op jit(solution)/shard_map/all_gather | solution.py:321
  1474.1 6.7 convert_element_type.345
  1480.8 74.2 %all-gather.30.cloned.1.call-done = bf16[1024,2048]{1,0:T(8,128)(2,1)} async-done(((bf16[256,2048]{1,0:T(8,128)(2,1)}), bf16[1024,2048]{1,0:T(8,128)(2,1)}) %all-gather.30.cloned.1.call-update) | async-done | bytes 4194320 | tf_op jit(solution)/shard_map/all_gather | solution.py:324
  1554.9 6.7 convert_element_type.347
  1561.6 74.0 %all-gather.32.cloned.1.call-done = bf16[1024,2048]{0,1:T(8,128)(2,1)} async-done(((bf16[256,2048]{0,1:T(8,128)(2,1)}), bf16[1024,2048]{0,1:T(8,128)(2,1)}) %all-gather.32.cloned.1.call-update) | async-done | bytes 4194320 | tf_op jit(solution)/shard_map/all_gather | solution.py:327
  1635.6 7.1 copy.51
  (184 shorter events, 22.5 us)
Async XLA Ops:
  7.2 11.5 copy-start.42
  7.2 15.9 copy-start.1
  7.2 60.5 %all-gather.14.cloned.1.call-start = ((), (), s32[]{:S(2)}) async-start(), calls=%async_computation.9 | async-start | bytes 3145728 | tf_op jit(solution)/shard_map/all_gather | solution.py:105
  7.9 76.9 %all-gather.16.cloned.1.call-start = ((), (), s32[]{:S(2)}) async-start(), calls=%async_computation.10 | async-start | bytes 3145728 | tf_op jit(solution)/shard_map/all_gather | solution.py:108
  8.7 116.0 %all-reduce.8.cloned.1.call-start = ((), (), s32[]{:S(2)}) async-start(), calls=%async_computation.11 | async-start | bytes 2097152 | tf_op jit(solution)/shard_map/psum | solution.py:173
  18.7 5.2 copy-start.12
  23.1 16.4 copy-start.23
  23.9 47.7 %copy-start.28 = (f32[256]{0:T(256)}, f32[256]{0:T(256)S(1)}, u32[]{:S(2)}) copy-start(f32[256]{0:T(256)S(1)} %get-tuple-element.126) | copy-start | bytes 3076
  39.5 37.2 %copy-start.16 = (bf16[1024,128]{0,1:T(8,128)(2,1)}, bf16[1024,128]{0,1:T(8,128)(2,1)S(1)}, u32[]{:S(2)}) copy-start(bf16[1024,128]{0,1:T(8,128)(2,1)S(1)} %copy.43) | copy-start | bytes 786436
  50.8 16.0 copy-start.5
  52.4 21.6 %copy-start.19 = (f32[256,32]{0,1:T(8,128)}, f32[256,32]{0,1:T(8,128)S(1)}, u32[]{:S(2)}) copy-start(f32[256,32]{0,1:T(8,128)S(1)} %get-tuple-element.124) | copy-start | bytes 98308
  66.8 7.4 copy-start.11
  75.6 3.4 copy-start
  80.5 7.7 copy-start.24
  88.2 142.3 %all-gather.18.cloned.1.call-start = ((), (), s32[]{:S(2)}) async-start(), calls=%async_computation.12 | async-start | bytes 12582912 | tf_op jit(solution)/shard_map/all_gather | solution.py:110
  88.8 247.1 %all-gather.20.cloned.1.call-start = ((), (), s32[]{:S(2)}) async-start(), calls=%async_computation.13 | async-start | bytes 12582912 | tf_op jit(solution)/shard_map/all_gather | solution.py:111
  89.4 352.0 %all-gather.22.cloned.1.call-start = ((), (), s32[]{:S(2)}) async-start(), calls=%async_computation.14 | async-start | bytes 12582912 | tf_op jit(solution)/shard_map/all_gather | solution.py:112
  90.0 406.7 %all-reduce.10.cloned.1.call-start = ((), (), s32[]{:S(2)}) async-start(), calls=%async_computation.15 | async-start | bytes 2097152 | tf_op jit(solution)/shard_map/psum | solution.py:193
  94.6 404.7 %copy-start.25 = (f32[2048]{0:T(1024)}, f32[2048]{0:T(1024)S(1)}, u32[]{:S(2)}) copy-start(f32[2048]{0:T(1024)S(1)} %convert_element_type.304) | copy-start | bytes 24580
  124.6 1.8 copy-start.3
  126.4 372.9 %copy-start.31 = (f32[256]{0:T(256)}, f32[256]{0:T(256)S(1)}, u32[]{:S(2)}) copy-start(f32[256]{0:T(256)S(1)} %get-tuple-element.128) | copy-start | bytes 3076
  126.4 372.9 %copy-start.36 = (f32[256]{0:T(256)}, f32[256]{0:T(256)S(1)}, u32[]{:S(2)}) copy-start(f32[256]{0:T(256)S(1)} %get-tuple-element.127) | copy-start | bytes 3076
  450.2 6.6 copy-start.18
  450.2 6.6 copy-start.17
  450.2 6.6 copy-start.44
  460.2 101.5 %reduce-scatter.10.cloned.1.call-start = ((), (), s32[]{:S(2)}) async-start(), calls=%async_computation.16 | async-start | bytes 327680 | tf_op jit(solution)/shard_map/reduce_scatter | solution.py:230
  496.6 3.2 copy-start.7
  496.6 3.2 copy-start.10
  504.2 5.4 slice-start
  504.3 5.9 slice-start.1
  510.2 1.8 copy-start.15
  512.0 2.1 copy-start.2
  514.1 50.3 %reduce-scatter.12.cloned.1.call-start = ((), (), s32[]{:S(2)}) async-start(), calls=%async_computation.17 | async-start | bytes 327680 | tf_op jit(solution)/shard_map/reduce_scatter | solution.py:233
  518.1 5.6 copy-start.20
  518.1 5.6 copy-start.21
  518.1 6.8 copy-start.29
  523.7 102.1 %reduce-scatter.14.cloned.1.call-start = ((), (), s32[]{:S(2)}) async-start(), calls=%async_computation.18 | async-start | bytes 2359296 | tf_op jit(solution)/shard_map/reduce_scatter | solution.py:277
  524.9 2.3 copy-start.26
  524.9 2.3 copy-start.32
  524.9 2.3 copy-start.37
  524.9 2.3 copy-start.40
  527.1 169.5 %reduce-scatter.20.cloned.1.call-start = ((), (), s32[]{:S(2)}) async-start(), calls=%async_computation.22 | async-start | bytes 2359296 | tf_op jit(solution)/shard_map/reduce_scatter | solution.py:286
  531.7 315.5 %reduce-scatter.22.cloned.1.call-start = ((), (), s32[]{:S(2)}) async-start(), calls=%async_computation.24 | async-start | bytes 9437184 | tf_op jit(solution)/shard_map/reduce_scatter | solution.py:292
  538.8 459.2 %reduce-scatter.24.cloned.1.call-start = ((), (), s32[]{:S(2)}) async-start(), calls=%async_computation.26 | async-start | bytes 9437184 | tf_op jit(solution)/shard_map/reduce_scatter | solution.py:295
  546.3 602.8 %reduce-scatter.26.cloned.1.call-start = ((), (), s32[]{:S(2)}) async-start(), calls=%async_computation.28 | async-start | bytes 9437184 | tf_op jit(solution)/shard_map/reduce_scatter | solution.py:298
  554.5 8.1 copy-start.6
  554.5 648.0 %all-reduce.12.cloned.1.call-start = ((), (), s32[]{:S(2)}) async-start(), calls=%async_computation.30 | async-start | bytes 4194304 | tf_op jit(solution)/shard_map/psum | solution.py:180
  561.7 2.8 copy-start.13
  564.4 1.6 copy-start.4
  569.5 2.1 copy-start.27
  569.5 699.5 %reduce-scatter.16.cloned.1.call-start = ((), (), s32[]{:S(2)}) async-start(), calls=%async_computation.20 | async-start | bytes 589824 | tf_op jit(solution)/shard_map/reduce_scatter | solution.py:280
  571.6 762.8 %reduce-scatter.18.cloned.1.call-start = ((), (), s32[]{:S(2)}) async-start(), calls=%async_computation.21 | async-start | bytes 589824 | tf_op jit(solution)/shard_map/reduce_scatter | solution.py:283
  573.0 576.1 %copy-start.45 = (u32[32]{0:T(128)S(1)}, u32[32]{0:T(128)}, u32[]{:S(2)}) copy-start(u32[32]{0:T(128)} %constant.84) | copy-start | bytes 388
  573.1 793.1 %all-gather.24.cloned.1.call-start = ((), (), s32[]{:S(2)}) async-start(), calls=%async_computation.19 | async-start | bytes 1310720 | tf_op jit(solution)/shard_map/all_gather | solution.py:306
  625.8 766.8 %all-gather.26.cloned.1.call-start = ((), (), s32[]{:S(2)}) async-start(), calls=%async_computation.23 | async-start | bytes 1310720 | tf_op jit(solution)/shard_map/all_gather | solution.py:315
  696.6 777.5 %all-gather.28.cloned.1.call-start = ((), (), s32[]{:S(2)}) async-start(), calls=%async_computation.25 | async-start | bytes 5242880 | tf_op jit(solution)/shard_map/all_gather | solution.py:321
  847.2 707.7 %all-gather.30.cloned.1.call-start = ((), (), s32[]{:S(2)}) async-start(), calls=%async_computation.27 | async-start | bytes 5242880 | tf_op jit(solution)/shard_map/all_gather | solution.py:324
  998.0 206.5 %copy-start.34 = (bf16[2048]{0:T(1024)(128)(2,1)S(1)}, bf16[2048]{0:T(1024)(128)(2,1)}, u32[]{:S(2)}) copy-start(bf16[2048]{0:T(1024)(128)(2,1)} %get-tuple-element.101) | copy-start | bytes 12292
  998.0 637.6 %all-gather.32.cloned.1.call-start = ((), (), s32[]{:S(2)}) async-start(), calls=%async_computation.29 | async-start | bytes 5242880 | tf_op jit(solution)/shard_map/all_gather | solution.py:327
  1202.5 159.5 %copy-start.9 = (bf16[1,256,2048]{2,1,0:T(8,128)(2,1)S(1)}, bf16[1,256,2048]{2,1,0:T(8,128)(2,1)}, u32[]{:S(2)}) copy-start(bf16[1,256,2048]{2,1,0:T(8,128)(2,1)} %param.13) | copy-start | bytes 3145732
  1202.5 159.5 %copy-start.33 = (f32[256]{0:T(256)S(1)}, f32[256]{0:T(256)}, u32[]{:S(2)}) copy-start(f32[256]{0:T(256)} %copy-done.31) | copy-start | bytes 3076
  1202.5 159.5 %copy-start.35 = (f32[256]{0:T(256)S(1)}, f32[256]{0:T(256)}, u32[]{:S(2)}) copy-start(f32[256]{0:T(256)} %get-tuple-element.125) | copy-start | bytes 3076
  1202.5 159.5 %copy-start.38 = (f32[256]{0:T(256)S(1)}, f32[256]{0:T(256)}, u32[]{:S(2)}) copy-start(f32[256]{0:T(256)} %copy-done.36) | copy-start | bytes 3076
  1202.5 159.5 %copy-start.41 = (f32[256]{0:T(256)S(1)}, f32[256]{0:T(256)}, u32[]{:S(2)}) copy-start(f32[256]{0:T(256)} %copy-done.39) | copy-start | bytes 3076
  (6 other events, 6.2 us)
Sparse Core Ops, SparseCore 0:
  9.6 40.5 all-gather.13
  51.7 33.0 all-gather.15
  88.3 36.2 all-reduce.7
  126.0 104.4 all-gather.17
  231.9 103.9 all-gather.19
  337.3 103.9 all-gather.21
  460.3 36.2 all-reduce.9
  514.2 20.4 reduce-scatter.9
  537.0 18.2 reduce-scatter.11
  559.2 66.4 reduce-scatter.13
  629.3 67.2 reduce-scatter.19
  700.7 146.4 reduce-scatter.21
  851.4 146.5 reduce-scatter.23
  1002.0 146.9 reduce-scatter.25
  1151.9 50.4 all-reduce.11
  1206.2 62.6 reduce-scatter.15
  1272.7 61.5 reduce-scatter.17
  1335.8 27.8 all-gather.23
  1365.2 27.3 all-gather.25
  1394.0 80.1 all-gather.27
  1475.7 79.2 all-gather.29
  1556.5 79.0 all-gather.31
where the time goes:
time: 1660 us; the launch traced here: 1650 us
  waiting for transfers between devices  1340 us (81%)
  blocking collectives  130 us (8%)
  matrix products  107 us (6%)
  other arithmetic  39.9 us (2%)
  local copies, waits for them, and re-layouts  18.7 us (1%)
    reduce_scatter x1, waiting for transfers between devices, local(): lax.psum_scatter(grad_down.astype(jnp.bfloat16), ('fsdp', 'ctx'), scatter...  151 us
    reduce_scatter x1, waiting for transfers between devices, local(): lax.psum_scatter(grad_up.astype(jnp.bfloat16), ('fsdp', 'ctx'), scatter_d...  151 us
    reduce_scatter x1, waiting for transfers between devices, local(): lax.psum_scatter(grad_gate.astype(jnp.bfloat16), ('fsdp', 'ctx'), scatter...  151 us
    all_gather x1, waiting for transfers between devices, local(): lax.all_gather(w_gate, 'fsdp', axis=0, tiled=True)  104 us
    all_gather x1, waiting for transfers between devices, local(): lax.all_gather(w_down, 'fsdp', axis=0, tiled=True)  98.4 us
    all_gather x1, waiting for transfers between devices, local(): lax.all_gather(w_up, 'fsdp', axis=0, tiled=True)  98.4 us
    all_gather x1, waiting for transfers between devices, local(): lax.all_gather(spread[6].astype(jnp.bfloat16), 'ctx', axis=0, tiled=True)  78.7 us
    all_gather x1, waiting for transfers between devices, local(): lax.all_gather(spread[7].astype(jnp.bfloat16), 'ctx', axis=0, tiled=True)  74.2 us
  transfers between devices with their start and end apart: 22, of which 18 were waited for; matrix products, arithmetic and copies ran while one was open for 7% of the time, Pallas kernels for 0%

commit v1 on v0

v1 whole, which is shorter than its diff:
```python
import math

import jax
import jax.numpy as jnp
from jax import lax
from jax.sharding import PartitionSpec as P

HEAD_SIZE = 64
EPSILON = 1e-05
THETA = 500000.0
MASKED = -1e30
CHUNKS = 2
F32 = jnp.float32
BF16 = jnp.bfloat16


def contract(left, right, left_dim, right_dim):
    return lax.dot_general(
        left, right, (((left_dim,), (right_dim,)), ((), ())), preferred_element_type=F32
    )


def rope_tables(row_start, row_count):
    position = (row_start + jnp.arange(row_count, dtype=jnp.int32)).astype(F32)
    exponent = jnp.arange(HEAD_SIZE // 2, dtype=jnp.int32).astype(F32) * (2.0 / HEAD_SIZE)
    angles = position[:, None] * jnp.power(THETA, -exponent)[None, :]
    return (jnp.cos(angles), jnp.sin(angles))


def apply_rotary(values, cosine_lookup, sine_lookup, direction):
    half_width = values.shape[-1] // 2
    leading = values[..., :half_width]
    trailing = values[..., half_width:]
    cos_wide = cosine_lookup[:, None, :]
    sin_wide = direction * sine_lookup[:, None, :]
    return jnp.concatenate(
        [leading * cos_wide - trailing * sin_wide, trailing * cos_wide + leading * sin_wide],
        axis=-1,
    )


def masked_scores(query_block, key_block, prefix_one, row_start):
    row_count = query_block.shape[0]
    length_total = key_block.shape[0]
    scores = jnp.einsum(
        "qkgd,pkd->kgqp", query_block, key_block, preferred_element_type=F32
    ) * (1.0 / math.sqrt(HEAD_SIZE))
    query_place = row_start + jnp.arange(row_count, dtype=jnp.int32)
    key_place = jnp.arange(length_total, dtype=jnp.int32)
    allowed = (key_place[None, :] <= query_place[:, None]) | (key_place[None, :] < prefix_one)
    return jnp.where(allowed, scores, MASKED)


def attend(query_block, key_block, value_block, prefix_one, row_start):
    scores = masked_scores(query_block, key_block, prefix_one, row_start)
    row_peak = jnp.max(scores, axis=-1, keepdims=True)
    weights = jnp.exp(scores - row_peak)
    row_total = jnp.sum(weights, axis=-1, keepdims=True)
    probabilities = (weights / row_total).astype(BF16)
    attended = jnp.einsum(
        "kgqp,pkd->qkgd", probabilities, value_block, preferred_element_type=F32
    )
    return (attended.astype(BF16), row_peak + jnp.log(row_total))


def attend_back(query_block, key_block, value_block, grad_block, log_total, prefix_one, row_start):
    scores = masked_scores(query_block, key_block, prefix_one, row_start)
    probabilities = jnp.exp(scores - log_total)
    rounded = probabilities.astype(BF16)
    grad_probs = jnp.einsum(
        "qkgd,pkd->kgqp", grad_block, value_block, preferred_element_type=F32
    )
    delta_rows = jnp.sum(probabilities * grad_probs, axis=-1, keepdims=True)
    grad_scores = (probabilities * (grad_probs - delta_rows)).astype(BF16)
    score_scale = 1.0 / math.sqrt(HEAD_SIZE)
    grad_queries = (
        jnp.einsum("kgqp,pkd->qkgd", grad_scores, key_block, preferred_element_type=F32)
        * score_scale
    )
    grad_keys = (
        jnp.einsum("kgqp,qkgd->pkd", grad_scores, query_block, preferred_element_type=F32)
        * score_scale
    )
    grad_values = jnp.einsum(
        "kgqp,qkgd->pkd", rounded, grad_block, preferred_element_type=F32
    )
    return (grad_queries, grad_keys, grad_values)


def make_local(ctx_size):
    swap_x = [(0, 1), (1, 0)]
    swap_z = [(i, i ^ 1) for i in range(ctx_size)]

    def swap_rows(array):
        return lax.ppermute(array, "fsdp", swap_x)

    def local(
        inputs, cotangent, prefix, attn_gain, w_query, key_projection, value_projection, w_out,
        ffn_gain, w_gate, w_up, w_down,
    ):
        side = lax.axis_index("fsdp")
        place = lax.axis_index("ctx")
        part = (place ^ (place >> 1)) & 1
        row_count, model_width = inputs.shape[1:]
        half_width = model_width // 2
        query_width = w_query.shape[1]
        key_width = key_projection.shape[1]
        ffn_width = w_gate.shape[1]
        ffn_half = ffn_width // 2
        chunk = ffn_half // CHUNKS
        query_heads = query_width // HEAD_SIZE
        kv_heads = key_width // HEAD_SIZE
        heads_per_group = query_heads // kv_heads
        row_start = place * row_count
        pair_start = (place // 2) * 2 * row_count

        def own_first(rows):
            a = lax.dynamic_slice_in_dim(rows, side * half_width, half_width, 1)
            b = lax.dynamic_slice_in_dim(rows, (1 - side) * half_width, half_width, 1)
            return jnp.concatenate([a, b], axis=1)

        gains = jnp.stack([attn_gain, ffn_gain])
        gains = jnp.concatenate([gains, swap_rows(gains)], axis=1).astype(F32)
        gain_first, gain_second = gains[0], gains[1]

        qkv_own = jnp.concatenate([w_query, key_projection, value_projection], axis=1)
        qkv_weight = jnp.concatenate([qkv_own, swap_rows(qkv_own)], axis=0)
        out_weight = jnp.concatenate([w_out, swap_rows(w_out)], axis=0)
        ffn_own = []
        for c in range(CHUNKS):
            start = part * ffn_half + c * chunk
            own = tuple(
                lax.dynamic_slice_in_dim(w, start, chunk, 1) for w in (w_gate, w_up, w_down)
            )
            ffn_own.append(own)
        ffn_weights = [
            tuple(jnp.concatenate([w, swap_rows(w)], axis=0) for w in own) for own in ffn_own
        ]

        cosine_lookup, sine_lookup = rope_tables(row_start, row_count)
        residual_low = own_first(inputs[0])
        cot_low = own_first(cotangent[0])
        cot_all = lax.all_gather(cot_low, "ctx", axis=0, tiled=True)
        residual = residual_low.astype(F32)
        rms_first = lax.rsqrt(jnp.mean(residual * residual, axis=-1, keepdims=True) + EPSILON)
        normalized_rows = (residual * rms_first * gain_first).astype(BF16)
        qkv = jnp.dot(normalized_rows, qkv_weight, preferred_element_type=F32)
        query_rot = apply_rotary(
            qkv[:, :query_width].reshape(row_count, query_heads, HEAD_SIZE),
            cosine_lookup, sine_lookup, 1.0,
        ).astype(BF16)
        key_rot = apply_rotary(
            qkv[:, query_width : query_width + key_width].reshape(row_count, kv_heads, HEAD_SIZE),
            cosine_lookup, sine_lookup, 1.0,
        ).astype(BF16).reshape(row_count, key_width)
        value_matrix = qkv[:, query_width + key_width :].astype(BF16)
        kv_whole = lax.all_gather(
            jnp.concatenate([key_rot, value_matrix], axis=1), "ctx", axis=0, tiled=True
        )
        length_total = kv_whole.shape[0]
        key_whole = kv_whole[:, :key_width].reshape(length_total, kv_heads, HEAD_SIZE)
        value_whole = kv_whole[:, key_width:].reshape(length_total, kv_heads, HEAD_SIZE)
        query_groups = query_rot.reshape(row_count, kv_heads, heads_per_group, HEAD_SIZE)
        prefix_one = prefix[0]
        attended, log_total = attend(query_groups, key_whole, value_whole, prefix_one, row_start)
        attended_flat = attended.reshape(row_count, query_width)
        attn_term = contract(attended_flat, out_weight, 1, 1)
        middle = residual + lax.psum(attn_term.astype(BF16), "tp").astype(F32)
        rms_second = lax.rsqrt(jnp.mean(middle * middle, axis=-1, keepdims=True) + EPSILON)
        normed_mid = (middle * rms_second * gain_second).astype(BF16)
        normed_all = lax.all_gather(normed_mid, "ctx", axis=0, tiled=True)

        ffn_term = 0.0
        mid_term = 0.0
        grads = []
        for c in range(CHUNKS):
            gate_w, up_w, down_w = ffn_weights[c]
            gating = jnp.dot(normed_all, gate_w, preferred_element_type=F32)
            upward = jnp.dot(normed_all, up_w, preferred_element_type=F32)
            grad_hidden = jnp.dot(cot_all, down_w, preferred_element_type=F32)
            sigmoid_gate = jax.nn.sigmoid(gating)
            hidden = (gating * sigmoid_gate * upward).astype(BF16)
            grad_gating = (
                grad_hidden * upward * sigmoid_gate * (1.0 + gating * (1.0 - sigmoid_gate))
            ).astype(BF16)
            grad_upward = (grad_hidden * gating * sigmoid_gate).astype(BF16)
            done = []
            for rows, cols in (
                (normed_all, grad_gating), (normed_all, grad_upward), (cot_all, hidden)
            ):
                far = contract(rows[:, half_width:], cols, 0, 0).astype(BF16)
                near = contract(rows[:, :half_width], cols, 0, 0)
                total = (near + swap_rows(far).astype(F32)).astype(BF16)
                done.append((total, lax.ppermute(total, "ctx", swap_z)))
            grads.append(done)

            def pair(rows):
                return lax.dynamic_slice_in_dim(rows, pair_start, 2 * row_count, 0)

            ffn_term += contract(pair(hidden), down_w, 1, 1)
            mid_term += contract(pair(grad_gating), gate_w, 1, 1) + contract(
                pair(grad_upward), up_w, 1, 1
            )

        def pair_reduce(term):
            lower = term[:row_count]
            upper = term[row_count:]
            low = (place % 2) == 0
            mine = jnp.where(low, lower, upper)
            theirs = jnp.where(low, upper, lower).astype(BF16)
            mine = mine + lax.ppermute(theirs, "ctx", swap_z).astype(F32)
            return lax.psum(mine.astype(BF16), "tp").astype(F32)

        grad_mid_norm = pair_reduce(mid_term)
        output_rows = (middle + pair_reduce(ffn_term)).astype(BF16)
        scaled_mid = grad_mid_norm * gain_second
        gain_grad_second = jnp.sum(grad_mid_norm * middle * rms_second, axis=0)
        cube_second = rms_second * rms_second * rms_second
        grad_middle = (
            cot_low.astype(F32)
            + rms_second * scaled_mid
            - middle * cube_second * jnp.mean(scaled_mid * middle, axis=-1, keepdims=True)
        )
        branch_low = grad_middle.astype(BF16)
        grad_out = contract(branch_low, attended_flat, 0, 0)
        grad_attended = jnp.dot(branch_low, out_weight, preferred_element_type=F32).astype(BF16)
        grad_attended = grad_attended.reshape(row_count, kv_heads, heads_per_group, HEAD_SIZE)
        grad_query_rot, grad_key_all, grad_value_all = attend_back(
            query_groups, key_whole, value_whole, grad_attended, log_total, prefix_one, row_start
        )
        grad_kv = jnp.concatenate(
            [
                grad_key_all.reshape(length_total, key_width),
                grad_value_all.reshape(length_total, key_width),
            ],
            axis=1,
        ).astype(BF16)
        grad_kv = lax.psum_scatter(grad_kv, "ctx", scatter_dimension=0, tiled=True).astype(F32)
        grad_query_pre = apply_rotary(
            grad_query_rot.reshape(row_count, query_heads, HEAD_SIZE),
            cosine_lookup, sine_lookup, -1.0,
        ).astype(BF16).reshape(row_count, query_width)
        grad_key_pre = apply_rotary(
            grad_kv[:, :key_width].reshape(row_count, kv_heads, HEAD_SIZE),
            cosine_lookup, sine_lookup, -1.0,
        ).astype(BF16).reshape(row_count, key_width)
        grad_value_pre = grad_kv[:, key_width:].astype(BF16)
        grad_qkv_pre = jnp.concatenate([grad_query_pre, grad_key_pre, grad_value_pre], axis=1)
        grad_qkv = contract(normalized_rows, grad_qkv_pre, 0, 0)
        grad_attn = jnp.concatenate([grad_qkv, grad_out], axis=1)
        grad_attn = grad_attn[:half_width] + swap_rows(grad_attn[half_width:].astype(BF16)).astype(
            F32
        )
        grad_attn = lax.psum(grad_attn.astype(BF16), "ctx").astype(F32)
        grad_normed = lax.psum(contract(grad_qkv_pre, qkv_weight, 1, 1).astype(BF16), "tp").astype(
            F32
        )
        scaled_first = grad_normed * gain_first
        gain_grad_first = jnp.sum(grad_normed * residual * rms_first, axis=0)
        cube_first = rms_first * rms_first * rms_first
        grad_full = (
            grad_middle
            + rms_first * scaled_first
            - residual * cube_first * jnp.mean(scaled_first * residual, axis=-1, keepdims=True)
        )
        gain_grads = jnp.stack([gain_grad_first, gain_grad_second])
        gain_grads = lax.psum(
            gain_grads[:, :half_width] + swap_rows(gain_grads[:, half_width:]), "ctx"
        )

        first_half = part == 0
        result = []
        for i in range(3):
            mine = jnp.concatenate([grads[c][i][0] for c in range(CHUNKS)], axis=1)
            other = jnp.concatenate([grads[c][i][1] for c in range(CHUNKS)], axis=1)
            result.append(
                jnp.concatenate(
                    [jnp.where(first_half, mine, other), jnp.where(first_half, other, mine)],
                    axis=1,
                ).astype(F32)
            )
        end_key = query_width + key_width
        end_value = end_key + key_width
        return (
            own_first(output_rows)[None],
            own_first(grad_full.astype(BF16))[None],
            gain_grads[0],
            grad_attn[:, :query_width],
            grad_attn[:, query_width:end_key],
            grad_attn[:, end_key:end_value],
            grad_attn[:, end_value:],
            gain_grads[1],
            result[0],
            result[1],
            result[2],
        )

    return local


def solution(mesh):
    return jax.shard_map(
        make_local(mesh.shape["ctx"]),
        mesh=mesh,
        in_specs=(
            P("fsdp", "ctx", None), P("fsdp", "ctx", None), P("fsdp"), P("fsdp"),
            P("fsdp", "tp"), P("fsdp", "tp"), P("fsdp", "tp"), P("fsdp", "tp"),
            P("fsdp"), P("fsdp", "tp"), P("fsdp", "tp"), P("fsdp", "tp"),
        ),
        out_specs=(
            P("fsdp", "ctx", None), P("fsdp", "ctx", None), P("fsdp"), P("fsdp", "tp"),
            P("fsdp", "tp"), P("fsdp", "tp"), P("fsdp", "tp"), P("fsdp"),
            P("fsdp", "tp"), P("fsdp", "tp"), P("fsdp", "tp"),
        ),
        check_vma=False,
    )
```

time: 1660 us -> 752 us (0.45)
  waiting for transfers between devices: 1340 us -> 413 us
  blocking collectives: 130 us -> 28.1 us
  local copies, waits for them, and re-layouts: 18.7 us -> 80.5 us
  starting transfers between devices: 1.5 us -> 27.9 us
  other arithmetic: 39.9 us -> 60.3 us
    reduce_scatter x9 -> x1, waiting for transfers between devices: 660 us -> 15 us  [local(): lax.psum_scatter(grad_kv, 'ctx', scatter_dimension=0, tiled=True)]
    all_gather x10 -> x2, waiting for transfers between devices: 555 us -> 86.4 us  [the longest x1 73.3 us: local(): normed_all = lax.all_gather(normed_mid, 'ctx', axis=0, tiled=True)]
    ppermute x0 -> x25, waiting for transfers between devices: none -> 175 us  [the longest x17 175 us: swap_rows(): return lax.ppermute(array, 'fsdp', swap_x)]
    all_gather x10 -> x1, blocking collectives: 108 us -> 15.4 us  [local(): lax.all_gather(jnp.concatenate([key_rot, value_matrix], axis=1), 'ctx', a...]
    unnamed x102 -> x147, local copies, waits for them, and re-layouts: 13.3 us -> 52.2 us
    ppermute x0 -> x25, starting transfers between devices: none -> 27.2 us  [the longest x17 22.7 us: swap_rows(): return lax.ppermute(array, 'fsdp', swap_x)]
    unnamed x1 -> x0, blocking collectives: 21.9 us -> none
    psum x3 -> x4, waiting for transfers between devices: 118 us -> 137 us  [the longest x1 85.4 us: local(): grad_attn = lax.psum(grad_attn.astype(BF16), 'ctx').astype(F32)]
  transfers between devices with their start and end apart: 22 -> 32, of which waited for: 18 -> 17; matrix products, arithmetic and copies ran while one was open for 7% -> 27% of each run, Pallas kernels for 0% -> 0%
where the time goes in v1:
time: 752 us; the launch traced here: 743 us
  waiting for transfers between devices  413 us (55%)
  matrix products  116 us (15%)
  local copies, waits for them, and re-layouts  80.5 us (11%)
  other arithmetic  60.3 us (8%)
  blocking collectives  28.1 us (4%)
  starting transfers between devices  27.9 us (4%)
  between operations  17.6 us (2%)
    ppermute x17, waiting for transfers between devices, swap_rows(): return lax.ppermute(array, 'fsdp', swap_x)  175 us
    psum x1, waiting for transfers between devices, local(): grad_attn = lax.psum(grad_attn.astype(BF16), 'ctx').astype(F32)  85.4 us
    all_gather x1, waiting for transfers between devices, local(): normed_all = lax.all_gather(normed_mid, 'ctx', axis=0, tiled=True)  73.3 us
    dot_general x22, matrix products, contract(): lax.dot_general(left, right, (((left_dim,), (right_dim,)), ((), ())), pre...  62.3 us
    unnamed x147, local copies, waits for them, and re-layouts  52.2 us
    psum x1, waiting for transfers between devices, local(): middle = residual + lax.psum(attn_term.astype(BF16), 'tp').astype(F32)  35.1 us
    ppermute x17, starting transfers between devices, swap_rows(): return lax.ppermute(array, 'fsdp', swap_x)  22.7 us
    psum x2, waiting for transfers between devices, pair_reduce(): return lax.psum(mine.astype(BF16), 'tp').astype(F32)  16.4 us
  transfers between devices with their start and end apart: 32, of which 17 were waited for; matrix products, arithmetic and copies ran while one was open for 27% of the time, Pallas kernels for 0%

profile of v1, /device:TPU:0, one launch (start us, length us, event | category | flops | bytes accessed | tf_op | source)
XLA Modules:
  0.0 743.2 jit_solution(14289029340147096593)
XLA Ops:
  8.1 2.4 constant_dynamic-update-slice_fusion.2
  12.0 3.0 collective-permute-start.1
  21.8 28.7 %collective-permute-done = bf16[2,1024]{1,0:T(2,128)(2,1)S(1)} collective-permute-done((bf16[2,1024]{1,0:T(2,128)(2,1)S(1)}, bf16[2,1024]{1,0:T(2,128)(2,1)S(1)}, u32[]{:S(2)}, u32[]{:S(2)}) %collective-permute-start) | collective-permute-done | bytes 4128 | tf_op jit(solution)/shard_map/ppermute | solution.py:95
  50.6 21.7 %collective-permute-done.2 = bf16[1024,512]{1,0:T(8,128)(2,1)} collective-permute-done((bf16[1024,512]{1,0:T(8,128)(2,1)}, bf16[1024,512]{1,0:T(8,128)(2,1)}, u32[]{:S(2)}, u32[]{:S(2)}) %collective-permute-start.2) | collective-permute-done | bytes 1048608 | tf_op jit(solution)/shard_map/ppermute | solution.py:95
  73.6 3.6 fusion.31
  78.4 15.4 %all_gather.9 = bf16[1024,256]{1,0:T(8,128)(2,1)S(1)} all-gather(bf16[256,256]{1,0:T(8,128)(2,1)S(1)} %pad_maximum_fusion.35), channel_id=1, replica_groups=mesh['fsdp'=2,'ctx'=4,'tp'=4] {'ctx'}, dimensions={0}, use_global_device_ids=true | all-gather | bytes 655360 | tf_op jit(solution)/shard_map/all_gather | solution.py:157
  99.8 2.4 fusion.134
  113.1 35.1 %all-reduce.6.cloned.1.call-done = bf16[256,2048]{1,0:T(8,128)(2,1)} async-done(((bf16[256,2048]{1,0:T(8,128)(2,1)}), bf16[256,2048]{1,0:T(8,128)(2,1)}) %all-reduce.6.cloned.1.call-update) | async-done | bytes 1048592 | tf_op jit(solution)/shard_map/psum | solution.py:168
  151.7 2.8 constant_dynamic-slice_fusion.7
  163.2 17.7 %collective-permute-done.8 = bf16[1024,512]{1,0:T(8,128)(2,1)} collective-permute-done((bf16[1024,512]{1,0:T(8,128)(2,1)}, bf16[1024,512]{1,0:T(8,128)(2,1)}, u32[]{:S(2)}, u32[]{:S(2)}) %collective-permute-start.8) | collective-permute-done | bytes 1048608 | tf_op jit(solution)/shard_map/ppermute | solution.py:95
  182.3 13.2 %all-gather.5.cloned.1.call-done = bf16[1024,2048]{1,0:T(8,128)(2,1)} async-done(((bf16[256,2048]{1,0:T(8,128)(2,1)}), bf16[1024,2048]{1,0:T(8,128)(2,1)}) %all-gather.5.cloned.1.call-update) | async-done | bytes 4194320 | tf_op jit(solution)/shard_map/all_gather | solution.py:143
  195.5 6.4 fusion.50
  203.3 73.3 %all-gather.3.cloned.1.call-done = bf16[1024,2048]{1,0:T(8,128)(2,1)} async-done(((bf16[256,2048]{1,0:T(8,128)(2,1)}), bf16[1024,2048]{1,0:T(8,128)(2,1)}) %all-gather.3.cloned.1.call-update) | async-done | bytes 4194320 | tf_op jit(solution)/shard_map/all_gather | solution.py:171
  276.6 5.3 fusion.53
  281.9 4.8 multiply_convert_fusion.1
  286.7 3.9 fusion.52
  290.7 3.9 fusion.59
  294.6 4.0 fusion.57
  298.7 4.9 multiply_convert_fusion.2
  303.6 3.9 fusion.58
  307.5 2.8 fusion.56
  310.4 2.9 add_add_fusion
  313.5 2.8 fusion.51
  316.4 2.7 convolution_add_fusion
  326.2 2.3 convolution_convert_fusion.4
  329.1 2.3 convolution_convert_fusion.3
  332.8 2.3 convolution_convert_fusion.2
  335.1 2.4 fusion.40
  337.6 2.3 fusion.43
  342.6 8.4 %collective-permute-done.13 = bf16[1024,512]{0,1:T(8,128)(2,1)} collective-permute-done((bf16[1024,512]{0,1:T(8,128)(2,1)}, bf16[1024,512]{0,1:T(8,128)(2,1)}, u32[]{:S(2)}, u32[]{:S(2)}) %collective-permute-start.13) | collective-permute-done | bytes 1048608 | tf_op jit(solution)/shard_map/ppermute | solution.py:95
  352.5 4.5 add_convert_fusion.5
  357.1 16.5 %collective-permute-done.14 = bf16[1024,512]{0,1:T(8,128)(2,1)} collective-permute-done((bf16[1024,512]{0,1:T(8,128)(2,1)}, bf16[1024,512]{0,1:T(8,128)(2,1)}, u32[]{:S(2)}, u32[]{:S(2)}) %collective-permute-start.14) | collective-permute-done | bytes 1048608 | tf_op jit(solution)/shard_map/ppermute | solution.py:95
  375.0 3.5 add_convert_fusion.4
  378.5 17.5 %collective-permute-done.17 = bf16[1024,512]{0,1:T(8,128)(2,1)} collective-permute-done((bf16[1024,512]{0,1:T(8,128)(2,1)}, bf16[1024,512]{0,1:T(8,128)(2,1)}, u32[]{:S(2)}, u32[]{:S(2)}) %collective-permute-start.17) | collective-permute-done | bytes 1048608 | tf_op jit(solution)/shard_map/ppermute | solution.py:95
  396.0 3.5 add_convert_fusion.3
  399.6 18.9 %collective-permute-done.18 = bf16[1024,512]{0,1:T(8,128)(2,1)} collective-permute-done((bf16[1024,512]{0,1:T(8,128)(2,1)}, bf16[1024,512]{0,1:T(8,128)(2,1)}, u32[]{:S(2)}, u32[]{:S(2)}) %collective-permute-start.18) | collective-permute-done | bytes 1048608 | tf_op jit(solution)/shard_map/ppermute | solution.py:95
  418.5 3.6 add_convert_fusion.2
  422.1 18.7 %collective-permute-done.21 = bf16[1024,512]{0,1:T(8,128)(2,1)S(1)} collective-permute-done((bf16[1024,512]{0,1:T(8,128)(2,1)}, bf16[1024,512]{0,1:T(8,128)(2,1)S(1)}, u32[]{:S(2)}, u32[]{:S(2)}) %collective-permute-start.21) | collective-permute-done | bytes 1048608 | tf_op jit(solution)/shard_map/ppermute | solution.py:95
  440.9 2.3 add_convert_fusion.1
  443.2 18.3 %collective-permute-done.22 = bf16[1024,512]{0,1:T(8,128)(2,1)S(1)} collective-permute-done((bf16[1024,512]{0,1:T(8,128)(2,1)S(1)}, bf16[1024,512]{0,1:T(8,128)(2,1)S(1)}, u32[]{:S(2)}, u32[]{:S(2)}) %collective-permute-start.22) | collective-permute-done | bytes 1048608 | tf_op jit(solution)/shard_map/ppermute | solution.py:95
  461.8 2.3 add_convert_fusion
  467.4 2.7 fusion.23
  474.3 4.9 fusion.84
  479.2 5.6 fusion
  489.6 3.1 convolution_multiply_fusion
  492.8 2.8 fusion.90
  500.4 15.0 %reduce-scatter.2.cloned.1.call-done = bf16[256,256]{0,1:T(8,128)(2,1)} async-done(((bf16[1024,256]{0,1:T(8,128)(2,1)}), bf16[256,256]{0,1:T(8,128)(2,1)}) %reduce-scatter.2.cloned.1.call-update) | async-done | bytes 131088 | tf_op jit(solution)/shard_map/reduce_scatter | solution.py:238
  523.4 3.4 broadcast_select_fusion.5
  526.8 4.5 maximum_convert_fusion
  531.3 9.1 %copy.72 = f32[1024,2048]{1,0:T(8,128)} copy(f32[1024,2048]{0,1:T(8,128)} %maximum_convert_fusion) | data formatting | bytes 16777216
  543.0 2.8 broadcast_select_fusion.3
  545.8 4.5 maximum_convert_fusion.1
  550.3 9.1 %copy.73 = f32[1024,2048]{1,0:T(8,128)} copy(f32[1024,2048]{0,1:T(8,128)} %maximum_convert_fusion.1) | data formatting | bytes 16777216
  564.0 3.9 convolution_convert_fusion.1
  568.2 5.6 broadcast_select_fusion.1
  573.8 7.0 collective-permute-done.12
  580.8 4.3 fusion.7
  585.1 6.7 maximum_convert_fusion.2
  591.8 9.2 %copy.74 = f32[1024,2048]{1,0:T(8,128)} copy(f32[1024,2048]{0,1:T(8,128)} %maximum_convert_fusion.2) | data formatting | bytes 16777216
  601.0 16.4 %all-reduce.12.cloned.1.call-done = (bf16[256,2048]{1,0:T(8,128)(2,1)}, bf16[256,2048]{1,0:T(8,128)(2,1)}) async-done(((bf16[256,2048]{1,0:T(8,128)(2,1)}, bf16[256,2048]{1,0:T(8,128)(2,1)}), (bf16[256,2048]{1,0:T(8,128)(2,1)}, bf16[256,2048]{1,0:T(8,128)(2,1)})) %all-reduce.12.cloned.1.call-update) | async-done | bytes 2097168 | tf_op jit(solution)/shard_map/psum | solution.py:212
  625.6 12.7 %psum.46 = f32[2,1024]{1,0:T(2,128)S(1)} all-reduce(f32[2,1024]{1,0:T(2,128)S(1)} %fusion.103), channel_id=1, replica_groups=mesh['fsdp'=2,'ctx'=4,'tp'=4] {'ctx'}, use_global_device_ids=true, to_apply=%region_14.15 | all-reduce | flops 2048 | bytes 16384 | tf_op jit(solution)/shard_map/psum | solution.py:267
  638.9 85.4 %all-reduce.10.cloned.1.call-done = bf16[1024,1280]{0,1:T(8,128)(2,1)} async-done(((bf16[1024,1280]{0,1:T(8,128)(2,1)}), bf16[1024,1280]{0,1:T(8,128)(2,1)}) %all-reduce.10.cloned.1.call-update) | async-done | bytes 2621456 | tf_op jit(solution)/shard_map/psum | solution.py:254
  724.3 3.3 fusion.128
  727.6 2.9 copy.68
  (270 shorter events, 103.5 us)
Async XLA Ops:
  8.0 6.9 copy-start.56
  8.0 6.9 copy-start.57
  8.1 9.1 %copy-start.26 = (bf16[1,256,2048]{2,1,0:T(8,128)(2,1)S(1)}, bf16[1,256,2048]{2,1,0:T(8,128)(2,1)}, u32[]{:S(2)}) copy-start(bf16[1,256,2048]{2,1,0:T(8,128)(2,1)} %param.12) | copy-start | bytes 3145732
  8.1 140.1 %all-reduce.6.cloned.1.call-start = ((), (), s32[]{:S(2)}) async-start(), calls=%async_computation.1 | async-start | bytes 2097152 | tf_op jit(solution)/shard_map/psum | solution.py:168
  12.0 61.5 %collective-permute-start.1 = (bf16[1024,768]{1,0:T(8,128)(2,1)}, bf16[1024,768]{1,0:T(8,128)(2,1)}, u32[]{:S(2)}, u32[]{:S(2)}) collective-permute-start(bf16[1024,768]{1,0:T(8,128)(2,1)} %constant_dynamic-update-slice_fusion), channel_id=1, source_target_pairs={{0,16},{16,0},{1,17},{17,1},{2,18},{18,2},{3,19},{19,3},{4,20},{20... | collective-permute-start | bytes 4718600 | tf_op jit(solution)/shard_map/ppermute | solution.py:95
  15.0 35.5 %collective-permute-start = (bf16[2,1024]{1,0:T(2,128)(2,1)S(1)}, bf16[2,1024]{1,0:T(2,128)(2,1)S(1)}, u32[]{:S(2)}, u32[]{:S(2)}) collective-permute-start(bf16[2,1024]{1,0:T(2,128)(2,1)S(1)} %pad_maximum_fusion.39), channel_id=1, source_target_pairs={{0,16},{16,0},{1,17},{17,1},{2,18},{18,2},{3,19},{19,3},{4,20},{20... | collective-permute-start | bytes 12296 | tf_op jit(solution)/shard_map/ppermute | solution.py:95
  15.1 57.1 %collective-permute-start.2 = (bf16[1024,512]{1,0:T(8,128)(2,1)}, bf16[1024,512]{1,0:T(8,128)(2,1)}, u32[]{:S(2)}, u32[]{:S(2)}) collective-permute-start(bf16[1024,512]{1,0:T(8,128)(2,1)} %param.19), channel_id=1, source_target_pairs={{0,16},{16,0},{1,17},{17,1},{2,18},{18,2},{3,19},{19,3},{4,20},{20... | collective-permute-start | bytes 3145736 | tf_op jit(solution)/shard_map/ppermute | solution.py:95
  18.1 55.5 %copy-start.53 = (f32[256]{0:T(256)}, f32[256]{0:T(256)S(1)}, u32[]{:S(2)}) copy-start(f32[256]{0:T(256)S(1)} %get-tuple-element.91) | copy-start | bytes 3076
  19.6 58.7 %copy-start.29 = (f32[256,32]{0,1:T(8,128)}, f32[256,32]{0,1:T(8,128)S(1)}, u32[]{:S(2)}) copy-start(f32[256,32]{0,1:T(8,128)S(1)} %get-tuple-element.89) | copy-start | bytes 98308
  19.6 58.7 %copy-start.32 = (f32[256,32]{0,1:T(8,128)}, f32[256,32]{0,1:T(8,128)S(1)}, u32[]{:S(2)}) copy-start(f32[256,32]{0,1:T(8,128)S(1)} %get-tuple-element.88) | copy-start | bytes 98308
  50.6 23.0 %copy-start.46 = (f32[1,2048]{1,0:T(1,128)}, f32[1,2048]{1,0:T(1,128)S(1)}, u32[]{:S(2)}) copy-start(f32[1,2048]{1,0:T(1,128)S(1)} %get-tuple-element.84) | copy-start | bytes 24580
  73.5 33.7 %copy-start.10 = (bf16[2048,512]{1,0:T(8,128)(2,1)}, bf16[2048,512]{1,0:T(8,128)(2,1)S(1)}, u32[]{:S(2)}) copy-start(bf16[2048,512]{1,0:T(8,128)(2,1)S(1)} %constant_dynamic-update-slice_fusion.3) | copy-start | bytes 6291460
  96.5 5.7 copy-start.18
  109.6 85.9 %all-gather.5.cloned.1.call-start = ((), (), s32[]{:S(2)}) async-start(), calls=%async_computation.3 | async-start | bytes 5242880 | tf_op jit(solution)/shard_map/all_gather | solution.py:143
  113.0 163.6 %all-gather.3.cloned.1.call-start = ((), (), s32[]{:S(2)}) async-start(), calls=%async_computation.2 | async-start | bytes 5242880 | tf_op jit(solution)/shard_map/all_gather | solution.py:171
  151.4 316.0 %all-reduce.8.cloned.1.call-start = ((), (), s32[]{:S(2)}) async-start(), calls=%async_computation.4 | async-start | bytes 2097152 | tf_op jit(solution)/shard_map/psum | solution.py:212
  154.5 26.3 %collective-permute-start.8 = (bf16[1024,512]{1,0:T(8,128)(2,1)}, bf16[1024,512]{1,0:T(8,128)(2,1)}, u32[]{:S(2)}, u32[]{:S(2)}) collective-permute-start(bf16[1024,512]{1,0:T(8,128)(2,1)} %get-tuple-element.56), channel_id=1, source_target_pairs={{0,16},{16,0},{1,17},{17,1},{2,18},{18,2},{3,19},{19,3},{4,20},{20... | collective-permute-start | bytes 3145736 | tf_op jit(solution)/shard_map/ppermute | solution.py:95
  157.6 5.6 copy-start.50
  157.6 5.6 copy-start.52
  157.6 45.8 %collective-permute-start.7 = (bf16[1024,512]{1,0:T(8,128)(2,1)}, bf16[1024,512]{1,0:T(8,128)(2,1)}, u32[]{:S(2)}, u32[]{:S(2)}) collective-permute-start(bf16[1024,512]{1,0:T(8,128)(2,1)} %get-tuple-element.54), channel_id=1, source_target_pairs={{0,16},{16,0},{1,17},{17,1},{2,18},{18,2},{3,19},{19,3},{4,20},{20... | collective-permute-start | bytes 3145736 | tf_op jit(solution)/shard_map/ppermute | solution.py:95
  159.7 122.2 %collective-permute-start.6 = (bf16[1024,512]{1,0:T(8,128)(2,1)}, bf16[1024,512]{1,0:T(8,128)(2,1)}, u32[]{:S(2)}, u32[]{:S(2)}) collective-permute-start(bf16[1024,512]{1,0:T(8,128)(2,1)} %get-tuple-element.52), channel_id=1, source_target_pairs={{0,16},{16,0},{1,17},{17,1},{2,18},{18,2},{3,19},{19,3},{4,20},{20... | collective-permute-start | bytes 3145736 | tf_op jit(solution)/shard_map/ppermute | solution.py:95
  161.2 129.5 %collective-permute-start.3 = (bf16[1024,512]{1,0:T(8,128)(2,1)}, bf16[1024,512]{1,0:T(8,128)(2,1)}, u32[]{:S(2)}, u32[]{:S(2)}) collective-permute-start(bf16[1024,512]{1,0:T(8,128)(2,1)} %get-tuple-element.51), channel_id=1, source_target_pairs={{0,16},{16,0},{1,17},{17,1},{2,18},{18,2},{3,19},{19,3},{4,20},{20... | collective-permute-start | bytes 3145736 | tf_op jit(solution)/shard_map/ppermute | solution.py:95
  161.7 132.9 %collective-permute-start.4 = (bf16[1024,512]{1,0:T(8,128)(2,1)}, bf16[1024,512]{1,0:T(8,128)(2,1)}, u32[]{:S(2)}, u32[]{:S(2)}) collective-permute-start(bf16[1024,512]{1,0:T(8,128)(2,1)} %get-tuple-element.53), channel_id=1, source_target_pairs={{0,16},{16,0},{1,17},{17,1},{2,18},{18,2},{3,19},{19,3},{4,20},{20... | collective-permute-start | bytes 3145736 | tf_op jit(solution)/shard_map/ppermute | solution.py:95
  180.9 117.8 %collective-permute-start.5 = (bf16[1024,512]{1,0:T(8,128)(2,1)S(1)}, bf16[1024,512]{1,0:T(8,128)(2,1)}, u32[]{:S(2)}, u32[]{:S(2)}) collective-permute-start(bf16[1024,512]{1,0:T(8,128)(2,1)S(1)} %get-tuple-element.55), channel_id=1, source_target_pairs={{0,16},{16,0},{1,17},{17,1},{2,18},{18,2},{3,19},{19,3},{4,20},{20... | collective-permute-start | bytes 3145736 | tf_op jit(solution)/shard_map/ppermute | solution.py:95
  286.7 39.5 %copy-start.35 = (bf16[1024,512]{1,0:T(8,128)(2,1)}, bf16[1024,512]{1,0:T(8,128)(2,1)S(1)}, u32[]{:S(2)}) copy-start(bf16[1024,512]{1,0:T(8,128)(2,1)S(1)} %get-tuple-element.45) | copy-start | bytes 3145732
  286.7 46.1 %copy-start.41 = (bf16[1024,512]{1,0:T(8,128)(2,1)}, bf16[1024,512]{1,0:T(8,128)(2,1)S(1)}, u32[]{:S(2)}) copy-start(bf16[1024,512]{1,0:T(8,128)(2,1)S(1)} %get-tuple-element.47) | copy-start | bytes 3145732
  286.7 50.8 %copy-start.39 = (bf16[1024,512]{1,0:T(8,128)(2,1)}, bf16[1024,512]{1,0:T(8,128)(2,1)S(1)}, u32[]{:S(2)}) copy-start(bf16[1024,512]{1,0:T(8,128)(2,1)S(1)} %get-tuple-element.46) | copy-start | bytes 3145732
  303.6 18.9 %copy-start.45 = (bf16[1024,512]{1,0:T(8,128)(2,1)}, bf16[1024,512]{1,0:T(8,128)(2,1)S(1)}, u32[]{:S(2)}) copy-start(bf16[1024,512]{1,0:T(8,128)(2,1)S(1)} %get-tuple-element.49) | copy-start | bytes 3145732
  303.6 25.5 %copy-start.43 = (bf16[1024,512]{1,0:T(8,128)(2,1)}, bf16[1024,512]{1,0:T(8,128)(2,1)S(1)}, u32[]{:S(2)}) copy-start(bf16[1024,512]{1,0:T(8,128)(2,1)S(1)} %get-tuple-element.48) | copy-start | bytes 3145732
  303.6 31.6 %copy-start.33 = (bf16[1024,512]{1,0:T(8,128)(2,1)}, bf16[1024,512]{1,0:T(8,128)(2,1)S(1)}, u32[]{:S(2)}) copy-start(bf16[1024,512]{1,0:T(8,128)(2,1)S(1)} %get-tuple-element.50) | copy-start | bytes 3145732
  313.5 26.4 %collective-permute-start.10 = (bf16[256,2048]{1,0:T(8,128)(2,1)S(1)}, bf16[256,2048]{1,0:T(8,128)(2,1)S(1)}, u32[]{:S(2)}, u32[]{:S(2)}) collective-permute-start(bf16[256,2048]{1,0:T(8,128)(2,1)S(1)} %select_convert_fusion), channel_id=1, source_target_pairs={{0,4},{4,0},{8,12},{12,8},{1,5},{5,1},{9,13},{13,9},{2,6},{6,2},{1... | collective-permute-start | bytes 3145736 | tf_op jit(solution)/shard_map/ppermute | solution.py:211
  316.4 6.1 copy-start.61
  320.4 143.7 %collective-permute-start.9 = (bf16[256,2048]{1,0:T(8,128)(2,1)}, bf16[256,2048]{1,0:T(8,128)(2,1)S(1)}, u32[]{:S(2)}, u32[]{:S(2)}) collective-permute-start(bf16[256,2048]{1,0:T(8,128)(2,1)} %select_convert_fusion.1), channel_id=1, source_target_pairs={{0,4},{4,0},{8,12},{12,8},{1,5},{5,1},{9,13},{13,9},{2,6},{6,2},{1... | collective-permute-start | bytes 3145736 | tf_op jit(solution)/shard_map/ppermute | solution.py:211
  324.7 26.3 %collective-permute-start.13 = (bf16[1024,512]{0,1:T(8,128)(2,1)}, bf16[1024,512]{0,1:T(8,128)(2,1)}, u32[]{:S(2)}, u32[]{:S(2)}) collective-permute-start(bf16[1024,512]{0,1:T(8,128)(2,1)} %convolution_convert_fusion.5), channel_id=1, source_target_pairs={{0,16},{16,0},{1,17},{17,1},{2,18},{18,2},{3,19},{19,3},{4,20},{20... | collective-permute-start | bytes 3145736 | tf_op jit(solution)/shard_map/ppermute | solution.py:95
  328.5 45.0 %collective-permute-start.14 = (bf16[1024,512]{0,1:T(8,128)(2,1)}, bf16[1024,512]{0,1:T(8,128)(2,1)}, u32[]{:S(2)}, u32[]{:S(2)}) collective-permute-start(bf16[1024,512]{0,1:T(8,128)(2,1)} %convolution_convert_fusion.4), channel_id=1, source_target_pairs={{0,16},{16,0},{1,17},{17,1},{2,18},{18,2},{3,19},{19,3},{4,20},{20... | collective-permute-start | bytes 3145736 | tf_op jit(solution)/shard_map/ppermute | solution.py:95
  331.3 64.7 %collective-permute-start.17 = (bf16[1024,512]{0,1:T(8,128)(2,1)}, bf16[1024,512]{0,1:T(8,128)(2,1)}, u32[]{:S(2)}, u32[]{:S(2)}) collective-permute-start(bf16[1024,512]{0,1:T(8,128)(2,1)} %convolution_convert_fusion.3), channel_id=1, source_target_pairs={{0,16},{16,0},{1,17},{17,1},{2,18},{18,2},{3,19},{19,3},{4,20},{20... | collective-permute-start | bytes 3145736 | tf_op jit(solution)/shard_map/ppermute | solution.py:95
  339.8 78.6 %collective-permute-start.18 = (bf16[1024,512]{0,1:T(8,128)(2,1)}, bf16[1024,512]{0,1:T(8,128)(2,1)}, u32[]{:S(2)}, u32[]{:S(2)}) collective-permute-start(bf16[1024,512]{0,1:T(8,128)(2,1)} %convolution_convert_fusion.2), channel_id=1, source_target_pairs={{0,16},{16,0},{1,17},{17,1},{2,18},{18,2},{3,19},{19,3},{4,20},{20... | collective-permute-start | bytes 3145736 | tf_op jit(solution)/shard_map/ppermute | solution.py:95
  342.5 172.9 %reduce-scatter.2.cloned.1.call-start = ((), (), s32[]{:S(2)}) async-start(), calls=%async_computation.5 | async-start | bytes 655360 | tf_op jit(solution)/shard_map/reduce_scatter | solution.py:238
  342.6 30.9 %copy-start.63 = (bf16[1024,512]{0,1:T(8,128)(2,1)S(1)}, bf16[1024,512]{0,1:T(8,128)(2,1)}, u32[]{:S(2)}) copy-start(bf16[1024,512]{0,1:T(8,128)(2,1)} %fusion.43) | copy-start | bytes 3145732
  342.6 32.4 %copy-start.36 = (bf16[1024,512]{1,0:T(8,128)(2,1)S(1)}, bf16[1024,512]{1,0:T(8,128)(2,1)}, u32[]{:S(2)}) copy-start(bf16[1024,512]{1,0:T(8,128)(2,1)} %copy-done.35) | copy-start | bytes 3145732
  342.6 32.4 %copy-start.62 = (bf16[1024,2048]{1,0:T(8,128)(2,1)S(1)}, bf16[1024,2048]{1,0:T(8,128)(2,1)}, u32[]{:S(2)}) copy-start(bf16[1024,2048]{1,0:T(8,128)(2,1)} %all-gather.3.cloned.1.call-done) | copy-start | bytes 12582916
  351.1 89.8 %collective-permute-start.21 = (bf16[1024,512]{0,1:T(8,128)(2,1)}, bf16[1024,512]{0,1:T(8,128)(2,1)S(1)}, u32[]{:S(2)}, u32[]{:S(2)}) collective-permute-start(bf16[1024,512]{0,1:T(8,128)(2,1)} %fusion.40), channel_id=1, source_target_pairs={{0,16},{16,0},{1,17},{17,1},{2,18},{18,2},{3,19},{19,3},{4,20},{20... | collective-permute-start | bytes 3145736 | tf_op jit(solution)/shard_map/ppermute | solution.py:95
  357.1 39.0 %copy-start.44 = (bf16[1024,512]{1,0:T(8,128)(2,1)S(1)}, bf16[1024,512]{1,0:T(8,128)(2,1)}, u32[]{:S(2)}) copy-start(bf16[1024,512]{1,0:T(8,128)(2,1)} %copy-done.43) | copy-start | bytes 3145732
  373.5 87.9 %collective-permute-start.22 = (bf16[1024,512]{0,1:T(8,128)(2,1)S(1)}, bf16[1024,512]{0,1:T(8,128)(2,1)S(1)}, u32[]{:S(2)}, u32[]{:S(2)}) collective-permute-start(bf16[1024,512]{0,1:T(8,128)(2,1)S(1)} %copy-done.63), channel_id=1, source_target_pairs={{0,16},{16,0},{1,17},{17,1},{2,18},{18,2},{3,19},{19,3},{4,20},{20... | collective-permute-start | bytes 3145736 | tf_op jit(solution)/shard_map/ppermute | solution.py:95
  378.5 40.0 %copy-start.42 = (bf16[1024,512]{1,0:T(8,128)(2,1)S(1)}, bf16[1024,512]{1,0:T(8,128)(2,1)}, u32[]{:S(2)}) copy-start(bf16[1024,512]{1,0:T(8,128)(2,1)} %copy-done.41) | copy-start | bytes 3145732
  396.0 99.6 %collective-permute-start.15 = (bf16[1024,512]{0,1:T(8,128)(2,1)}, bf16[1024,512]{0,1:T(8,128)(2,1)}, u32[]{:S(2)}, u32[]{:S(2)}) collective-permute-start(bf16[1024,512]{0,1:T(8,128)(2,1)} %add_convert_fusion.5), channel_id=1, source_target_pairs={{0,4},{4,0},{8,12},{12,8},{1,5},{5,1},{9,13},{13,9},{2,6},{6,2},{1... | collective-permute-start | bytes 3145736 | tf_op jit(solution)/shard_map/ppermute | solution.py:194
  399.6 41.3 %copy-start.34 = (bf16[1024,512]{1,0:T(8,128)(2,1)S(1)}, bf16[1024,512]{1,0:T(8,128)(2,1)}, u32[]{:S(2)}) copy-start(bf16[1024,512]{1,0:T(8,128)(2,1)} %copy-done.33) | copy-start | bytes 3145732
  399.6 41.3 %copy-start.59 = (bf16[1024,2048]{1,0:T(8,128)(2,1)S(1)}, bf16[1024,2048]{1,0:T(8,128)(2,1)}, u32[]{:S(2)}) copy-start(bf16[1024,2048]{1,0:T(8,128)(2,1)} %all-gather.5.cloned.1.call-done) | copy-start | bytes 12582916
  418.5 79.7 %collective-permute-start.16 = (bf16[1024,512]{0,1:T(8,128)(2,1)}, bf16[1024,512]{0,1:T(8,128)(2,1)}, u32[]{:S(2)}, u32[]{:S(2)}) collective-permute-start(bf16[1024,512]{0,1:T(8,128)(2,1)} %add_convert_fusion.4), channel_id=1, source_target_pairs={{0,4},{4,0},{8,12},{12,8},{1,5},{5,1},{9,13},{13,9},{2,6},{6,2},{1... | collective-permute-start | bytes 3145736 | tf_op jit(solution)/shard_map/ppermute | solution.py:194
  422.1 39.7 %copy-start.40 = (bf16[1024,512]{1,0:T(8,128)(2,1)S(1)}, bf16[1024,512]{1,0:T(8,128)(2,1)}, u32[]{:S(2)}) copy-start(bf16[1024,512]{1,0:T(8,128)(2,1)} %copy-done.39) | copy-start | bytes 3145732
  440.8 99.6 %collective-permute-start.19 = (bf16[1024,512]{0,1:T(8,128)(2,1)}, bf16[1024,512]{0,1:T(8,128)(2,1)}, u32[]{:S(2)}, u32[]{:S(2)}) collective-permute-start(bf16[1024,512]{0,1:T(8,128)(2,1)} %add_convert_fusion.3), channel_id=1, source_target_pairs={{0,4},{4,0},{8,12},{12,8},{1,5},{5,1},{9,13},{13,9},{2,6},{6,2},{1... | collective-permute-start | bytes 3145736 | tf_op jit(solution)/shard_map/ppermute | solution.py:194
  461.5 80.3 %collective-permute-start.20 = (bf16[1024,512]{0,1:T(8,128)(2,1)}, bf16[1024,512]{0,1:T(8,128)(2,1)}, u32[]{:S(2)}, u32[]{:S(2)}) collective-permute-start(bf16[1024,512]{0,1:T(8,128)(2,1)} %add_convert_fusion.2), channel_id=1, source_target_pairs={{0,4},{4,0},{8,12},{12,8},{1,5},{5,1},{9,13},{13,9},{2,6},{6,2},{1... | collective-permute-start | bytes 3145736 | tf_op jit(solution)/shard_map/ppermute | solution.py:194
  464.1 95.3 %collective-permute-start.23 = (bf16[1024,512]{0,1:T(8,128)(2,1)}, bf16[1024,512]{0,1:T(8,128)(2,1)}, u32[]{:S(2)}, u32[]{:S(2)}) collective-permute-start(bf16[1024,512]{0,1:T(8,128)(2,1)} %add_convert_fusion.1), channel_id=1, source_target_pairs={{0,4},{4,0},{8,12},{12,8},{1,5},{5,1},{9,13},{13,9},{2,6},{6,2},{1... | collective-permute-start | bytes 3145736 | tf_op jit(solution)/shard_map/ppermute | solution.py:194
  474.3 10.6 %slice-start = ((s8[8388608]{0:T(1024)(128)(4,1)}), s8[4194304]{0:T(1024)(128)(4,1)S(1)}, s32[]{:S(2)}) async-start(s8[8388608]{0:T(1024)(128)(4,1)} %bitcast.108), calls=%async_computation.8 | async-start | bytes 8388608
  489.5 127.9 %all-reduce.12.cloned.1.call-start = ((), (), s32[]{:S(2)}) async-start(), calls=%async_computation.7 | async-start | bytes 4194304 | tf_op jit(solution)/shard_map/psum | solution.py:212
  495.6 20.8 %copy-start.47 = (f32[1,2048]{1,0:T(1,128)S(1)}, f32[1,2048]{1,0:T(1,128)}, u32[]{:S(2)}) copy-start(f32[1,2048]{1,0:T(1,128)} %copy-done.46) | copy-start | bytes 24580
  495.6 20.8 %copy-start.54 = (f32[256]{0:T(256)S(1)}, f32[256]{0:T(256)}, u32[]{:S(2)}) copy-start(f32[256]{0:T(256)} %copy-done.53) | copy-start | bytes 3076
  495.6 66.1 %collective-permute-start.24 = (bf16[1024,512]{0,1:T(8,128)(2,1)}, bf16[1024,512]{0,1:T(8,128)(2,1)}, u32[]{:S(2)}, u32[]{:S(2)}) collective-permute-start(bf16[1024,512]{0,1:T(8,128)(2,1)} %add_convert_fusion), channel_id=1, source_target_pairs={{0,4},{4,0},{8,12},{12,8},{1,5},{5,1},{9,13},{13,9},{2,6},{6,2},{1... | collective-permute-start | bytes 3145736 | tf_op jit(solution)/shard_map/ppermute | solution.py:194
  521.9 58.9 %collective-permute-start.12 = (bf16[1024,1280]{0,1:T(8,128)(2,1)}, bf16[1024,1280]{0,1:T(8,128)(2,1)}, u32[]{:S(2)}, u32[]{:S(2)}) collective-permute-start(bf16[1024,1280]{0,1:T(8,128)(2,1)} %fusion.8), channel_id=1, source_target_pairs={{0,16},{16,0},{1,17},{17,1},{2,18},{18,2},{3,19},{19,3},{4,20},{20... | collective-permute-start | bytes 7864328 | tf_op jit(solution)/shard_map/ppermute | solution.py:95
  567.9 156.3 %all-reduce.10.cloned.1.call-start = ((), (), s32[]{:S(2)}) async-start(), calls=%async_computation.6 | async-start | bytes 5242880 | tf_op jit(solution)/shard_map/psum | solution.py:254
  568.2 12.6 %copy-start.5 = (f32[2048,512]{0,1:T(8,128)S(1)}, f32[2048,512]{0,1:T(8,128)}, u32[]{:S(2)}) copy-start(f32[2048,512]{0,1:T(8,128)} %fusion.90) | copy-start | bytes 12582916
  601.0 18.4 %copy-start.48 = (f32[2048]{0:T(1024)S(1)}, f32[2048]{0:T(1024)}, u32[]{:S(2)}) copy-start(f32[2048]{0:T(1024)} %get-tuple-element.33) | copy-start | bytes 24580
  601.0 20.0 %copy-start.55 = (f32[256]{0:T(256)S(1)}, f32[256]{0:T(256)}, u32[]{:S(2)}) copy-start(f32[256]{0:T(256)} %get-tuple-element.90) | copy-start | bytes 3076
  619.4 6.1 collective-permute-start.11
  (35 other events, 110.7 us)
Sparse Core Ops, SparseCore 0:
  109.8 38.3 all-reduce.5
  342.6 34.3 all-reduce.7
  568.0 49.3 all-reduce.11
  619.6 104.5 all-reduce.9
Sparse Core Ops, SparseCore 1:
  113.1 82.3 all-gather.4
  197.5 79.1 all-gather.2
  489.6 25.7 reduce-scatter.1

commit v2 on v1

--- a/solution.py
+++ b/solution.py
@@ -3,6 +3,8 @@
 import jax
 import jax.numpy as jnp
 from jax import lax
+from jax.experimental import pallas as pl
+from jax.experimental.pallas import tpu as pltpu
 from jax.sharding import PartitionSpec as P
 
 HEAD_SIZE = 64
@@ -87,7 +89,455 @@
     return (grad_queries, grad_keys, grad_values)
 
 
-def make_local(ctx_size):
+MESH = pl.DeviceIdType.MESH
+HBM_SPEC = pl.BlockSpec(memory_space=pl.ANY)
+VMEM_SPEC = pl.BlockSpec(memory_space=pltpu.VMEM)
+DMA = pltpu.SemaphoreType.DMA
+
+
+def remote(src, dst, send, recv, peer):
+    return pltpu.make_async_remote_copy(
+        src_ref=src, dst_ref=dst, send_sem=send, recv_sem=recv, device_id=peer, device_id_type=MESH
+    )
+
+
+def rows_at(ref, start, count):
+    return ref.at[pl.ds(pl.multiple_of(start, count), count)]
+
+
+def guarded(condition, body):
+    if condition is None:
+        body()
+    else:
+        pl.when(condition)(body)
+
+
+def tp_peers(tp_size):
+    me = lax.axis_index("tp")
+    core = lax.rem(me, 2)
+    level = me // 2
+    levels = tp_size // 2
+    partner = me + 1 - 2 * core
+    others = [lax.rem(level + step, levels) * 2 + core for step in range(1, levels)]
+    return me, core, level, partner, others
+
+
+def enter(ctx_size, tp_size, along=False, pair=False, side=False, tensor=True):
+    place = lax.axis_index("ctx")
+    barrier = pltpu.get_barrier_semaphore()
+
+    def greet(peer):
+        pl.semaphore_signal(barrier, inc=1, device_id=peer, device_id_type=MESH)
+
+    count = 0
+    if tensor:
+        _, _, _, partner, others = tp_peers(tp_size)
+        for peer in [partner] + others:
+            greet({"tp": peer})
+        count = count + 1 + len(others)
+    if side:
+        greet({"fsdp": 1 - lax.axis_index("fsdp")})
+        count = count + 1
+    if along:
+        up = place + 1 < ctx_size
+        down = place > 0
+
+        @pl.when(up)
+        def _():
+            greet({"ctx": place + 1})
+
+        @pl.when(down)
+        def _():
+            greet({"ctx": place - 1})
+
+        count = count + up.astype(jnp.int32) + down.astype(jnp.int32)
+    if pair:
+        greet({"ctx": place + 1 - 2 * lax.rem(place, 2)})
+        count = count + 1
+    pl.semaphore_wait(barrier, count)
+
+
+def gather_sems(ctx_size, tp_size):
+    spread = 2 * ctx_size - 1
+    levels = tp_size // 2
+    chips = max(levels - 1, 1)
+    return [
+        DMA((spread + 1,)), DMA((spread,)), DMA((chips, spread)), DMA((chips, spread)),
+        DMA((levels, spread)), DMA((levels, spread)), DMA((1,)),
+    ]
+
+
+def gather_rows(mine, all_ref, ctx_size, tp_size, sems, block=None):
+    hop_send, hop_recv, chip_send, chip_recv, core_send, core_recv, own_sem = sems
+    place = lax.axis_index("ctx") if ctx_size > 1 else 0
+    me, core, level, partner, others = tp_peers(tp_size)
+    levels = tp_size // 2
+    rows = mine.shape[0]
+    middle = ctx_size - 1
+    offsets = [0]
+    for step in range(1, ctx_size):
+        offsets += [-step, step]
+
+    def spot(offset, who):
+        return rows_at(all_ref, ((place + offset) * tp_size + who) * rows, rows)
+
+    def hop(offset, step, src):
+        slot = 2 * middle + 1 if offset == 0 and step < 0 else middle + offset
+        return remote(
+            src, spot(offset, me), hop_send.at[slot], hop_recv.at[middle + offset - step],
+            {"ctx": place + step},
+        )
+
+    def hop_arrival(offset):
+        step = -1 if offset < 0 else 1
+        return remote(
+            spot(offset, me), spot(offset, me), hop_send.at[middle + offset],
+            hop_recv.at[middle + offset], {"ctx": place + step},
+        )
+
+    def chip(offset, index, src):
+        return remote(
+            src, spot(offset, me), chip_send.at[index, middle + offset],
+            chip_recv.at[levels - 2 - index, middle + offset], {"tp": others[index]},
+        )
+
+    def chip_arrival(offset, index):
+        where = spot(offset, others[index])
+        return remote(
+            where, where, chip_send.at[index, middle + offset],
+            chip_recv.at[index, middle + offset], {"tp": others[index]},
+        )
+
+    def to_core(offset, index, who, src):
+        return remote(
+            src, spot(offset, who), core_send.at[index, middle + offset],
+            core_recv.at[index, middle + offset], {"tp": partner},
+        )
+
+    def valid(offset):
+        if offset == 0:
+            return None
+        return place + offset >= 0 if offset < 0 else place + offset < ctx_size
+
+    def onward(offset):
+        if offset < 0:
+            return 1, jnp.logical_and(place + offset >= 0, place + 1 < ctx_size)
+        return -1, jnp.logical_and(place + offset < ctx_size, place > 0)
+
+    def fan_out(offset, src):
+        for index in range(levels - 1):
+            chip(offset, index, src).start()
+        to_core(offset, 0, me, src).start()
+
+    if block is None:
+        own = pltpu.make_async_copy(mine, spot(0, me), own_sem.at[0])
+    else:
+        own = pltpu.make_async_copy(
+            block, rows_at(all_ref, place * block.shape[0], block.shape[0]), own_sem.at[0]
+        )
+    own.start()
+    if ctx_size > 1:
+        @pl.when(place + 1 < ctx_size)
+        def _():
+            hop(0, 1, mine).start()
+
+        @pl.when(place > 0)
+        def _():
+            hop(0, -1, mine).start()
+
+    if block is None:
+        fan_out(0, mine)
+    for offset in offsets[1:]:
+        def arrived(offset=offset):
+            hop_arrival(offset).wait_recv()
+            fan_out(offset, spot(offset, me))
+
+        guarded(valid(offset), arrived)
+        step, more = onward(offset)
+
+        @pl.when(more)
+        def _(offset=offset, step=step):
+            hop(offset, step, spot(offset, me)).start()
+
+    shared = offsets if block is None else offsets[1:]
+    for offset in shared:
+        def relay(offset=offset):
+            for index in range(levels - 1):
+                chip_arrival(offset, index).wait_recv()
+                to_core(offset, 1 + index, others[index], spot(offset, others[index])).start()
+
+        guarded(valid(offset), relay)
+
+    for offset in shared:
+        def drain(offset=offset):
+            for index in range(levels):
+                to_core(offset, index, me, spot(offset, me)).wait()
+            for index in range(levels - 1):
+                chip(offset, index, spot(offset, me)).wait_send()
+
+        guarded(valid(offset), drain)
+    own.wait()
+    if ctx_size > 1:
+        @pl.when(place + 1 < ctx_size)
+        def _():
+            hop(0, 1, mine).wait_send()
+
+        @pl.when(place > 0)
+        def _():
+            hop(0, -1, mine).wait_send()
+
+        for offset in offsets[1:]:
+            step, more = onward(offset)
+
+            @pl.when(more)
+            def _(offset=offset, step=step):
+                hop(offset, step, spot(offset, me)).wait_send()
+
+
+def reduce_gather(term, extras, finish, side_shapes, mesh_shape, identity, blocks, across):
+    ctx_size, tp_size = mesh_shape
+    levels = tp_size // 2
+    width = term.shape[1]
+    block_rows = term.shape[0] // blocks
+    rows = block_rows // tp_size
+    reach = ctx_size if across else 1
+
+    def kernel(term_ref, *refs):
+        extra_refs = refs[: len(extras)]
+        refs = refs[len(extras) :]
+        all_ref = refs[0]
+        side_refs = refs[1 : 1 + len(side_shapes)]
+        refs = refs[1 + len(side_shapes) :]
+        from_core, stage, from_chip, mine = refs[:4]
+        refs = refs[4:]
+        if blocks == 2:
+            pair_stage, from_pair = refs[:2]
+            refs = refs[2:]
+        sems = refs[:7]
+        core_send, core_recv, chip_send, chip_recv, pair_sems = refs[7:]
+        place = lax.axis_index("ctx")
+        me, core, level, partner, others = tp_peers(tp_size)
+        enter(ctx_size, tp_size, along=across, pair=blocks == 2)
+
+        def to_core(block, lev):
+            slot = block * levels + lev
+            return remote(
+                rows_at(term_ref, block * block_rows + (2 * lev + 1 - core) * rows, rows),
+                from_core.at[slot], core_send.at[slot], core_recv.at[slot], {"tp": partner},
+            )
+
+        def to_chip(index):
+            return remote(
+                stage.at[index], from_chip.at[levels - 2 - index], chip_send.at[index],
+                chip_recv.at[levels - 2 - index], {"tp": others[index]},
+            )
+
+        def chip_sum(block, lev):
+            own = term_ref[
+                pl.ds(pl.multiple_of(block * block_rows + (2 * lev + core) * rows, rows), rows), :
+            ]
+            return own.astype(F32) + from_core[block * levels + lev].astype(F32)
+
+        for lev in range(levels):
+            for block in range(blocks):
+                to_core(block, lev).start()
+        for lev in range(levels):
+            for block in range(blocks):
+                to_core(block, lev).wait_recv()
+        for index in range(levels - 1):
+            lev = lax.rem(level + 1 + index, levels)
+            for block in range(blocks):
+                stage[index, block * rows : (block + 1) * rows, :] = chip_sum(block, lev).astype(
+                    BF16
+                )
+            to_chip(index).start()
+        for index in range(levels - 1):
+            to_chip(index).wait_recv()
+
+        def tp_sum(block):
+            total = chip_sum(block, level)
+            for index in range(levels - 1):
+                total += from_chip[
+                    index, pl.ds(pl.multiple_of(block * rows, rows), rows), :
+                ].astype(F32)
+            return total
+
+        if blocks == 2:
+            low = lax.rem(place, 2)
+            pair_stage[...] = tp_sum(1 - low).astype(BF16)
+            swap = remote(
+                pair_stage, from_pair, pair_sems.at[0], pair_sems.at[1], {"ctx": place + 1 - 2 * low}
+            )
+            swap.start()
+            total = tp_sum(low)
+            swap.wait_recv()
+            total += from_pair[...].astype(F32)
+        else:
+            total = tp_sum(0)
+        start = pl.multiple_of(me * rows, rows)
+        mine[...] = finish(total, start, *extra_refs, *side_refs)
+        gather_rows(mine, all_ref, reach, tp_size, sems)
+        for lev in range(levels):
+            for block in range(blocks):
+                to_core(block, lev).wait_send()
+        for index in range(levels - 1):
+            to_chip(index).wait_send()
+        if blocks == 2:
+            swap.wait_send()
+
+    chips = max(levels - 1, 1)
+    scratch = [
+        pltpu.VMEM((blocks * levels, rows, width), BF16),
+        pltpu.VMEM((chips, blocks * rows, width), BF16),
+        pltpu.VMEM((chips, blocks * rows, width), BF16),
+        pltpu.VMEM((rows, width), BF16),
+    ]
+    if blocks == 2:
+        scratch += [pltpu.VMEM((rows, width), BF16)] * 2
+    scratch += gather_sems(reach, tp_size)
+    scratch += [
+        DMA((blocks * levels,)), DMA((blocks * levels,)), DMA((chips,)), DMA((chips,)), DMA((2,)),
+    ]
+    return pl.pallas_call(
+        kernel,
+        out_shape=(
+            jax.ShapeDtypeStruct((reach * block_rows, width), BF16),
+            *(jax.ShapeDtypeStruct(shape, F32) for shape in side_shapes),
+        ),
+        in_specs=[VMEM_SPEC] * (1 + len(extras)),
+        out_specs=(HBM_SPEC,) + (VMEM_SPEC,) * len(side_shapes),
+        scratch_shapes=scratch,
+        compiler_params=pltpu.CompilerParams(
+            collective_id=identity, has_side_effects=True, vmem_limit_bytes=32 << 20
+        ),
+    )(term, *extras)
+
+
+def opening(cot_rows, weights, mesh_shape, identity):
+    ctx_size, tp_size = mesh_shape
+    block_rows, width = cot_rows.shape
+    rows = block_rows // tp_size
+    depth = weights[0].shape[0]
+    columns = sum(w.shape[1] for w in weights)
+
+    def kernel(cot_ref, *refs):
+        weight_refs = refs[: len(weights)]
+        all_ref, whole_ref = refs[len(weights) : len(weights) + 2]
+        sems = refs[len(weights) + 2 : len(weights) + 9]
+        send, recv = refs[len(weights) + 9 :]
+        enter(ctx_size, tp_size, along=True, side=True)
+        far = {"fsdp": 1 - lax.axis_index("fsdp")}
+        swaps = []
+        at = 0
+        for i, ref in enumerate(weight_refs):
+            wide = ref.shape[1]
+            swaps.append(
+                remote(
+                    ref, whole_ref.at[pl.ds(depth, depth), pl.ds(at, wide)], send.at[i], recv.at[i],
+                    far,
+                )
+            )
+            swaps[-1].start()
+            at += wide
+        at = 0
+        for ref in weight_refs:
+            wide = ref.shape[1]
+            whole_ref[0:depth, at : at + wide] = ref[...]
+            at += wide
+        mine = rows_at(cot_ref, lax.axis_index("tp") * rows, rows)
+        gather_rows(mine, all_ref, ctx_size, tp_size, sems, block=cot_ref)
+        for swap in swaps:
+            swap.wait()
+
+    return pl.pallas_call(
+        kernel,
+        out_shape=(
+            jax.ShapeDtypeStruct((ctx_size * block_rows, width), BF16),
+            jax.ShapeDtypeStruct((2 * depth, columns), BF16),
+        ),
+        in_specs=[VMEM_SPEC] * (1 + len(weights)),
+        out_specs=(HBM_SPEC, VMEM_SPEC),
+        scratch_shapes=gather_sems(ctx_size, tp_size)
+        + [DMA((len(weights),)), DMA((len(weights),))],
+        compiler_params=pltpu.CompilerParams(
+            collective_id=identity, has_side_effects=True, vmem_limit_bytes=32 << 20
+        ),
+    )(cot_rows, *weights)
+
+
+def place_halves(part, mine, other):
+    pieces = len(mine)
+    depth, wide = mine[0].shape
+    tile = min(depth, 256)
+
+    def kernel(part_ref, *refs):
+        out_ref = refs[-1]
+        step = pl.program_id(1)
+        for k in range(2 * pieces):
+            @pl.when(step == k)
+            def _(k=k):
+                out_ref[...] = refs[k][...].astype(F32)
+
+    def target(i, step, part_ref):
+        half = jnp.where(step < pieces, part_ref[0], 1 - part_ref[0])
+        return i, half * pieces + lax.rem(step, pieces)
+
+    return pl.pallas_call(
+        kernel,
+        grid_spec=pltpu.PrefetchScalarGridSpec(
+            num_scalar_prefetch=1,
+            grid=(depth // tile, 2 * pieces),
+            in_specs=[pl.BlockSpec((tile, wide), lambda i, step, part_ref: (i, 0))] * (2 * pieces),
+            out_specs=pl.BlockSpec((tile, wide), target),
+        ),
+        out_shape=jax.ShapeDtypeStruct((depth, 2 * pieces * wide), F32),
+        cost_estimate=pl.CostEstimate(
+            flops=0, bytes_accessed=depth * 2 * pieces * wide * 6, transcendentals=0
+        ),
+    )(part.reshape(1), *mine, *other)
+
+
+def mean_square(rows):
+    return jnp.mean(rows * rows, axis=-1, keepdims=True)
+
+
+def finish_middle(total, start, resid_ref, gain_ref, middle_ref):
+    rows = total.shape[0]
+    middle = resid_ref[pl.ds(start, rows), :].astype(F32) + total
+    middle_ref[...] = middle
+    return (middle * lax.rsqrt(mean_square(middle) + EPSILON) * gain_ref[...]).astype(BF16)
+
+
+def norm_back(grad, base, values, gain):
+    rms = lax.rsqrt(mean_square(values) + EPSILON)
+    scaled = grad * gain
+    gain_grad = jnp.sum(grad * values * rms, axis=0, keepdims=True)
+    cube = rms * rms * rms
+    full = base + rms * scaled - values * cube * jnp.mean(scaled * values, axis=-1, keepdims=True)
+    return full, gain_grad
+
+
+def finish_grad_middle(total, start, middle_ref, cot_ref, gain_ref, grad_ref, gain_grad_ref):
+    base = cot_ref[pl.ds(start, total.shape[0]), :].astype(F32)
+    full, gain_grad = norm_back(total, base, middle_ref[...], gain_ref[...])
+    grad_ref[...] = full
+    gain_grad_ref[...] = gain_grad
+    return full.astype(BF16)
+
+
+def finish_grad_input(total, start, grad_ref, resid_ref, gain_ref, gain_grad_ref):
+    values = resid_ref[pl.ds(start, total.shape[0]), :].astype(F32)
+    full, gain_grad = norm_back(total, grad_ref[...], values, gain_ref[...])
+    gain_grad_ref[...] = gain_grad
+    return full.astype(BF16)
+
+
+def finish_output(total, start, middle_ref):
+    return (middle_ref[...] + total).astype(BF16)
+
+
+def make_local(ctx_size, tp_size):
+    mesh_shape = (ctx_size, tp_size)
     swap_x = [(0, 1), (1, 0)]
     swap_z = [(i, i ^ 1) for i in range(ctx_size)]
 
@@ -123,8 +573,16 @@
         gains = jnp.concatenate([gains, swap_rows(gains)], axis=1).astype(F32)
         gain_first, gain_second = gains[0], gains[1]
 
-        qkv_own = jnp.concatenate([w_query, key_projection, value_projection], axis=1)
-        qkv_weight = jnp.concatenate([qkv_own, swap_rows(qkv_own)], axis=0)
+        residual_low = own_first(inputs[0])
+        cot_low = own_first(cotangent[0])
+        cot_all, qkv_weight = opening(
+            cot_low,
+            (w_query, jnp.concatenate([key_projection, value_projection], axis=1)),
+            mesh_shape, 0,
+        )
+        w_out, w_gate, w_up, w_down, _ = lax.optimization_barrier(
+            (w_out, w_gate, w_up, w_down, qkv_weight)
+        )
         out_weight = jnp.concatenate([w_out, swap_rows(w_out)], axis=0)
         ffn_own = []
         for c in range(CHUNKS):
@@ -138,9 +596,6 @@
         ]
 
         cosine_lookup, sine_lookup = rope_tables(row_start, row_count)
-        residual_low = own_first(inputs[0])
-        cot_low = own_first(cotangent[0])
-        cot_all = lax.all_gather(cot_low, "ctx", axis=0, tiled=True)
         residual = residual_low.astype(F32)
         rms_first = lax.rsqrt(jnp.mean(residual * residual, axis=-1, keepdims=True) + EPSILON)
         normalized_rows = (residual * rms_first * gain_first).astype(BF16)
@@ -165,10 +620,11 @@
         attended, log_total = attend(query_groups, key_whole, value_whole, prefix_one, row_start)
         attended_flat = attended.reshape(row_count, query_width)
         attn_term = contract(attended_flat, out_weight, 1, 1)
-        middle = residual + lax.psum(attn_term.astype(BF16), "tp").astype(F32)
-        rms_second = lax.rsqrt(jnp.mean(middle * middle, axis=-1, keepdims=True) + EPSILON)
-        normed_mid = (middle * rms_second * gain_second).astype(BF16)
-        normed_all = lax.all_gather(normed_mid, "ctx", axis=0, tiled=True)
+        slice_shape = (row_count // tp_size, model_width)
+        normed_all, middle = reduce_gather(
+            attn_term.astype(BF16), (residual_low, gain_second[None]), finish_middle,
+            (slice_shape,), mesh_shape, 1, 1, True,
+        )
 
         ffn_term = 0.0
         mid_term = 0.0
@@ -202,26 +658,13 @@
                 pair(grad_upward), up_w, 1, 1
             )
 
-        def pair_reduce(term):
-            lower = term[:row_count]
-            upper = term[row_count:]
-            low = (place % 2) == 0
-            mine = jnp.where(low, lower, upper)
-            theirs = jnp.where(low, upper, lower).astype(BF16)
-            mine = mine + lax.ppermute(theirs, "ctx", swap_z).astype(F32)
-            return lax.psum(mine.astype(BF16), "tp").astype(F32)
-
-        grad_mid_norm = pair_reduce(mid_term)
-        output_rows = (middle + pair_reduce(ffn_term)).astype(BF16)
-        scaled_mid = grad_mid_norm * gain_second
-        gain_grad_second = jnp.sum(grad_mid_norm * middle * rms_second, axis=0)
-        cube_second = rms_second * rms_second * rms_second
-        grad_middle = (
-            cot_low.astype(F32)
-            + rms_second * scaled_mid
-            - middle * cube_second * jnp.mean(scaled_mid * middle, axis=-1, keepdims=True)
-        )
-        branch_low = grad_middle.astype(BF16)
+        branch_low, grad_middle, gain_grad_second = reduce_gather(
+            mid_term.astype(BF16), (middle, cot_low, gain_second[None]), finish_grad_middle,
+            (slice_shape, (1, model_width)), mesh_shape, 2, 2, False,
+        )
+        (output_rows,) = reduce_gather(
+            ffn_term.astype(BF16), (middle,), finish_output, (), mesh_shape, 3, 2, False
+        )
         grad_out = contract(branch_low, attended_flat, 0, 0)
         grad_attended = jnp.dot(branch_low, out_weight, preferred_element_type=F32).astype(BF16)
         grad_attended = grad_attended.reshape(row_count, kv_heads, heads_per_group, HEAD_SIZE)
@@ -252,38 +695,25 @@
             F32
         )
         grad_attn = lax.psum(grad_attn.astype(BF16), "ctx").astype(F32)
-        grad_normed = lax.psum(contract(grad_qkv_pre, qkv_weight, 1, 1).astype(BF16), "tp").astype(
-            F32
-        )
-        scaled_first = grad_normed * gain_first
-        gain_grad_first = jnp.sum(grad_normed * residual * rms_first, axis=0)
-        cube_first = rms_first * rms_first * rms_first
-        grad_full = (
-            grad_middle
-            + rms_first * scaled_first
-            - residual * cube_first * jnp.mean(scaled_first * residual, axis=-1, keepdims=True)
-        )
-        gain_grads = jnp.stack([gain_grad_first, gain_grad_second])
+        input_rows, gain_grad_first = reduce_gather(
+            contract(grad_qkv_pre, qkv_weight, 1, 1).astype(BF16),
+            (grad_middle, residual_low, gain_first[None]), finish_grad_input,
+            ((1, model_width),), mesh_shape, 4, 1, False,
+        )
+        gain_grads = jnp.concatenate([gain_grad_first, gain_grad_second], axis=0)
         gain_grads = lax.psum(
-            gain_grads[:, :half_width] + swap_rows(gain_grads[:, half_width:]), "ctx"
-        )
-
-        first_half = part == 0
-        result = []
-        for i in range(3):
-            mine = jnp.concatenate([grads[c][i][0] for c in range(CHUNKS)], axis=1)
-            other = jnp.concatenate([grads[c][i][1] for c in range(CHUNKS)], axis=1)
-            result.append(
-                jnp.concatenate(
-                    [jnp.where(first_half, mine, other), jnp.where(first_half, other, mine)],
-                    axis=1,
-                ).astype(F32)
-            )
+            gain_grads[:, :half_width] + swap_rows(gain_grads[:, half_width:]), ("ctx", "tp")
+        )
+
+        result = [
+            place_halves(part, [done[i][0] for done in grads], [done[i][1] for done in grads])
+            for i in range(3)
+        ]
         end_key = query_width + key_width
         end_value = end_key + key_width
         return (
             own_first(output_rows)[None],
-            own_first(grad_full.astype(BF16))[None],
+            own_first(input_rows)[None],
             gain_grads[0],
             grad_attn[:, :query_width],
             grad_attn[:, query_width:end_key],
@@ -300,7 +730,7 @@
 
 def solution(mesh):
     return jax.shard_map(
-        make_local(mesh.shape["ctx"]),
+        make_local(mesh.shape["ctx"], mesh.shape["tp"]),
         mesh=mesh,
         in_specs=(
             P("fsdp", "ctx", None), P("fsdp", "ctx", None), P("fsdp"), P("fsdp"),

time: 752 us -> 711 us (0.945)
  waiting for transfers between devices: 413 us -> 145 us
  Pallas kernels: 0 us -> 197 us
  blocking collectives: 28.1 us -> 178 us
  other arithmetic: 60.3 us -> 10.6 us
  local copies, waits for them, and re-layouts: 80.5 us -> 38.7 us
  matrix products: 116 us -> 98.8 us
  starting transfers between devices: 27.9 us -> 18.2 us
    pallas_call x0 -> x8, Pallas kernels: none -> 197 us  [the longest x4 126 us: reduce_gather(): pl.pallas_call(kernel, out_shape=(jax.ShapeDtypeStruct((reach * block_row...]
    psum x1, blocking collectives: 12.7 us -> 162 us  [local(): lax.psum(gain_grads[:, :half_width] + swap_rows(gain_grads[:, half_width:...]
    all_gather x2 -> x0, waiting for transfers between devices: 86.4 us -> none  [the longest x1 73.3 us: local(): normed_all = lax.all_gather(normed_mid, 'ctx', axis=0, tiled=True)]
    psum x1, waiting for transfers between devices: 85.4 us -> 0.01 us  [local(): grad_attn = lax.psum(grad_attn.astype(BF16), 'ctx').astype(F32)]
    psum x3 -> x0, waiting for transfers between devices: 51.5 us -> none  [the longest x1 35.1 us: local(): middle = residual + lax.psum(attn_term.astype(BF16), 'tp').astype(F32)]
    ppermute x17 -> x16, waiting for transfers between devices: 175 us -> 133 us  [swap_rows(): return lax.ppermute(array, 'fsdp', swap_x)]
    unnamed x147 -> x131, local copies, waits for them, and re-layouts: 52.2 us -> 19.7 us
    convert_element_type x10 -> x0, other arithmetic: 23.9 us -> none  [the longest x3 15.7 us: local(): result.append(jnp.concatenate([jnp.where(first_half, mine, other), jnp.wh...]
  transfers between devices with their start and end apart: 32 -> 24, of which waited for: 17 -> 9; matrix products, arithmetic and copies ran while one was open for 27% -> 13% of each run, Pallas kernels for 0% -> 18%
where the time goes in v2:
time: 711 us; the launch traced here: 703 us
  Pallas kernels  197 us (28%)
  blocking collectives  178 us (25%)
  waiting for transfers between devices  145 us (20%)
  matrix products  98.8 us (14%)
  local copies, waits for them, and re-layouts  38.7 us (5%)
  starting transfers between devices  18.2 us (3%)
  between operations  16.3 us (2%)
  other arithmetic  10.6 us (1%)
    psum x1, blocking collectives, local(): lax.psum(gain_grads[:, :half_width] + swap_rows(gain_grads[:, half_width:...  162 us
    ppermute x16, waiting for transfers between devices, swap_rows(): return lax.ppermute(array, 'fsdp', swap_x)  133 us
    pallas_call x4, Pallas kernels, reduce_gather(): pl.pallas_call(kernel, out_shape=(jax.ShapeDtypeStruct((reach * block_row...  126 us
    dot_general x22, matrix products, contract(): lax.dot_general(left, right, (((left_dim,), (right_dim,)), ((), ())), pre...  54.9 us
    pallas_call x1, Pallas kernels, opening(): pl.pallas_call(kernel, out_shape=(jax.ShapeDtypeStruct((ctx_size * block_...  39.2 us
    pallas_call x3, Pallas kernels, place_halves(): pl.pallas_call(kernel, grid_spec=pltpu.PrefetchScalarGridSpec(num_scalar_...  31.3 us
    unnamed x131, local copies, waits for them, and re-layouts  19.7 us
    all_gather x1, blocking collectives, local(): lax.all_gather(jnp.concatenate([key_rot, value_matrix], axis=1), 'ctx', a...  16.1 us
  transfers between devices with their start and end apart: 24, of which 9 were waited for; matrix products, arithmetic and copies ran while one was open for 13% of the time, Pallas kernels for 18%

profile of v2, /device:TPU:0, one launch (start us, length us, event | category | flops | bytes accessed | tf_op | source)
XLA Modules:
  0.0 702.6 jit_solution(1710846479896330219)
XLA Ops:
  7.2 1.7 dynamic-slice_bitcast_fusion.1
  10.7 39.2 %shard_map.203 = (bf16[1024,2048]{1,0:T(8,128)(2,1)S(1)}, bf16[2048,768]{1,0:T(8,128)(2,1)S(1)}) custom-call(bf16[256,2048]{1,0:T(8,128)(2,1)S(1)} %pad_maximum_fusion.20.cot_ref.refs_1_, bf16[1024,512]{1,0:T(8,128)(2,1)S(1)} %copy-done.2, bf16[1024,256]{1,0:T(8,128)(2,1)S(1)} %pad_maximum_fusion.21.refs_1_), custom_call_target="tpu_custom_call" | custom-call | tf_op jit(solution)/shard_map/pallas_call | solution.py:452
  50.0 2.0 copy-done.5
  52.0 1.6 copy-done.14
  53.6 3.2 constant_dynamic-slice_fusion.7
  57.4 1.6 collective-permute-start
  59.5 1.7 constant_dynamic-slice_fusion.8
  61.1 1.5 collective-permute-start.6
  62.6 1.6 constant_dynamic-slice_fusion.9
  66.9 2.3 constant_dynamic-update-slice_fusion.1
  69.2 14.0 %collective-permute-done = bf16[2,1024]{1,0:T(2,128)(2,1)S(1)} collective-permute-done((bf16[2,1024]{1,0:T(2,128)(2,1)S(1)}, bf16[2,1024]{1,0:T(2,128)(2,1)S(1)}, u32[]{:S(2)}, u32[]{:S(2)}) %collective-permute-start) | collective-permute-done | bytes 4128 | tf_op jit(solution)/shard_map/ppermute | solution.py:545
  83.7 2.9 fusion.82
  87.8 16.1 %all_gather.3 = bf16[1024,256]{1,0:T(8,128)(2,1)S(1)} all-gather(bf16[256,256]{1,0:T(8,128)(2,1)S(1)} %pad_maximum_fusion.30), channel_id=1, replica_groups=mesh['fsdp'=2,'ctx'=4,'tp'=4] {'ctx'}, dimensions={0}, use_global_device_ids=true | all-gather | bytes 655360 | tf_op jit(solution)/shard_map/all_gather | solution.py:612
  109.0 1.5 fusion.72
  111.6 1.5 collective-permute-start.2
  115.3 42.9 %shard_map.204 = (bf16[1024,2048]{1,0:T(8,128)(2,1)S(1)}, f32[64,2048]{1,0:T(8,128)S(1)}) custom-call(bf16[256,2048]{1,0:T(8,128)(2,1)S(1)} %convolution_convert_fusion.term_ref, bf16[256,2048]{1,0:T(8,128)(2,1)S(1)} %pad_maximum_fusion.19.refs_0_.refs_1_, f32[1,2048]{1,0:T(1,128)S(1)} %get-tuple-element.95.refs_1_.refs_2_), custom_call_target="tpu_custom_call" | custom-call | tf_op jit(solution)/shard_map/pallas_call | solution.py:401
  158.6 5.1 fusion.34
  163.7 3.9 fusion.37
  167.6 5.8 multiply_convert_fusion.1
  173.3 3.6 fusion.36
  176.9 18.5 %collective-permute-done.2 = bf16[1024,512]{1,0:T(8,128)(2,1)S(1)} collective-permute-done((bf16[1024,512]{1,0:T(8,128)(2,1)S(1)}, bf16[1024,512]{1,0:T(8,128)(2,1)S(1)}, u32[]{:S(2)}, u32[]{:S(2)}) %collective-permute-start.2) | collective-permute-done | bytes 1048608 | tf_op jit(solution)/shard_map/ppermute | solution.py:545
  195.5 2.3 fusion.43
  197.8 18.1 %collective-permute-done.3 = bf16[1024,512]{1,0:T(8,128)(2,1)S(1)} collective-permute-done((bf16[1024,512]{1,0:T(8,128)(2,1)S(1)}, bf16[1024,512]{1,0:T(8,128)(2,1)S(1)}, u32[]{:S(2)}, u32[]{:S(2)}) %collective-permute-start.3) | collective-permute-done | bytes 1048608 | tf_op jit(solution)/shard_map/ppermute | solution.py:545
  215.9 2.3 fusion.41
  218.3 5.4 multiply_convert_fusion.2
  226.5 2.9 add_convert_fusion.term_ref
  229.4 34.0 %shard_map.206 = (bf16[256,2048]{1,0:T(8,128)(2,1)S(1)}, f32[64,2048]{1,0:T(8,128)S(1)}, f32[1,2048]{1,0:T(1,128)S(1)}) custom-call(bf16[512,2048]{1,0:T(8,128)(2,1)S(1)} %add_convert_fusion.term_ref, f32[64,2048]{1,0:T(8,128)S(1)} %get-tuple-element.30.refs_0_, bf16[256,2048]{1,0:T(8,128)(2,1)S(1)} %pad_maximum_fusion.20.cot_ref.refs_1_, ...), custom_call_target="tpu_custom_call" | custom-call | tf_op jit(solution)/shard_map/pallas_call | solution.py:401
  265.0 4.9 fusion.68
  270.0 5.3 fusion
  275.4 1.8 fusion.2
  279.5 2.8 fusion.116
  283.5 2.3 convolution_convert_fusion.5
  287.7 3.0 fusion.35
  290.8 2.2 convolution_convert_fusion.4
  293.0 2.5 add_convert_fusion.1.term_ref
  295.6 12.3 %reduce-scatter.2.cloned.1.call-done = bf16[256,256]{0,1:T(8,128)(2,1)} async-done(((bf16[1024,256]{0,1:T(8,128)(2,1)}), bf16[256,256]{0,1:T(8,128)(2,1)}) %reduce-scatter.2.cloned.1.call-update) | async-done | bytes 131088 | tf_op jit(solution)/shard_map/reduce_scatter | solution.py:681
  308.8 2.5 fusion.80
  311.7 1.5 collective-permute-start.9
  313.8 2.2 convolution_convert_fusion.3
  316.0 2.3 convolution_convert_fusion.2
  318.9 2.3 fusion.24
  322.7 2.2 fusion.27
  324.9 29.7 %shard_map.205 = bf16[256,2048]{1,0:T(8,128)(2,1)S(1)} custom-call(bf16[512,2048]{1,0:T(8,128)(2,1)S(1)} %add_convert_fusion.1.term_ref, f32[64,2048]{1,0:T(8,128)S(1)} %copy-done.1), custom_call_target="tpu_custom_call" | custom-call | tf_op jit(solution)/shard_map/pallas_call | solution.py:401
  357.9 19.9 %shard_map.207 = (bf16[256,2048]{1,0:T(8,128)(2,1)S(1)}, f32[1,2048]{1,0:T(1,128)S(1)}) custom-call(bf16[256,2048]{1,0:T(8,128)(2,1)S(1)} %convolution_convert_fusion.1.term_ref, f32[64,2048]{1,0:T(8,128)S(1)} %copy-done.4, bf16[256,2048]{1,0:T(8,128)(2,1)S(1)} %pad_maximum_fusion.19.refs_0_.refs_1_, f32[1,2048]{1,0:T(1,128)S(1)} %get-tuple-element.96.refs_2_), custom_call_target="tpu_custom_call" | custom-call | tf_op jit(solution)/shard_map/pallas_call | solution.py:401
  378.5 2.5 add_convert_fusion.7.refs_0_
  381.0 13.0 %collective-permute-done.11 = bf16[1024,512]{1,0:T(8,128)(2,1)S(1)} collective-permute-done((bf16[1024,512]{1,0:T(8,128)(2,1)S(1)}, bf16[1024,512]{1,0:T(8,128)(2,1)S(1)}, u32[]{:S(2)}, u32[]{:S(2)}) %collective-permute-start.11) | collective-permute-done | bytes 1048608 | tf_op jit(solution)/shard_map/ppermute | solution.py:545
  395.5 2.3 add_convert_fusion.6.refs_1_
  398.3 2.3 fusion.7
  400.7 15.9 %collective-permute-done.14 = bf16[1024,512]{1,0:T(8,128)(2,1)} collective-permute-done((bf16[1024,512]{1,0:T(8,128)(2,1)}, bf16[1024,512]{1,0:T(8,128)(2,1)}, u32[]{:S(2)}, u32[]{:S(2)}) %collective-permute-start.14) | collective-permute-done | bytes 1048608 | tf_op jit(solution)/shard_map/ppermute | solution.py:545
  416.6 4.4 add_convert_fusion.5.refs_0_
  421.0 18.0 %collective-permute-done.15 = bf16[1024,512]{1,0:T(8,128)(2,1)} collective-permute-done((bf16[1024,512]{1,0:T(8,128)(2,1)}, bf16[1024,512]{1,0:T(8,128)(2,1)}, u32[]{:S(2)}, u32[]{:S(2)}) %collective-permute-start.15) | collective-permute-done | bytes 1048608 | tf_op jit(solution)/shard_map/ppermute | solution.py:545
  439.1 3.5 add_convert_fusion.4.refs_1_
  442.5 19.0 %collective-permute-done.18 = bf16[1024,512]{1,0:T(8,128)(2,1)} collective-permute-done((bf16[1024,512]{1,0:T(8,128)(2,1)}, bf16[1024,512]{1,0:T(8,128)(2,1)}, u32[]{:S(2)}, u32[]{:S(2)}) %collective-permute-start.18) | collective-permute-done | bytes 1048608 | tf_op jit(solution)/shard_map/ppermute | solution.py:545
  461.5 3.5 add_convert_fusion.3.refs_0_
  465.0 16.4 %collective-permute-done.19 = bf16[1024,512]{1,0:T(8,128)(2,1)} collective-permute-done((bf16[1024,512]{1,0:T(8,128)(2,1)}, bf16[1024,512]{1,0:T(8,128)(2,1)}, u32[]{:S(2)}, u32[]{:S(2)}) %collective-permute-start.19) | collective-permute-done | bytes 1048608 | tf_op jit(solution)/shard_map/ppermute | solution.py:545
  481.8 3.5 add_convert_fusion.2.refs_1_
  485.3 1.6 collective-permute-start.20
  489.5 161.7 %psum.14 = f32[2,1024]{1,0:T(2,128)S(1)} all-reduce(f32[2,1024]{1,0:T(2,128)S(1)} %fusion.85), channel_id=1, replica_groups=mesh['fsdp'=2,'ctx'=4,'tp'=4] {'ctx','tp'}, use_global_device_ids=true, to_apply=%region_5.6 | all-reduce | flops 2048 | bytes 16384 | tf_op jit(solution)/shard_map/psum | solution.py:704
  651.9 10.4 %shard_map.208 = f32[1024,2048]{1,0:T(8,128)} custom-call(s32[1]{0:T(128)} %bitcast.46.part_ref, bf16[1024,512]{1,0:T(8,128)(2,1)} %copy-done.34, bf16[1024,512]{1,0:T(8,128)(2,1)} %add_convert_fusion.6.refs_1_, bf16[1024,512]{1,0:T(8,128)(2,1)} %copy-done.35, bf16[1024,512]{1,0:T(8,128)(2,1)} %collective-permute-done.13.refs_3_), custom_call_target="tpu_custom_call" | custom-call | bytes 12582912 | tf_op jit(solution)/shard_map/pallas_call | solution.py:485
  662.4 10.5 %shard_map.209 = f32[1024,2048]{1,0:T(8,128)} custom-call(s32[1]{0:T(128)} %bitcast.46.part_ref, bf16[1024,512]{1,0:T(8,128)(2,1)} %add_convert_fusion.5.refs_0_, bf16[1024,512]{1,0:T(8,128)(2,1)} %add_convert_fusion.4.refs_1_, bf16[1024,512]{1,0:T(8,128)(2,1)} %collective-permute-done.16.refs_2_, bf16[1024,512]{1,0:T(8,128)(2,1)} %collective-permute-done.17.refs_3_), custom_call_target="tpu_custom_call" | custom-call | bytes 12582912 | tf_op jit(solution)/shard_map/pallas_call | solution.py:485
  673.8 10.4 %shard_map.210 = f32[1024,2048]{1,0:T(8,128)} custom-call(s32[1]{0:T(128)} %bitcast.46.part_ref, bf16[1024,512]{1,0:T(8,128)(2,1)} %add_convert_fusion.3.refs_0_, bf16[1024,512]{1,0:T(8,128)(2,1)} %add_convert_fusion.2.refs_1_, bf16[1024,512]{1,0:T(8,128)(2,1)} %collective-permute-done.20.refs_2_, bf16[1024,512]{1,0:T(8,128)(2,1)} %copy-done.36), custom_call_target="tpu_custom_call" | custom-call | bytes 12582912 | tf_op jit(solution)/shard_map/pallas_call | solution.py:485
  684.2 3.3 fusion.109
  687.5 2.9 copy.53
  693.5 1.8 copy.56
  (219 shorter events, 42.3 us)
Async XLA Ops:
  7.2 300.7 %reduce-scatter.2.cloned.1.call-start = ((), (), s32[]{:S(2)}) async-start(), calls=%async_computation.1 | async-start | bytes 655360 | tf_op jit(solution)/shard_map/reduce_scatter | solution.py:681
  9.0 74.7 %copy-start.18 = (bf16[256,1024]{1,0:T(8,128)(2,1)}, bf16[256,1024]{1,0:T(8,128)(2,1)S(1)}, u32[]{:S(2)}) copy-start(bf16[256,1024]{1,0:T(8,128)(2,1)S(1)} %get-tuple-element.106) | copy-start | bytes 1572868
  9.0 74.7 %copy-start.19 = (bf16[256,1024]{1,0:T(8,128)(2,1)}, bf16[256,1024]{1,0:T(8,128)(2,1)S(1)}, u32[]{:S(2)}) copy-start(bf16[256,1024]{1,0:T(8,128)(2,1)S(1)} %get-tuple-element.107) | copy-start | bytes 1572868
  53.6 3.7 copy-start.58
  53.6 3.7 copy-start.59
  53.6 5.8 copy-start.37
  56.8 101.4 %collective-permute-start.7 = (bf16[1024,512]{1,0:T(8,128)(2,1)}, bf16[1024,512]{1,0:T(8,128)(2,1)}, u32[]{:S(2)}, u32[]{:S(2)}) collective-permute-start(bf16[1024,512]{1,0:T(8,128)(2,1)} %get-tuple-element.70), channel_id=1, source_target_pairs={{0,16},{16,0},{1,17},{17,1},{2,18},{18,2},{3,19},{19,3},{4,20},{20... | collective-permute-start | bytes 3145736 | tf_op jit(solution)/shard_map/ppermute | solution.py:545
  57.4 5.3 copy-start.38
  57.4 25.7 %collective-permute-start = (bf16[2,1024]{1,0:T(2,128)(2,1)S(1)}, bf16[2,1024]{1,0:T(2,128)(2,1)S(1)}, u32[]{:S(2)}, u32[]{:S(2)}) collective-permute-start(bf16[2,1024]{1,0:T(2,128)(2,1)S(1)} %pad_maximum_fusion.34), channel_id=1, source_target_pairs={{0,16},{16,0},{1,17},{17,1},{2,18},{18,2},{3,19},{19,3},{4,20},{20... | collective-permute-start | bytes 12296 | tf_op jit(solution)/shard_map/ppermute | solution.py:545
  58.9 52.7 %collective-permute-start.1 = (bf16[1024,512]{1,0:T(8,128)(2,1)}, bf16[1024,512]{1,0:T(8,128)(2,1)}, u32[]{:S(2)}, u32[]{:S(2)}) collective-permute-start(bf16[1024,512]{1,0:T(8,128)(2,1)} %param.19), channel_id=1, source_target_pairs={{0,16},{16,0},{1,17},{17,1},{2,18},{18,2},{3,19},{19,3},{4,20},{20... | collective-permute-start | bytes 3145736 | tf_op jit(solution)/shard_map/ppermute | solution.py:545
  61.1 102.6 %collective-permute-start.6 = (bf16[1024,512]{1,0:T(8,128)(2,1)}, bf16[1024,512]{1,0:T(8,128)(2,1)}, u32[]{:S(2)}, u32[]{:S(2)}) collective-permute-start(bf16[1024,512]{1,0:T(8,128)(2,1)} %get-tuple-element.68), channel_id=1, source_target_pairs={{0,16},{16,0},{1,17},{17,1},{2,18},{18,2},{3,19},{19,3},{4,20},{20... | collective-permute-start | bytes 3145736 | tf_op jit(solution)/shard_map/ppermute | solution.py:545
  64.2 103.4 %collective-permute-start.5 = (bf16[1024,512]{1,0:T(8,128)(2,1)}, bf16[1024,512]{1,0:T(8,128)(2,1)}, u32[]{:S(2)}, u32[]{:S(2)}) collective-permute-start(bf16[1024,512]{1,0:T(8,128)(2,1)} %get-tuple-element.66), channel_id=1, source_target_pairs={{0,16},{16,0},{1,17},{17,1},{2,18},{18,2},{3,19},{19,3},{4,20},{20... | collective-permute-start | bytes 3145736 | tf_op jit(solution)/shard_map/ppermute | solution.py:545
  83.1 135.2 %collective-permute-start.4 = (bf16[1024,512]{1,0:T(8,128)(2,1)}, bf16[1024,512]{1,0:T(8,128)(2,1)}, u32[]{:S(2)}, u32[]{:S(2)}) collective-permute-start(bf16[1024,512]{1,0:T(8,128)(2,1)} %get-tuple-element.69), channel_id=1, source_target_pairs={{0,16},{16,0},{1,17},{17,1},{2,18},{18,2},{3,19},{19,3},{4,20},{20... | collective-permute-start | bytes 3145736 | tf_op jit(solution)/shard_map/ppermute | solution.py:545
  104.0 2.4 copy-start.25
  107.8 3.8 copy-start.16
  109.0 2.7 copy-start.24
  109.0 4.2 copy-start.20
  111.6 3.7 copy-start.26
  111.6 83.8 %collective-permute-start.2 = (bf16[1024,512]{1,0:T(8,128)(2,1)S(1)}, bf16[1024,512]{1,0:T(8,128)(2,1)S(1)}, u32[]{:S(2)}, u32[]{:S(2)}) collective-permute-start(bf16[1024,512]{1,0:T(8,128)(2,1)S(1)} %copy-done.24), channel_id=1, source_target_pairs={{0,16},{16,0},{1,17},{17,1},{2,18},{18,2},{3,19},{19,3},{4,20},{20... | collective-permute-start | bytes 3145736 | tf_op jit(solution)/shard_map/ppermute | solution.py:545
  114.5 43.7 %copy-start.23 = (bf16[1024,512]{1,0:T(8,128)(2,1)S(1)}, bf16[1024,512]{1,0:T(8,128)(2,1)}, u32[]{:S(2)}) copy-start(bf16[1024,512]{1,0:T(8,128)(2,1)} %get-tuple-element.67) | copy-start | bytes 3145732
  114.5 44.1 %copy-start.6 = (bf16[1024,2048]{1,0:T(8,128)(2,1)S(1)}, bf16[1024,2048]{1,0:T(8,128)(2,1)}, u32[]{:S(2)}) copy-start(bf16[1024,2048]{1,0:T(8,128)(2,1)} %copy-done.5) | copy-start | bytes 12582916
  158.2 57.8 %copy-start.9 = (bf16[1024,2048]{1,0:T(8,128)(2,1)}, bf16[1024,2048]{1,0:T(8,128)(2,1)S(1)}, u32[]{:S(2)}) copy-start(bf16[1024,2048]{1,0:T(8,128)(2,1)S(1)} %get-tuple-element.26) | copy-start | bytes 12582916
  158.2 71.2 %copy-start = (f32[64,2048]{1,0:T(8,128)}, f32[64,2048]{1,0:T(8,128)S(1)}, u32[]{:S(2)}) copy-start(f32[64,2048]{1,0:T(8,128)S(1)} %get-tuple-element.30.refs_0_) | copy-start | bytes 1572868
  158.2 57.8 %collective-permute-start.3 = (bf16[1024,512]{1,0:T(8,128)(2,1)S(1)}, bf16[1024,512]{1,0:T(8,128)(2,1)S(1)}, u32[]{:S(2)}, u32[]{:S(2)}) collective-permute-start(bf16[1024,512]{1,0:T(8,128)(2,1)S(1)} %copy-done.23), channel_id=1, source_target_pairs={{0,16},{16,0},{1,17},{17,1},{2,18},{18,2},{3,19},{19,3},{4,20},{20... | collective-permute-start | bytes 3145736 | tf_op jit(solution)/shard_map/ppermute | solution.py:545
  173.3 3.6 copy-start.50
  173.3 53.1 %copy-start.42 = (bf16[1024,512]{1,0:T(8,128)(2,1)}, bf16[1024,512]{1,0:T(8,128)(2,1)S(1)}, u32[]{:S(2)}) copy-start(bf16[1024,512]{1,0:T(8,128)(2,1)S(1)} %get-tuple-element.59) | copy-start | bytes 3145732
  197.8 20.5 %copy-start.21 = (bf16[1024,512]{1,0:T(8,128)(2,1)S(1)}, bf16[1024,512]{1,0:T(8,128)(2,1)}, u32[]{:S(2)}) copy-start(bf16[1024,512]{1,0:T(8,128)(2,1)} %get-tuple-element.69) | copy-start | bytes 3145732
  265.0 5.0 copy-start.33
  265.0 10.3 %slice-start = ((s8[8388608]{0:T(1024)(128)(4,1)}), s8[4194304]{0:T(1024)(128)(4,1)S(1)}, s32[]{:S(2)}) async-start(s8[8388608]{0:T(1024)(128)(4,1)} %bitcast.112), calls=%async_computation.3 | async-start | bytes 8388608
  270.0 5.4 slice-start.1
  279.5 3.5 copy-start.10
  279.5 4.0 copy-start.56
  286.7 397.5 %all-reduce.2.cloned.1.call-start = ((), (), s32[]{:S(2)}) async-start(), calls=%async_computation.2 | async-start | bytes 5242880 | tf_op jit(solution)/shard_map/psum | solution.py:697
  287.0 90.9 %collective-permute-start.10 = (bf16[1024,512]{1,0:T(8,128)(2,1)}, bf16[1024,512]{1,0:T(8,128)(2,1)}, u32[]{:S(2)}, u32[]{:S(2)}) collective-permute-start(bf16[1024,512]{1,0:T(8,128)(2,1)} %convolution_convert_fusion.5), channel_id=1, source_target_pairs={{0,16},{16,0},{1,17},{17,1},{2,18},{18,2},{3,19},{19,3},{4,20},{20... | collective-permute-start | bytes 3145736 | tf_op jit(solution)/shard_map/ppermute | solution.py:545
  287.7 3.0 copy-start.11
  287.7 3.1 copy-start.43
  308.8 2.5 copy-start.17
  311.3 2.5 copy-start.54
  311.7 4.3 copy-start.51
  311.7 86.1 %collective-permute-start.9 = (bf16[1024,1280]{0,1:T(8,128)(2,1)S(1)}, bf16[1024,1280]{0,1:T(8,128)(2,1)S(1)}, u32[]{:S(2)}, u32[]{:S(2)}) collective-permute-start(bf16[1024,1280]{0,1:T(8,128)(2,1)S(1)} %fusion.8), channel_id=1, source_target_pairs={{0,16},{16,0},{1,17},{17,1},{2,18},{18,2},{3,19},{19,3},{4,20},{20... | collective-permute-start | bytes 7864328 | tf_op jit(solution)/shard_map/ppermute | solution.py:545
  316.0 2.9 copy-start.40
  318.9 3.8 copy-start.48
  321.2 3.7 copy-start.1
  321.2 72.8 %collective-permute-start.11 = (bf16[1024,512]{1,0:T(8,128)(2,1)S(1)}, bf16[1024,512]{1,0:T(8,128)(2,1)S(1)}, u32[]{:S(2)}, u32[]{:S(2)}) collective-permute-start(bf16[1024,512]{1,0:T(8,128)(2,1)S(1)} %copy-done.60), channel_id=1, source_target_pairs={{0,16},{16,0},{1,17},{17,1},{2,18},{18,2},{3,19},{19,3},{4,20},{20... | collective-permute-start | bytes 3145736 | tf_op jit(solution)/shard_map/ppermute | solution.py:545
  324.9 31.9 %copy-start.15 = (bf16[2048,768]{1,0:T(8,128)(2,1)S(1)}, bf16[2048,768]{1,0:T(8,128)(2,1)}, u32[]{:S(2)}) copy-start(bf16[2048,768]{1,0:T(8,128)(2,1)} %copy-done.14) | copy-start | bytes 9437188
  354.6 62.0 %collective-permute-start.14 = (bf16[1024,512]{1,0:T(8,128)(2,1)}, bf16[1024,512]{1,0:T(8,128)(2,1)}, u32[]{:S(2)}, u32[]{:S(2)}) collective-permute-start(bf16[1024,512]{1,0:T(8,128)(2,1)} %convolution_convert_fusion.3), channel_id=1, source_target_pairs={{0,16},{16,0},{1,17},{17,1},{2,18},{18,2},{3,19},{19,3},{4,20},{20... | collective-permute-start | bytes 3145736 | tf_op jit(solution)/shard_map/ppermute | solution.py:545
  355.2 83.8 %collective-permute-start.15 = (bf16[1024,512]{1,0:T(8,128)(2,1)}, bf16[1024,512]{1,0:T(8,128)(2,1)}, u32[]{:S(2)}, u32[]{:S(2)}) collective-permute-start(bf16[1024,512]{1,0:T(8,128)(2,1)} %convolution_convert_fusion.2), channel_id=1, source_target_pairs={{0,16},{16,0},{1,17},{17,1},{2,18},{18,2},{3,19},{19,3},{4,20},{20... | collective-permute-start | bytes 3145736 | tf_op jit(solution)/shard_map/ppermute | solution.py:545
  357.8 20.6 %copy-start.57 = (bf16[1024,512]{1,0:T(8,128)(2,1)S(1)}, bf16[1024,512]{1,0:T(8,128)(2,1)}, u32[]{:S(2)}) copy-start(bf16[1024,512]{1,0:T(8,128)(2,1)} %copy-done.55) | copy-start | bytes 3145732
  377.8 17.7 %copy-start.44 = (bf16[1024,512]{1,0:T(8,128)(2,1)S(1)}, bf16[1024,512]{1,0:T(8,128)(2,1)}, u32[]{:S(2)}) copy-start(bf16[1024,512]{1,0:T(8,128)(2,1)} %copy-done.42) | copy-start | bytes 3145732
  377.8 83.7 %collective-permute-start.18 = (bf16[1024,512]{1,0:T(8,128)(2,1)}, bf16[1024,512]{1,0:T(8,128)(2,1)}, u32[]{:S(2)}, u32[]{:S(2)}) collective-permute-start(bf16[1024,512]{1,0:T(8,128)(2,1)} %fusion.24), channel_id=1, source_target_pairs={{0,16},{16,0},{1,17},{17,1},{2,18},{18,2},{3,19},{19,3},{4,20},{20... | collective-permute-start | bytes 3145736 | tf_op jit(solution)/shard_map/ppermute | solution.py:545
  381.0 35.6 %copy-start.34 = (bf16[1024,512]{1,0:T(8,128)(2,1)}, bf16[1024,512]{1,0:T(8,128)(2,1)S(1)}, u32[]{:S(2)}) copy-start(bf16[1024,512]{1,0:T(8,128)(2,1)S(1)} %add_convert_fusion.7.refs_0_) | copy-start | bytes 3145732
  394.0 87.4 %collective-permute-start.19 = (bf16[1024,512]{1,0:T(8,128)(2,1)}, bf16[1024,512]{1,0:T(8,128)(2,1)}, u32[]{:S(2)}, u32[]{:S(2)}) collective-permute-start(bf16[1024,512]{1,0:T(8,128)(2,1)} %fusion.27), channel_id=1, source_target_pairs={{0,16},{16,0},{1,17},{17,1},{2,18},{18,2},{3,19},{19,3},{4,20},{20... | collective-permute-start | bytes 3145736 | tf_op jit(solution)/shard_map/ppermute | solution.py:545
  397.8 87.5 %collective-permute-start.8 = (f32[2,1024]{1,0:T(2,128)S(1)}, f32[2,1024]{1,0:T(2,128)S(1)}, u32[]{:S(2)}, u32[]{:S(2)}) collective-permute-start(f32[2,1024]{1,0:T(2,128)S(1)} %pad_maximum_fusion.33), channel_id=1, source_target_pairs={{0,16},{16,0},{1,17},{17,1},{2,18},{18,2},{3,19},{19,3},{4,20},{20... | collective-permute-start | bytes 24584 | tf_op jit(solution)/shard_map/ppermute | solution.py:545
  400.7 38.4 %copy-start.13 = (bf16[1024,2048]{1,0:T(8,128)(2,1)S(1)}, bf16[1024,2048]{1,0:T(8,128)(2,1)}, u32[]{:S(2)}) copy-start(bf16[1024,2048]{1,0:T(8,128)(2,1)} %copy-done.9) | copy-start | bytes 12582916
  400.7 38.4 %copy-start.52 = (bf16[1024,512]{1,0:T(8,128)(2,1)S(1)}, bf16[1024,512]{1,0:T(8,128)(2,1)}, u32[]{:S(2)}) copy-start(bf16[1024,512]{1,0:T(8,128)(2,1)} %copy-done.50) | copy-start | bytes 3145732
  416.6 70.3 %collective-permute-start.12 = (bf16[1024,512]{1,0:T(8,128)(2,1)S(1)}, bf16[1024,512]{1,0:T(8,128)(2,1)S(1)}, u32[]{:S(2)}, u32[]{:S(2)}) collective-permute-start(bf16[1024,512]{1,0:T(8,128)(2,1)S(1)} %add_convert_fusion.7.refs_0_), channel_id=1, source_target_pairs={{0,4},{4,0},{8,12},{12,8},{1,5},{5,1},{9,13},{13,9},{2,6},{6,2},{1... | collective-permute-start | bytes 3145736 | tf_op jit(solution)/shard_map/ppermute | solution.py:650
  421.0 40.5 %copy-start.8 = (bf16[1024,2048]{1,0:T(8,128)(2,1)S(1)}, bf16[1024,2048]{1,0:T(8,128)(2,1)}, u32[]{:S(2)}) copy-start(bf16[1024,2048]{1,0:T(8,128)(2,1)} %copy-done.5) | copy-start | bytes 12582916
  421.0 40.5 %copy-start.41 = (bf16[1024,512]{1,0:T(8,128)(2,1)S(1)}, bf16[1024,512]{1,0:T(8,128)(2,1)}, u32[]{:S(2)}) copy-start(bf16[1024,512]{1,0:T(8,128)(2,1)} %get-tuple-element.64) | copy-start | bytes 3145732
  439.0 212.9 %collective-permute-start.13 = (bf16[1024,512]{1,0:T(8,128)(2,1)}, bf16[1024,512]{1,0:T(8,128)(2,1)}, u32[]{:S(2)}, u32[]{:S(2)}) collective-permute-start(bf16[1024,512]{1,0:T(8,128)(2,1)} %add_convert_fusion.6.refs_1_), channel_id=1, source_target_pairs={{0,4},{4,0},{8,12},{12,8},{1,5},{5,1},{9,13},{13,9},{2,6},{6,2},{1... | collective-permute-start | bytes 3145736 | tf_op jit(solution)/shard_map/ppermute | solution.py:650
  442.5 39.3 %copy-start.49 = (bf16[1024,512]{1,0:T(8,128)(2,1)S(1)}, bf16[1024,512]{1,0:T(8,128)(2,1)}, u32[]{:S(2)}) copy-start(bf16[1024,512]{1,0:T(8,128)(2,1)} %get-tuple-element.60) | copy-start | bytes 3145732
  461.5 200.8 %collective-permute-start.16 = (bf16[1024,512]{1,0:T(8,128)(2,1)}, bf16[1024,512]{1,0:T(8,128)(2,1)}, u32[]{:S(2)}, u32[]{:S(2)}) collective-permute-start(bf16[1024,512]{1,0:T(8,128)(2,1)} %add_convert_fusion.5.refs_0_), channel_id=1, source_target_pairs={{0,4},{4,0},{8,12},{12,8},{1,5},{5,1},{9,13},{13,9},{2,6},{6,2},{1... | collective-permute-start | bytes 3145736 | tf_op jit(solution)/shard_map/ppermute | solution.py:650
  481.4 181.0 %collective-permute-start.17 = (bf16[1024,512]{1,0:T(8,128)(2,1)}, bf16[1024,512]{1,0:T(8,128)(2,1)}, u32[]{:S(2)}, u32[]{:S(2)}) collective-permute-start(bf16[1024,512]{1,0:T(8,128)(2,1)} %add_convert_fusion.4.refs_1_), channel_id=1, source_target_pairs={{0,4},{4,0},{8,12},{12,8},{1,5},{5,1},{9,13},{13,9},{2,6},{6,2},{1... | collective-permute-start | bytes 3145736 | tf_op jit(solution)/shard_map/ppermute | solution.py:650
  485.3 187.5 %collective-permute-start.20 = (bf16[1024,512]{1,0:T(8,128)(2,1)}, bf16[1024,512]{1,0:T(8,128)(2,1)}, u32[]{:S(2)}, u32[]{:S(2)}) collective-permute-start(bf16[1024,512]{1,0:T(8,128)(2,1)} %add_convert_fusion.3.refs_0_), channel_id=1, source_target_pairs={{0,4},{4,0},{8,12},{12,8},{1,5},{5,1},{9,13},{13,9},{2,6},{6,2},{1... | collective-permute-start | bytes 3145736 | tf_op jit(solution)/shard_map/ppermute | solution.py:650
  486.9 185.9 %collective-permute-start.21 = (bf16[1024,512]{1,0:T(8,128)(2,1)}, bf16[1024,512]{1,0:T(8,128)(2,1)S(1)}, u32[]{:S(2)}, u32[]{:S(2)}) collective-permute-start(bf16[1024,512]{1,0:T(8,128)(2,1)} %add_convert_fusion.2.refs_1_), channel_id=1, source_target_pairs={{0,4},{4,0},{8,12},{12,8},{1,5},{5,1},{9,13},{13,9},{2,6},{6,2},{1... | collective-permute-start | bytes 3145736 | tf_op jit(solution)/shard_map/ppermute | solution.py:650
  (23 other events, 36.8 us)
Sparse Core Ops, SparseCore 0:
  286.8 20.9 reduce-scatter.1
  400.8 174.3 all-reduce.1

commit v3 on v2

--- a/solution.py
+++ b/solution.py
@@ -122,7 +122,7 @@
     return me, core, level, partner, others
 
 
-def enter(ctx_size, tp_size, along=False, pair=False, side=False, tensor=True):
+def enter(ctx_size, tp_size, along=False, pair=False, side=False, tensor=True, line=False):
     place = lax.axis_index("ctx")
     barrier = pltpu.get_barrier_semaphore()
 
@@ -154,6 +154,10 @@
     if pair:
         greet({"ctx": place + 1 - 2 * lax.rem(place, 2)})
         count = count + 1
+    if line:
+        for step in range(1, ctx_size):
+            greet({"ctx": lax.rem(place + step, ctx_size)})
+        count = count + ctx_size - 1
     pl.semaphore_wait(barrier, count)
 
 
@@ -294,30 +298,274 @@
                 hop(offset, step, spot(offset, me)).wait_send()
 
 
-def reduce_gather(term, extras, finish, side_shapes, mesh_shape, identity, blocks, across):
+def line_sems(ctx_size):
+    spread = 2 * ctx_size - 1
+    return [DMA((spread + 1,)), DMA((spread,)), DMA((1,))]
+
+
+def line_gather(mine, all_ref, ctx_size, sems):
+    hop_send, hop_recv, own_sem = sems
+    place = lax.axis_index("ctx")
+    rows = mine.shape[0]
+    middle = ctx_size - 1
+    offsets = [o for step in range(1, ctx_size) for o in (-step, step)]
+
+    def spot(offset):
+        return rows_at(all_ref, (place + offset) * rows, rows)
+
+    def hop(offset, step, src):
+        slot = 2 * middle + 1 if offset == 0 and step < 0 else middle + offset
+        return remote(
+            src, spot(offset), hop_send.at[slot], hop_recv.at[middle + offset - step],
+            {"ctx": place + step},
+        )
+
+    def arrival(offset):
+        step = -1 if offset < 0 else 1
+        return remote(
+            spot(offset), spot(offset), hop_send.at[middle + offset],
+            hop_recv.at[middle + offset], {"ctx": place + step},
+        )
+
+    def valid(offset):
+        return place + offset >= 0 if offset < 0 else place + offset < ctx_size
+
+    def onward(offset):
+        if offset < 0:
+            return 1, jnp.logical_and(place + offset >= 0, place + 1 < ctx_size)
+        return -1, jnp.logical_and(place + offset < ctx_size, place > 0)
+
+    own = pltpu.make_async_copy(mine, spot(0), own_sem.at[0])
+    ends = ((1, place + 1 < ctx_size), (-1, place > 0))
+
+    def begin():
+        for step, there in ends:
+            @pl.when(there)
+            def _(step=step):
+                hop(0, step, mine).start()
+
+        own.start()
+
+    def finish():
+        for offset in offsets:
+            @pl.when(valid(offset))
+            def _(offset=offset):
+                arrival(offset).wait_recv()
+
+            step, more = onward(offset)
+
+            @pl.when(more)
+            def _(offset=offset, step=step):
+                hop(offset, step, spot(offset)).start()
+
+        own.wait()
+        for step, there in ends:
+            @pl.when(there)
+            def _(step=step):
+                hop(0, step, mine).wait_send()
+
+        for offset in offsets:
+            step, more = onward(offset)
+
+            @pl.when(more)
+            def _(offset=offset, step=step):
+                hop(offset, step, spot(offset)).wait_send()
+
+    return begin, finish
+
+
+class AttnTail:
+    def __init__(self, pre_slabs, norm_all, gain_second, mesh_shape):
+        self.ctx_size, self.tp_size = mesh_shape
+        self.inputs = (pre_slabs, norm_all, gain_second)
+        self.wide, self.rows = pre_slabs.shape[1:]
+        self.half = norm_all.shape[1] // 2
+        levels = self.tp_size // 2
+        self.levels = levels
+        self.outs = (
+            jax.ShapeDtypeStruct((self.ctx_size * self.wide, self.half), BF16),
+            jax.ShapeDtypeStruct((2, self.half), F32),
+        )
+        self.out_specs = (HBM_SPEC, VMEM_SPEC)
+        chips = max(levels - 1, 1)
+        self.scratch = [
+            pltpu.VMEM(pre_slabs.shape, BF16),
+            pltpu.VMEM((self.wide, self.half), F32),
+            pltpu.VMEM((self.wide, self.half), BF16),
+            pltpu.VMEM((self.wide, self.half), BF16),
+            pltpu.VMEM((self.wide, self.half), BF16),
+            pltpu.VMEM((4, 2, self.half), F32),
+            pltpu.VMEM((levels, 2, self.half), F32),
+            pltpu.VMEM((self.ctx_size, 2, self.half), F32),
+            DMA((self.ctx_size,)), DMA((self.ctx_size,)),
+            DMA((6,)),
+            DMA((chips,)), DMA((chips,)),
+            DMA((self.ctx_size,)), DMA((self.ctx_size,)),
+        ] + line_sems(self.ctx_size)
+
+    def bind(self, in_refs, out_refs, side_refs, scratch):
+        pre_ref, norm_ref, gain_second_ref = in_refs
+        all_ref, gains_ref = out_refs
+        slabs, own_half, far_half, from_far, quarter, swaps, by_level, by_place = scratch[:8]
+        all_send, all_recv, duo, lev_send, lev_recv, ctx_send, ctx_recv = scratch[8:15]
+        ctx_size, levels, half, rows = self.ctx_size, self.levels, self.half, self.rows
+        place = lax.axis_index("ctx")
+        _, _, level, partner, others = tp_peers(self.tp_size)
+        far = {"fsdp": 1 - lax.axis_index("fsdp")}
+        tile = min(512, half)
+        line_begin, line_finish = line_gather(quarter, all_ref, ctx_size, scratch[15:18])
+
+        def slab(step):
+            peer = lax.rem(place + step, ctx_size)
+            return remote(
+                pre_ref.at[peer], slabs.at[place], all_send.at[step], all_recv.at[step], {"ctx": peer}
+            )
+
+        def slab_arrival(step):
+            src = lax.rem(place + ctx_size - step, ctx_size)
+            return remote(
+                slabs.at[src], slabs.at[src], all_send.at[step], all_recv.at[step], {"ctx": src}
+            )
+
+        grads = remote(far_half, from_far, duo.at[0], duo.at[1], far)
+        gain_x = remote(swaps.at[0], swaps.at[1], duo.at[2], duo.at[3], far)
+        gain_core = remote(swaps.at[2], swaps.at[3], duo.at[4], duo.at[5], {"tp": partner})
+
+        def gain_level(index):
+            return remote(
+                by_level.at[level], by_level.at[level], lev_send.at[index],
+                lev_recv.at[levels - 2 - index], {"tp": others[index]},
+            )
+
+        def gain_level_arrival(index):
+            where = by_level.at[lax.rem(level + 1 + index, levels)]
+            return remote(where, where, lev_send.at[index], lev_recv.at[index], {"tp": others[index]})
+
+        def gain_place(step):
+            peer = lax.rem(place + step, ctx_size)
+            return remote(
+                by_place.at[place], by_place.at[place], ctx_send.at[step], ctx_recv.at[step],
+                {"ctx": peer},
+            )
+
+        def gain_place_arrival(step):
+            src = lax.rem(place + ctx_size - step, ctx_size)
+            where = by_place.at[src]
+            return remote(where, where, ctx_send.at[step], ctx_recv.at[step], {"ctx": src})
+
+        def product(at):
+            columns = pl.ds(pl.multiple_of(at, tile), tile)
+            total = jnp.dot(
+                slabs[0], norm_ref[0:rows, columns], preferred_element_type=F32
+            )
+            for z in range(1, ctx_size):
+                total += jnp.dot(
+                    slabs[z], norm_ref[z * rows : (z + 1) * rows, columns],
+                    preferred_element_type=F32,
+                )
+            return total
+
+        def begin():
+            for step in range(1, ctx_size):
+                slab(step).start()
+            slabs[place] = pre_ref[place]
+
+        def middle():
+            for step in range(1, ctx_size):
+                slab_arrival(step).wait_recv()
+
+            @pl.loop(0, half // tile)
+            def _(i):
+                far_half[:, pl.ds(pl.multiple_of(i * tile, tile), tile)] = product(
+                    half + i * tile
+                ).astype(BF16)
+
+            grads.start()
+
+            @pl.loop(0, half // tile)
+            def _(i):
+                own_half[:, pl.ds(pl.multiple_of(i * tile, tile), tile)] = product(i * tile)
+
+        def end():
+            gain_first = side_refs[0]
+            swaps[0, 0:1, :] = gain_first[:, half:]
+            swaps[0, 1:2, :] = gain_second_ref[:, half:]
+            gain_x.start()
+            grads.wait_recv()
+            quarter[...] = (own_half[...] + from_far[...].astype(F32)).astype(BF16)
+            line_begin()
+            gain_x.wait_recv()
+            swaps[2, 0:1, :] = gain_first[:, :half] + swaps[1, 0:1, :]
+            swaps[2, 1:2, :] = gain_second_ref[:, :half] + swaps[1, 1:2, :]
+            gain_core.start()
+            gain_core.wait_recv()
+            by_level[level] = swaps[2] + swaps[3]
+            for index in range(levels - 1):
+                gain_level(index).start()
+            for index in range(levels - 1):
+                gain_level_arrival(index).wait_recv()
+            total = by_level[0]
+            for lev in range(1, levels):
+                total += by_level[lev]
+            by_place[place] = total
+            for step in range(1, ctx_size):
+                gain_place(step).start()
+            for step in range(1, ctx_size):
+                gain_place_arrival(step).wait_recv()
+            total = by_place[0]
+            for z in range(1, ctx_size):
+                total += by_place[z]
+            gains_ref[...] = total
+            line_finish()
+            for step in range(1, ctx_size):
+                slab(step).wait_send()
+                gain_place(step).wait_send()
+            for index in range(levels - 1):
+                gain_level(index).wait_send()
+            grads.wait_send()
+            gain_x.wait_send()
+            gain_core.wait_send()
+
+        return begin, middle, end
+
+
+def reduce_gather(term, extras, finish, side_shapes, mesh_shape, identity, blocks, across, aside=None):
     ctx_size, tp_size = mesh_shape
     levels = tp_size // 2
     width = term.shape[1]
     block_rows = term.shape[0] // blocks
     rows = block_rows // tp_size
     reach = ctx_size if across else 1
+    beside = aside is not None
+    aside_inputs = aside.inputs if beside else ()
+    aside_outs = aside.outs if beside else ()
+    aside_scratch = aside.scratch if beside else []
 
     def kernel(term_ref, *refs):
         extra_refs = refs[: len(extras)]
         refs = refs[len(extras) :]
+        aside_in = refs[: len(aside_inputs)]
+        refs = refs[len(aside_inputs) :]
         all_ref = refs[0]
         side_refs = refs[1 : 1 + len(side_shapes)]
         refs = refs[1 + len(side_shapes) :]
+        aside_out = refs[: len(aside_outs)]
+        refs = refs[len(aside_outs) :]
         from_core, stage, from_chip, mine = refs[:4]
         refs = refs[4:]
         if blocks == 2:
             pair_stage, from_pair = refs[:2]
             refs = refs[2:]
         sems = refs[:7]
-        core_send, core_recv, chip_send, chip_recv, pair_sems = refs[7:]
+        core_send, core_recv, chip_send, chip_recv, pair_sems = refs[7:12]
         place = lax.axis_index("ctx")
         me, core, level, partner, others = tp_peers(tp_size)
-        enter(ctx_size, tp_size, along=across, pair=blocks == 2)
+        enter(ctx_size, tp_size, along=across, pair=blocks == 2, side=beside, line=beside)
+        if beside:
+            aside_begin, aside_middle, aside_end = aside.bind(
+                aside_in, aside_out, side_refs, refs[12:]
+            )
+            aside_begin()
 
         def to_core(block, lev):
             slot = block * levels + lev
@@ -351,6 +599,8 @@
                     BF16
                 )
             to_chip(index).start()
+        if beside:
+            aside_middle()
         for index in range(levels - 1):
             to_chip(index).wait_recv()
 
@@ -377,6 +627,8 @@
         start = pl.multiple_of(me * rows, rows)
         mine[...] = finish(total, start, *extra_refs, *side_refs)
         gather_rows(mine, all_ref, reach, tp_size, sems)
+        if beside:
+            aside_end()
         for lev in range(levels):
             for block in range(blocks):
                 to_core(block, lev).wait_send()
@@ -398,52 +650,64 @@
     scratch += [
         DMA((blocks * levels,)), DMA((blocks * levels,)), DMA((chips,)), DMA((chips,)), DMA((2,)),
     ]
+    scratch += aside_scratch
     return pl.pallas_call(
         kernel,
         out_shape=(
             jax.ShapeDtypeStruct((reach * block_rows, width), BF16),
             *(jax.ShapeDtypeStruct(shape, F32) for shape in side_shapes),
+            *aside_outs,
         ),
-        in_specs=[VMEM_SPEC] * (1 + len(extras)),
-        out_specs=(HBM_SPEC,) + (VMEM_SPEC,) * len(side_shapes),
+        in_specs=[VMEM_SPEC] * (1 + len(extras) + len(aside_inputs)),
+        out_specs=(HBM_SPEC,) + (VMEM_SPEC,) * len(side_shapes)
+        + (aside.out_specs if beside else ()),
         scratch_shapes=scratch,
         compiler_params=pltpu.CompilerParams(
             collective_id=identity, has_side_effects=True, vmem_limit_bytes=32 << 20
         ),
-    )(term, *extras)
-
-
-def opening(cot_rows, weights, mesh_shape, identity):
+    )(term, *extras, *aside_inputs)
+
+
+def opening(cot_rows, groups, gains, mesh_shape, identity):
     ctx_size, tp_size = mesh_shape
     block_rows, width = cot_rows.shape
     rows = block_rows // tp_size
+    weights = [w for group in groups for w in group]
     depth = weights[0].shape[0]
-    columns = sum(w.shape[1] for w in weights)
+    places = []
+    for g, group in enumerate(groups):
+        at = 0
+        for w in group:
+            places.append((g, at, w.shape[1]))
+            at += w.shape[1]
+    wholes = [
+        jax.ShapeDtypeStruct((2 * depth, sum(w.shape[1] for w in group)), BF16) for group in groups
+    ]
 
     def kernel(cot_ref, *refs):
         weight_refs = refs[: len(weights)]
-        all_ref, whole_ref = refs[len(weights) : len(weights) + 2]
-        sems = refs[len(weights) + 2 : len(weights) + 9]
-        send, recv = refs[len(weights) + 9 :]
+        gain_ref = refs[len(weights)]
+        refs = refs[len(weights) + 1 :]
+        all_ref, gain_far_ref = refs[:2]
+        whole_refs = refs[2 : 2 + len(groups)]
+        refs = refs[2 + len(groups) :]
+        sems = refs[:7]
+        send, recv = refs[7:]
         enter(ctx_size, tp_size, along=True, side=True)
         far = {"fsdp": 1 - lax.axis_index("fsdp")}
-        swaps = []
-        at = 0
-        for i, ref in enumerate(weight_refs):
-            wide = ref.shape[1]
+        last = len(weights)
+        swaps = [remote(gain_ref, gain_far_ref, send.at[last], recv.at[last], far)]
+        for i, (g, at, wide) in enumerate(places):
             swaps.append(
                 remote(
-                    ref, whole_ref.at[pl.ds(depth, depth), pl.ds(at, wide)], send.at[i], recv.at[i],
-                    far,
+                    weight_refs[i], whole_refs[g].at[pl.ds(depth, depth), pl.ds(at, wide)],
+                    send.at[i], recv.at[i], far,
                 )
             )
-            swaps[-1].start()
-            at += wide
-        at = 0
-        for ref in weight_refs:
-            wide = ref.shape[1]
-            whole_ref[0:depth, at : at + wide] = ref[...]
-            at += wide
+        for swap in swaps:
+            swap.start()
+        for i, (g, at, wide) in enumerate(places):
+            whole_refs[g][0:depth, at : at + wide] = weight_refs[i][...]
         mine = rows_at(cot_ref, lax.axis_index("tp") * rows, rows)
         gather_rows(mine, all_ref, ctx_size, tp_size, sems, block=cot_ref)
         for swap in swaps:
@@ -453,22 +717,24 @@
         kernel,
         out_shape=(
             jax.ShapeDtypeStruct((ctx_size * block_rows, width), BF16),
-            jax.ShapeDtypeStruct((2 * depth, columns), BF16),
+            jax.ShapeDtypeStruct(gains.shape, F32),
+            *wholes,
         ),
-        in_specs=[VMEM_SPEC] * (1 + len(weights)),
-        out_specs=(HBM_SPEC, VMEM_SPEC),
+        in_specs=[VMEM_SPEC] * (2 + len(weights)),
+        out_specs=(HBM_SPEC,) + (VMEM_SPEC,) * (1 + len(groups)),
         scratch_shapes=gather_sems(ctx_size, tp_size)
-        + [DMA((len(weights),)), DMA((len(weights),))],
+        + [DMA((len(weights) + 1,)), DMA((len(weights) + 1,))],
         compiler_params=pltpu.CompilerParams(
-            collective_id=identity, has_side_effects=True, vmem_limit_bytes=32 << 20
+            collective_id=identity, has_side_effects=True, vmem_limit_bytes=40 << 20
         ),
-    )(cot_rows, *weights)
-
-
-def place_halves(part, mine, other):
+    )(cot_rows, *weights, gains)
+
+
+def place_halves(part, mine, other, wide):
     pieces = len(mine)
-    depth, wide = mine[0].shape
-    tile = min(depth, 256)
+    depth = mine[0][0].shape[0]
+    tile = min(depth, 512)
+    parts = list(mine) + list(other)
 
     def kernel(part_ref, *refs):
         out_ref = refs[-1]
@@ -487,14 +753,17 @@
         grid_spec=pltpu.PrefetchScalarGridSpec(
             num_scalar_prefetch=1,
             grid=(depth // tile, 2 * pieces),
-            in_specs=[pl.BlockSpec((tile, wide), lambda i, step, part_ref: (i, 0))] * (2 * pieces),
+            in_specs=[
+                pl.BlockSpec((tile, wide), lambda i, step, part_ref, at=at: (i, at))
+                for _, at in parts
+            ],
             out_specs=pl.BlockSpec((tile, wide), target),
         ),
         out_shape=jax.ShapeDtypeStruct((depth, 2 * pieces * wide), F32),
         cost_estimate=pl.CostEstimate(
             flops=0, bytes_accessed=depth * 2 * pieces * wide * 6, transcendentals=0
         ),
-    )(part.reshape(1), *mine, *other)
+    )(part.reshape(1), *(array for array, _ in parts))
 
 
 def mean_square(rows):
@@ -569,31 +838,30 @@
             b = lax.dynamic_slice_in_dim(rows, (1 - side) * half_width, half_width, 1)
             return jnp.concatenate([a, b], axis=1)
 
-        gains = jnp.stack([attn_gain, ffn_gain])
-        gains = jnp.concatenate([gains, swap_rows(gains)], axis=1).astype(F32)
-        gain_first, gain_second = gains[0], gains[1]
-
+        gains = jnp.stack([attn_gain, ffn_gain]).astype(F32)
         residual_low = own_first(inputs[0])
         cot_low = own_first(cotangent[0])
-        cot_all, qkv_weight = opening(
-            cot_low,
-            (w_query, jnp.concatenate([key_projection, value_projection], axis=1)),
-            mesh_shape, 0,
-        )
-        w_out, w_gate, w_up, w_down, _ = lax.optimization_barrier(
-            (w_out, w_gate, w_up, w_down, qkv_weight)
-        )
-        out_weight = jnp.concatenate([w_out, swap_rows(w_out)], axis=0)
+        rows_all, gains_far, qkv_weight, out_weight = opening(
+            jnp.concatenate([cot_low, residual_low], axis=1),
+            ((w_query, jnp.concatenate([key_projection, value_projection], axis=1)), (w_out,)),
+            gains, mesh_shape, 0,
+        )
+        cot_all = rows_all[:, :model_width]
+        residual_all = rows_all[:, model_width:].astype(F32)
+        gains = jnp.concatenate([gains, gains_far], axis=1)
+        gain_first, gain_second = gains[0], gains[1]
+        w_gate, w_up, w_down, _ = lax.optimization_barrier((w_gate, w_up, w_down, qkv_weight))
         ffn_own = []
         for c in range(CHUNKS):
             start = part * ffn_half + c * chunk
-            own = tuple(
+            gate_own, up_own, down_own = (
                 lax.dynamic_slice_in_dim(w, start, chunk, 1) for w in (w_gate, w_up, w_down)
             )
-            ffn_own.append(own)
-        ffn_weights = [
-            tuple(jnp.concatenate([w, swap_rows(w)], axis=0) for w in own) for own in ffn_own
-        ]
+            ffn_own.append((jnp.concatenate([gate_own, up_own], axis=1), down_own))
+        ffn_far = [[swap_rows(w) for w in ffn_own[0]]]
+        for c in range(1, CHUNKS):
+            ffn_own[c], ffn_far[c - 1] = lax.optimization_barrier((ffn_own[c], ffn_far[c - 1]))
+            ffn_far.append([swap_rows(w) for w in ffn_own[c]])
 
         cosine_lookup, sine_lookup = rope_tables(row_start, row_count)
         residual = residual_low.astype(F32)
@@ -619,20 +887,26 @@
         prefix_one = prefix[0]
         attended, log_total = attend(query_groups, key_whole, value_whole, prefix_one, row_start)
         attended_flat = attended.reshape(row_count, query_width)
-        attn_term = contract(attended_flat, out_weight, 1, 1)
+        attn_term = contract(attended_flat, out_weight, 1, 1).astype(BF16)
+        attn_term, ffn_far[0] = lax.optimization_barrier((attn_term, ffn_far[0]))
         slice_shape = (row_count // tp_size, model_width)
         normed_all, middle = reduce_gather(
-            attn_term.astype(BF16), (residual_low, gain_second[None]), finish_middle,
+            attn_term, (residual_low, gain_second[None]), finish_middle,
             (slice_shape,), mesh_shape, 1, 1, True,
         )
 
         ffn_term = 0.0
         mid_term = 0.0
-        grads = []
+        sides = []
+        fars = []
         for c in range(CHUNKS):
-            gate_w, up_w, down_w = ffn_weights[c]
-            gating = jnp.dot(normed_all, gate_w, preferred_element_type=F32)
-            upward = jnp.dot(normed_all, up_w, preferred_element_type=F32)
+            if c:
+                ffn_far[c], fars[-1] = lax.optimization_barrier((ffn_far[c], fars[-1]))
+            pair_w, down_w = (
+                jnp.concatenate([w, far], axis=0) for w, far in zip(ffn_own[c], ffn_far[c])
+            )
+            both = jnp.dot(normed_all, pair_w, preferred_element_type=F32)
+            gating, upward = both[:, :chunk], both[:, chunk:]
             grad_hidden = jnp.dot(cot_all, down_w, preferred_element_type=F32)
             sigmoid_gate = jax.nn.sigmoid(gating)
             hidden = (gating * sigmoid_gate * upward).astype(BF16)
@@ -640,32 +914,39 @@
                 grad_hidden * upward * sigmoid_gate * (1.0 + gating * (1.0 - sigmoid_gate))
             ).astype(BF16)
             grad_upward = (grad_hidden * gating * sigmoid_gate).astype(BF16)
-            done = []
-            for rows, cols in (
-                (normed_all, grad_gating), (normed_all, grad_upward), (cot_all, hidden)
-            ):
-                far = contract(rows[:, half_width:], cols, 0, 0).astype(BF16)
-                near = contract(rows[:, :half_width], cols, 0, 0)
-                total = (near + swap_rows(far).astype(F32)).astype(BF16)
-                done.append((total, lax.ppermute(total, "ctx", swap_z)))
-            grads.append(done)
+            grad_both = jnp.concatenate([grad_gating, grad_upward], axis=1)
+            sides.append(((normed_all, grad_both), (cot_all, hidden)))
+            fars.append(
+                [contract(rows[:, half_width:], cols, 0, 0).astype(BF16) for rows, cols in sides[c]]
+            )
 
             def pair(rows):
                 return lax.dynamic_slice_in_dim(rows, pair_start, 2 * row_count, 0)
 
             ffn_term += contract(pair(hidden), down_w, 1, 1)
-            mid_term += contract(pair(grad_gating), gate_w, 1, 1) + contract(
-                pair(grad_upward), up_w, 1, 1
-            )
+            mid_term += contract(pair(grad_both), pair_w, 1, 1)
+
+        mid_low, fars[-1] = lax.optimization_barrier((mid_term.astype(BF16), fars[-1]))
+        received = [[swap_rows(far) for far in chunk_fars] for chunk_fars in fars]
+
+        def summed(c):
+            return [
+                (contract(rows[:, :half_width], cols, 0, 0) + far.astype(F32)).astype(BF16)
+                for (rows, cols), far in zip(sides[c], received[c])
+            ]
 
         branch_low, grad_middle, gain_grad_second = reduce_gather(
-            mid_term.astype(BF16), (middle, cot_low, gain_second[None]), finish_grad_middle,
+            mid_low, (middle, cot_low, gain_second[None]), finish_grad_middle,
             (slice_shape, (1, model_width)), mesh_shape, 2, 2, False,
         )
-        (output_rows,) = reduce_gather(
-            ffn_term.astype(BF16), (middle,), finish_output, (), mesh_shape, 3, 2, False
-        )
+        totals = [None] * CHUNKS
+        branch_low, received[0] = lax.optimization_barrier((branch_low, received[0]))
+        totals[0] = summed(0)
+        branch_low, totals[0] = lax.optimization_barrier((branch_low, totals[0]))
+        swapped = [None] * CHUNKS
+        swapped[0] = [lax.ppermute(total, "ctx", swap_z) for total in totals[0]]
         grad_out = contract(branch_low, attended_flat, 0, 0)
+        grad_out_far = swap_rows(grad_out[half_width:].astype(BF16))
         grad_attended = jnp.dot(branch_low, out_weight, preferred_element_type=F32).astype(BF16)
         grad_attended = grad_attended.reshape(row_count, kv_heads, heads_per_group, HEAD_SIZE)
         grad_query_rot, grad_key_all, grad_value_all = attend_back(
@@ -678,7 +959,14 @@
             ],
             axis=1,
         ).astype(BF16)
-        grad_kv = lax.psum_scatter(grad_kv, "ctx", scatter_dimension=0, tiled=True).astype(F32)
+        grad_kv = lax.psum_scatter(grad_kv, "ctx", scatter_dimension=0, tiled=True)
+        ffn_low, grad_kv = lax.optimization_barrier((ffn_term.astype(BF16), grad_kv))
+        grad_kv = grad_kv.astype(F32)
+        (output_rows,) = reduce_gather(
+            ffn_low, (middle,), finish_output, (), mesh_shape, 3, 2, False
+        )
+        grad_out = grad_out[:half_width] + grad_out_far.astype(F32)
+        grad_out = lax.psum(grad_out.astype(BF16), "ctx").astype(F32)
         grad_query_pre = apply_rotary(
             grad_query_rot.reshape(row_count, query_heads, HEAD_SIZE),
             cosine_lookup, sine_lookup, -1.0,
@@ -689,26 +977,33 @@
         ).astype(BF16).reshape(row_count, key_width)
         grad_value_pre = grad_kv[:, key_width:].astype(BF16)
         grad_qkv_pre = jnp.concatenate([grad_query_pre, grad_key_pre, grad_value_pre], axis=1)
-        grad_qkv = contract(normalized_rows, grad_qkv_pre, 0, 0)
-        grad_attn = jnp.concatenate([grad_qkv, grad_out], axis=1)
-        grad_attn = grad_attn[:half_width] + swap_rows(grad_attn[half_width:].astype(BF16)).astype(
-            F32
-        )
-        grad_attn = lax.psum(grad_attn.astype(BF16), "ctx").astype(F32)
-        input_rows, gain_grad_first = reduce_gather(
-            contract(grad_qkv_pre, qkv_weight, 1, 1).astype(BF16),
+        attn_width = grad_qkv_pre.shape[1]
+        pre_slabs = grad_qkv_pre.T.reshape(ctx_size, attn_width // ctx_size, row_count)
+        normed_term = contract(grad_qkv_pre, qkv_weight, 1, 1).astype(BF16)
+        normed_term, received[1], output_rows = lax.optimization_barrier(
+            (normed_term, received[1], output_rows)
+        )
+        totals[1] = summed(1)
+        normed_term, totals[1] = lax.optimization_barrier((normed_term, totals[1]))
+        swapped[1] = [lax.ppermute(total, "ctx", swap_z) for total in totals[1]]
+        rms_all = lax.rsqrt(jnp.mean(residual_all * residual_all, axis=-1, keepdims=True) + EPSILON)
+        norm_all = (residual_all * rms_all * gain_first).astype(BF16)
+        input_rows, _, grad_attn, gain_grads = reduce_gather(
+            normed_term,
             (grad_middle, residual_low, gain_first[None]), finish_grad_input,
             ((1, model_width),), mesh_shape, 4, 1, False,
-        )
-        gain_grads = jnp.concatenate([gain_grad_first, gain_grad_second], axis=0)
-        gain_grads = lax.psum(
-            gain_grads[:, :half_width] + swap_rows(gain_grads[:, half_width:]), ("ctx", "tp")
-        )
-
-        result = [
-            place_halves(part, [done[i][0] for done in grads], [done[i][1] for done in grads])
-            for i in range(3)
-        ]
+            AttnTail(pre_slabs, norm_all, gain_grad_second, mesh_shape),
+        )
+        grad_attn = grad_attn.T.astype(F32)
+
+        def result(which, block):
+            return place_halves(
+                part,
+                [(totals[c][which], block) for c in range(CHUNKS)],
+                [(swapped[c][which], block) for c in range(CHUNKS)],
+                chunk,
+            )
+
         end_key = query_width + key_width
         end_value = end_key + key_width
         return (
@@ -718,11 +1013,11 @@
             grad_attn[:, :query_width],
             grad_attn[:, query_width:end_key],
             grad_attn[:, end_key:end_value],
-            grad_attn[:, end_value:],
+            grad_out,
             gain_grads[1],
-            result[0],
-            result[1],
-            result[2],
+            result(0, 0),
+            result(0, 1),
+            result(1, 0),
         )
 
     return local

time: 711 us -> 664 us (0.934)
  Pallas kernels: 197 us -> 372 us
  blocking collectives: 178 us -> 15 us
  waiting for transfers between devices: 145 us -> 60.3 us
  other arithmetic: 10.6 us -> 39.8 us
  local copies, waits for them, and re-layouts: 38.7 us -> 48.9 us
  starting transfers between devices: 18.2 us -> 10.2 us
    psum x1 -> x0, blocking collectives: 162 us -> none  [local(): lax.psum(gain_grads[:, :half_width] + swap_rows(gain_grads[:, half_width:...]
    pallas_call x4, Pallas kernels: 126 us -> 288 us  [reduce_gather(): pl.pallas_call(kernel, out_shape=(jax.ShapeDtypeStruct((reach * block_row...]
    ppermute x16 -> x9, waiting for transfers between devices: 133 us -> 41.1 us  [swap_rows(): return lax.ppermute(array, 'fsdp', swap_x)]
    pallas_call x1, Pallas kernels: 39.2 us -> 61.9 us  [opening(): pl.pallas_call(kernel, out_shape=(jax.ShapeDtypeStruct((ctx_size * block_...]
    convert_element_type x2 -> x9, other arithmetic: 2.33 us -> 21.4 us  [the longest x4 12.9 us: summed(): (contract(rows[:, :half_width], cols, 0, 0) + far.astype(F32)).astype(BF16)]
    dot_general x22 -> x15, matrix products: 54.9 us -> 45.8 us  [contract(): lax.dot_general(left, right, (((left_dim,), (right_dim,)), ((), ())), pre...]
    pallas_call x3, Pallas kernels: 31.3 us -> 22.2 us  [place_halves(): pl.pallas_call(kernel, grid_spec=pltpu.PrefetchScalarGridSpec(num_scalar_...]
    ppermute x16 -> x9, starting transfers between devices: 15.5 us -> 7.94 us  [swap_rows(): return lax.ppermute(array, 'fsdp', swap_x)]
  transfers between devices with their start and end apart: 24 -> 15, of which waited for: 9 -> 3; matrix products, arithmetic and copies ran while one was open for 13% -> 20% of each run, Pallas kernels for 18% -> 45%
where the time goes in v3:
time: 664 us; the launch traced here: 655 us
  Pallas kernels  372 us (56%)
  matrix products  92.5 us (14%)
  waiting for transfers between devices  60.3 us (9%)
  local copies, waits for them, and re-layouts  48.9 us (7%)
  other arithmetic  39.8 us (6%)
  between operations  16.2 us (2%)
  blocking collectives  15 us (2%)
  starting transfers between devices  10.2 us (2%)
    pallas_call x4, Pallas kernels, reduce_gather(): pl.pallas_call(kernel, out_shape=(jax.ShapeDtypeStruct((reach * block_row...  288 us
    pallas_call x1, Pallas kernels, opening(): pl.pallas_call(kernel, out_shape=(jax.ShapeDtypeStruct((ctx_size * block_...  61.9 us
    dot_general x15, matrix products, contract(): lax.dot_general(left, right, (((left_dim,), (right_dim,)), ((), ())), pre...  45.8 us
    ppermute x9, waiting for transfers between devices, swap_rows(): return lax.ppermute(array, 'fsdp', swap_x)  41.1 us
    unnamed x135, local copies, waits for them, and re-layouts  25.2 us
    pallas_call x3, Pallas kernels, place_halves(): pl.pallas_call(kernel, grid_spec=pltpu.PrefetchScalarGridSpec(num_scalar_...  22.2 us
    reduce_scatter x1, waiting for transfers between devices, local(): grad_kv = lax.psum_scatter(grad_kv, 'ctx', scatter_dimension=0, tiled=True)  19.2 us
    dot_general x2, matrix products, local(): both = jnp.dot(normed_all, pair_w, preferred_element_type=F32)  16.8 us
  transfers between devices with their start and end apart: 15, of which 3 were waited for; matrix products, arithmetic and copies ran while one was open for 20% of the time, Pallas kernels for 45%

profile of v3, /device:TPU:0, one launch (start us, length us, event | category | flops | bytes accessed | tf_op | source)
XLA Modules:
  0.0 655.0 jit_solution(8044854210371700531)
XLA Ops:
  9.7 1.7 dynamic-slice_bitcast_fusion.1
  13.7 61.9 %shard_map.203 = (bf16[1024,4096]{1,0:T(8,128)(2,1)}, f32[2,1024]{1,0:T(2,128)S(1)}, bf16[2048,768]{1,0:T(8,128)(2,1)S(1)}, bf16[2048,512]{1,0:T(8,128)(2,1)S(1)}) custom-call(bf16[256,4096]{1,0:T(8,128)(2,1)S(1)} %pad_maximum_fusion.3.cot_ref, bf16[1024,512]{1,0:T(8,128)(2,1)S(1)} %copy-done.8, bf16[1024,256]{1,0:T(8,128)(2,1)S(1)} %pad_maximum_fusion.17.refs_1_, ...), custom_call_target="tpu_custom_call" | custom-call | tf_op jit(solution)/shard_map/pallas_call | solution.py:716
  75.6 1.6 copy-done.12
  77.3 3.5 constant_dynamic-slice_fusion.4
  81.2 1.3 constant_dynamic-slice_fusion.5
  82.5 1.6 pad_maximum_fusion.5
  85.9 1.6 constant_dynamic-slice_fusion.9
  90.0 15.0 %all_gather.3 = bf16[1024,256]{1,0:T(8,128)(2,1)S(1)} all-gather(bf16[256,256]{1,0:T(8,128)(2,1)S(1)} %pad_maximum_fusion.24), channel_id=1, replica_groups=mesh['fsdp'=2,'ctx'=4,'tp'=4] {'ctx'}, dimensions={0}, use_global_device_ids=true | all-gather | bytes 655360 | tf_op jit(solution)/shard_map/all_gather | solution.py:880
  110.9 3.1 fusion
  114.2 1.4 fusion.84
  115.7 3.4 copy-done.15
  120.3 1.6 pad_maximum_fusion.4
  121.9 1.6 pad_maximum_fusion.15.refs_0_.refs_1_
  124.9 1.5 fusion.51
  127.2 26.3 %collective-permute-done.1 = bf16[1024,512]{1,0:T(8,128)(2,1)} collective-permute-done((bf16[1024,512]{1,0:T(8,128)(2,1)}, bf16[1024,512]{1,0:T(8,128)(2,1)}, u32[]{:S(2)}, u32[]{:S(2)}) %collective-permute-start.1) | collective-permute-done | bytes 1048608 | tf_op jit(solution)/shard_map/ppermute | solution.py:814
  153.5 1.3 constant_dynamic-update-slice_fusion.1
  155.4 1.5 collective-permute-start.2
  156.9 1.5 constant_dynamic-update-slice_fusion.3
  158.4 43.6 %shard_map.204 = (bf16[1024,2048]{1,0:T(8,128)(2,1)S(1)}, f32[64,2048]{1,0:T(8,128)S(1)}) custom-call(bf16[256,2048]{1,0:T(8,128)(2,1)S(1)} %convolution_convert_fusion.term_ref, bf16[256,2048]{1,0:T(8,128)(2,1)S(1)} %pad_maximum_fusion.15.refs_0_.refs_1_, f32[1,2048]{1,0:T(1,128)S(1)} %get-tuple-element.155.refs_1_.refs_2_), custom_call_target="tpu_custom_call" | custom-call | tf_op jit(solution)/shard_map/pallas_call | solution.py:654
  202.1 8.5 %fusion.35 = f32[1024,1024]{0,1:T(8,128)} fusion(bf16[1024,2048]{1,0:T(8,128)(2,1)S(1)} %get-tuple-element.66, bf16[1024,1024]{1,0:T(8,128)(2,1)} %collective-permute-done, bf16[1024,512]{1,0:T(8,128)(2,1)S(1)} %copy-done.32, bf16[1024,512]{1,0:T(8,128)(2,1)S(1)} %copy-done.35), kind=kOutput, calls=%fused_computation.76 | convolution fusion | flops 4307550208 | bytes 12582912 | tf_op jit(solution)/shard_map/dot_general | solution.py:908
  210.6 6.1 multiply_convert_fusion.5
  216.8 2.3 fusion.36
  219.1 2.9 fusion.42
  222.0 4.2 convolution_convert_fusion.3
  226.2 4.5 fusion.26
  230.7 1.3 fusion.22
  232.8 5.9 fusion.34
  238.8 3.1 constant_dynamic-update-slice_fusion.2
  241.9 8.3 %fusion.85 = f32[1024,1024]{0,1:T(8,128)} fusion(bf16[1024,2048]{1,0:T(8,128)(2,1)S(1)} %get-tuple-element.66, bf16[2048,1024]{1,0:T(8,128)(2,1)} %constant_dynamic-update-slice_fusion.2), kind=kOutput, calls=%fused_computation.171 | convolution fusion | flops 4294967296 | bytes 12582912 | tf_op jit(solution)/shard_map/dot_general | solution.py:908
  251.5 5.9 multiply_convert_fusion.1
  257.4 2.3 fusion.39
  260.4 1.4 collective-permute-start.5
  261.7 3.8 convolution_convert_fusion.2
  265.5 6.2 add_convert_fusion.3.term_ref
  271.7 2.6 fusion.20
  275.0 1.4 collective-permute-start.7
  276.3 33.3 %shard_map.205 = (bf16[256,2048]{1,0:T(8,128)(2,1)S(1)}, f32[64,2048]{1,0:T(8,128)S(1)}, f32[1,2048]{1,0:T(1,128)S(1)}) custom-call(bf16[512,2048]{1,0:T(8,128)(2,1)S(1)} %add_convert_fusion.3.term_ref, f32[64,2048]{1,0:T(8,128)S(1)} %get-tuple-element.73.refs_0_, bf16[256,2048]{1,0:T(8,128)(2,1)S(1)} %pad_maximum_fusion.16.refs_1_, ...), custom_call_target="tpu_custom_call" | custom-call | tf_op jit(solution)/shard_map/pallas_call | solution.py:654
  309.7 1.4 add_convert_fusion.1.term_ref
  311.8 4.4 fusion.24
  316.2 14.7 %collective-permute-done.5 = bf16[1024,512]{1,0:T(8,128)(2,1)S(1)} collective-permute-done((bf16[1024,512]{1,0:T(8,128)(2,1)}, bf16[1024,512]{1,0:T(8,128)(2,1)S(1)}, u32[]{:S(2)}, u32[]{:S(2)}) %collective-permute-start.5) | collective-permute-done | bytes 1048608 | tf_op jit(solution)/shard_map/ppermute | solution.py:814
  330.9 3.7 add_convert_fusion.2.refs_0_
  334.6 1.3 add_convert_fusion.5.refs_0_
  336.5 1.4 convolution_convert_fusion.4
  339.1 5.0 fusion.47
  344.0 5.3 fusion.3
  349.4 1.8 fusion.5
  351.2 2.0 copy-done.17
  353.2 1.4 fusion.50
  355.6 2.2 fusion.86
  360.6 19.2 %reduce-scatter.2.cloned.1.call-done = bf16[256,256]{0,1:T(8,128)(2,1)} async-done(((bf16[1024,256]{0,1:T(8,128)(2,1)}), bf16[256,256]{0,1:T(8,128)(2,1)}) %reduce-scatter.2.cloned.1.call-update) | async-done | bytes 131088 | tf_op jit(solution)/shard_map/reduce_scatter | solution.py:962
  381.8 44.4 %shard_map.206 = bf16[256,2048]{1,0:T(8,128)(2,1)S(1)} custom-call(bf16[512,2048]{1,0:T(8,128)(2,1)S(1)} %add_convert_fusion.1.term_ref, f32[64,2048]{1,0:T(8,128)S(1)} %copy-done.5), custom_call_target="tpu_custom_call" | custom-call | tf_op jit(solution)/shard_map/pallas_call | solution.py:654
  427.5 4.1 add_convert_fusion.4.refs_1_
  431.5 3.8 add_convert_fusion.refs_1_
  435.5 2.7 fusion.2.refs_4_
  438.1 1.9 collective-permute-start.11
  440.1 2.6 fusion.19
  442.9 2.2 copy-done
  446.1 166.7 %shard_map.207 = (bf16[256,2048]{1,0:T(8,128)(2,1)S(1)}, f32[1,2048]{1,0:T(1,128)}, bf16[768,1024]{1,0:T(8,128)(2,1)S(1)}, f32[2,1024]{1,0:T(2,128)S(1)}) custom-call(bf16[256,2048]{1,0:T(8,128)(2,1)S(1)} %convolution_convert_fusion.1.term_ref, f32[64,2048]{1,0:T(8,128)S(1)} %copy-done.11, bf16[256,2048]{1,0:T(8,128)(2,1)S(1)} %pad_maximum_fusion.15.refs_0_.refs_1_, ...), custom_call_target="tpu_custom_call" | custom-call | tf_op jit(solution)/shard_map/pallas_call | solution.py:654
  613.3 1.5 slice.165
  614.8 3.0 copy.54
  622.7 2.8 convert_element_type.192
  625.5 7.4 %shard_map.210 = f32[1024,2048]{1,0:T(8,128)} custom-call(s32[1]{0:T(128)} %bitcast.49.part_ref, bf16[1024,512]{1,0:T(8,128)(2,1)} %add_convert_fusion.5.refs_0_, bf16[1024,512]{1,0:T(8,128)(2,1)} %add_convert_fusion.4.refs_1_, bf16[1024,512]{1,0:T(8,128)(2,1)} %collective-permute-done.11.refs_2_, bf16[1024,512]{1,0:T(8,128)(2,1)} %collective-permute-done.12.refs_3_), custom_call_target="tpu_custom_call" | custom-call | bytes 12582912 | tf_op jit(solution)/shard_map/pallas_call | solution.py:751
  632.9 7.4 %shard_map.208 = f32[1024,2048]{1,0:T(8,128)} custom-call(s32[1]{0:T(128)} %bitcast.49.part_ref, bf16[1024,1024]{1,0:T(8,128)(2,1)} %add_convert_fusion.2.refs_0_, bf16[1024,1024]{1,0:T(8,128)(2,1)} %add_convert_fusion.refs_1_, bf16[1024,1024]{1,0:T(8,128)(2,1)} %collective-permute-done.9.refs_2_, bf16[1024,1024]{1,0:T(8,128)(2,1)} %collective-permute-done.10.refs_3_), custom_call_target="tpu_custom_call" | custom-call | bytes 12582912 | tf_op jit(solution)/shard_map/pallas_call | solution.py:751
  640.3 7.4 %shard_map.209 = f32[1024,2048]{1,0:T(8,128)} custom-call(s32[1]{0:T(128)} %bitcast.49.part_ref, bf16[1024,1024]{1,0:T(8,128)(2,1)} %add_convert_fusion.2.refs_0_, bf16[1024,1024]{1,0:T(8,128)(2,1)} %add_convert_fusion.refs_1_, bf16[1024,1024]{1,0:T(8,128)(2,1)} %collective-permute-done.9.refs_2_, bf16[1024,1024]{1,0:T(8,128)(2,1)} %collective-permute-done.10.refs_3_), custom_call_target="tpu_custom_call" | custom-call | bytes 12582912 | tf_op jit(solution)/shard_map/pallas_call | solution.py:751
  (208 shorter events, 38.3 us)
Async XLA Ops:
  7.2 372.7 %reduce-scatter.2.cloned.1.call-start = ((), (), s32[]{:S(2)}) async-start(), calls=%async_computation.1 | async-start | bytes 655360 | tf_op jit(solution)/shard_map/reduce_scatter | solution.py:962
  11.5 2.3 copy-start.9
  77.3 49.1 %copy-start.6 = (bf16[2048,512]{1,0:T(8,128)(2,1)}, bf16[2048,512]{1,0:T(8,128)(2,1)S(1)}, u32[]{:S(2)}) copy-start(bf16[2048,512]{1,0:T(8,128)(2,1)S(1)} %get-tuple-element.59) | copy-start | bytes 6291460
  77.3 4.0 copy-start.46
  81.2 2.9 copy-start.31
  82.5 4.9 copy-start.34
  82.5 3.3 copy-start.47
  84.1 3.8 copy-start.22
  84.1 3.8 copy-start.24
  84.1 4.2 copy-start.13
  84.1 69.4 %collective-permute-start = (bf16[1024,1024]{1,0:T(8,128)(2,1)}, bf16[1024,1024]{1,0:T(8,128)(2,1)}, u32[]{:S(2)}, u32[]{:S(2)}) collective-permute-start(bf16[1024,1024]{1,0:T(8,128)(2,1)} %pad_maximum_fusion.5), channel_id=1, source_target_pairs={{0,16},{16,0},{1,17},{17,1},{2,18},{18,2},{3,19},{19,3},{4,20},{20... | collective-permute-start | bytes 6291464 | tf_op jit(solution)/shard_map/ppermute | solution.py:814
  87.4 66.1 %collective-permute-start.1 = (bf16[1024,512]{1,0:T(8,128)(2,1)}, bf16[1024,512]{1,0:T(8,128)(2,1)}, u32[]{:S(2)}, u32[]{:S(2)}) collective-permute-start(bf16[1024,512]{1,0:T(8,128)(2,1)} %get-tuple-element.127), channel_id=1, source_target_pairs={{0,16},{16,0},{1,17},{17,1},{2,18},{18,2},{3,19},{19,3},{4,20},{20... | collective-permute-start | bytes 3145736 | tf_op jit(solution)/shard_map/ppermute | solution.py:814
  106.9 17.9 %copy-start.44 = (bf16[1024,128]{0,1:T(8,128)(2,1)}, bf16[1024,128]{0,1:T(8,128)(2,1)S(1)}, u32[]{:S(2)}) copy-start(bf16[1024,128]{0,1:T(8,128)(2,1)S(1)} %copy.48) | copy-start | bytes 786436
  108.1 6.1 copy-start.38
  110.2 5.5 copy-start.40
  110.2 5.5 copy-start.42
  115.7 3.4 copy-start.15
  120.3 4.5 copy-start.16
  126.4 27.1 %copy-start.48 = (bf16[2,64,4,256]{3,1,2,0:T(8,128)(2,1)}, bf16[2,64,4,256]{3,1,2,0:T(8,128)(2,1)S(1)}, u32[]{:S(2)}) copy-start(bf16[2,64,4,256]{3,1,2,0:T(8,128)(2,1)S(1)} %fusion.51) | copy-start | bytes 786436
  154.8 47.3 %copy-start.32 = (bf16[1024,512]{1,0:T(8,128)(2,1)S(1)}, bf16[1024,512]{1,0:T(8,128)(2,1)}, u32[]{:S(2)}) copy-start(bf16[1024,512]{1,0:T(8,128)(2,1)} %copy-done.31) | copy-start | bytes 3145732
  154.8 47.3 %copy-start.35 = (bf16[1024,512]{1,0:T(8,128)(2,1)S(1)}, bf16[1024,512]{1,0:T(8,128)(2,1)}, u32[]{:S(2)}) copy-start(bf16[1024,512]{1,0:T(8,128)(2,1)} %copy-done.34) | copy-start | bytes 3145732
  154.8 83.9 %collective-permute-start.3 = (bf16[1024,512]{1,0:T(8,128)(2,1)}, bf16[1024,512]{1,0:T(8,128)(2,1)}, u32[]{:S(2)}, u32[]{:S(2)}) collective-permute-start(bf16[1024,512]{1,0:T(8,128)(2,1)} %get-tuple-element.68), channel_id=1, source_target_pairs={{0,16},{16,0},{1,17},{17,1},{2,18},{18,2},{3,19},{19,3},{4,20},{20... | collective-permute-start | bytes 3145736 | tf_op jit(solution)/shard_map/ppermute | solution.py:814
  155.4 83.3 %collective-permute-start.2 = (bf16[1024,1024]{1,0:T(8,128)(2,1)S(1)}, bf16[1024,1024]{1,0:T(8,128)(2,1)}, u32[]{:S(2)}, u32[]{:S(2)}) collective-permute-start(bf16[1024,1024]{1,0:T(8,128)(2,1)S(1)} %pad_maximum_fusion.4), channel_id=1, source_target_pairs={{0,16},{16,0},{1,17},{17,1},{2,18},{18,2},{3,19},{19,3},{4,20},{20... | collective-permute-start | bytes 6291464 | tf_op jit(solution)/shard_map/ppermute | solution.py:814
  158.4 52.2 %slice-start.2 = ((s8[8388608]{0:T(1024)(128)(4,1)}), s8[4194304]{0:T(1024)(128)(4,1)S(1)}, s32[]{:S(2)}) async-start(s8[8388608]{0:T(1024)(128)(4,1)} %bitcast.112), calls=%async_computation.5 | async-start | bytes 8388608
  202.1 74.3 %copy-start.4 = (f32[64,2048]{1,0:T(8,128)}, f32[64,2048]{1,0:T(8,128)S(1)}, u32[]{:S(2)}) copy-start(f32[64,2048]{1,0:T(8,128)S(1)} %get-tuple-element.73.refs_0_) | copy-start | bytes 1572868
  202.1 8.5 %slice-start.3 = ((s8[8388608]{0:T(1024)(128)(4,1)}), s8[4194304]{0:T(1024)(128)(4,1)S(1)}, s32[]{:S(2)}) async-start(s8[8388608]{0:T(1024)(128)(4,1)} %bitcast.112), calls=%async_computation.6 | async-start | bytes 8388608
  216.7 9.4 %copy-start.55 = (bf16[1024,512]{0,1:T(8,128)(2,1)}, bf16[1024,512]{0,1:T(8,128)(2,1)S(1)}, u32[]{:S(2)}) copy-start(bf16[1024,512]{0,1:T(8,128)(2,1)S(1)} %get-tuple-element.123) | copy-start | bytes 3145732
  216.8 9.4 %copy-start.57 = (bf16[1024,512]{0,1:T(8,128)(2,1)}, bf16[1024,512]{0,1:T(8,128)(2,1)S(1)}, u32[]{:S(2)}) copy-start(bf16[1024,512]{0,1:T(8,128)(2,1)S(1)} %get-tuple-element.124) | copy-start | bytes 3145732
  230.7 2.2 copy-start.58
  251.5 5.9 copy-start.25
  257.4 4.4 copy-start.51
  257.4 4.3 copy-start.53
  259.7 71.2 %collective-permute-start.4 = (bf16[1024,1024]{1,0:T(8,128)(2,1)}, bf16[1024,1024]{1,0:T(8,128)(2,1)}, u32[]{:S(2)}, u32[]{:S(2)}) collective-permute-start(bf16[1024,1024]{1,0:T(8,128)(2,1)} %convolution_convert_fusion.3), channel_id=1, source_target_pairs={{0,16},{16,0},{1,17},{17,1},{2,18},{18,2},{3,19},{19,3},{4,20},{20... | collective-permute-start | bytes 6291464 | tf_op jit(solution)/shard_map/ppermute | solution.py:814
  260.4 70.5 %collective-permute-start.5 = (bf16[1024,512]{1,0:T(8,128)(2,1)}, bf16[1024,512]{1,0:T(8,128)(2,1)S(1)}, u32[]{:S(2)}, u32[]{:S(2)}) collective-permute-start(bf16[1024,512]{1,0:T(8,128)(2,1)} %fusion.36), channel_id=1, source_target_pairs={{0,16},{16,0},{1,17},{17,1},{2,18},{18,2},{3,19},{19,3},{4,20},{20... | collective-permute-start | bytes 3145736 | tf_op jit(solution)/shard_map/ppermute | solution.py:814
  274.3 35.3 %copy-start.26 = (bf16[2048,512]{1,0:T(8,128)(2,1)S(1)}, bf16[2048,512]{1,0:T(8,128)(2,1)}, u32[]{:S(2)}) copy-start(bf16[2048,512]{1,0:T(8,128)(2,1)} %copy-done.25) | copy-start | bytes 6291460
  274.3 153.1 %collective-permute-start.6 = (bf16[1024,1024]{1,0:T(8,128)(2,1)}, bf16[1024,1024]{1,0:T(8,128)(2,1)}, u32[]{:S(2)}, u32[]{:S(2)}) collective-permute-start(bf16[1024,1024]{1,0:T(8,128)(2,1)} %convolution_convert_fusion.2), channel_id=1, source_target_pairs={{0,16},{16,0},{1,17},{17,1},{2,18},{18,2},{3,19},{19,3},{4,20},{20... | collective-permute-start | bytes 6291464 | tf_op jit(solution)/shard_map/ppermute | solution.py:814
  275.0 152.5 %collective-permute-start.7 = (bf16[1024,512]{1,0:T(8,128)(2,1)}, bf16[1024,512]{1,0:T(8,128)(2,1)}, u32[]{:S(2)}, u32[]{:S(2)}) collective-permute-start(bf16[1024,512]{1,0:T(8,128)(2,1)} %fusion.39), channel_id=1, source_target_pairs={{0,16},{16,0},{1,17},{17,1},{2,18},{18,2},{3,19},{19,3},{4,20},{20... | collective-permute-start | bytes 3145736 | tf_op jit(solution)/shard_map/ppermute | solution.py:814
  309.6 26.2 %copy-start.3 = (bf16[256,2048]{1,0:T(8,128)(2,1)}, bf16[256,2048]{1,0:T(8,128)(2,1)S(1)}, u32[]{:S(2)}) copy-start(bf16[256,2048]{1,0:T(8,128)(2,1)S(1)} %get-tuple-element.80) | copy-start | bytes 3145732
  309.7 2.1 copy-start.54
  311.8 19.1 %copy-start.30 = (f32[1024,1024]{1,0:T(8,128)S(1)}, f32[1024,1024]{1,0:T(8,128)}, u32[]{:S(2)}) copy-start(f32[1024,1024]{1,0:T(8,128)} %fusion.26) | copy-start | bytes 12582916
  339.0 5.0 copy-start.45
  339.0 10.3 %slice-start = ((s8[8388608]{0:T(1024)(128)(4,1)}), s8[4194304]{0:T(1024)(128)(4,1)S(1)}, s32[]{:S(2)}) async-start(s8[8388608]{0:T(1024)(128)(4,1)} %bitcast.110), calls=%async_computation.3 | async-start | bytes 8388608
  344.0 5.4 slice-start.1
  349.4 3.8 copy-start.41
  349.4 3.8 copy-start.43
  355.5 4.2 copy-start.39
  355.5 267.2 %all-reduce.2.cloned.1.call-start = ((), (), s32[]{:S(2)}) async-start(), calls=%async_computation.2 | async-start | bytes 2097152 | tf_op jit(solution)/shard_map/psum | solution.py:969
  355.5 4.1 copy-start.18
  357.7 2.8 copy-start.19
  359.0 81.0 %collective-permute-start.8 = (bf16[1024,512]{1,0:T(8,128)(2,1)}, bf16[1024,512]{1,0:T(8,128)(2,1)}, u32[]{:S(2)}, u32[]{:S(2)}) collective-permute-start(bf16[1024,512]{1,0:T(8,128)(2,1)} %slice.233), channel_id=1, source_target_pairs={{0,16},{16,0},{1,17},{17,1},{2,18},{18,2},{3,19},{19,3},{4,20},{20... | collective-permute-start | bytes 3145736 | tf_op jit(solution)/shard_map/ppermute | solution.py:814
  359.7 273.2 %collective-permute-start.9 = (bf16[1024,1024]{1,0:T(8,128)(2,1)}, bf16[1024,1024]{1,0:T(8,128)(2,1)}, u32[]{:S(2)}, u32[]{:S(2)}) collective-permute-start(bf16[1024,1024]{1,0:T(8,128)(2,1)} %add_convert_fusion.2.refs_0_), channel_id=1, source_target_pairs={{0,4},{4,0},{8,12},{12,8},{1,5},{5,1},{9,13},{13,9},{2,6},{6,2},{1... | collective-permute-start | bytes 6291464 | tf_op jit(solution)/shard_map/ppermute | solution.py:947
  380.7 45.6 %copy-start.49 = (bf16[256,128]{0,1:T(8,128)(2,1)}, bf16[256,128]{0,1:T(8,128)(2,1)S(1)}, u32[]{:S(2)}) copy-start(bf16[256,128]{0,1:T(8,128)(2,1)S(1)} %get-tuple-element.154) | copy-start | bytes 196612
  381.8 44.5 %copy-start.14 = (bf16[2048,768]{1,0:T(8,128)(2,1)S(1)}, bf16[2048,768]{1,0:T(8,128)(2,1)}, u32[]{:S(2)}) copy-start(bf16[2048,768]{1,0:T(8,128)(2,1)} %copy-done.12) | copy-start | bytes 9437188
  426.3 5.2 copy-start.1
  426.4 5.2 copy-start.29
  426.4 9.1 %slice-start.4 = ((s8[8388608]{0:T(1024)(128)(4,1)}), s8[4194304]{0:T(1024)(128)(4,1)S(1)}, s32[]{:S(2)}) async-start(s8[8388608]{0:T(1024)(128)(4,1)} %bitcast.114), calls=%async_computation.7 | async-start | bytes 8388608
  427.4 8.0 %slice-start.5 = ((s8[8388608]{0:T(1024)(128)(4,1)}), s8[4194304]{0:T(1024)(128)(4,1)S(1)}, s32[]{:S(2)}) async-start(s8[8388608]{0:T(1024)(128)(4,1)} %bitcast.114), calls=%async_computation.8 | async-start | bytes 8388608
  435.3 4.7 copy-start.20
  435.3 197.5 %collective-permute-start.10 = (bf16[1024,1024]{1,0:T(8,128)(2,1)}, bf16[1024,1024]{1,0:T(8,128)(2,1)}, u32[]{:S(2)}, u32[]{:S(2)}) collective-permute-start(bf16[1024,1024]{1,0:T(8,128)(2,1)} %add_convert_fusion.refs_1_), channel_id=1, source_target_pairs={{0,4},{4,0},{8,12},{12,8},{1,5},{5,1},{9,13},{13,9},{2,6},{6,2},{1... | collective-permute-start | bytes 6291464 | tf_op jit(solution)/shard_map/ppermute | solution.py:988
  438.1 4.7 copy-start.50
  438.1 187.4 %collective-permute-start.11 = (bf16[1024,512]{1,0:T(8,128)(2,1)}, bf16[1024,512]{1,0:T(8,128)(2,1)}, u32[]{:S(2)}, u32[]{:S(2)}) collective-permute-start(bf16[1024,512]{1,0:T(8,128)(2,1)} %add_convert_fusion.5.refs_0_), channel_id=1, source_target_pairs={{0,4},{4,0},{8,12},{12,8},{1,5},{5,1},{9,13},{13,9},{2,6},{6,2},{1... | collective-permute-start | bytes 3145736 | tf_op jit(solution)/shard_map/ppermute | solution.py:947
  442.7 182.8 %collective-permute-start.12 = (bf16[1024,512]{1,0:T(8,128)(2,1)}, bf16[1024,512]{1,0:T(8,128)(2,1)}, u32[]{:S(2)}, u32[]{:S(2)}) collective-permute-start(bf16[1024,512]{1,0:T(8,128)(2,1)} %add_convert_fusion.4.refs_1_), channel_id=1, source_target_pairs={{0,4},{4,0},{8,12},{12,8},{1,5},{5,1},{9,13},{13,9},{2,6},{6,2},{1... | collective-permute-start | bytes 3145736 | tf_op jit(solution)/shard_map/ppermute | solution.py:988
  442.9 2.2 copy-start
  614.8 5.0 copy-start.2
  (16 other events, 23.0 us)
Sparse Core Ops, SparseCore 0:
  355.6 24.2 reduce-scatter.1
  442.8 82.3 all-reduce.1

commit v4 on v3

--- a/solution.py
+++ b/solution.py
@@ -11,7 +11,6 @@
 EPSILON = 1e-05
 THETA = 500000.0
 MASKED = -1e30
-CHUNKS = 2
 F32 = jnp.float32
 BF16 = jnp.bfloat16
 
@@ -30,63 +29,97 @@
 
 
 def apply_rotary(values, cosine_lookup, sine_lookup, direction):
-    half_width = values.shape[-1] // 2
-    leading = values[..., :half_width]
-    trailing = values[..., half_width:]
-    cos_wide = cosine_lookup[:, None, :]
-    sin_wide = direction * sine_lookup[:, None, :]
+    half_width = values.shape[1] // 2
+    leading = values[:, :half_width]
+    trailing = values[:, half_width:]
+    sin = direction * sine_lookup
     return jnp.concatenate(
-        [leading * cos_wide - trailing * sin_wide, trailing * cos_wide + leading * sin_wide],
-        axis=-1,
+        [leading * cosine_lookup - trailing * sin, trailing * cosine_lookup + leading * sin],
+        axis=1,
     )
 
 
-def masked_scores(query_block, key_block, prefix_one, row_start):
-    row_count = query_block.shape[0]
-    length_total = key_block.shape[0]
-    scores = jnp.einsum(
-        "qkgd,pkd->kgqp", query_block, key_block, preferred_element_type=F32
-    ) * (1.0 / math.sqrt(HEAD_SIZE))
-    query_place = row_start + jnp.arange(row_count, dtype=jnp.int32)
-    key_place = jnp.arange(length_total, dtype=jnp.int32)
-    allowed = (key_place[None, :] <= query_place[:, None]) | (key_place[None, :] < prefix_one)
-    return jnp.where(allowed, scores, MASKED)
-
-
-def attend(query_block, key_block, value_block, prefix_one, row_start):
-    scores = masked_scores(query_block, key_block, prefix_one, row_start)
-    row_peak = jnp.max(scores, axis=-1, keepdims=True)
-    weights = jnp.exp(scores - row_peak)
-    row_total = jnp.sum(weights, axis=-1, keepdims=True)
-    probabilities = (weights / row_total).astype(BF16)
-    attended = jnp.einsum(
-        "kgqp,pkd->qkgd", probabilities, value_block, preferred_element_type=F32
-    )
-    return (attended.astype(BF16), row_peak + jnp.log(row_total))
-
-
-def attend_back(query_block, key_block, value_block, grad_block, log_total, prefix_one, row_start):
-    scores = masked_scores(query_block, key_block, prefix_one, row_start)
-    probabilities = jnp.exp(scores - log_total)
-    rounded = probabilities.astype(BF16)
-    grad_probs = jnp.einsum(
-        "qkgd,pkd->kgqp", grad_block, value_block, preferred_element_type=F32
-    )
-    delta_rows = jnp.sum(probabilities * grad_probs, axis=-1, keepdims=True)
-    grad_scores = (probabilities * (grad_probs - delta_rows)).astype(BF16)
-    score_scale = 1.0 / math.sqrt(HEAD_SIZE)
-    grad_queries = (
-        jnp.einsum("kgqp,pkd->qkgd", grad_scores, key_block, preferred_element_type=F32)
-        * score_scale
-    )
-    grad_keys = (
-        jnp.einsum("kgqp,qkgd->pkd", grad_scores, query_block, preferred_element_type=F32)
-        * score_scale
-    )
-    grad_values = jnp.einsum(
-        "kgqp,qkgd->pkd", rounded, grad_block, preferred_element_type=F32
-    )
-    return (grad_queries, grad_keys, grad_values)
+def allowed_pairs(bounds_ref, shape):
+    key_place = lax.broadcasted_iota(jnp.int32, shape, 0)
+    query_place = bounds_ref[1] + lax.broadcasted_iota(jnp.int32, shape, 1)
+    return (key_place <= query_place) | (key_place < bounds_ref[0])
+
+
+SCORE_SCALE = 1.0 / math.sqrt(HEAD_SIZE)
+SMEM_SPEC = pl.BlockSpec(memory_space=pltpu.SMEM)
+
+
+def attend(bounds, queries, keys, values_flat):
+    heads, _, rows = queries.shape
+    places = keys.shape[1]
+    group = heads // keys.shape[0]
+
+    def kernel(bounds_ref, query_ref, key_ref, value_ref, out_ref, log_ref):
+        @pl.loop(0, heads)
+        def _(h):
+            k = h // group
+            scores = jnp.dot(key_ref[k], query_ref[h], preferred_element_type=F32) * SCORE_SCALE
+            scores = jnp.where(allowed_pairs(bounds_ref, (places, rows)), scores, MASKED)
+            peak = jnp.max(scores, axis=0, keepdims=True)
+            weights = jnp.exp(scores - peak)
+            total = jnp.sum(weights, axis=0, keepdims=True)
+            probabilities = (weights * (1.0 / total)).astype(BF16)
+            out_ref[h] = jnp.dot(
+                value_ref[k], probabilities, preferred_element_type=F32
+            ).astype(BF16)
+            log_ref[h] = peak + jnp.log(total)
+
+    return pl.pallas_call(
+        kernel,
+        out_shape=(
+            jax.ShapeDtypeStruct(queries.shape, BF16),
+            jax.ShapeDtypeStruct((heads, 1, rows), F32),
+        ),
+        in_specs=[SMEM_SPEC] + [pl.BlockSpec(memory_space=pltpu.VMEM)] * 3,
+        out_specs=(pl.BlockSpec(memory_space=pltpu.VMEM),) * 2,
+        compiler_params=pltpu.CompilerParams(vmem_limit_bytes=24 << 20),
+    )(bounds, queries, keys, values_flat)
+
+
+def attend_back(bounds, queries, keys, keys_flat, values, grads, log_total):
+    heads, size, rows = queries.shape
+    key_heads, places, _ = keys.shape
+    group = heads // key_heads
+
+    def kernel(
+        bounds_ref, query_ref, key_ref, key_flat_ref, value_ref, grad_ref, log_ref, query_grad_ref,
+        both_grad_ref, totals,
+    ):
+        totals[...] = jnp.zeros_like(totals)
+
+        @pl.loop(0, heads)
+        def _(h):
+            k = h // group
+            scores = jnp.dot(key_ref[k], query_ref[h], preferred_element_type=F32) * SCORE_SCALE
+            scores = jnp.where(allowed_pairs(bounds_ref, (places, rows)), scores, MASKED)
+            probabilities = jnp.exp(scores - log_ref[h])
+            grad_probs = jnp.dot(value_ref[k], grad_ref[h], preferred_element_type=F32)
+            delta = jnp.sum(probabilities * grad_probs, axis=0, keepdims=True)
+            grad_scores = (probabilities * (grad_probs - delta)).astype(BF16)
+            query_grad_ref[h] = SCORE_SCALE * jnp.dot(
+                key_flat_ref[k], grad_scores, preferred_element_type=F32
+            )
+            totals[k] += SCORE_SCALE * contract(query_ref[h], grad_scores, 1, 1)
+            totals[key_heads + k] += contract(grad_ref[h], probabilities.astype(BF16), 1, 1)
+
+        both_grad_ref[...] = totals[...].astype(BF16)
+
+    return pl.pallas_call(
+        kernel,
+        out_shape=(
+            jax.ShapeDtypeStruct(queries.shape, F32),
+            jax.ShapeDtypeStruct((2 * key_heads, size, places), BF16),
+        ),
+        in_specs=[SMEM_SPEC] + [pl.BlockSpec(memory_space=pltpu.VMEM)] * 6,
+        out_specs=(pl.BlockSpec(memory_space=pltpu.VMEM),) * 2,
+        scratch_shapes=[pltpu.VMEM((2 * key_heads, size, places), F32)],
+        compiler_params=pltpu.CompilerParams(vmem_limit_bytes=32 << 20),
+    )(bounds, queries, keys, keys_flat, values, grads, log_total)
 
 
 MESH = pl.DeviceIdType.MESH
@@ -374,16 +407,72 @@
     return begin, finish
 
 
+class KvSum:
+    side = False
+
+    def __init__(self, grad_kv, ctx_size):
+        self.ctx_size = ctx_size
+        self.inputs = (grad_kv,)
+        self.rows = grad_kv.shape[1] // ctx_size
+        self.block = (grad_kv.shape[0], self.rows)
+        self.outs = (jax.ShapeDtypeStruct(self.block, F32),)
+        self.out_specs = (VMEM_SPEC,)
+        self.scratch = [
+            pltpu.VMEM((ctx_size, *self.block), BF16), DMA((ctx_size,)), DMA((ctx_size,)),
+        ]
+
+    def bind(self, in_refs, out_refs, side_refs, scratch):
+        (grad_ref,) = in_refs
+        (sum_ref,) = out_refs
+        slots, send, recv = scratch
+        ctx_size, rows = self.ctx_size, self.rows
+        place = lax.axis_index("ctx")
+
+        def to(step):
+            peer = lax.rem(place + step, ctx_size)
+            return remote(
+                grad_ref.at[:, pl.ds(pl.multiple_of(peer * rows, rows), rows)], slots.at[place],
+                send.at[step], recv.at[step], {"ctx": peer},
+            )
+
+        def arrival(step):
+            src = lax.rem(place + ctx_size - step, ctx_size)
+            return remote(slots.at[src], slots.at[src], send.at[step], recv.at[step], {"ctx": src})
+
+        def begin():
+            for step in range(1, ctx_size):
+                to(step).start()
+            slots[place] = grad_ref[:, pl.ds(pl.multiple_of(place * rows, rows), rows)]
+
+        def middle():
+            pass
+
+        def end():
+            for step in range(1, ctx_size):
+                arrival(step).wait_recv()
+            total = slots[0].astype(F32)
+            for z in range(1, ctx_size):
+                total += slots[z].astype(F32)
+            sum_ref[...] = total
+            for step in range(1, ctx_size):
+                to(step).wait_send()
+
+        return begin, middle, end
+
+
 class AttnTail:
-    def __init__(self, pre_slabs, norm_all, gain_second, mesh_shape):
+    side = True
+
+    def __init__(self, pre_slabs, norm_all, gain_second, out_rows, mesh_shape):
         self.ctx_size, self.tp_size = mesh_shape
-        self.inputs = (pre_slabs, norm_all, gain_second)
+        self.inputs = (pre_slabs, norm_all, gain_second, out_rows)
         self.wide, self.rows = pre_slabs.shape[1:]
+        self.out_wide = out_rows.shape[0] // self.ctx_size
         self.half = norm_all.shape[1] // 2
         levels = self.tp_size // 2
         self.levels = levels
         self.outs = (
-            jax.ShapeDtypeStruct((self.ctx_size * self.wide, self.half), BF16),
+            jax.ShapeDtypeStruct((self.ctx_size * (self.wide + self.out_wide), self.half), BF16),
             jax.ShapeDtypeStruct((2, self.half), F32),
         )
         self.out_specs = (HBM_SPEC, VMEM_SPEC)
@@ -393,7 +482,7 @@
             pltpu.VMEM((self.wide, self.half), F32),
             pltpu.VMEM((self.wide, self.half), BF16),
             pltpu.VMEM((self.wide, self.half), BF16),
-            pltpu.VMEM((self.wide, self.half), BF16),
+            pltpu.VMEM((self.wide + self.out_wide, self.half), BF16),
             pltpu.VMEM((4, 2, self.half), F32),
             pltpu.VMEM((levels, 2, self.half), F32),
             pltpu.VMEM((self.ctx_size, 2, self.half), F32),
@@ -401,10 +490,13 @@
             DMA((6,)),
             DMA((chips,)), DMA((chips,)),
             DMA((self.ctx_size,)), DMA((self.ctx_size,)),
-        ] + line_sems(self.ctx_size)
+        ] + line_sems(self.ctx_size) + [
+            pltpu.VMEM((self.ctx_size, self.out_wide, self.half), BF16),
+            DMA((self.ctx_size,)), DMA((self.ctx_size,)),
+        ]
 
     def bind(self, in_refs, out_refs, side_refs, scratch):
-        pre_ref, norm_ref, gain_second_ref = in_refs
+        pre_ref, norm_ref, gain_second_ref, out_ref = in_refs
         all_ref, gains_ref = out_refs
         slabs, own_half, far_half, from_far, quarter, swaps, by_level, by_place = scratch[:8]
         all_send, all_recv, duo, lev_send, lev_recv, ctx_send, ctx_recv = scratch[8:15]
@@ -414,6 +506,20 @@
         far = {"fsdp": 1 - lax.axis_index("fsdp")}
         tile = min(512, half)
         line_begin, line_finish = line_gather(quarter, all_ref, ctx_size, scratch[15:18])
+        out_slots, out_send, out_recv = scratch[18:21]
+        wide, out_wide = self.wide, self.out_wide
+
+        def out_slab(step):
+            peer = lax.rem(place + step, ctx_size)
+            return remote(
+                rows_at(out_ref, peer * out_wide, out_wide), out_slots.at[place],
+                out_send.at[step], out_recv.at[step], {"ctx": peer},
+            )
+
+        def out_arrival(step):
+            src = lax.rem(place + ctx_size - step, ctx_size)
+            where = out_slots.at[src]
+            return remote(where, where, out_send.at[step], out_recv.at[step], {"ctx": src})
 
         def slab(step):
             peer = lax.rem(place + step, ctx_size)
@@ -468,7 +574,10 @@
         def begin():
             for step in range(1, ctx_size):
                 slab(step).start()
+            for step in range(1, ctx_size):
+                out_slab(step).start()
             slabs[place] = pre_ref[place]
+            out_slots[place] = out_ref[pl.ds(pl.multiple_of(place * out_wide, out_wide), out_wide), :]
 
         def middle():
             for step in range(1, ctx_size):
@@ -491,8 +600,14 @@
             swaps[0, 0:1, :] = gain_first[:, half:]
             swaps[0, 1:2, :] = gain_second_ref[:, half:]
             gain_x.start()
+            for step in range(1, ctx_size):
+                out_arrival(step).wait_recv()
+            total = out_slots[0].astype(F32)
+            for z in range(1, ctx_size):
+                total += out_slots[z].astype(F32)
+            quarter[wide : wide + out_wide, :] = total.astype(BF16)
             grads.wait_recv()
-            quarter[...] = (own_half[...] + from_far[...].astype(F32)).astype(BF16)
+            quarter[0:wide, :] = (own_half[...] + from_far[...].astype(F32)).astype(BF16)
             line_begin()
             gain_x.wait_recv()
             swaps[2, 0:1, :] = gain_first[:, :half] + swaps[1, 0:1, :]
@@ -519,6 +634,7 @@
             line_finish()
             for step in range(1, ctx_size):
                 slab(step).wait_send()
+                out_slab(step).wait_send()
                 gain_place(step).wait_send()
             for index in range(levels - 1):
                 gain_level(index).wait_send()
@@ -560,7 +676,10 @@
         core_send, core_recv, chip_send, chip_recv, pair_sems = refs[7:12]
         place = lax.axis_index("ctx")
         me, core, level, partner, others = tp_peers(tp_size)
-        enter(ctx_size, tp_size, along=across, pair=blocks == 2, side=beside, line=beside)
+        enter(
+            ctx_size, tp_size, along=across, pair=blocks == 2 and not beside,
+            side=beside and aside.side, line=beside,
+        )
         if beside:
             aside_begin, aside_middle, aside_end = aside.bind(
                 aside_in, aside_out, side_refs, refs[12:]
@@ -730,40 +849,35 @@
     )(cot_rows, *weights, gains)
 
 
-def place_halves(part, mine, other, wide):
-    pieces = len(mine)
-    depth = mine[0][0].shape[0]
-    tile = min(depth, 512)
-    parts = list(mine) + list(other)
-
-    def kernel(part_ref, *refs):
+def place_blocks(table, pieces, wide):
+    count = len(pieces)
+    depth = pieces[0][0].shape[0]
+    tile = min(depth, 1024)
+
+    def kernel(table_ref, *refs):
         out_ref = refs[-1]
         step = pl.program_id(1)
-        for k in range(2 * pieces):
+        for k in range(count):
             @pl.when(step == k)
             def _(k=k):
                 out_ref[...] = refs[k][...].astype(F32)
-
-    def target(i, step, part_ref):
-        half = jnp.where(step < pieces, part_ref[0], 1 - part_ref[0])
-        return i, half * pieces + lax.rem(step, pieces)
 
     return pl.pallas_call(
         kernel,
         grid_spec=pltpu.PrefetchScalarGridSpec(
             num_scalar_prefetch=1,
-            grid=(depth // tile, 2 * pieces),
+            grid=(depth // tile, count),
             in_specs=[
-                pl.BlockSpec((tile, wide), lambda i, step, part_ref, at=at: (i, at))
-                for _, at in parts
+                pl.BlockSpec((tile, wide), lambda i, step, table_ref, at=at: (i, at))
+                for _, at in pieces
             ],
-            out_specs=pl.BlockSpec((tile, wide), target),
+            out_specs=pl.BlockSpec((tile, wide), lambda i, step, table_ref: (i, table_ref[step])),
         ),
-        out_shape=jax.ShapeDtypeStruct((depth, 2 * pieces * wide), F32),
+        out_shape=jax.ShapeDtypeStruct((depth, count * wide), F32),
         cost_estimate=pl.CostEstimate(
-            flops=0, bytes_accessed=depth * 2 * pieces * wide * 6, transcendentals=0
+            flops=0, bytes_accessed=depth * count * wide * 6, transcendentals=0
         ),
-    )(part.reshape(1), *(array for array, _ in parts))
+    )(table, *(array for array, _ in pieces))
 
 
 def mean_square(rows):
@@ -825,11 +939,9 @@
         query_width = w_query.shape[1]
         key_width = key_projection.shape[1]
         ffn_width = w_gate.shape[1]
-        ffn_half = ffn_width // 2
-        chunk = ffn_half // CHUNKS
+        unit = ffn_width // 8
         query_heads = query_width // HEAD_SIZE
         kv_heads = key_width // HEAD_SIZE
-        heads_per_group = query_heads // kv_heads
         row_start = place * row_count
         pair_start = (place // 2) * 2 * row_count
 
@@ -850,45 +962,50 @@
         residual_all = rows_all[:, model_width:].astype(F32)
         gains = jnp.concatenate([gains, gains_far], axis=1)
         gain_first, gain_second = gains[0], gains[1]
-        w_gate, w_up, w_down, _ = lax.optimization_barrier((w_gate, w_up, w_down, qkv_weight))
-        ffn_own = []
-        for c in range(CHUNKS):
-            start = part * ffn_half + c * chunk
-            gate_own, up_own, down_own = (
-                lax.dynamic_slice_in_dim(w, start, chunk, 1) for w in (w_gate, w_up, w_down)
-            )
-            ffn_own.append((jnp.concatenate([gate_own, up_own], axis=1), down_own))
-        ffn_far = [[swap_rows(w) for w in ffn_own[0]]]
-        for c in range(1, CHUNKS):
-            ffn_own[c], ffn_far[c - 1] = lax.optimization_barrier((ffn_own[c], ffn_far[c - 1]))
-            ffn_far.append([swap_rows(w) for w in ffn_own[c]])
-
-        cosine_lookup, sine_lookup = rope_tables(row_start, row_count)
+        low = place & 1
+        base = 2 + 3 * part
+        units = [base, base + 1, base + 2, low, 1 - low]
+        def own_columns(weights, at):
+            return jnp.concatenate(
+                [lax.dynamic_slice_in_dim(w, at * unit, unit, 1) for w in weights], axis=1
+            )
+
+        ffn_weights = (w_gate, w_up, w_down)
+        ffn_weights, _ = lax.optimization_barrier((ffn_weights, qkv_weight))
+        owns = [own_columns(ffn_weights, units[0])]
+        ffn_weights, owns[0] = lax.optimization_barrier((ffn_weights, owns[0]))
+        owns += [own_columns(ffn_weights, at) for at in units[1:]]
+        others = [swap_rows(owns[0]), swap_rows(owns[1]), None, None, None]
+
+        cosine_lookup, sine_lookup = (table.T for table in rope_tables(row_start, row_count))
         residual = residual_low.astype(F32)
         rms_first = lax.rsqrt(jnp.mean(residual * residual, axis=-1, keepdims=True) + EPSILON)
         normalized_rows = (residual * rms_first * gain_first).astype(BF16)
-        qkv = jnp.dot(normalized_rows, qkv_weight, preferred_element_type=F32)
-        query_rot = apply_rotary(
-            qkv[:, :query_width].reshape(row_count, query_heads, HEAD_SIZE),
+        qkv = contract(qkv_weight, normalized_rows, 0, 1)
+        queries = apply_rotary(
+            qkv[:query_width].reshape(query_heads, HEAD_SIZE, row_count),
             cosine_lookup, sine_lookup, 1.0,
         ).astype(BF16)
         key_rot = apply_rotary(
-            qkv[:, query_width : query_width + key_width].reshape(row_count, kv_heads, HEAD_SIZE),
+            qkv[query_width : query_width + key_width].reshape(kv_heads, HEAD_SIZE, row_count),
             cosine_lookup, sine_lookup, 1.0,
-        ).astype(BF16).reshape(row_count, key_width)
-        value_matrix = qkv[:, query_width + key_width :].astype(BF16)
+        ).astype(BF16)
+        value_rows = qkv[query_width + key_width :].astype(BF16)
+        kv_own = jnp.concatenate([key_rot, value_rows.reshape(kv_heads, HEAD_SIZE, row_count)], axis=0)
         kv_whole = lax.all_gather(
-            jnp.concatenate([key_rot, value_matrix], axis=1), "ctx", axis=0, tiled=True
+            kv_own.reshape(2 * key_width, row_count).T, "ctx", axis=0, tiled=True
         )
         length_total = kv_whole.shape[0]
-        key_whole = kv_whole[:, :key_width].reshape(length_total, kv_heads, HEAD_SIZE)
-        value_whole = kv_whole[:, key_width:].reshape(length_total, kv_heads, HEAD_SIZE)
-        query_groups = query_rot.reshape(row_count, kv_heads, heads_per_group, HEAD_SIZE)
-        prefix_one = prefix[0]
-        attended, log_total = attend(query_groups, key_whole, value_whole, prefix_one, row_start)
-        attended_flat = attended.reshape(row_count, query_width)
-        attn_term = contract(attended_flat, out_weight, 1, 1).astype(BF16)
-        attn_term, ffn_far[0] = lax.optimization_barrier((attn_term, ffn_far[0]))
+        by_place = kv_whole.reshape(length_total, 2 * kv_heads, HEAD_SIZE).transpose(1, 0, 2)
+        by_feature = kv_whole.T.reshape(2 * kv_heads, HEAD_SIZE, length_total)
+        bounds = jnp.stack([prefix[0], row_start.astype(jnp.int32)])
+        attended, log_total = attend(
+            bounds, queries, by_place[:kv_heads], by_feature[kv_heads:]
+        )
+        attended_flat = attended.reshape(query_width, row_count)
+        attn_term = contract(attended_flat, out_weight, 0, 1).astype(BF16)
+        attn_term, owns[2], others[0] = lax.optimization_barrier((attn_term, owns[2], others[0]))
+        others[2] = swap_rows(owns[2])
         slice_shape = (row_count // tp_size, model_width)
         normed_all, middle = reduce_gather(
             attn_term, (residual_low, gain_second[None]), finish_middle,
@@ -899,14 +1016,23 @@
         mid_term = 0.0
         sides = []
         fars = []
-        for c in range(CHUNKS):
-            if c:
-                ffn_far[c], fars[-1] = lax.optimization_barrier((ffn_far[c], fars[-1]))
-            pair_w, down_w = (
-                jnp.concatenate([w, far], axis=0) for w, far in zip(ffn_own[c], ffn_far[c])
-            )
+        received = []
+
+        def pair(rows):
+            return lax.dynamic_slice_in_dim(rows, pair_start, 2 * row_count, 0)
+
+        def outer(sides_of, part_of):
+            return [contract(part_of(rows), cols, 0, 0) for rows, cols in sides_of]
+
+        def summed(c):
+            near = jnp.concatenate(outer(sides[c], lambda rows: rows[:, :half_width]), axis=1)
+            return (near + received[c].astype(F32)).astype(BF16)
+
+        def forward(c):
+            both_w = jnp.concatenate([owns[c], others[c]], axis=0)
+            pair_w, down_w = both_w[:, : 2 * unit], both_w[:, 2 * unit :]
             both = jnp.dot(normed_all, pair_w, preferred_element_type=F32)
-            gating, upward = both[:, :chunk], both[:, chunk:]
+            gating, upward = both[:, :unit], both[:, unit:]
             grad_hidden = jnp.dot(cot_all, down_w, preferred_element_type=F32)
             sigmoid_gate = jax.nn.sigmoid(gating)
             hidden = (gating * sigmoid_gate * upward).astype(BF16)
@@ -916,93 +1042,98 @@
             grad_upward = (grad_hidden * gating * sigmoid_gate).astype(BF16)
             grad_both = jnp.concatenate([grad_gating, grad_upward], axis=1)
             sides.append(((normed_all, grad_both), (cot_all, hidden)))
-            fars.append(
-                [contract(rows[:, half_width:], cols, 0, 0).astype(BF16) for rows, cols in sides[c]]
-            )
-
-            def pair(rows):
-                return lax.dynamic_slice_in_dim(rows, pair_start, 2 * row_count, 0)
-
+            far = outer(sides[c], lambda rows: rows[:, half_width:])
+            fars.append(jnp.concatenate([f.astype(BF16) for f in far], axis=1))
+            return pair_w, down_w, grad_both, hidden
+
+        for c in range(4):
+            if c:
+                others[c], fars[-1] = lax.optimization_barrier((others[c], fars[-1]))
+            if c == 1:
+                owns[3], others[1] = lax.optimization_barrier((owns[3], others[1]))
+                others[3] = swap_rows(owns[3])
+            pair_w, down_w, grad_both, hidden = forward(c)
             ffn_term += contract(pair(hidden), down_w, 1, 1)
             mid_term += contract(pair(grad_both), pair_w, 1, 1)
 
-        mid_low, fars[-1] = lax.optimization_barrier((mid_term.astype(BF16), fars[-1]))
-        received = [[swap_rows(far) for far in chunk_fars] for chunk_fars in fars]
-
-        def summed(c):
-            return [
-                (contract(rows[:, :half_width], cols, 0, 0) + far.astype(F32)).astype(BF16)
-                for (rows, cols), far in zip(sides[c], received[c])
-            ]
-
+        def swap_ctx(total):
+            return lax.ppermute(total, "ctx", swap_z)
+
+        others[4] = lax.ppermute(others[3], "ctx", swap_z)
+        received = [swap_rows(fars[0]), swap_rows(fars[1])]
+        mid_low, fars[2], fars[3] = lax.optimization_barrier(
+            (mid_term.astype(BF16), fars[2], fars[3])
+        )
+        received.append(swap_rows(fars[2]))
         branch_low, grad_middle, gain_grad_second = reduce_gather(
             mid_low, (middle, cot_low, gain_second[None]), finish_grad_middle,
             (slice_shape, (1, model_width)), mesh_shape, 2, 2, False,
         )
-        totals = [None] * CHUNKS
-        branch_low, received[0] = lax.optimization_barrier((branch_low, received[0]))
-        totals[0] = summed(0)
-        branch_low, totals[0] = lax.optimization_barrier((branch_low, totals[0]))
-        swapped = [None] * CHUNKS
-        swapped[0] = [lax.ppermute(total, "ctx", swap_z) for total in totals[0]]
-        grad_out = contract(branch_low, attended_flat, 0, 0)
-        grad_out_far = swap_rows(grad_out[half_width:].astype(BF16))
-        grad_attended = jnp.dot(branch_low, out_weight, preferred_element_type=F32).astype(BF16)
-        grad_attended = grad_attended.reshape(row_count, kv_heads, heads_per_group, HEAD_SIZE)
-        grad_query_rot, grad_key_all, grad_value_all = attend_back(
-            query_groups, key_whole, value_whole, grad_attended, log_total, prefix_one, row_start
-        )
-        grad_kv = jnp.concatenate(
-            [
-                grad_key_all.reshape(length_total, key_width),
-                grad_value_all.reshape(length_total, key_width),
-            ],
-            axis=1,
-        ).astype(BF16)
-        grad_kv = lax.psum_scatter(grad_kv, "ctx", scatter_dimension=0, tiled=True)
-        ffn_low, grad_kv = lax.optimization_barrier((ffn_term.astype(BF16), grad_kv))
-        grad_kv = grad_kv.astype(F32)
-        (output_rows,) = reduce_gather(
-            ffn_low, (middle,), finish_output, (), mesh_shape, 3, 2, False
-        )
-        grad_out = grad_out[:half_width] + grad_out_far.astype(F32)
-        grad_out = lax.psum(grad_out.astype(BF16), "ctx").astype(F32)
+        branch_low, others[4], received[0], received[1], fars[3] = lax.optimization_barrier(
+            (branch_low, others[4], received[0], received[1], fars[3])
+        )
+        totals = [summed(0), summed(1)]
+        branch_low, totals = lax.optimization_barrier((branch_low, totals))
+        swapped = [swap_ctx(total) for total in totals]
+        grad_out = jnp.dot(attended_flat, branch_low, preferred_element_type=F32)
+        grad_out_far = swap_rows(grad_out[:, half_width:].astype(BF16))
+        received.append(swap_rows(fars[3]))
+        forward(4)
+        grad_attended = contract(out_weight, branch_low, 0, 1).astype(BF16)
+        grad_query_rot, grad_kv = attend_back(
+            bounds, queries, by_place[:kv_heads], by_feature[:kv_heads], by_place[kv_heads:],
+            grad_attended.reshape(query_heads, HEAD_SIZE, row_count), log_total,
+        )
+        grad_kv = grad_kv.reshape(2 * key_width, length_total)
+        grad_kv, fars[4], received[2] = lax.optimization_barrier((grad_kv, fars[4], received[2]))
+        totals.append(summed(2))
+        grad_kv, totals[2] = lax.optimization_barrier((grad_kv, totals[2]))
+        swapped.append(swap_ctx(totals[2]))
+        received.append(swap_rows(fars[4]))
+        output_rows, grad_kv = reduce_gather(
+            ffn_term.astype(BF16), (middle,), finish_output, (), mesh_shape, 3, 2, False,
+            KvSum(grad_kv, ctx_size),
+        )
+        output_rows, grad_kv, grad_out_far, received[3], swapped[0] = lax.optimization_barrier(
+            (output_rows, grad_kv, grad_out_far, received[3], swapped[0])
+        )
         grad_query_pre = apply_rotary(
-            grad_query_rot.reshape(row_count, query_heads, HEAD_SIZE),
+            grad_query_rot, cosine_lookup, sine_lookup, -1.0
+        ).astype(BF16).reshape(query_width, row_count)
+        grad_key_pre = apply_rotary(
+            grad_kv[:key_width].reshape(kv_heads, HEAD_SIZE, row_count),
             cosine_lookup, sine_lookup, -1.0,
-        ).astype(BF16).reshape(row_count, query_width)
-        grad_key_pre = apply_rotary(
-            grad_kv[:, :key_width].reshape(row_count, kv_heads, HEAD_SIZE),
-            cosine_lookup, sine_lookup, -1.0,
-        ).astype(BF16).reshape(row_count, key_width)
-        grad_value_pre = grad_kv[:, key_width:].astype(BF16)
-        grad_qkv_pre = jnp.concatenate([grad_query_pre, grad_key_pre, grad_value_pre], axis=1)
-        attn_width = grad_qkv_pre.shape[1]
-        pre_slabs = grad_qkv_pre.T.reshape(ctx_size, attn_width // ctx_size, row_count)
-        normed_term = contract(grad_qkv_pre, qkv_weight, 1, 1).astype(BF16)
-        normed_term, received[1], output_rows = lax.optimization_barrier(
-            (normed_term, received[1], output_rows)
-        )
-        totals[1] = summed(1)
-        normed_term, totals[1] = lax.optimization_barrier((normed_term, totals[1]))
-        swapped[1] = [lax.ppermute(total, "ctx", swap_z) for total in totals[1]]
+        ).astype(BF16).reshape(key_width, row_count)
+        grad_value_pre = grad_kv[key_width:].astype(BF16)
+        grad_qkv_pre = jnp.concatenate([grad_query_pre, grad_key_pre, grad_value_pre], axis=0)
+        attn_width = grad_qkv_pre.shape[0]
+        pre_slabs = grad_qkv_pre.reshape(ctx_size, attn_width // ctx_size, row_count)
+        normed_term = contract(grad_qkv_pre, qkv_weight, 0, 1).astype(BF16)
+        grad_out_rows = (grad_out[:, :half_width] + grad_out_far.astype(F32)).astype(BF16)
+        totals.append(summed(3))
+        normed_term, totals[3] = lax.optimization_barrier((normed_term, totals[3]))
         rms_all = lax.rsqrt(jnp.mean(residual_all * residual_all, axis=-1, keepdims=True) + EPSILON)
         norm_all = (residual_all * rms_all * gain_first).astype(BF16)
         input_rows, _, grad_attn, gain_grads = reduce_gather(
             normed_term,
             (grad_middle, residual_low, gain_first[None]), finish_grad_input,
             ((1, model_width),), mesh_shape, 4, 1, False,
-            AttnTail(pre_slabs, norm_all, gain_grad_second, mesh_shape),
-        )
-        grad_attn = grad_attn.T.astype(F32)
-
-        def result(which, block):
-            return place_halves(
-                part,
-                [(totals[c][which], block) for c in range(CHUNKS)],
-                [(swapped[c][which], block) for c in range(CHUNKS)],
-                chunk,
-            )
+            AttnTail(pre_slabs, norm_all, gain_grad_second, grad_out_rows, mesh_shape),
+        )
+        grad_attn, received[4], swapped[1], swapped[2] = lax.optimization_barrier(
+            (grad_attn, received[4], swapped[1], swapped[2])
+        )
+        grad_attn = grad_attn.reshape(ctx_size, -1, half_width)
+        part_width = attn_width // ctx_size
+        grad_out = grad_attn[:, part_width:].reshape(query_width, half_width).T.astype(F32)
+        grad_attn = grad_attn[:, :part_width].reshape(attn_width, half_width).T.astype(F32)
+
+        totals.append(summed(4))
+        far_base = 2 + 3 * (1 - part)
+        table = jnp.stack(units + [far_base, far_base + 1, far_base + 2])
+
+        def result(block):
+            return place_blocks(table, [(piece, block) for piece in totals + swapped], unit)
 
         end_key = query_width + key_width
         end_value = end_key + key_width
@@ -1015,9 +1146,9 @@
             grad_attn[:, end_key:end_value],
             grad_out,
             gain_grads[1],
-            result(0, 0),
-            result(0, 1),
-            result(1, 0),
+            result(0),
+            result(1),
+            result(2),
         )
 
     return local

time: 664 us -> 594 us (0.89)
  waiting for transfers between devices: 60.3 us -> 4.27 us
  Pallas kernels: 372 us -> 344 us
  between operations: 16.2 us -> 2.83 us
  other arithmetic: 39.8 us -> 49.6 us
  matrix products: 92.5 us -> 100 us
    pallas_call x4, Pallas kernels: 288 us -> 243 us  [reduce_gather(): pl.pallas_call(kernel, out_shape=(jax.ShapeDtypeStruct((reach * block_row...]
    ppermute x9 -> x10, waiting for transfers between devices: 41.1 us -> 4.26 us  [swap_rows(): return lax.ppermute(array, 'fsdp', swap_x)]
    dot_general x15 -> x32, matrix products: 45.8 us -> 69.5 us  [contract(): lax.dot_general(left, right, (((left_dim,), (right_dim,)), ((), ())), pre...]
    reduce_scatter x1 -> x0, waiting for transfers between devices: 19.2 us -> none  [local(): grad_kv = lax.psum_scatter(grad_kv, 'ctx', scatter_dimension=0, tiled=True)]
    pallas_call x3 -> x5, Pallas kernels: 22.2 us -> 39.8 us  [the longest x3 22.4 us: place_blocks(): pl.pallas_call(kernel, grid_spec=pltpu.PrefetchScalarGridSpec(num_scalar_...]
    concatenate x8 -> x15, other arithmetic: 4.11 us -> 21.7 us  [the longest x1 8.48 us: forward(): both_w = jnp.concatenate([owns[c], others[c]], axis=0)]
    dot_general x12 -> x11, matrix products: 46.7 us -> 30.7 us  [the longest x5 16.6 us: forward(): grad_hidden = jnp.dot(cot_all, down_w, preferred_element_type=F32)]
    convert_element_type x8 -> x9, other arithmetic: 20.5 us -> 16.3 us  [the longest x5 13.9 us: summed(): return (near + received[c].astype(F32)).astype(BF16)]
  transfers between devices with their start and end apart: 15 -> 14, of which waited for: 3 -> 1; matrix products, arithmetic and copies ran while one was open for 20% -> 28% of each run, Pallas kernels for 45% -> 44%
where the time goes in v4:
time: 594 us; the launch traced here: 586 us
  Pallas kernels  344 us (58%)
  matrix products  100 us (17%)
  local copies, waits for them, and re-layouts  55.3 us (9%)
  other arithmetic  49.6 us (8%)
  blocking collectives  15.4 us (3%)
  starting transfers between devices  14.4 us (2%)
    pallas_call x4, Pallas kernels, reduce_gather(): pl.pallas_call(kernel, out_shape=(jax.ShapeDtypeStruct((reach * block_row...  243 us
    dot_general x32, matrix products, contract(): lax.dot_general(left, right, (((left_dim,), (right_dim,)), ((), ())), pre...  69.5 us
    pallas_call x1, Pallas kernels, opening(): pl.pallas_call(kernel, out_shape=(jax.ShapeDtypeStruct((ctx_size * block_...  61.9 us
    unnamed x188, local copies, waits for them, and re-layouts  25.5 us
    pallas_call x3, Pallas kernels, place_blocks(): pl.pallas_call(kernel, grid_spec=pltpu.PrefetchScalarGridSpec(num_scalar_...  22.4 us
    dot_general x5, matrix products, forward(): grad_hidden = jnp.dot(cot_all, down_w, preferred_element_type=F32)  16.6 us
    all_gather x1, blocking collectives, local(): lax.all_gather(kv_own.reshape(2 * key_width, row_count).T, 'ctx', axis=0,...  15.4 us
    convert_element_type x5, other arithmetic, summed(): return (near + received[c].astype(F32)).astype(BF16)  13.9 us
  transfers between devices with their start and end apart: 14, of which 1 were waited for; matrix products, arithmetic and copies ran while one was open for 28% of the time, Pallas kernels for 44%

profile of v4, /device:TPU:0, one launch (start us, length us, event | category | flops | bytes accessed | tf_op | source)
XLA Modules:
  0.0 586.1 jit_solution(10922537390917903433)
XLA Ops:
  3.1 1.7 dynamic-slice_bitcast_fusion.1
  7.4 61.9 %shard_map.203 = (bf16[1024,4096]{1,0:T(8,128)(2,1)}, f32[2,1024]{1,0:T(2,128)S(1)}, bf16[2048,768]{1,0:T(8,128)(2,1)S(1)}, bf16[2048,512]{1,0:T(8,128)(2,1)S(1)}) custom-call(bf16[256,4096]{1,0:T(8,128)(2,1)S(1)} %pad_maximum_fusion.7.cot_ref, bf16[1024,512]{1,0:T(8,128)(2,1)S(1)} %copy-done.4, bf16[1024,256]{1,0:T(8,128)(2,1)S(1)} %pad_maximum_fusion.35.refs_1_, ...), custom_call_target="tpu_custom_call" | custom-call | tf_op jit(solution)/shard_map/pallas_call | solution.py:835
  69.3 1.7 copy-done.8
  76.0 2.9 constant_dynamic-slice_fusion.4
  80.6 1.6 copy-done.51
  86.8 3.0 fusion.69
  90.6 2.7 constant_dynamic-update-slice_fusion.1
  95.7 15.4 %all_gather.3 = bf16[1024,256]{0,1:T(8,128)(2,1)S(1)} all-gather(bf16[256,256]{0,1:T(8,128)(2,1)S(1)} %bitcast.96), channel_id=1, replica_groups=mesh['fsdp'=2,'ctx'=4,'tp'=4] {'ctx'}, dimensions={0}, use_global_device_ids=true | all-gather | bytes 655360 | tf_op jit(solution)/shard_map/all_gather | solution.py:995
  114.5 3.1 fusion
  117.8 2.6 pad_maximum_fusion.9
  120.4 7.7 %shard_map.204 = (bf16[8,64,256]{2,1,0:T(8,128)(2,1)S(1)}, f32[8,1,256]{2,1,0:T(1,128)S(1)}) custom-call(s32[2]{0:T(128)S(1)} %pad_add_fusion.bounds_ref, bf16[8,64,256]{2,1,0:T(8,128)(2,1)S(1)} %pad_maximum_fusion.37.query_ref, bf16[2,1024,64]{2,1,0:T(8,128)(2,1)S(1)} %get-tuple-element.182.key_ref, bf16[2,64,1024]{2,1,0:T(8,128)(2,1)S(1)} %bitcast.81), custom_call_target="tpu_custom_call" | custom-call | tf_op jit(solution)/shard_map/pallas_call | solution.py:72
  129.5 2.8 pad_maximum_fusion.11
  134.0 2.9 fusion.2.refs_4_
  136.9 2.8 constant_dynamic-update-slice_fusion.3
  141.8 43.4 %shard_map.205 = (bf16[1024,2048]{1,0:T(8,128)(2,1)S(1)}, f32[64,2048]{1,0:T(8,128)S(1)}) custom-call(bf16[256,2048]{1,0:T(8,128)(2,1)S(1)} %convolution_convert_fusion.term_ref, bf16[256,2048]{1,0:T(8,128)(2,1)S(1)} %pad_maximum_fusion.22.refs_0_.refs_1_, f32[1,2048]{1,0:T(1,128)S(1)} %get-tuple-element.197.refs_1_.refs_2_), custom_call_target="tpu_custom_call" | custom-call | tf_op jit(solution)/shard_map/pallas_call | solution.py:773
  185.2 2.4 fusion.37
  187.6 1.7 multiply_convert_fusion.13
  192.7 2.7 constant_dynamic-update-slice_fusion.5
  197.0 1.7 fusion.47
  198.7 2.6 fusion.57
  201.4 8.5 %pad_maximum_fusion = bf16[2048,768]{1,0:T(8,128)(2,1)S(1)} fusion(bf16[1024,768]{1,0:T(8,128)(2,1)} %collective-permute-done.1, bf16[1024,256]{1,0:T(8,128)(2,1)S(1)} %copy-done.21, bf16[1024,256]{1,0:T(8,128)(2,1)S(1)} %copy-done.23, bf16[1024,256]{1,0:T(8,128)(2,1)S(1)} %copy-done.25), kind=kLoop, calls=%fused_computation.7 | loop fusion | flops 12582912 | bytes 6291456 | tf_op jit(solution)/shard_map/concatenate | solution.py:1032
  209.8 2.4 fusion.33
  212.3 2.7 multiply_convert_fusion.10
  215.8 1.8 fusion.45
  217.6 1.8 fusion.98
  222.5 2.6 fusion.55
  227.7 3.5 fusion.31
  232.7 2.4 fusion.29
  235.2 3.9 multiply_convert_fusion.7
  239.1 2.5 convolution_convert_fusion.9
  244.2 3.4 fusion.43
  247.6 2.6 fusion.53
  250.2 3.3 fusion.27
  255.1 2.4 fusion.25
  257.6 4.3 multiply_convert_fusion.3
  261.9 2.7 convolution_convert_fusion.8
  267.2 5.8 add_convert_fusion.term_ref
  275.1 32.4 %shard_map.206 = (bf16[256,2048]{1,0:T(8,128)(2,1)S(1)}, f32[64,2048]{1,0:T(8,128)S(1)}, f32[1,2048]{1,0:T(1,128)S(1)}) custom-call(bf16[512,2048]{1,0:T(8,128)(2,1)S(1)} %add_convert_fusion.term_ref, f32[64,2048]{1,0:T(8,128)S(1)} %get-tuple-element.95.refs_0_, bf16[256,2048]{1,0:T(8,128)(2,1)S(1)} %pad_maximum_fusion.23.refs_1_, ...), custom_call_target="tpu_custom_call" | custom-call | tf_op jit(solution)/shard_map/pallas_call | solution.py:773
  307.5 3.4 fusion.41
  310.9 2.6 fusion.51
  313.6 2.1 fusion.83
  315.6 2.2 add_convert_fusion.1.term_ref
  317.9 2.7 fusion.3.refs_0_
  320.9 2.5 fusion.4.refs_1_
  327.6 2.0 collective-permute-start.10
  329.6 3.6 fusion.22
  333.2 4.0 multiply_convert_fusion.2
  337.3 2.9 convolution_convert_fusion.7
  343.5 9.7 %shard_map.207 = (f32[8,64,256]{2,1,0:T(8,128)S(1)}, bf16[4,64,1024]{2,1,0:T(8,128)(2,1)S(1)}) custom-call(s32[2]{0:T(128)S(1)} %pad_add_fusion.bounds_ref, bf16[8,64,256]{2,1,0:T(8,128)(2,1)S(1)} %pad_maximum_fusion.37.query_ref, bf16[2,1024,64]{2,1,0:T(8,128)(2,1)S(1)} %get-tuple-element.182.key_ref, bf16[2,64,1024]{2,1,0:T(8,128)(2,1)S(1)} %bitcast.80, ...), custom_call_target="tpu_custom_call" | custom-call | tf_op jit(solution)/shard_map/pallas_call | solution.py:112
  353.2 2.0 fusion.5.refs_2_
  356.6 3.3 fusion.39
  359.9 2.6 fusion.49
  362.6 4.2 collective-permute-done.8
  366.8 2.0 collective-permute-start.13
  369.0 85.3 %shard_map.208 = (bf16[256,2048]{1,0:T(8,128)(2,1)S(1)}, f32[256,256]{1,0:T(8,128)S(1)}) custom-call(bf16[512,2048]{1,0:T(8,128)(2,1)S(1)} %add_convert_fusion.1.term_ref, f32[64,2048]{1,0:T(8,128)S(1)} %get-tuple-element.95.refs_0_, bf16[256,1024]{1,0:T(8,128)(2,1)S(1)} %bitcast.82), custom_call_target="tpu_custom_call" | custom-call | tf_op jit(solution)/shard_map/pallas_call | solution.py:773
  454.5 3.6 fusion.6.refs_3_
  459.2 1.7 fusion.21.refs_6_
  460.9 81.4 %shard_map.209 = (bf16[256,2048]{1,0:T(8,128)(2,1)S(1)}, f32[1,2048]{1,0:T(1,128)}, bf16[1280,1024]{1,0:T(8,128)(2,1)S(1)}, f32[2,1024]{1,0:T(2,128)S(1)}) custom-call(bf16[256,2048]{1,0:T(8,128)(2,1)S(1)} %convolution_convert_fusion.1.term_ref, f32[64,2048]{1,0:T(8,128)S(1)} %get-tuple-element.122.refs_0_, bf16[256,2048]{1,0:T(8,128)(2,1)S(1)} %copy-done.1, ...), custom_call_target="tpu_custom_call" | custom-call | tf_op jit(solution)/shard_map/pallas_call | solution.py:773
  548.0 3.1 fusion.7.refs_4_
  551.1 7.5 %shard_map.210 = f32[1024,2048]{1,0:T(8,128)} custom-call(s32[8]{0:T(128)} %stack.55.table_ref, bf16[1024,768]{1,0:T(8,128)(2,1)} %copy-done.10, bf16[1024,768]{1,0:T(8,128)(2,1)} %copy-done.11, bf16[1024,768]{1,0:T(8,128)(2,1)} %copy-done.12, bf16[1024,768]{1,0:T(8,128)(2,1)} %fusion.6.refs_3_, bf16[1024,768]{1,0:T(8,128)(2,1)} %fusion.7.refs_4_, ...), custom_call_target="tpu_custom_call" | custom-call | bytes 12582912 | tf_op jit(solution)/shard_map/pallas_call | solution.py:865
  558.6 7.5 %shard_map.211 = f32[1024,2048]{1,0:T(8,128)} custom-call(s32[8]{0:T(128)} %stack.55.table_ref, bf16[1024,768]{1,0:T(8,128)(2,1)} %copy-done.10, bf16[1024,768]{1,0:T(8,128)(2,1)} %copy-done.11, bf16[1024,768]{1,0:T(8,128)(2,1)} %copy-done.12, bf16[1024,768]{1,0:T(8,128)(2,1)} %fusion.6.refs_3_, bf16[1024,768]{1,0:T(8,128)(2,1)} %fusion.7.refs_4_, ...), custom_call_target="tpu_custom_call" | custom-call | bytes 12582912 | tf_op jit(solution)/shard_map/pallas_call | solution.py:865
  566.1 7.5 %shard_map.212 = f32[1024,2048]{1,0:T(8,128)} custom-call(s32[8]{0:T(128)} %stack.55.table_ref, bf16[1024,768]{1,0:T(8,128)(2,1)} %copy-done.10, bf16[1024,768]{1,0:T(8,128)(2,1)} %copy-done.11, bf16[1024,768]{1,0:T(8,128)(2,1)} %copy-done.12, bf16[1024,768]{1,0:T(8,128)(2,1)} %fusion.6.refs_3_, bf16[1024,768]{1,0:T(8,128)(2,1)} %fusion.7.refs_4_, ...), custom_call_target="tpu_custom_call" | custom-call | bytes 12582912 | tf_op jit(solution)/shard_map/pallas_call | solution.py:865
  576.3 2.9 copy.67
  581.5 1.8 copy.64
  (283 shorter events, 72.7 us)
Async XLA Ops:
  4.9 81.9 %copy-start.16 = (bf16[256,1024]{1,0:T(8,128)(2,1)}, bf16[256,1024]{1,0:T(8,128)(2,1)S(1)}, u32[]{:S(2)}) copy-start(bf16[256,1024]{1,0:T(8,128)(2,1)S(1)} %get-tuple-element.185) | copy-start | bytes 1572868
  4.9 81.9 %copy-start.18 = (bf16[256,1024]{1,0:T(8,128)(2,1)}, bf16[256,1024]{1,0:T(8,128)(2,1)S(1)}, u32[]{:S(2)}) copy-start(bf16[256,1024]{1,0:T(8,128)(2,1)S(1)} %get-tuple-element.186) | copy-start | bytes 1572868
  75.5 61.4 %collective-permute-start = (bf16[1024,768]{1,0:T(8,128)(2,1)}, bf16[1024,768]{1,0:T(8,128)(2,1)}, u32[]{:S(2)}, u32[]{:S(2)}) collective-permute-start(bf16[1024,768]{1,0:T(8,128)(2,1)} %pad_maximum_fusion.8), channel_id=1, source_target_pairs={{0,16},{16,0},{1,17},{17,1},{2,18},{18,2},{3,19},{19,3},{4,20},{20... | collective-permute-start | bytes 4718600 | tf_op jit(solution)/shard_map/ppermute | solution.py:928
  76.0 3.3 copy-start.50
  79.3 4.3 copy-start.20
  79.3 2.9 copy-start.51
  84.9 107.8 %collective-permute-start.1 = (bf16[1024,768]{1,0:T(8,128)(2,1)}, bf16[1024,768]{1,0:T(8,128)(2,1)}, u32[]{:S(2)}, u32[]{:S(2)}) collective-permute-start(bf16[1024,768]{1,0:T(8,128)(2,1)} %pad_maximum_fusion.10), channel_id=1, source_target_pairs={{0,16},{16,0},{1,17},{17,1},{2,18},{18,2},{3,19},{19,3},{4,20},{20... | collective-permute-start | bytes 4718600 | tf_op jit(solution)/shard_map/ppermute | solution.py:928
  90.6 4.2 slice-start.2
  90.6 5.0 slice-start.3
  114.5 3.2 copy-start.62
  114.5 3.2 copy-start.63
  129.5 2.8 copy-start.17
  129.5 2.8 copy-start.19
  129.5 2.9 copy-start.36
  129.5 2.9 copy-start.38
  132.4 9.4 %copy-start = (bf16[256,2048]{1,0:T(8,128)(2,1)}, bf16[256,2048]{1,0:T(8,128)(2,1)S(1)}, u32[]{:S(2)}) copy-start(bf16[256,2048]{1,0:T(8,128)(2,1)S(1)} %pad_maximum_fusion.22.refs_0_.refs_1_) | copy-start | bytes 3145732
  136.9 3.4 copy-start.28
  139.7 91.5 %collective-permute-start.2 = (bf16[1024,768]{1,0:T(8,128)(2,1)}, bf16[1024,768]{1,0:T(8,128)(2,1)}, u32[]{:S(2)}, u32[]{:S(2)}) collective-permute-start(bf16[1024,768]{1,0:T(8,128)(2,1)} %pad_maximum_fusion.9), channel_id=1, source_target_pairs={{0,16},{16,0},{1,17},{17,1},{2,18},{18,2},{3,19},{19,3},{4,20},{20... | collective-permute-start | bytes 4718600 | tf_op jit(solution)/shard_map/ppermute | solution.py:928
  141.8 45.8 %copy-start.29 = (bf16[2048,768]{1,0:T(8,128)(2,1)}, bf16[2048,768]{1,0:T(8,128)(2,1)S(1)}, u32[]{:S(2)}) copy-start(bf16[2048,768]{1,0:T(8,128)(2,1)S(1)} %constant_dynamic-update-slice_fusion) | copy-start | bytes 9437188
  141.8 45.8 %slice-start = ((s8[8388608]{0:T(1024)(128)(4,1)}), s8[4194304]{0:T(1024)(128)(4,1)S(1)}, s32[]{:S(2)}) async-start(s8[8388608]{0:T(1024)(128)(4,1)} %bitcast.86), calls=%async_computation | async-start | bytes 8388608
  189.3 7.6 %copy-start.81 = (bf16[1024,256]{0,1:T(8,128)(2,1)}, bf16[1024,256]{0,1:T(8,128)(2,1)S(1)}, u32[]{:S(2)}) copy-start(bf16[1024,256]{0,1:T(8,128)(2,1)S(1)} %get-tuple-element.176) | copy-start | bytes 1572868
  189.4 9.3 %copy-start.67 = (bf16[1024,256]{0,1:T(8,128)(2,1)}, bf16[1024,256]{0,1:T(8,128)(2,1)S(1)}, u32[]{:S(2)}) copy-start(bf16[1024,256]{0,1:T(8,128)(2,1)S(1)} %get-tuple-element.170) | copy-start | bytes 1572868
  189.4 9.3 %copy-start.69 = (bf16[1024,256]{0,1:T(8,128)(2,1)}, bf16[1024,256]{0,1:T(8,128)(2,1)S(1)}, u32[]{:S(2)}) copy-start(bf16[1024,256]{0,1:T(8,128)(2,1)S(1)} %get-tuple-element.171) | copy-start | bytes 1572868
  195.4 58.2 %collective-permute-start.3 = (bf16[1024,768]{1,0:T(8,128)(2,1)}, bf16[1024,768]{1,0:T(8,128)(2,1)}, u32[]{:S(2)}, u32[]{:S(2)}) collective-permute-start(bf16[1024,768]{1,0:T(8,128)(2,1)} %pad_maximum_fusion.11), channel_id=1, source_target_pairs={{0,16},{16,0},{1,17},{17,1},{2,18},{18,2},{3,19},{19,3},{4,20},{20... | collective-permute-start | bytes 4718600 | tf_op jit(solution)/shard_map/ppermute | solution.py:928
  215.0 7.5 %copy-start.71 = (bf16[1024,256]{0,1:T(8,128)(2,1)}, bf16[1024,256]{0,1:T(8,128)(2,1)S(1)}, u32[]{:S(2)}) copy-start(bf16[1024,256]{0,1:T(8,128)(2,1)S(1)} %get-tuple-element.168) | copy-start | bytes 1572868
  215.0 7.5 %copy-start.73 = (bf16[1024,256]{0,1:T(8,128)(2,1)}, bf16[1024,256]{0,1:T(8,128)(2,1)S(1)}, u32[]{:S(2)}) copy-start(bf16[1024,256]{0,1:T(8,128)(2,1)S(1)} %get-tuple-element.169) | copy-start | bytes 1572868
  219.4 98.5 %collective-permute-start.5 = (bf16[1024,768]{1,0:T(8,128)(2,1)}, bf16[1024,768]{1,0:T(8,128)(2,1)}, u32[]{:S(2)}, u32[]{:S(2)}) collective-permute-start(bf16[1024,768]{1,0:T(8,128)(2,1)} %pad_maximum_fusion.12), channel_id=1, source_target_pairs={{0,16},{16,0},{1,17},{17,1},{2,18},{18,2},{3,19},{19,3},{4,20},{20... | collective-permute-start | bytes 4718600 | tf_op jit(solution)/shard_map/ppermute | solution.py:928
  227.7 3.5 copy-start.31
  232.7 17.5 %copy-start.32 = (bf16[2048,768]{1,0:T(8,128)(2,1)}, bf16[2048,768]{1,0:T(8,128)(2,1)S(1)}, u32[]{:S(2)}) copy-start(bf16[2048,768]{1,0:T(8,128)(2,1)S(1)} %constant_dynamic-update-slice_fusion.2) | copy-start | bytes 9437188
  239.1 5.1 copy-start.79
  250.2 3.4 copy-start.26
  253.6 64.3 %collective-permute-start.4 = (bf16[1024,768]{1,0:T(8,128)(2,1)}, bf16[1024,768]{1,0:T(8,128)(2,1)}, u32[]{:S(2)}, u32[]{:S(2)}) collective-permute-start(bf16[1024,768]{1,0:T(8,128)(2,1)} %collective-permute-done.3), channel_id=1, source_target_pairs={{0,4},{4,0},{8,12},{12,8},{1,5},{5,1},{9,13},{13,9},{2,6},{6,2},{1... | collective-permute-start | bytes 4718600 | tf_op jit(solution)/shard_map/ppermute | solution.py:1062
  273.0 34.5 %copy-start.77 = (bf16[1024,256]{0,1:T(8,128)(2,1)S(1)}, bf16[1024,256]{0,1:T(8,128)(2,1)}, u32[]{:S(2)}) copy-start(bf16[1024,256]{0,1:T(8,128)(2,1)} %copy-done.76) | copy-start | bytes 1572868
  273.0 44.9 %collective-permute-start.6 = (bf16[1024,768]{1,0:T(8,128)(2,1)}, bf16[1024,768]{1,0:T(8,128)(2,1)}, u32[]{:S(2)}, u32[]{:S(2)}) collective-permute-start(bf16[1024,768]{1,0:T(8,128)(2,1)} %pad_maximum_fusion.13), channel_id=1, source_target_pairs={{0,16},{16,0},{1,17},{17,1},{2,18},{18,2},{3,19},{19,3},{4,20},{20... | collective-permute-start | bytes 4718600 | tf_op jit(solution)/shard_map/ppermute | solution.py:928
  274.6 78.5 %collective-permute-start.7 = (bf16[1024,768]{1,0:T(8,128)(2,1)}, bf16[1024,768]{1,0:T(8,128)(2,1)}, u32[]{:S(2)}, u32[]{:S(2)}) collective-permute-start(bf16[1024,768]{1,0:T(8,128)(2,1)} %pad_maximum_fusion.14), channel_id=1, source_target_pairs={{0,16},{16,0},{1,17},{17,1},{2,18},{18,2},{3,19},{19,3},{4,20},{20... | collective-permute-start | bytes 4718600 | tf_op jit(solution)/shard_map/ppermute | solution.py:928
  307.5 3.4 copy-start.61
  317.9 2.9 copy-start.56
  320.9 6.8 %copy-start.10 = (bf16[1024,768]{1,0:T(8,128)(2,1)}, bf16[1024,768]{1,0:T(8,128)(2,1)S(1)}, u32[]{:S(2)}) copy-start(bf16[1024,768]{1,0:T(8,128)(2,1)S(1)} %fusion.3.refs_0_) | copy-start | bytes 4718596
  323.4 33.1 %copy-start.11 = (bf16[1024,768]{1,0:T(8,128)(2,1)}, bf16[1024,768]{1,0:T(8,128)(2,1)S(1)}, u32[]{:S(2)}) copy-start(bf16[1024,768]{1,0:T(8,128)(2,1)S(1)} %fusion.4.refs_1_) | copy-start | bytes 4718596
  323.4 6.2 %copy-start.65 = (bf16[1024,256]{1,0:T(8,128)(2,1)S(1)}, bf16[1024,256]{1,0:T(8,128)(2,1)}, u32[]{:S(2)}) copy-start(bf16[1024,256]{1,0:T(8,128)(2,1)} %get-tuple-element.152) | copy-start | bytes 1572868
  323.4 6.2 %copy-start.66 = (bf16[1024,256]{1,0:T(8,128)(2,1)S(1)}, bf16[1024,256]{1,0:T(8,128)(2,1)}, u32[]{:S(2)}) copy-start(bf16[1024,256]{1,0:T(8,128)(2,1)} %get-tuple-element.148) | copy-start | bytes 1572868
  324.1 5.5 copy-start.64
  325.3 41.5 %collective-permute-start.8 = (bf16[512,1024]{1,0:T(8,128)(2,1)}, bf16[512,1024]{1,0:T(8,128)(2,1)}, u32[]{:S(2)}, u32[]{:S(2)}) collective-permute-start(bf16[512,1024]{1,0:T(8,128)(2,1)} %slice.419), channel_id=1, source_target_pairs={{0,16},{16,0},{1,17},{17,1},{2,18},{18,2},{3,19},{19,3},{4,20},{20... | collective-permute-start | bytes 3145736 | tf_op jit(solution)/shard_map/ppermute | solution.py:928
  326.8 127.5 %collective-permute-start.9 = (bf16[1024,768]{1,0:T(8,128)(2,1)S(1)}, bf16[1024,768]{1,0:T(8,128)(2,1)}, u32[]{:S(2)}, u32[]{:S(2)}) collective-permute-start(bf16[1024,768]{1,0:T(8,128)(2,1)S(1)} %copy-done.52), channel_id=1, source_target_pairs={{0,16},{16,0},{1,17},{17,1},{2,18},{18,2},{3,19},{19,3},{4,20},{20... | collective-permute-start | bytes 4718600 | tf_op jit(solution)/shard_map/ppermute | solution.py:928
  327.6 126.7 %collective-permute-start.10 = (bf16[1024,768]{1,0:T(8,128)(2,1)S(1)}, bf16[1024,768]{1,0:T(8,128)(2,1)S(1)}, u32[]{:S(2)}, u32[]{:S(2)}) collective-permute-start(bf16[1024,768]{1,0:T(8,128)(2,1)S(1)} %fusion.3.refs_0_), channel_id=1, source_target_pairs={{0,4},{4,0},{8,12},{12,8},{1,5},{5,1},{9,13},{13,9},{2,6},{6,2},{1... | collective-permute-start | bytes 4718600 | tf_op jit(solution)/shard_map/ppermute | solution.py:1060
  337.2 3.0 copy-start.83
  337.3 3.7 copy-start.85
  337.3 3.7 copy-start.87
  342.5 10.6 %copy-start.41 = (f32[1024,512]{1,0:T(8,128)S(1)}, f32[1024,512]{1,0:T(8,128)}, u32[]{:S(2)}) copy-start(f32[1024,512]{1,0:T(8,128)} %fusion.53) | copy-start | bytes 6291460
  342.6 10.5 %copy-start.54 = (f32[1024,256]{1,0:T(8,128)S(1)}, f32[1024,256]{1,0:T(8,128)}, u32[]{:S(2)}) copy-start(f32[1024,256]{1,0:T(8,128)} %fusion.43) | copy-start | bytes 3145732
  353.2 3.4 copy-start.84
  355.2 11.6 %copy-start.12 = (bf16[1024,768]{1,0:T(8,128)(2,1)}, bf16[1024,768]{1,0:T(8,128)(2,1)S(1)}, u32[]{:S(2)}) copy-start(bf16[1024,768]{1,0:T(8,128)(2,1)S(1)} %fusion.5.refs_2_) | copy-start | bytes 4718596
  355.2 4.7 copy-start.86
  355.2 4.7 copy-start.88
  355.2 187.1 %collective-permute-start.11 = (bf16[1024,768]{1,0:T(8,128)(2,1)S(1)}, bf16[1024,768]{1,0:T(8,128)(2,1)}, u32[]{:S(2)}, u32[]{:S(2)}) collective-permute-start(bf16[1024,768]{1,0:T(8,128)(2,1)S(1)} %pad_maximum_fusion.16), channel_id=1, source_target_pairs={{0,16},{16,0},{1,17},{17,1},{2,18},{18,2},{3,19},{19,3},{4,20},{20... | collective-permute-start | bytes 4718600 | tf_op jit(solution)/shard_map/ppermute | solution.py:928
  356.5 185.7 %collective-permute-start.12 = (bf16[1024,768]{1,0:T(8,128)(2,1)S(1)}, bf16[1024,768]{1,0:T(8,128)(2,1)S(1)}, u32[]{:S(2)}, u32[]{:S(2)}) collective-permute-start(bf16[1024,768]{1,0:T(8,128)(2,1)S(1)} %fusion.4.refs_1_), channel_id=1, source_target_pairs={{0,4},{4,0},{8,12},{12,8},{1,5},{5,1},{9,13},{13,9},{2,6},{6,2},{1... | collective-permute-start | bytes 4718600 | tf_op jit(solution)/shard_map/ppermute | solution.py:1060
  359.9 8.9 %copy-start.59 = (f32[32,256]{1,0:T(8,128)S(1)}, f32[32,256]{1,0:T(8,128)}, u32[]{:S(2)}) copy-start(f32[32,256]{1,0:T(8,128)} %copy-done.58) | copy-start | bytes 98308
  359.9 8.9 %copy-start.75 = (f32[32,256]{1,0:T(8,128)S(1)}, f32[32,256]{1,0:T(8,128)}, u32[]{:S(2)}) copy-start(f32[32,256]{1,0:T(8,128)} %get-tuple-element.201) | copy-start | bytes 98308
  366.8 175.5 %collective-permute-start.13 = (bf16[1024,768]{1,0:T(8,128)(2,1)S(1)}, bf16[1024,768]{1,0:T(8,128)(2,1)S(1)}, u32[]{:S(2)}, u32[]{:S(2)}) collective-permute-start(bf16[1024,768]{1,0:T(8,128)(2,1)S(1)} %fusion.5.refs_2_), channel_id=1, source_target_pairs={{0,4},{4,0},{8,12},{12,8},{1,5},{5,1},{9,13},{13,9},{2,6},{6,2},{1... | collective-permute-start | bytes 4718600 | tf_op jit(solution)/shard_map/ppermute | solution.py:1060
  368.9 85.5 %copy-start.40 = (f32[1024,512]{1,0:T(8,128)S(1)}, f32[1024,512]{1,0:T(8,128)}, u32[]{:S(2)}) copy-start(f32[1024,512]{1,0:T(8,128)} %fusion.51) | copy-start | bytes 6291460
  368.9 85.5 %copy-start.53 = (f32[1024,256]{1,0:T(8,128)S(1)}, f32[1024,256]{1,0:T(8,128)}, u32[]{:S(2)}) copy-start(f32[1024,256]{1,0:T(8,128)} %fusion.41) | copy-start | bytes 3145732
  454.4 3.7 copy-start.13
  454.5 3.6 copy-start.9
  576.3 2.9 copy-start.45
  (43 other events, 76.8 us)

commit v5 on v4

--- a/solution.py
+++ b/solution.py
@@ -787,7 +787,14 @@
     )(term, *extras, *aside_inputs)
 
 
-def opening(cot_rows, groups, gains, mesh_shape, identity):
+def unit_places(place):
+    low = place % 2
+    part = ((place + 1) // 2) % 2
+    base = 2 + 3 * part
+    return [base, base + 1, base + 2, low, 1 - low], part
+
+
+def opening(cot_rows, groups, gains, hidden_weights, mesh_shape, identity):
     ctx_size, tp_size = mesh_shape
     block_rows, width = cot_rows.shape
     rows = block_rows // tp_size
@@ -803,15 +810,30 @@
         jax.ShapeDtypeStruct((2 * depth, sum(w.shape[1] for w in group)), BF16) for group in groups
     ]
 
+    unit = hidden_weights[0].shape[1] // 8
+    kinds = len(hidden_weights)
+
     def kernel(cot_ref, *refs):
         weight_refs = refs[: len(weights)]
         gain_ref = refs[len(weights)]
         refs = refs[len(weights) + 1 :]
+        hidden_refs = refs[:kinds]
+        refs = refs[kinds:]
         all_ref, gain_far_ref = refs[:2]
         whole_refs = refs[2 : 2 + len(groups)]
         refs = refs[2 + len(groups) :]
+        pack_refs = refs[:5]
+        refs = refs[5:]
         sems = refs[:7]
-        send, recv = refs[7:]
+        send, recv, pack_sems = refs[7:]
+        units, _ = unit_places(lax.axis_index("ctx"))
+        packs = [
+            pltpu.make_async_copy(
+                hidden_refs[k].at[:, pl.ds(pl.multiple_of(at * unit, unit), unit)],
+                pack_refs[c].at[:, pl.ds(k * unit, unit)], pack_sems.at[c * kinds + k],
+            )
+            for c, at in enumerate(units) for k in range(kinds)
+        ]
         enter(ctx_size, tp_size, along=True, side=True)
         far = {"fsdp": 1 - lax.axis_index("fsdp")}
         last = len(weights)
@@ -825,10 +847,14 @@
             )
         for swap in swaps:
             swap.start()
+        for pack in packs:
+            pack.start()
         for i, (g, at, wide) in enumerate(places):
             whole_refs[g][0:depth, at : at + wide] = weight_refs[i][...]
         mine = rows_at(cot_ref, lax.axis_index("tp") * rows, rows)
         gather_rows(mine, all_ref, ctx_size, tp_size, sems, block=cot_ref)
+        for pack in packs:
+            pack.wait()
         for swap in swaps:
             swap.wait()
 
@@ -838,18 +864,19 @@
             jax.ShapeDtypeStruct((ctx_size * block_rows, width), BF16),
             jax.ShapeDtypeStruct(gains.shape, F32),
             *wholes,
+            *[jax.ShapeDtypeStruct((depth, kinds * unit), BF16)] * 5,
         ),
-        in_specs=[VMEM_SPEC] * (2 + len(weights)),
-        out_specs=(HBM_SPEC,) + (VMEM_SPEC,) * (1 + len(groups)),
+        in_specs=[VMEM_SPEC] * (2 + len(weights)) + [HBM_SPEC] * kinds,
+        out_specs=(HBM_SPEC,) + (VMEM_SPEC,) * (6 + len(groups)),
         scratch_shapes=gather_sems(ctx_size, tp_size)
-        + [DMA((len(weights) + 1,)), DMA((len(weights) + 1,))],
+        + [DMA((len(weights) + 1,)), DMA((len(weights) + 1,)), DMA((5 * kinds,))],
         compiler_params=pltpu.CompilerParams(
             collective_id=identity, has_side_effects=True, vmem_limit_bytes=40 << 20
         ),
-    )(cot_rows, *weights, gains)
-
-
-def place_blocks(table, pieces, wide):
+    )(cot_rows, *weights, gains, *hidden_weights)
+
+
+def place_blocks(table, pieces, wide, blocks, base=None):
     count = len(pieces)
     depth = pieces[0][0].shape[0]
     tile = min(depth, 1024)
@@ -870,14 +897,36 @@
             in_specs=[
                 pl.BlockSpec((tile, wide), lambda i, step, table_ref, at=at: (i, at))
                 for _, at in pieces
-            ],
+            ]
+            + ([] if base is None else [HBM_SPEC]),
             out_specs=pl.BlockSpec((tile, wide), lambda i, step, table_ref: (i, table_ref[step])),
         ),
-        out_shape=jax.ShapeDtypeStruct((depth, count * wide), F32),
-        cost_estimate=pl.CostEstimate(
-            flops=0, bytes_accessed=depth * count * wide * 6, transcendentals=0
-        ),
-    )(table, *(array for array, _ in pieces))
+        out_shape=jax.ShapeDtypeStruct((depth, blocks * wide), F32),
+        input_output_aliases={} if base is None else {1 + count: 0},
+    )(table, *(array for array, _ in pieces), *(() if base is None else (base,)))
+
+
+def transposed_grads(slices, first, widths):
+    count, columns, depth = slices.shape
+    tile = min(depth, 256)
+
+    def kernel(in_ref, *out_refs):
+        head = jnp.concatenate([in_ref[z, 0:first, :] for z in range(count)], axis=0)
+        head = head.astype(F32).T
+        at = 0
+        for out_ref, wide in zip(out_refs[:-1], widths[:-1]):
+            out_ref[...] = head[:, at : at + wide]
+            at += wide
+        last = jnp.concatenate([in_ref[z, first:columns, :] for z in range(count)], axis=0)
+        out_refs[-1][...] = last.astype(F32).T
+
+    return pl.pallas_call(
+        kernel,
+        grid=(depth // tile,),
+        in_specs=[pl.BlockSpec((count, columns, tile), lambda i: (0, 0, i))],
+        out_specs=tuple(pl.BlockSpec((tile, wide), lambda i: (i, 0)) for wide in widths),
+        out_shape=tuple(jax.ShapeDtypeStruct((depth, wide), F32) for wide in widths),
+    )(slices)
 
 
 def mean_square(rows):
@@ -933,7 +982,7 @@
     ):
         side = lax.axis_index("fsdp")
         place = lax.axis_index("ctx")
-        part = (place ^ (place >> 1)) & 1
+        units, part = unit_places(place)
         row_count, model_width = inputs.shape[1:]
         half_width = model_width // 2
         query_width = w_query.shape[1]
@@ -953,28 +1002,14 @@
         gains = jnp.stack([attn_gain, ffn_gain]).astype(F32)
         residual_low = own_first(inputs[0])
         cot_low = own_first(cotangent[0])
-        rows_all, gains_far, qkv_weight, out_weight = opening(
+        rows_all, gains_far, qkv_weight, out_weight, *owns = opening(
             jnp.concatenate([cot_low, residual_low], axis=1),
             ((w_query, jnp.concatenate([key_projection, value_projection], axis=1)), (w_out,)),
-            gains, mesh_shape, 0,
+            gains, (w_gate, w_up, w_down), mesh_shape, 0,
         )
         cot_all = rows_all[:, :model_width]
-        residual_all = rows_all[:, model_width:].astype(F32)
         gains = jnp.concatenate([gains, gains_far], axis=1)
         gain_first, gain_second = gains[0], gains[1]
-        low = place & 1
-        base = 2 + 3 * part
-        units = [base, base + 1, base + 2, low, 1 - low]
-        def own_columns(weights, at):
-            return jnp.concatenate(
-                [lax.dynamic_slice_in_dim(w, at * unit, unit, 1) for w in weights], axis=1
-            )
-
-        ffn_weights = (w_gate, w_up, w_down)
-        ffn_weights, _ = lax.optimization_barrier((ffn_weights, qkv_weight))
-        owns = [own_columns(ffn_weights, units[0])]
-        ffn_weights, owns[0] = lax.optimization_barrier((ffn_weights, owns[0]))
-        owns += [own_columns(ffn_weights, at) for at in units[1:]]
         others = [swap_rows(owns[0]), swap_rows(owns[1]), None, None, None]
 
         cosine_lookup, sine_lookup = (table.T for table in rope_tables(row_start, row_count))
@@ -1024,8 +1059,11 @@
         def outer(sides_of, part_of):
             return [contract(part_of(rows), cols, 0, 0) for rows, cols in sides_of]
 
-        def summed(c):
-            near = jnp.concatenate(outer(sides[c], lambda rows: rows[:, :half_width]), axis=1)
+        def near_of(c):
+            return jnp.concatenate(outer(sides[c], lambda rows: rows[:, :half_width]), axis=1)
+
+        def summed(c, near=None):
+            near = near_of(c) if near is None else near
             return (near + received[c].astype(F32)).astype(BF16)
 
         def forward(c):
@@ -1059,43 +1097,69 @@
         def swap_ctx(total):
             return lax.ppermute(total, "ctx", swap_z)
 
-        others[4] = lax.ppermute(others[3], "ctx", swap_z)
         received = [swap_rows(fars[0]), swap_rows(fars[1])]
-        mid_low, fars[2], fars[3] = lax.optimization_barrier(
-            (mid_term.astype(BF16), fars[2], fars[3])
+        mid_low, fars[2], fars[3], received[0] = lax.optimization_barrier(
+            (mid_term.astype(BF16), fars[2], fars[3], received[0])
         )
         received.append(swap_rows(fars[2]))
+        totals = [summed(0)]
+        mid_low, totals[0] = lax.optimization_barrier((mid_low, totals[0]))
+        swapped = [swap_ctx(totals[0])]
         branch_low, grad_middle, gain_grad_second = reduce_gather(
             mid_low, (middle, cot_low, gain_second[None]), finish_grad_middle,
             (slice_shape, (1, model_width)), mesh_shape, 2, 2, False,
         )
-        branch_low, others[4], received[0], received[1], fars[3] = lax.optimization_barrier(
-            (branch_low, others[4], received[0], received[1], fars[3])
-        )
-        totals = [summed(0), summed(1)]
-        branch_low, totals = lax.optimization_barrier((branch_low, totals))
-        swapped = [swap_ctx(total) for total in totals]
+        branch_low, received[1], owns[4], swapped[0], rows_all = lax.optimization_barrier(
+            (branch_low, received[1], owns[4], swapped[0], rows_all)
+        )
+        others[4] = swap_rows(owns[4])
+        totals.append(summed(1))
+        branch_low, totals[1] = lax.optimization_barrier((branch_low, totals[1]))
+        swapped.append(swap_ctx(totals[1]))
         grad_out = jnp.dot(attended_flat, branch_low, preferred_element_type=F32)
-        grad_out_far = swap_rows(grad_out[:, half_width:].astype(BF16))
-        received.append(swap_rows(fars[3]))
-        forward(4)
+        grad_out_half = grad_out[:, half_width:].astype(BF16)
         grad_attended = contract(out_weight, branch_low, 0, 1).astype(BF16)
         grad_query_rot, grad_kv = attend_back(
             bounds, queries, by_place[:kv_heads], by_feature[:kv_heads], by_place[kv_heads:],
             grad_attended.reshape(query_heads, HEAD_SIZE, row_count), log_total,
         )
         grad_kv = grad_kv.reshape(2 * key_width, length_total)
-        grad_kv, fars[4], received[2] = lax.optimization_barrier((grad_kv, fars[4], received[2]))
+        far_base = 2 + 3 * (1 - part)
+        table = jnp.stack(units + [far_base, far_base + 1, far_base + 2])
+        grad_kv, received[2] = lax.optimization_barrier((grad_kv, received[2]))
         totals.append(summed(2))
-        grad_kv, totals[2] = lax.optimization_barrier((grad_kv, totals[2]))
+        grad_kv, totals[2], others[4], fars[3], grad_out_half = lax.optimization_barrier(
+            (grad_kv, totals[2], others[4], fars[3], grad_out_half)
+        )
         swapped.append(swap_ctx(totals[2]))
+        grad_out_far = swap_rows(grad_out_half)
+        received.append(swap_rows(fars[3]))
+        forward(4)
+        near_four = near_of(4)
+        early = totals + swapped[:1]
+        placed = [
+            place_blocks(
+                jnp.stack([table[0], table[1], table[2], table[5]]),
+                [(piece, block) for piece in early], unit, 8,
+            )
+            for block in range(3)
+        ]
+        near_three = near_of(3)
+        residual_all = rows_all[:, model_width:].astype(F32)
+        rms_all = lax.rsqrt(jnp.mean(residual_all * residual_all, axis=-1, keepdims=True) + EPSILON)
+        norm_all = (residual_all * rms_all * gain_first).astype(BF16)
+        grad_kv, placed, near_three, near_four, norm_all, fars[4], swapped[1] = (
+            lax.optimization_barrier(
+                (grad_kv, placed, near_three, near_four, norm_all, fars[4], swapped[1])
+            )
+        )
         received.append(swap_rows(fars[4]))
         output_rows, grad_kv = reduce_gather(
             ffn_term.astype(BF16), (middle,), finish_output, (), mesh_shape, 3, 2, False,
             KvSum(grad_kv, ctx_size),
         )
-        output_rows, grad_kv, grad_out_far, received[3], swapped[0] = lax.optimization_barrier(
-            (output_rows, grad_kv, grad_out_far, received[3], swapped[0])
+        output_rows, grad_kv, swapped[2] = lax.optimization_barrier(
+            (output_rows, grad_kv, swapped[2])
         )
         grad_query_pre = apply_rotary(
             grad_query_rot, cosine_lookup, sine_lookup, -1.0
@@ -1110,40 +1174,36 @@
         pre_slabs = grad_qkv_pre.reshape(ctx_size, attn_width // ctx_size, row_count)
         normed_term = contract(grad_qkv_pre, qkv_weight, 0, 1).astype(BF16)
         grad_out_rows = (grad_out[:, :half_width] + grad_out_far.astype(F32)).astype(BF16)
-        totals.append(summed(3))
+        normed_term, received[3], grad_out_far = lax.optimization_barrier(
+            (normed_term, received[3], grad_out_far)
+        )
+        totals.append(summed(3, near_three))
         normed_term, totals[3] = lax.optimization_barrier((normed_term, totals[3]))
-        rms_all = lax.rsqrt(jnp.mean(residual_all * residual_all, axis=-1, keepdims=True) + EPSILON)
-        norm_all = (residual_all * rms_all * gain_first).astype(BF16)
         input_rows, _, grad_attn, gain_grads = reduce_gather(
             normed_term,
             (grad_middle, residual_low, gain_first[None]), finish_grad_input,
             ((1, model_width),), mesh_shape, 4, 1, False,
             AttnTail(pre_slabs, norm_all, gain_grad_second, grad_out_rows, mesh_shape),
         )
-        grad_attn, received[4], swapped[1], swapped[2] = lax.optimization_barrier(
-            (grad_attn, received[4], swapped[1], swapped[2])
-        )
-        grad_attn = grad_attn.reshape(ctx_size, -1, half_width)
-        part_width = attn_width // ctx_size
-        grad_out = grad_attn[:, part_width:].reshape(query_width, half_width).T.astype(F32)
-        grad_attn = grad_attn[:, :part_width].reshape(attn_width, half_width).T.astype(F32)
-
-        totals.append(summed(4))
-        far_base = 2 + 3 * (1 - part)
-        table = jnp.stack(units + [far_base, far_base + 1, far_base + 2])
+        grad_attn, received[4] = lax.optimization_barrier((grad_attn, received[4]))
+        grad_query, grad_key, grad_value, grad_out = transposed_grads(
+            grad_attn.reshape(ctx_size, -1, half_width), attn_width // ctx_size,
+            (query_width, key_width, key_width, query_width),
+        )
+        totals.append(summed(4, near_four))
 
         def result(block):
-            return place_blocks(table, [(piece, block) for piece in totals + swapped], unit)
-
-        end_key = query_width + key_width
-        end_value = end_key + key_width
+            pieces = [(piece, block) for piece in totals[3:] + swapped[1:]]
+            late = jnp.stack([table[3], table[4], table[6], table[7]])
+            return place_blocks(late, pieces, unit, 8, placed[block])
+
         return (
             own_first(output_rows)[None],
             own_first(input_rows)[None],
             gain_grads[0],
-            grad_attn[:, :query_width],
-            grad_attn[:, query_width:end_key],
-            grad_attn[:, end_key:end_value],
+            grad_query,
+            grad_key,
+            grad_value,
             grad_out,
             gain_grads[1],
             result(0),

time: 594 us -> 539 us (0.907)
  Pallas kernels: 344 us -> 311 us
  local copies, waits for them, and re-layouts: 55.3 us -> 30.4 us
  waiting for transfers between devices: 4.27 us -> 27 us
  other arithmetic: 49.6 us -> 38.9 us
  matrix products: 100 us -> 91.9 us
    pallas_call x4, Pallas kernels: 243 us -> 194 us  [reduce_gather(): pl.pallas_call(kernel, out_shape=(jax.ShapeDtypeStruct((reach * block_row...]
    ppermute x10 -> x11, waiting for transfers between devices: 4.26 us -> 27 us  [swap_rows(): return lax.ppermute(array, 'fsdp', swap_x)]
    concatenate x5 -> x2, other arithmetic: 16.5 us -> 3.77 us  [near_of(): jnp.concatenate(outer(sides[c], lambda rows: rows[:, :half_width]), axis=1)]
    dot_general x32, matrix products: 69.5 us -> 58 us  [contract(): lax.dot_general(left, right, (((left_dim,), (right_dim,)), ((), ())), pre...]
    unnamed x188 -> x153, local copies, waits for them, and re-layouts: 25.5 us -> 14.5 us
    dynamic_slice x6 -> x0, local copies, waits for them, and re-layouts: 8.72 us -> none  [own_columns(): lax.dynamic_slice_in_dim(w, at * unit, unit, 1)]
    pallas_call x3 -> x6, Pallas kernels: 22.4 us -> 28.6 us  [place_blocks(): pl.pallas_call(kernel, grid_spec=pltpu.PrefetchScalarGridSpec(num_scalar_...]
    ppermute x10 -> x11, starting transfers between devices: 10.4 us -> 12 us  [swap_rows(): return lax.ppermute(array, 'fsdp', swap_x)]
  transfers between devices with their start and end apart: 14 -> 14, of which waited for: 1 -> 3; matrix products, arithmetic and copies ran while one was open for 28% -> 26% of each run, Pallas kernels for 44% -> 42%
where the time goes in v5:
time: 539 us; the launch traced here: 532 us
  Pallas kernels  311 us (58%)
  matrix products  91.9 us (17%)
  other arithmetic  38.9 us (7%)
  local copies, waits for them, and re-layouts  30.4 us (6%)
  waiting for transfers between devices  27 us (5%)
  starting transfers between devices  15.1 us (3%)
  blocking collectives  15 us (3%)
    pallas_call x4, Pallas kernels, reduce_gather(): pl.pallas_call(kernel, out_shape=(jax.ShapeDtypeStruct((reach * block_row...  194 us
    pallas_call x1, Pallas kernels, opening(): pl.pallas_call(kernel, out_shape=(jax.ShapeDtypeStruct((ctx_size * block_...  66.3 us
    dot_general x32, matrix products, contract(): lax.dot_general(left, right, (((left_dim,), (right_dim,)), ((), ())), pre...  58 us
    pallas_call x6, Pallas kernels, place_blocks(): pl.pallas_call(kernel, grid_spec=pltpu.PrefetchScalarGridSpec(num_scalar_...  28.6 us
    ppermute x11, waiting for transfers between devices, swap_rows(): return lax.ppermute(array, 'fsdp', swap_x)  27 us
    dot_general x5, matrix products, forward(): both = jnp.dot(normed_all, pair_w, preferred_element_type=F32)  17.8 us
    dot_general x5, matrix products, forward(): grad_hidden = jnp.dot(cot_all, down_w, preferred_element_type=F32)  15.3 us
    all_gather x1, blocking collectives, local(): lax.all_gather(kv_own.reshape(2 * key_width, row_count).T, 'ctx', axis=0,...  15 us
  transfers between devices with their start and end apart: 14, of which 3 were waited for; matrix products, arithmetic and copies ran while one was open for 26% of the time, Pallas kernels for 42%

profile of v5, /device:TPU:0, one launch (start us, length us, event | category | flops | bytes accessed | tf_op | source)
XLA Modules:
  0.0 532.5 jit_solution(5503981888627115909)
XLA Ops:
  3.1 1.7 dynamic-slice_bitcast_fusion.1
  5.8 1.5 pad_maximum_fusion.2.cot_ref
  7.3 66.3 %shard_map.203 = (bf16[1024,4096]{1,0:T(8,128)(2,1)}, f32[2,1024]{1,0:T(2,128)S(1)}, bf16[2048,768]{1,0:T(8,128)(2,1)}, bf16[2048,512]{1,0:T(8,128)(2,1)S(1)}, b...) custom-call(bf16[256,4096]{1,0:T(8,128)(2,1)} %pad_maximum_fusion.2., ...), custom_call_target="tpu_custom_call" | custom-call | tf_op jit(solution)/shard_map/pallas_call | solution.py:861
  74.2 1.5 collective-permute-start.1
  76.1 3.0 fusion.67
  80.9 15.0 %all_gather.3 = bf16[1024,256]{0,1:T(8,128)(2,1)S(1)} all-gather(bf16[256,256]{0,1:T(8,128)(2,1)S(1)} %bitcast.88), channel_id=1, replica_groups=mesh['fsdp'=2,'ctx'=4,'tp'=4] {'ctx'}, dimensions={0}, use_global_device_ids=true | all-gather | bytes 655360 | tf_op jit(solution)/shard_map/all_gather | solution.py:1030
  97.2 2.1 fusion.118
  101.4 7.7 %shard_map.204 = (bf16[8,64,256]{2,1,0:T(8,128)(2,1)S(1)}, f32[8,1,256]{2,1,0:T(1,128)S(1)}) custom-call(s32[2]{0:T(128)S(1)} %pad_add_fusion.bounds_ref, bf16[8,64,256]{2,1,0:T(8,128)(2,1)S(1)} %pad_maximum_fusion.27.query_ref, bf16[2,1024,64]{2,1,0:T(8,128)(2,1)S(1)} %get-tuple-element.183.key_ref, bf16[2,64,1024]{2,1,0:T(8,128)(2,1)S(1)} %bitcast.71), custom_call_target="tpu_custom_call" | custom-call | tf_op jit(solution)/shard_map/pallas_call | solution.py:72
  110.2 1.6 constant_dynamic-update-slice_fusion.3
  111.8 1.6 constant_dynamic-update-slice_fusion.1
  116.1 1.5 constant_dynamic-update-slice_fusion
  117.6 44.1 %shard_map.205 = (bf16[1024,2048]{1,0:T(8,128)(2,1)S(1)}, f32[64,2048]{1,0:T(8,128)S(1)}) custom-call(bf16[256,2048]{1,0:T(8,128)(2,1)S(1)} %convolution_convert_fusion.term_ref, bf16[256,2048]{1,0:T(8,128)(2,1)S(1)} %pad_maximum_fusion.12.refs_0_.refs_1_, f32[1,2048]{1,0:T(1,128)S(1)} %get-tuple-element.198.refs_1_.refs_2_), custom_call_target="tpu_custom_call" | custom-call | tf_op jit(solution)/shard_map/pallas_call | solution.py:773
  161.7 2.4 fusion.35
  165.4 1.7 multiply_convert_fusion.13
  172.4 1.4 collective-permute-start.3
  173.8 1.7 fusion.45
  175.5 2.7 fusion.55
  178.2 1.5 constant_dynamic-update-slice_fusion.2
  179.7 3.7 fusion.31
  183.5 3.5 multiply_convert_fusion.10
  187.7 1.7 fusion.43
  190.8 2.6 fusion.53
  201.4 3.8 fusion.27
  205.1 4.9 multiply_convert_fusion.7
  210.0 2.9 convolution_convert_fusion.9
  215.5 3.6 fusion.41
  220.4 5.5 %fusion.23 = f32[1024,512]{0,1:T(8,128)} fusion(bf16[1024,2048]{1,0:T(8,128)(2,1)S(1)} %get-tuple-element.94, bf16[2048,768]{1,0:T(8,128)(2,1)} %constant_dynamic-update-slice_fusion.6), kind=kOutput, calls=%fused_computation.41 | convolution fusion | flops 2147483648 | bytes 8388608 | tf_op jit(solution)/shard_map/dot_general | solution.py:1072
  225.8 3.6 multiply_convert_fusion.3
  232.8 2.6 fusion.49
  235.4 3.5 fusion.25
  239.0 4.5 add_convert_fusion.term_ref
  244.1 1.9 fusion.3.refs_0_
  248.2 2.4 fusion.39
  250.6 1.6 collective-permute-start.7
  252.2 2.0 fusion.75
  254.2 2.3 add_convert_fusion.1.term_ref
  256.5 1.9 pad_maximum_fusion
  258.4 35.8 %shard_map.206 = (bf16[256,2048]{1,0:T(8,128)(2,1)S(1)}, f32[64,2048]{1,0:T(8,128)S(1)}, f32[1,2048]{1,0:T(1,128)S(1)}) custom-call(bf16[512,2048]{1,0:T(8,128)(2,1)S(1)} %add_convert_fusion.term_ref, f32[64,2048]{1,0:T(8,128)S(1)} %get-tuple-element.105.refs_0_, bf16[256,2048]{1,0:T(8,128)(2,1)S(1)} %pad_maximum_fusion.13.refs_1_, ...), custom_call_target="tpu_custom_call" | custom-call | tf_op jit(solution)/shard_map/pallas_call | solution.py:773
  296.2 3.2 fusion.4.refs_1_
  299.5 1.6 collective-permute-start.8
  301.8 9.8 %shard_map.207 = (f32[8,64,256]{2,1,0:T(8,128)S(1)}, bf16[4,64,1024]{2,1,0:T(8,128)(2,1)S(1)}) custom-call(s32[2]{0:T(128)S(1)} %pad_add_fusion.bounds_ref, bf16[8,64,256]{2,1,0:T(8,128)(2,1)S(1)} %pad_maximum_fusion.27.query_ref, bf16[2,1024,64]{2,1,0:T(8,128)(2,1)S(1)} %get-tuple-element.183.key_ref, bf16[2,64,1024]{2,1,0:T(8,128)(2,1)S(1)} %bitcast.70, ...), custom_call_target="tpu_custom_call" | custom-call | tf_op jit(solution)/shard_map/pallas_call | solution.py:112
  312.5 4.7 collective-permute-done.7
  318.3 1.6 collective-permute-start.9
  321.6 3.1 fusion.5.refs_2_
  324.7 2.7 fusion.2.refs_4_
  327.5 21.7 %collective-permute-done.8 = bf16[1024,768]{1,0:T(8,128)(2,1)S(1)} collective-permute-done((bf16[1024,768]{1,0:T(8,128)(2,1)S(1)}, bf16[1024,768]{1,0:T(8,128)(2,1)S(1)}, u32[]{:S(2)}, u32[]{:S(2)}) %collective-permute-start.8) | collective-permute-done | bytes 1572896 | tf_op jit(solution)/shard_map/ppermute | solution.py:977
  349.3 2.4 fusion.20
  351.7 1.7 multiply_convert_fusion.2
  355.9 1.8 fusion.37
  361.0 4.7 shard_map.208.refs_4_
  365.7 4.7 shard_map.209.refs_4_
  370.4 5.0 shard_map.210.refs_4_
  375.5 3.1 fusion.47
  378.6 1.9 pad_maximum_fusion.1
  381.6 33.8 %shard_map.211 = (bf16[256,2048]{1,0:T(8,128)(2,1)S(1)}, f32[256,256]{1,0:T(8,128)S(1)}) custom-call(bf16[512,2048]{1,0:T(8,128)(2,1)S(1)} %add_convert_fusion.1.term_ref, f32[64,2048]{1,0:T(8,128)S(1)} %get-tuple-element.105.refs_0_, bf16[256,1024]{1,0:T(8,128)(2,1)S(1)} %bitcast.72), custom_call_target="tpu_custom_call" | custom-call | tf_op jit(solution)/shard_map/pallas_call | solution.py:773
  415.4 1.7 fusion.19.refs_6_
  419.2 3.1 add_convert_fusion.3.refs_0_
  422.3 80.3 %shard_map.212 = (bf16[256,2048]{1,0:T(8,128)(2,1)S(1)}, f32[1,2048]{1,0:T(1,128)}, bf16[1280,1024]{1,0:T(8,128)(2,1)S(1)}, f32[2,1024]{1,0:T(2,128)S(1)}) custom-call(bf16[256,2048]{1,0:T(8,128)(2,1)S(1)} %convolution_convert_fusion.1.term_ref, f32[64,2048]{1,0:T(8,128)S(1)} %copy-done.16, bf16[256,2048]{1,0:T(8,128)(2,1)S(1)} %copy-done.2, ...), custom_call_target="tpu_custom_call" | custom-call | tf_op jit(solution)/shard_map/pallas_call | solution.py:773
  502.6 1.5 copy-done.3
  508.1 4.8 shard_map.213
  512.8 2.9 add_convert_fusion.2.refs_1_
  515.7 4.7 shard_map.214
  520.4 4.7 shard_map.215
  525.1 4.8 shard_map.216
  (239 shorter events, 60.6 us)
Async XLA Ops:
  4.9 71.2 %copy-start.26 = (bf16[256,1024]{1,0:T(8,128)(2,1)}, bf16[256,1024]{1,0:T(8,128)(2,1)S(1)}, u32[]{:S(2)}) copy-start(bf16[256,1024]{1,0:T(8,128)(2,1)S(1)} %get-tuple-element.187) | copy-start | bytes 1572868
  73.6 5.5 %copy-start.7 = (bf16[1024,768]{1,0:T(8,128)(2,1)}, bf16[1024,768]{1,0:T(8,128)(2,1)S(1)}, u32[]{:S(2)}) copy-start(bf16[1024,768]{1,0:T(8,128)(2,1)S(1)} %get-tuple-element.123) | copy-start | bytes 4718596
  73.6 5.5 %copy-start.9 = (bf16[1024,768]{1,0:T(8,128)(2,1)}, bf16[1024,768]{1,0:T(8,128)(2,1)S(1)}, u32[]{:S(2)}) copy-start(bf16[1024,768]{1,0:T(8,128)(2,1)S(1)} %get-tuple-element.103) | copy-start | bytes 4718596
  73.6 5.5 %copy-start.11 = (bf16[1024,768]{1,0:T(8,128)(2,1)}, bf16[1024,768]{1,0:T(8,128)(2,1)S(1)}, u32[]{:S(2)}) copy-start(bf16[1024,768]{1,0:T(8,128)(2,1)S(1)} %get-tuple-element.101) | copy-start | bytes 4718596
  73.6 40.0 %copy-start.4 = (bf16[2048,512]{1,0:T(8,128)(2,1)}, bf16[2048,512]{1,0:T(8,128)(2,1)S(1)}, u32[]{:S(2)}) copy-start(bf16[2048,512]{1,0:T(8,128)(2,1)S(1)} %get-tuple-element.90) | copy-start | bytes 6291460
  73.6 40.8 %collective-permute-start = (bf16[1024,768]{1,0:T(8,128)(2,1)}, bf16[1024,768]{1,0:T(8,128)(2,1)}, u32[]{:S(2)}, u32[]{:S(2)}) collective-permute-start(bf16[1024,768]{1,0:T(8,128)(2,1)} %get-tuple-element.92), channel_id=1, source_target_pairs={{0,16},{16,0},{1,17},{17,1},{2,18},{18,2},{3,19},{19,3},{4,20},{20... | collective-permute-start | bytes 4718600 | tf_op jit(solution)/shard_map/ppermute | solution.py:977
  74.2 96.3 %collective-permute-start.1 = (bf16[1024,768]{1,0:T(8,128)(2,1)}, bf16[1024,768]{1,0:T(8,128)(2,1)}, u32[]{:S(2)}, u32[]{:S(2)}) collective-permute-start(bf16[1024,768]{1,0:T(8,128)(2,1)} %get-tuple-element.96), channel_id=1, source_target_pairs={{0,16},{16,0},{1,17},{17,1},{2,18},{18,2},{3,19},{19,3},{4,20},{20... | collective-permute-start | bytes 4718600 | tf_op jit(solution)/shard_map/ppermute | solution.py:977
  110.2 3.2 copy-start.27
  113.6 4.0 copy-start.1
  115.5 85.8 %collective-permute-start.2 = (bf16[1024,768]{1,0:T(8,128)(2,1)S(1)}, bf16[1024,768]{1,0:T(8,128)(2,1)S(1)}, u32[]{:S(2)}, u32[]{:S(2)}) collective-permute-start(bf16[1024,768]{1,0:T(8,128)(2,1)S(1)} %copy-done.12), channel_id=1, source_target_pairs={{0,16},{16,0},{1,17},{17,1},{2,18},{18,2},{3,19},{19,3},{4,20},{20... | collective-permute-start | bytes 4718600 | tf_op jit(solution)/shard_map/ppermute | solution.py:977
  117.6 77.8 %copy-start.32 = (bf16[2048,768]{1,0:T(8,128)(2,1)}, bf16[2048,768]{1,0:T(8,128)(2,1)S(1)}, u32[]{:S(2)}) copy-start(bf16[2048,768]{1,0:T(8,128)(2,1)S(1)} %constant_dynamic-update-slice_fusion) | copy-start | bytes 9437188
  117.6 46.6 %slice-start = ((s8[8388608]{0:T(1024)(128)(4,1)}), s8[4194304]{0:T(1024)(128)(4,1)S(1)}, s32[]{:S(2)}) async-start(s8[8388608]{0:T(1024)(128)(4,1)} %bitcast.76), calls=%async_computation | async-start | bytes 8388608
  161.7 196.8 %copy-start.19 = (bf16[1024,2048]{1,0:T(8,128)(2,1)}, bf16[1024,2048]{1,0:T(8,128)(2,1)S(1)}, u32[]{:S(2)}) copy-start(bf16[1024,2048]{1,0:T(8,128)(2,1)S(1)} %get-tuple-element.94) | copy-start | bytes 12582916
  161.7 3.7 slice-start.1
  172.4 46.7 %collective-permute-start.3 = (bf16[1024,768]{1,0:T(8,128)(2,1)S(1)}, bf16[1024,768]{1,0:T(8,128)(2,1)S(1)}, u32[]{:S(2)}, u32[]{:S(2)}) collective-permute-start(bf16[1024,768]{1,0:T(8,128)(2,1)S(1)} %copy-done.10), channel_id=1, source_target_pairs={{0,16},{16,0},{1,17},{17,1},{2,18},{18,2},{3,19},{19,3},{4,20},{20... | collective-permute-start | bytes 4718600 | tf_op jit(solution)/shard_map/ppermute | solution.py:977
  179.7 16.4 %copy-start.30 = (bf16[2048,768]{1,0:T(8,128)(2,1)}, bf16[2048,768]{1,0:T(8,128)(2,1)S(1)}, u32[]{:S(2)}) copy-start(bf16[2048,768]{1,0:T(8,128)(2,1)S(1)} %constant_dynamic-update-slice_fusion.2) | copy-start | bytes 9437188
  193.4 50.7 %collective-permute-start.4 = (bf16[1024,768]{1,0:T(8,128)(2,1)}, bf16[1024,768]{1,0:T(8,128)(2,1)}, u32[]{:S(2)}, u32[]{:S(2)}) collective-permute-start(bf16[1024,768]{1,0:T(8,128)(2,1)} %pad_maximum_fusion.3), channel_id=1, source_target_pairs={{0,16},{16,0},{1,17},{17,1},{2,18},{18,2},{3,19},{19,3},{4,20},{20... | collective-permute-start | bytes 4718600 | tf_op jit(solution)/shard_map/ppermute | solution.py:977
  201.3 3.8 copy-start.28
  210.0 2.9 copy-start.54
  210.0 2.9 copy-start.57
  210.0 5.5 %copy-start.62 = (bf16[1024,256]{0,1:T(8,128)(2,1)}, bf16[1024,256]{0,1:T(8,128)(2,1)S(1)}, u32[]{:S(2)}) copy-start(bf16[1024,256]{0,1:T(8,128)(2,1)S(1)} %get-tuple-element.175) | copy-start | bytes 1572868
  215.5 10.3 %slice-start.2 = ((s8[8388608]{0:T(1024)(128)(4,1)}), s8[4194304]{0:T(1024)(128)(4,1)S(1)}, s32[]{:S(2)}) async-start(s8[8388608]{0:T(1024)(128)(4,1)} %bitcast.78), calls=%async_computation.2 | async-start | bytes 8388608
  220.4 5.5 %slice-start.3 = ((s8[8388608]{0:T(1024)(128)(4,1)}), s8[4194304]{0:T(1024)(128)(4,1)S(1)}, s32[]{:S(2)}) async-start(s8[8388608]{0:T(1024)(128)(4,1)} %bitcast.78), calls=%async_computation.3 | async-start | bytes 8388608
  232.8 2.6 copy-start.29
  232.8 2.6 copy-start.55
  232.8 2.6 copy-start.58
  239.0 5.2 copy-start.40
  239.0 5.2 copy-start.52
  243.5 2.5 copy-start.46
  243.5 4.7 copy-start.61
  246.0 4.6 copy-start.20
  246.0 6.1 %copy-start.63 = (bf16[1024,256]{0,1:T(8,128)(2,1)S(1)}, bf16[1024,256]{0,1:T(8,128)(2,1)}, u32[]{:S(2)}) copy-start(bf16[1024,256]{0,1:T(8,128)(2,1)} %copy-done.62) | copy-start | bytes 1572868
  246.1 49.5 %collective-permute-start.5 = (bf16[1024,768]{1,0:T(8,128)(2,1)S(1)}, bf16[1024,768]{1,0:T(8,128)(2,1)}, u32[]{:S(2)}, u32[]{:S(2)}) collective-permute-start(bf16[1024,768]{1,0:T(8,128)(2,1)S(1)} %copy-done.46), channel_id=1, source_target_pairs={{0,16},{16,0},{1,17},{17,1},{2,18},{18,2},{3,19},{19,3},{4,20},{20... | collective-permute-start | bytes 4718600 | tf_op jit(solution)/shard_map/ppermute | solution.py:977
  247.0 48.5 %collective-permute-start.6 = (bf16[1024,768]{1,0:T(8,128)(2,1)S(1)}, bf16[1024,768]{1,0:T(8,128)(2,1)S(1)}, u32[]{:S(2)}, u32[]{:S(2)}) collective-permute-start(bf16[1024,768]{1,0:T(8,128)(2,1)S(1)} %fusion.3.refs_0_), channel_id=1, source_target_pairs={{0,4},{4,0},{8,12},{12,8},{1,5},{5,1},{9,13},{13,9},{2,6},{6,2},{1... | collective-permute-start | bytes 4718600 | tf_op jit(solution)/shard_map/ppermute | solution.py:1098
  250.6 66.6 %collective-permute-start.7 = (bf16[1024,768]{1,0:T(8,128)(2,1)}, bf16[1024,768]{1,0:T(8,128)(2,1)}, u32[]{:S(2)}, u32[]{:S(2)}) collective-permute-start(bf16[1024,768]{1,0:T(8,128)(2,1)} %pad_maximum_fusion.5), channel_id=1, source_target_pairs={{0,16},{16,0},{1,17},{17,1},{2,18},{18,2},{3,19},{19,3},{4,20},{20... | collective-permute-start | bytes 4718600 | tf_op jit(solution)/shard_map/ppermute | solution.py:977
  258.4 35.8 %copy-start.56 = (bf16[1024,256]{0,1:T(8,128)(2,1)S(1)}, bf16[1024,256]{0,1:T(8,128)(2,1)}, u32[]{:S(2)}) copy-start(bf16[1024,256]{0,1:T(8,128)(2,1)} %copy-done.54) | copy-start | bytes 1572868
  258.4 35.8 %copy-start.59 = (bf16[1024,256]{0,1:T(8,128)(2,1)S(1)}, bf16[1024,256]{0,1:T(8,128)(2,1)}, u32[]{:S(2)}) copy-start(bf16[1024,256]{0,1:T(8,128)(2,1)} %copy-done.57) | copy-start | bytes 1572868
  295.5 3.9 copy-start.23
  296.2 3.3 copy-start.8
  296.2 4.8 copy-start.5
  299.5 49.7 %collective-permute-start.8 = (bf16[1024,768]{1,0:T(8,128)(2,1)S(1)}, bf16[1024,768]{1,0:T(8,128)(2,1)S(1)}, u32[]{:S(2)}, u32[]{:S(2)}) collective-permute-start(bf16[1024,768]{1,0:T(8,128)(2,1)S(1)} %copy-done.8), channel_id=1, source_target_pairs={{0,16},{16,0},{1,17},{17,1},{2,18},{18,2},{3,19},{19,3},{4,20},{20... | collective-permute-start | bytes 4718600 | tf_op jit(solution)/shard_map/ppermute | solution.py:977
  301.8 18.9 %slice-start.4 = ((s8[8388608]{0:T(1024)(128)(4,1)}), s8[4194304]{0:T(1024)(128)(4,1)S(1)}, s32[]{:S(2)}) async-start(s8[8388608]{0:T(1024)(128)(4,1)} %bitcast.80), calls=%async_computation.4 | async-start | bytes 8388608
  311.8 8.9 %slice-start.5 = ((s8[8388608]{0:T(1024)(128)(4,1)}), s8[4194304]{0:T(1024)(128)(4,1)S(1)}, s32[]{:S(2)}) async-start(s8[8388608]{0:T(1024)(128)(4,1)} %bitcast.80), calls=%async_computation.5 | async-start | bytes 8388608
  312.5 9.1 %copy-start.21 = (f32[512,2048]{1,0:T(8,128)}, f32[512,2048]{1,0:T(8,128)S(1)}, u32[]{:S(2)}) copy-start(f32[512,2048]{1,0:T(8,128)S(1)} %fusion.121) | copy-start | bytes 12582916
  318.3 3.3 copy-start.50
  318.3 62.1 %collective-permute-start.9 = (bf16[1024,768]{1,0:T(8,128)(2,1)}, bf16[1024,768]{1,0:T(8,128)(2,1)}, u32[]{:S(2)}, u32[]{:S(2)}) collective-permute-start(bf16[1024,768]{1,0:T(8,128)(2,1)} %fusion.4.refs_1_), channel_id=1, source_target_pairs={{0,4},{4,0},{8,12},{12,8},{1,5},{5,1},{9,13},{13,9},{2,6},{6,2},{1... | collective-permute-start | bytes 4718600 | tf_op jit(solution)/shard_map/ppermute | solution.py:1098
  353.4 5.0 copy-start.65
  353.4 5.0 copy-start.67
  353.4 63.7 %collective-permute-start.10 = (bf16[1024,768]{1,0:T(8,128)(2,1)}, bf16[1024,768]{1,0:T(8,128)(2,1)}, u32[]{:S(2)}, u32[]{:S(2)}) collective-permute-start(bf16[1024,768]{1,0:T(8,128)(2,1)} %fusion.5.refs_2_), channel_id=1, source_target_pairs={{0,4},{4,0},{8,12},{12,8},{1,5},{5,1},{9,13},{13,9},{2,6},{6,2},{1... | collective-permute-start | bytes 4718600 | tf_op jit(solution)/shard_map/ppermute | solution.py:1098
  353.9 64.9 %collective-permute-start.11 = (bf16[1024,768]{1,0:T(8,128)(2,1)}, bf16[1024,768]{1,0:T(8,128)(2,1)}, u32[]{:S(2)}, u32[]{:S(2)}) collective-permute-start(bf16[1024,768]{1,0:T(8,128)(2,1)} %pad_maximum_fusion.6), channel_id=1, source_target_pairs={{0,16},{16,0},{1,17},{17,1},{2,18},{18,2},{3,19},{19,3},{4,20},{20... | collective-permute-start | bytes 4718600 | tf_op jit(solution)/shard_map/ppermute | solution.py:977
  355.0 60.4 %collective-permute-start.12 = (bf16[512,1024]{1,0:T(8,128)(2,1)}, bf16[512,1024]{1,0:T(8,128)(2,1)}, u32[]{:S(2)}, u32[]{:S(2)}) collective-permute-start(bf16[512,1024]{1,0:T(8,128)(2,1)} %slice.405), channel_id=1, source_target_pairs={{0,16},{16,0},{1,17},{17,1},{2,18},{18,2},{3,19},{19,3},{4,20},{20... | collective-permute-start | bytes 3145736 | tf_op jit(solution)/shard_map/ppermute | solution.py:977
  370.4 5.0 copy-start.66
  375.4 3.1 copy-start.53
  378.5 3.0 copy-start.18
  378.6 36.8 %copy-start.22 = (f32[512,2048]{1,0:T(8,128)S(1)}, f32[512,2048]{1,0:T(8,128)}, u32[]{:S(2)}) copy-start(f32[512,2048]{1,0:T(8,128)} %copy-done.21) | copy-start | bytes 12582916
  380.4 126.5 %collective-permute-start.13 = (bf16[1024,768]{1,0:T(8,128)(2,1)S(1)}, bf16[1024,768]{1,0:T(8,128)(2,1)S(1)}, u32[]{:S(2)}, u32[]{:S(2)}) collective-permute-start(bf16[1024,768]{1,0:T(8,128)(2,1)S(1)} %copy-done.47), channel_id=1, source_target_pairs={{0,16},{16,0},{1,17},{17,1},{2,18},{18,2},{3,19},{19,3},{4,20},{20... | collective-permute-start | bytes 4718600 | tf_op jit(solution)/shard_map/ppermute | solution.py:977
  418.7 3.6 copy-start
  418.7 3.6 copy-start.2
  418.7 3.6 copy-start.16
  504.2 8.7 %copy-start.25 = (f32[1024,768]{1,0:T(8,128)S(1)}, f32[1024,768]{1,0:T(8,128)}, u32[]{:S(2)}) copy-start(f32[1024,768]{1,0:T(8,128)} %pad_maximum_fusion.1) | copy-start | bytes 9437188
  525.1 4.8 copy-start.42
  525.1 4.8 copy-start.43
  525.1 5.9 %copy-start.44 = (bf16[256,1024]{1,0:T(8,128)(2,1)S(1)}, bf16[256,1024]{1,0:T(8,128)(2,1)}, u32[]{:S(2)}) copy-start(bf16[256,1024]{1,0:T(8,128)(2,1)} %get-tuple-element.178) | copy-start | bytes 1572868
  525.1 5.9 %copy-start.45 = (bf16[256,1024]{1,0:T(8,128)(2,1)S(1)}, bf16[256,1024]{1,0:T(8,128)(2,1)}, u32[]{:S(2)}) copy-start(bf16[256,1024]{1,0:T(8,128)(2,1)} %get-tuple-element.179) | copy-start | bytes 1572868
  (24 other events, 41.1 us)

commit v6 on v5

--- a/solution.py
+++ b/solution.py
@@ -379,18 +379,19 @@
 
         own.start()
 
-    def finish():
-        for offset in offsets:
+    def stage(step):
+        for offset in (-step, step):
             @pl.when(valid(offset))
             def _(offset=offset):
                 arrival(offset).wait_recv()
 
-            step, more = onward(offset)
+            way, more = onward(offset)
 
             @pl.when(more)
-            def _(offset=offset, step=step):
-                hop(offset, step, spot(offset)).start()
-
+            def _(offset=offset, way=way):
+                hop(offset, way, spot(offset)).start()
+
+    def drain():
         own.wait()
         for step, there in ends:
             @pl.when(there)
@@ -404,7 +405,7 @@
             def _(offset=offset, step=step):
                 hop(offset, step, spot(offset)).wait_send()
 
-    return begin, finish
+    return begin, stage, drain
 
 
 class KvSum:
@@ -472,17 +473,18 @@
         levels = self.tp_size // 2
         self.levels = levels
         self.outs = (
-            jax.ShapeDtypeStruct((self.ctx_size * (self.wide + self.out_wide), self.half), BF16),
+            jax.ShapeDtypeStruct((self.ctx_size * self.wide, self.half), BF16),
+            jax.ShapeDtypeStruct((self.ctx_size * self.out_wide, self.half), BF16),
             jax.ShapeDtypeStruct((2, self.half), F32),
         )
-        self.out_specs = (HBM_SPEC, VMEM_SPEC)
+        self.out_specs = (HBM_SPEC, HBM_SPEC, VMEM_SPEC)
         chips = max(levels - 1, 1)
         self.scratch = [
             pltpu.VMEM(pre_slabs.shape, BF16),
             pltpu.VMEM((self.wide, self.half), F32),
             pltpu.VMEM((self.wide, self.half), BF16),
             pltpu.VMEM((self.wide, self.half), BF16),
-            pltpu.VMEM((self.wide + self.out_wide, self.half), BF16),
+            pltpu.VMEM((self.wide, self.half), BF16),
             pltpu.VMEM((4, 2, self.half), F32),
             pltpu.VMEM((levels, 2, self.half), F32),
             pltpu.VMEM((self.ctx_size, 2, self.half), F32),
@@ -493,11 +495,12 @@
         ] + line_sems(self.ctx_size) + [
             pltpu.VMEM((self.ctx_size, self.out_wide, self.half), BF16),
             DMA((self.ctx_size,)), DMA((self.ctx_size,)),
-        ]
+            pltpu.VMEM((self.out_wide, self.half), BF16),
+        ] + line_sems(self.ctx_size)
 
     def bind(self, in_refs, out_refs, side_refs, scratch):
         pre_ref, norm_ref, gain_second_ref, out_ref = in_refs
-        all_ref, gains_ref = out_refs
+        all_ref, out_all_ref, gains_ref = out_refs
         slabs, own_half, far_half, from_far, quarter, swaps, by_level, by_place = scratch[:8]
         all_send, all_recv, duo, lev_send, lev_recv, ctx_send, ctx_recv = scratch[8:15]
         ctx_size, levels, half, rows = self.ctx_size, self.levels, self.half, self.rows
@@ -505,9 +508,12 @@
         _, _, level, partner, others = tp_peers(self.tp_size)
         far = {"fsdp": 1 - lax.axis_index("fsdp")}
         tile = min(512, half)
-        line_begin, line_finish = line_gather(quarter, all_ref, ctx_size, scratch[15:18])
-        out_slots, out_send, out_recv = scratch[18:21]
-        wide, out_wide = self.wide, self.out_wide
+        line_begin, line_stage, line_drain = line_gather(quarter, all_ref, ctx_size, scratch[15:18])
+        out_slots, out_send, out_recv, out_quarter = scratch[18:22]
+        out_wide = self.out_wide
+        out_begin, out_stage, out_drain = line_gather(
+            out_quarter, out_all_ref, ctx_size, scratch[22:25]
+        )
 
         def out_slab(step):
             peer = lax.rem(place + step, ctx_size)
@@ -574,14 +580,14 @@
         def begin():
             for step in range(1, ctx_size):
                 slab(step).start()
-            for step in range(1, ctx_size):
-                out_slab(step).start()
             slabs[place] = pre_ref[place]
             out_slots[place] = out_ref[pl.ds(pl.multiple_of(place * out_wide, out_wide), out_wide), :]
 
         def middle():
             for step in range(1, ctx_size):
                 slab_arrival(step).wait_recv()
+            for step in range(1, ctx_size):
+                out_slab(step).start()
 
             @pl.loop(0, half // tile)
             def _(i):
@@ -600,23 +606,25 @@
             swaps[0, 0:1, :] = gain_first[:, half:]
             swaps[0, 1:2, :] = gain_second_ref[:, half:]
             gain_x.start()
+            grads.wait_recv()
+            quarter[...] = (own_half[...] + from_far[...].astype(F32)).astype(BF16)
+            line_begin()
+            gain_x.wait_recv()
+            swaps[2, 0:1, :] = gain_first[:, :half] + swaps[1, 0:1, :]
+            swaps[2, 1:2, :] = gain_second_ref[:, :half] + swaps[1, 1:2, :]
+            gain_core.start()
             for step in range(1, ctx_size):
                 out_arrival(step).wait_recv()
             total = out_slots[0].astype(F32)
             for z in range(1, ctx_size):
                 total += out_slots[z].astype(F32)
-            quarter[wide : wide + out_wide, :] = total.astype(BF16)
-            grads.wait_recv()
-            quarter[0:wide, :] = (own_half[...] + from_far[...].astype(F32)).astype(BF16)
-            line_begin()
-            gain_x.wait_recv()
-            swaps[2, 0:1, :] = gain_first[:, :half] + swaps[1, 0:1, :]
-            swaps[2, 1:2, :] = gain_second_ref[:, :half] + swaps[1, 1:2, :]
-            gain_core.start()
+            out_quarter[...] = total.astype(BF16)
+            out_begin()
             gain_core.wait_recv()
             by_level[level] = swaps[2] + swaps[3]
             for index in range(levels - 1):
                 gain_level(index).start()
+            line_stage(1)
             for index in range(levels - 1):
                 gain_level_arrival(index).wait_recv()
             total = by_level[0]
@@ -625,13 +633,18 @@
             by_place[place] = total
             for step in range(1, ctx_size):
                 gain_place(step).start()
+            out_stage(1)
+            for step in range(2, ctx_size):
+                line_stage(step)
+                out_stage(step)
             for step in range(1, ctx_size):
                 gain_place_arrival(step).wait_recv()
             total = by_place[0]
             for z in range(1, ctx_size):
                 total += by_place[z]
             gains_ref[...] = total
-            line_finish()
+            line_drain()
+            out_drain()
             for step in range(1, ctx_size):
                 slab(step).wait_send()
                 out_slab(step).wait_send()
@@ -791,7 +804,7 @@
     low = place % 2
     part = ((place + 1) // 2) % 2
     base = 2 + 3 * part
-    return [base, base + 1, base + 2, low, 1 - low], part
+    return [base, low, base + 1, base + 2, 1 - low], part
 
 
 def opening(cot_rows, groups, gains, hidden_weights, mesh_shape, identity):
@@ -906,27 +919,28 @@
     )(table, *(array for array, _ in pieces), *(() if base is None else (base,)))
 
 
-def transposed_grads(slices, first, widths):
-    count, columns, depth = slices.shape
+def transposed_grads(columns, widths, last):
+    depth = columns.shape[1]
     tile = min(depth, 256)
-
-    def kernel(in_ref, *out_refs):
-        head = jnp.concatenate([in_ref[z, 0:first, :] for z in range(count)], axis=0)
-        head = head.astype(F32).T
+    widths = list(widths) + [last.shape[0]]
+
+    def kernel(in_ref, last_ref, *out_refs):
+        head = in_ref[...].astype(F32).T
         at = 0
         for out_ref, wide in zip(out_refs[:-1], widths[:-1]):
             out_ref[...] = head[:, at : at + wide]
             at += wide
-        last = jnp.concatenate([in_ref[z, first:columns, :] for z in range(count)], axis=0)
-        out_refs[-1][...] = last.astype(F32).T
+        out_refs[-1][...] = last_ref[...].astype(F32).T
 
     return pl.pallas_call(
         kernel,
         grid=(depth // tile,),
-        in_specs=[pl.BlockSpec((count, columns, tile), lambda i: (0, 0, i))],
+        in_specs=[
+            pl.BlockSpec((array.shape[0], tile), lambda i: (0, i)) for array in (columns, last)
+        ],
         out_specs=tuple(pl.BlockSpec((tile, wide), lambda i: (i, 0)) for wide in widths),
         out_shape=tuple(jax.ShapeDtypeStruct((depth, wide), F32) for wide in widths),
-    )(slices)
+    )(columns, last)
 
 
 def mean_square(rows):
@@ -1090,6 +1104,9 @@
             if c == 1:
                 owns[3], others[1] = lax.optimization_barrier((owns[3], others[1]))
                 others[3] = swap_rows(owns[3])
+                others[4] = lax.ppermute(others[1], "ctx", swap_z)
+            if c == 3:
+                others[3], others[4] = lax.optimization_barrier((others[3], others[4]))
             pair_w, down_w, grad_both, hidden = forward(c)
             ffn_term += contract(pair(hidden), down_w, 1, 1)
             mid_term += contract(pair(grad_both), pair_w, 1, 1)
@@ -1097,25 +1114,32 @@
         def swap_ctx(total):
             return lax.ppermute(total, "ctx", swap_z)
 
-        received = [swap_rows(fars[0]), swap_rows(fars[1])]
-        mid_low, fars[2], fars[3], received[0] = lax.optimization_barrier(
-            (mid_term.astype(BF16), fars[2], fars[3], received[0])
-        )
-        received.append(swap_rows(fars[2]))
-        totals = [summed(0)]
+        received = {0: swap_rows(fars[0]), 2: swap_rows(fars[2])}
+        totals, swapped = {}, {}
+        mid_low, fars[1], fars[3], received[0] = lax.optimization_barrier(
+            (mid_term.astype(BF16), fars[1], fars[3], received[0])
+        )
+        received[3] = swap_rows(fars[3])
+        totals[0] = summed(0)
         mid_low, totals[0] = lax.optimization_barrier((mid_low, totals[0]))
-        swapped = [swap_ctx(totals[0])]
+        swapped[0] = swap_ctx(totals[0])
         branch_low, grad_middle, gain_grad_second = reduce_gather(
             mid_low, (middle, cot_low, gain_second[None]), finish_grad_middle,
             (slice_shape, (1, model_width)), mesh_shape, 2, 2, False,
         )
-        branch_low, received[1], owns[4], swapped[0], rows_all = lax.optimization_barrier(
-            (branch_low, received[1], owns[4], swapped[0], rows_all)
-        )
-        others[4] = swap_rows(owns[4])
-        totals.append(summed(1))
-        branch_low, totals[1] = lax.optimization_barrier((branch_low, totals[1]))
-        swapped.append(swap_ctx(totals[1]))
+        branch_low, received[2], fars[1], swapped[0], rows_all = lax.optimization_barrier(
+            (branch_low, received[2], fars[1], swapped[0], rows_all)
+        )
+        received[1] = swap_rows(fars[1])
+        totals[2] = summed(2)
+        near_one = near_of(1)
+        residual_all = rows_all[:, model_width:].astype(F32)
+        rms_all = lax.rsqrt(jnp.mean(residual_all * residual_all, axis=-1, keepdims=True) + EPSILON)
+        norm_all = (residual_all * rms_all * gain_first).astype(BF16)
+        branch_low, totals[2], near_one, norm_all = lax.optimization_barrier(
+            (branch_low, totals[2], near_one, norm_all)
+        )
+        swapped[2] = swap_ctx(totals[2])
         grad_out = jnp.dot(attended_flat, branch_low, preferred_element_type=F32)
         grad_out_half = grad_out[:, half_width:].astype(BF16)
         grad_attended = contract(out_weight, branch_low, 0, 1).astype(BF16)
@@ -1126,40 +1150,35 @@
         grad_kv = grad_kv.reshape(2 * key_width, length_total)
         far_base = 2 + 3 * (1 - part)
         table = jnp.stack(units + [far_base, far_base + 1, far_base + 2])
-        grad_kv, received[2] = lax.optimization_barrier((grad_kv, received[2]))
-        totals.append(summed(2))
-        grad_kv, totals[2], others[4], fars[3], grad_out_half = lax.optimization_barrier(
-            (grad_kv, totals[2], others[4], fars[3], grad_out_half)
-        )
-        swapped.append(swap_ctx(totals[2]))
+        grad_kv, received[3] = lax.optimization_barrier((grad_kv, received[3]))
+        totals[3] = summed(3)
+        grad_kv, totals[3] = lax.optimization_barrier((grad_kv, totals[3]))
+        swapped[3] = swap_ctx(totals[3])
+        early = [totals[0], totals[2], totals[3], swapped[0]]
+        placed = [
+            place_blocks(
+                jnp.stack([table[0], table[2], table[3], table[5]]),
+                [(piece, block) for piece in early], unit, 8,
+            )
+            for block in range(3)
+        ]
+        others[4], placed, swapped[2], received[1], grad_out_half = lax.optimization_barrier(
+            (others[4], placed, swapped[2], received[1], grad_out_half)
+        )
         grad_out_far = swap_rows(grad_out_half)
-        received.append(swap_rows(fars[3]))
         forward(4)
         near_four = near_of(4)
-        early = totals + swapped[:1]
-        placed = [
-            place_blocks(
-                jnp.stack([table[0], table[1], table[2], table[5]]),
-                [(piece, block) for piece in early], unit, 8,
-            )
-            for block in range(3)
-        ]
-        near_three = near_of(3)
-        residual_all = rows_all[:, model_width:].astype(F32)
-        rms_all = lax.rsqrt(jnp.mean(residual_all * residual_all, axis=-1, keepdims=True) + EPSILON)
-        norm_all = (residual_all * rms_all * gain_first).astype(BF16)
-        grad_kv, placed, near_three, near_four, norm_all, fars[4], swapped[1] = (
-            lax.optimization_barrier(
-                (grad_kv, placed, near_three, near_four, norm_all, fars[4], swapped[1])
-            )
-        )
-        received.append(swap_rows(fars[4]))
+        totals[1] = summed(1, near_one)
+        grad_kv, near_four, fars[4], totals[1] = lax.optimization_barrier(
+            (grad_kv, near_four, fars[4], totals[1])
+        )
+        received[4] = swap_rows(fars[4])
         output_rows, grad_kv = reduce_gather(
             ffn_term.astype(BF16), (middle,), finish_output, (), mesh_shape, 3, 2, False,
             KvSum(grad_kv, ctx_size),
         )
-        output_rows, grad_kv, swapped[2] = lax.optimization_barrier(
-            (output_rows, grad_kv, swapped[2])
+        output_rows, grad_kv, swapped[3], grad_out_far = lax.optimization_barrier(
+            (output_rows, grad_kv, swapped[3], grad_out_far)
         )
         grad_query_pre = apply_rotary(
             grad_query_rot, cosine_lookup, sine_lookup, -1.0
@@ -1174,12 +1193,7 @@
         pre_slabs = grad_qkv_pre.reshape(ctx_size, attn_width // ctx_size, row_count)
         normed_term = contract(grad_qkv_pre, qkv_weight, 0, 1).astype(BF16)
         grad_out_rows = (grad_out[:, :half_width] + grad_out_far.astype(F32)).astype(BF16)
-        normed_term, received[3], grad_out_far = lax.optimization_barrier(
-            (normed_term, received[3], grad_out_far)
-        )
-        totals.append(summed(3, near_three))
-        normed_term, totals[3] = lax.optimization_barrier((normed_term, totals[3]))
-        input_rows, _, grad_attn, gain_grads = reduce_gather(
+        input_rows, _, grad_attn, grad_out, gain_grads = reduce_gather(
             normed_term,
             (grad_middle, residual_low, gain_first[None]), finish_grad_input,
             ((1, model_width),), mesh_shape, 4, 1, False,
@@ -1187,14 +1201,13 @@
         )
         grad_attn, received[4] = lax.optimization_barrier((grad_attn, received[4]))
         grad_query, grad_key, grad_value, grad_out = transposed_grads(
-            grad_attn.reshape(ctx_size, -1, half_width), attn_width // ctx_size,
-            (query_width, key_width, key_width, query_width),
-        )
-        totals.append(summed(4, near_four))
+            grad_attn, (query_width, key_width, key_width), grad_out
+        )
+        totals[4] = summed(4, near_four)
 
         def result(block):
-            pieces = [(piece, block) for piece in totals[3:] + swapped[1:]]
-            late = jnp.stack([table[3], table[4], table[6], table[7]])
+            pieces = [(piece, block) for piece in (totals[1], totals[4], swapped[2], swapped[3])]
+            late = jnp.stack([table[1], table[4], table[6], table[7]])
             return place_blocks(late, pieces, unit, 8, placed[block])
 
         return (

time: 539 us -> 521 us (0.967)
  waiting for transfers between devices: 27 us -> 8.46 us
  Pallas kernels: 311 us -> 322 us
  matrix products: 91.9 us -> 82.5 us
  local copies, waits for them, and re-layouts: 30.4 us -> 36.3 us
    ppermute x11 -> x10, waiting for transfers between devices: 27 us -> 2.79 us  [swap_rows(): return lax.ppermute(array, 'fsdp', swap_x)]
    pallas_call x4, Pallas kernels: 194 us -> 205 us  [reduce_gather(): pl.pallas_call(kernel, out_shape=(jax.ShapeDtypeStruct((reach * block_row...]
    dot_general x32, matrix products: 58 us -> 52.4 us  [contract(): lax.dot_general(left, right, (((left_dim,), (right_dim,)), ((), ())), pre...]
    unnamed x153 -> x161, local copies, waits for them, and re-layouts: 14.5 us -> 18.4 us
    ppermute x11 -> x10, starting transfers between devices: 12 us -> 9.56 us  [swap_rows(): return lax.ppermute(array, 'fsdp', swap_x)]
  transfers between devices with their start and end apart: 14 -> 14, of which waited for: 3 -> 3; matrix products, arithmetic and copies ran while one was open for 26% -> 26% of each run, Pallas kernels for 42% -> 46%
where the time goes in v6:
time: 521 us; the launch traced here: 514 us
  Pallas kernels  322 us (62%)
  matrix products  82.5 us (16%)
  local copies, waits for them, and re-layouts  36.3 us (7%)
  other arithmetic  35.5 us (7%)
  blocking collectives  15 us (3%)
  starting transfers between devices  12 us (2%)
  waiting for transfers between devices  8.46 us (2%)
    pallas_call x4, Pallas kernels, reduce_gather(): pl.pallas_call(kernel, out_shape=(jax.ShapeDtypeStruct((reach * block_row...  205 us
    pallas_call x1, Pallas kernels, opening(): pl.pallas_call(kernel, out_shape=(jax.ShapeDtypeStruct((ctx_size * block_...  66.2 us
    dot_general x32, matrix products, contract(): lax.dot_general(left, right, (((left_dim,), (right_dim,)), ((), ())), pre...  52.4 us
    pallas_call x6, Pallas kernels, place_blocks(): pl.pallas_call(kernel, grid_spec=pltpu.PrefetchScalarGridSpec(num_scalar_...  28.4 us
    unnamed x161, local copies, waits for them, and re-layouts  18.4 us
    dot_general x5, matrix products, forward(): both = jnp.dot(normed_all, pair_w, preferred_element_type=F32)  15.2 us
    all_gather x1, blocking collectives, local(): lax.all_gather(kv_own.reshape(2 * key_width, row_count).T, 'ctx', axis=0,...  15 us
    dot_general x5, matrix products, forward(): grad_hidden = jnp.dot(cot_all, down_w, preferred_element_type=F32)  12.9 us
  transfers between devices with their start and end apart: 14, of which 3 were waited for; matrix products, arithmetic and copies ran while one was open for 26% of the time, Pallas kernels for 46%

profile of v6, /device:TPU:0, one launch (start us, length us, event | category | flops | bytes accessed | tf_op | source)
XLA Modules:
  0.0 514.5 jit_solution(5651057300335897534)
XLA Ops:
  3.1 1.7 dynamic-slice_bitcast_fusion.1
  5.8 1.5 pad_maximum_fusion.2.cot_ref
  7.8 66.2 %shard_map.203 = (bf16[1024,4096]{1,0:T(8,128)(2,1)}, f32[2,1024]{1,0:T(2,128)S(1)}, bf16[2048,768]{1,0:T(8,128)(2,1)}, bf16[2048,512]{1,0:T(8,128)(2,1)S(1)}, b...) custom-call(bf16[256,4096]{1,0:T(8,128)(2,1)} %pad_maximum_fusion.2., ...), custom_call_target="tpu_custom_call" | custom-call | tf_op jit(solution)/shard_map/pallas_call | solution.py:874
  74.6 1.5 collective-permute-start.1
  77.0 3.0 fusion.67
  84.5 15.0 %all_gather.3 = bf16[1024,256]{0,1:T(8,128)(2,1)S(1)} all-gather(bf16[256,256]{0,1:T(8,128)(2,1)S(1)} %bitcast.86), channel_id=1, replica_groups=mesh['fsdp'=2,'ctx'=4,'tp'=4] {'ctx'}, dimensions={0}, use_global_device_ids=true | all-gather | bytes 655360 | tf_op jit(solution)/shard_map/all_gather | solution.py:1044
  100.8 2.1 fusion.118
  102.9 1.8 fusion.119
  104.8 7.6 %shard_map.204 = (bf16[8,64,256]{2,1,0:T(8,128)(2,1)S(1)}, f32[8,1,256]{2,1,0:T(1,128)S(1)}) custom-call(s32[2]{0:T(128)S(1)} %pad_add_fusion.bounds_ref, bf16[8,64,256]{2,1,0:T(8,128)(2,1)S(1)} %pad_maximum_fusion.27.query_ref, bf16[2,1024,64]{2,1,0:T(8,128)(2,1)S(1)} %get-tuple-element.185.key_ref, bf16[2,64,1024]{2,1,0:T(8,128)(2,1)S(1)} %bitcast.69), custom_call_target="tpu_custom_call" | custom-call | tf_op jit(solution)/shard_map/pallas_call | solution.py:72
  113.7 1.6 constant_dynamic-update-slice_fusion.3
  115.3 1.6 constant_dynamic-update-slice_fusion.1
  121.1 1.5 constant_dynamic-update-slice_fusion
  122.6 44.5 %shard_map.205 = (bf16[1024,2048]{1,0:T(8,128)(2,1)S(1)}, f32[64,2048]{1,0:T(8,128)S(1)}) custom-call(bf16[256,2048]{1,0:T(8,128)(2,1)S(1)} %convolution_convert_fusion.term_ref, bf16[256,2048]{1,0:T(8,128)(2,1)S(1)} %pad_maximum_fusion.12.refs_0_.refs_1_, f32[1,2048]{1,0:T(1,128)S(1)} %get-tuple-element.200.refs_1_.refs_2_), custom_call_target="tpu_custom_call" | custom-call | tf_op jit(solution)/shard_map/pallas_call | solution.py:786
  167.2 2.4 fusion.35
  170.9 1.7 multiply_convert_fusion.13
  177.9 1.6 collective-permute-start.3
  179.4 1.7 fusion.45
  181.2 2.6 fusion.55
  183.8 1.5 constant_dynamic-update-slice_fusion.2
  185.3 2.4 fusion.31
  187.8 1.9 multiply_convert_fusion.10
  194.3 2.0 pad_maximum_fusion
  202.7 1.5 constant_dynamic-update-slice_fusion.4
  204.2 2.4 fusion.27
  206.6 4.1 multiply_convert_fusion.7
  210.8 2.9 convolution_convert_fusion.9
  216.3 4.2 collective-permute-done.4
  221.7 5.5 %fusion.23 = f32[1024,512]{0,1:T(8,128)} fusion(bf16[1024,2048]{1,0:T(8,128)(2,1)S(1)} %get-tuple-element.95, bf16[2048,768]{1,0:T(8,128)(2,1)} %constant_dynamic-update-slice_fusion.6), kind=kOutput, calls=%fused_computation.41 | convolution fusion | flops 2147483648 | bytes 8388608 | tf_op jit(solution)/shard_map/dot_general | solution.py:1086
  227.2 3.6 multiply_convert_fusion.3
  234.6 2.6 fusion.53
  237.2 3.3 fusion.25
  240.6 5.0 add_convert_fusion.term_ref
  245.6 2.8 collective-permute-done.5
  248.3 1.9 fusion.3.refs_0_
  250.3 1.6 collective-permute-start.6
  252.4 45.9 %shard_map.206 = (bf16[256,2048]{1,0:T(8,128)(2,1)S(1)}, f32[64,2048]{1,0:T(8,128)S(1)}, f32[1,2048]{1,0:T(1,128)S(1)}) custom-call(bf16[512,2048]{1,0:T(8,128)(2,1)S(1)} %add_convert_fusion.term_ref, f32[64,2048]{1,0:T(8,128)S(1)} %get-tuple-element.107.refs_0_, bf16[256,2048]{1,0:T(8,128)(2,1)S(1)} %pad_maximum_fusion.13.refs_1_, ...), custom_call_target="tpu_custom_call" | custom-call | tf_op jit(solution)/shard_map/pallas_call | solution.py:786
  298.4 2.9 fusion.43
  302.7 2.1 fusion.75
  304.8 2.1 add_convert_fusion.1.term_ref
  307.0 3.7 fusion
  310.7 1.7 fusion.4.refs_1_
  312.4 4.2 fusion.2.refs_4_
  317.7 2.4 fusion.39
  321.2 9.6 %shard_map.207 = (f32[8,64,256]{2,1,0:T(8,128)S(1)}, bf16[4,64,1024]{2,1,0:T(8,128)(2,1)S(1)}) custom-call(s32[2]{0:T(128)S(1)} %pad_add_fusion.bounds_ref, bf16[8,64,256]{2,1,0:T(8,128)(2,1)S(1)} %pad_maximum_fusion.27.query_ref, bf16[2,1024,64]{2,1,0:T(8,128)(2,1)S(1)} %get-tuple-element.185.key_ref, bf16[2,64,1024]{2,1,0:T(8,128)(2,1)S(1)} %bitcast.68, ...), custom_call_target="tpu_custom_call" | custom-call | tf_op jit(solution)/shard_map/pallas_call | solution.py:112
  332.4 1.6 fusion.5.refs_2_
  334.0 4.8 shard_map.208.refs_4_
  338.9 4.7 shard_map.209.refs_4_
  343.6 4.8 shard_map.210.refs_4_
  348.4 1.8 collective-permute-start.11
  350.2 2.1 fusion.121
  352.6 1.5 collective-permute-done.9.refs_2_
  354.1 2.1 constant_dynamic-update-slice_fusion.8
  356.2 2.4 fusion.20
  358.7 1.7 multiply_convert_fusion.2
  366.1 1.6 copy-done.31
  367.8 2.9 add_convert_fusion.3.refs_0_
  371.6 40.8 %shard_map.211 = (bf16[256,2048]{1,0:T(8,128)(2,1)S(1)}, f32[256,256]{1,0:T(8,128)S(1)}) custom-call(bf16[512,2048]{1,0:T(8,128)(2,1)S(1)} %add_convert_fusion.1.term_ref, f32[64,2048]{1,0:T(8,128)S(1)} %get-tuple-element.107.refs_0_, bf16[256,1024]{1,0:T(8,128)(2,1)S(1)} %bitcast.70), custom_call_target="tpu_custom_call" | custom-call | tf_op jit(solution)/shard_map/pallas_call | solution.py:786
  415.1 1.9 copy-done
  417.0 73.9 %shard_map.212 = (bf16[256,2048]{1,0:T(8,128)(2,1)S(1)}, f32[1,2048]{1,0:T(1,128)}, bf16[768,1024]{1,0:T(8,128)(2,1)S(1)}, bf16[512,1024]{1,0:T(8,128)(2,1)S(1)}, f32[2,1024]{1,0:T(2,128)S(1)}) custom-call(bf16[256,2048]{1,0:T(8,128)(2,1)S(1)} %convolution_convert_fusion.1.term_ref, f32[64,2048]{1,0:T(8,128)S(1)} %copy-done.21, ...), custom_call_target="tpu_custom_call" | custom-call | tf_op jit(solution)/shard_map/pallas_call | solution.py:786
  494.0 1.5 add_convert_fusion.2.refs_1_
  495.5 4.7 shard_map.214
  500.1 4.7 shard_map.215
  504.8 4.7 shard_map.216
  509.5 4.7 shard_map.213
  (247 shorter events, 59.1 us)
Async XLA Ops:
  4.9 72.1 %copy-start.32 = (bf16[256,1024]{1,0:T(8,128)(2,1)}, bf16[256,1024]{1,0:T(8,128)(2,1)S(1)}, u32[]{:S(2)}) copy-start(bf16[256,1024]{1,0:T(8,128)(2,1)S(1)} %get-tuple-element.188) | copy-start | bytes 1572868
  4.9 72.1 %copy-start.34 = (bf16[256,1024]{1,0:T(8,128)(2,1)}, bf16[256,1024]{1,0:T(8,128)(2,1)S(1)}, u32[]{:S(2)}) copy-start(bf16[256,1024]{1,0:T(8,128)(2,1)S(1)} %get-tuple-element.189) | copy-start | bytes 1572868
  4.9 2.9 copy-start.19
  74.0 6.0 %copy-start.8 = (bf16[1024,768]{1,0:T(8,128)(2,1)}, bf16[1024,768]{1,0:T(8,128)(2,1)S(1)}, u32[]{:S(2)}) copy-start(bf16[1024,768]{1,0:T(8,128)(2,1)S(1)} %get-tuple-element.104) | copy-start | bytes 4718596
  74.0 6.0 %copy-start.10 = (bf16[1024,768]{1,0:T(8,128)(2,1)}, bf16[1024,768]{1,0:T(8,128)(2,1)S(1)}, u32[]{:S(2)}) copy-start(bf16[1024,768]{1,0:T(8,128)(2,1)S(1)} %get-tuple-element.102) | copy-start | bytes 4718596
  74.0 6.0 %copy-start.12 = (bf16[1024,768]{1,0:T(8,128)(2,1)}, bf16[1024,768]{1,0:T(8,128)(2,1)S(1)}, u32[]{:S(2)}) copy-start(bf16[1024,768]{1,0:T(8,128)(2,1)S(1)} %get-tuple-element.127) | copy-start | bytes 4718596
  74.0 44.7 %copy-start.3 = (bf16[2048,512]{1,0:T(8,128)(2,1)}, bf16[2048,512]{1,0:T(8,128)(2,1)S(1)}, u32[]{:S(2)}) copy-start(bf16[2048,512]{1,0:T(8,128)(2,1)S(1)} %get-tuple-element.91) | copy-start | bytes 6291460
  74.0 45.4 %collective-permute-start = (bf16[1024,768]{1,0:T(8,128)(2,1)}, bf16[1024,768]{1,0:T(8,128)(2,1)}, u32[]{:S(2)}, u32[]{:S(2)}) collective-permute-start(bf16[1024,768]{1,0:T(8,128)(2,1)} %get-tuple-element.93), channel_id=1, source_target_pairs={{0,16},{16,0},{1,17},{17,1},{2,18},{18,2},{3,19},{19,3},{4,20},{20... | collective-permute-start | bytes 4718600 | tf_op jit(solution)/shard_map/ppermute | solution.py:991
  74.6 101.3 %collective-permute-start.1 = (bf16[1024,768]{1,0:T(8,128)(2,1)}, bf16[1024,768]{1,0:T(8,128)(2,1)}, u32[]{:S(2)}, u32[]{:S(2)}) collective-permute-start(bf16[1024,768]{1,0:T(8,128)(2,1)} %get-tuple-element.97), channel_id=1, source_target_pairs={{0,16},{16,0},{1,17},{17,1},{2,18},{18,2},{3,19},{19,3},{4,20},{20... | collective-permute-start | bytes 4718600 | tf_op jit(solution)/shard_map/ppermute | solution.py:991
  83.6 21.0 %copy-start.57 = (bf16[8,32,256]{2,1,0:T(8,128)(2,1)S(1)}, bf16[8,32,256]{2,1,0:T(8,128)(2,1)}, u32[]{:S(2)}) copy-start(bf16[8,32,256]{2,1,0:T(8,128)(2,1)} %get-tuple-element.193) | copy-start | bytes 393220
  99.5 3.4 copy-start.40
  112.4 6.3 %copy-start.6 = (bf16[8,64,256]{2,1,0:T(8,128)(2,1)}, bf16[8,64,256]{2,1,0:T(8,128)(2,1)S(1)}, u32[]{:S(2)}) copy-start(bf16[8,64,256]{2,1,0:T(8,128)(2,1)S(1)} %get-tuple-element.90) | copy-start | bytes 786436
  113.7 3.3 copy-start.13
  115.3 2.9 copy-start.33
  115.3 2.9 copy-start.35
  118.6 4.0 copy-start.1
  120.5 82.2 %collective-permute-start.2 = (bf16[1024,768]{1,0:T(8,128)(2,1)S(1)}, bf16[1024,768]{1,0:T(8,128)(2,1)}, u32[]{:S(2)}, u32[]{:S(2)}) collective-permute-start(bf16[1024,768]{1,0:T(8,128)(2,1)S(1)} %copy-done.11), channel_id=1, source_target_pairs={{0,16},{16,0},{1,17},{17,1},{2,18},{18,2},{3,19},{19,3},{4,20},{20... | collective-permute-start | bytes 4718600 | tf_op jit(solution)/shard_map/ppermute | solution.py:991
  122.6 47.0 %slice-start = ((s8[8388608]{0:T(1024)(128)(4,1)}), s8[4194304]{0:T(1024)(128)(4,1)S(1)}, s32[]{:S(2)}) async-start(s8[8388608]{0:T(1024)(128)(4,1)} %bitcast.74), calls=%async_computation | async-start | bytes 8388608
  167.1 134.2 %copy-start.26 = (bf16[1024,2048]{1,0:T(8,128)(2,1)}, bf16[1024,2048]{1,0:T(8,128)(2,1)S(1)}, u32[]{:S(2)}) copy-start(bf16[1024,2048]{1,0:T(8,128)(2,1)S(1)} %get-tuple-element.95) | copy-start | bytes 12582916
  167.2 3.7 slice-start.1
  172.6 6.9 %copy-start.67 = (bf16[1024,256]{0,1:T(8,128)(2,1)}, bf16[1024,256]{0,1:T(8,128)(2,1)S(1)}, u32[]{:S(2)}) copy-start(bf16[1024,256]{0,1:T(8,128)(2,1)S(1)} %get-tuple-element.179) | copy-start | bytes 1572868
  177.9 38.4 %collective-permute-start.3 = (bf16[1024,768]{1,0:T(8,128)(2,1)S(1)}, bf16[1024,768]{1,0:T(8,128)(2,1)S(1)}, u32[]{:S(2)}, u32[]{:S(2)}) collective-permute-start(bf16[1024,768]{1,0:T(8,128)(2,1)S(1)} %copy-done.9), channel_id=1, source_target_pairs={{0,16},{16,0},{1,17},{17,1},{2,18},{18,2},{3,19},{19,3},{4,20},{20... | collective-permute-start | bytes 4718600 | tf_op jit(solution)/shard_map/ppermute | solution.py:991
  183.8 36.7 %collective-permute-start.4 = (bf16[1024,768]{1,0:T(8,128)(2,1)}, bf16[1024,768]{1,0:T(8,128)(2,1)}, u32[]{:S(2)}, u32[]{:S(2)}) collective-permute-start(bf16[1024,768]{1,0:T(8,128)(2,1)} %collective-permute-done.1), channel_id=1, source_target_pairs={{0,4},{4,0},{8,12},{12,8},{1,5},{5,1},{9,13},{13,9},{2,6},{6,2},{1... | collective-permute-start | bytes 4718600 | tf_op jit(solution)/shard_map/ppermute | solution.py:1107
  185.3 13.1 %copy-start.38 = (bf16[2048,768]{1,0:T(8,128)(2,1)}, bf16[2048,768]{1,0:T(8,128)(2,1)S(1)}, u32[]{:S(2)}) copy-start(bf16[2048,768]{1,0:T(8,128)(2,1)S(1)} %constant_dynamic-update-slice_fusion.2) | copy-start | bytes 9437188
  193.8 54.5 %collective-permute-start.5 = (bf16[1024,768]{1,0:T(8,128)(2,1)}, bf16[1024,768]{1,0:T(8,128)(2,1)}, u32[]{:S(2)}, u32[]{:S(2)}) collective-permute-start(bf16[1024,768]{1,0:T(8,128)(2,1)} %pad_maximum_fusion.3), channel_id=1, source_target_pairs={{0,16},{16,0},{1,17},{17,1},{2,18},{18,2},{3,19},{19,3},{4,20},{20... | collective-permute-start | bytes 4718600 | tf_op jit(solution)/shard_map/ppermute | solution.py:991
  210.7 2.9 copy-start.65
  210.7 2.9 copy-start.58
  210.8 2.9 copy-start.60
  215.0 12.2 %slice-start.2 = ((s8[8388608]{0:T(1024)(128)(4,1)}), s8[4194304]{0:T(1024)(128)(4,1)S(1)}, s32[]{:S(2)}) async-start(s8[8388608]{0:T(1024)(128)(4,1)} %bitcast.76), calls=%async_computation.2 | async-start | bytes 8388608
  221.7 5.5 %slice-start.3 = ((s8[8388608]{0:T(1024)(128)(4,1)}), s8[4194304]{0:T(1024)(128)(4,1)S(1)}, s32[]{:S(2)}) async-start(s8[8388608]{0:T(1024)(128)(4,1)} %bitcast.76), calls=%async_computation.3 | async-start | bytes 8388608
  230.8 9.8 %copy-start.53 = (bf16[1024,256]{0,1:T(8,128)(2,1)}, bf16[1024,256]{0,1:T(8,128)(2,1)S(1)}, u32[]{:S(2)}) copy-start(bf16[1024,256]{0,1:T(8,128)(2,1)S(1)} %get-tuple-element.167) | copy-start | bytes 1572868
  230.8 9.7 %copy-start.55 = (bf16[1024,256]{0,1:T(8,128)(2,1)}, bf16[1024,256]{0,1:T(8,128)(2,1)S(1)}, u32[]{:S(2)}) copy-start(bf16[1024,256]{0,1:T(8,128)(2,1)S(1)} %get-tuple-element.168) | copy-start | bytes 1572868
  234.6 2.6 copy-start.37
  240.6 7.8 %copy-start.45 = (f32[1024,512]{1,0:T(8,128)S(1)}, f32[1024,512]{1,0:T(8,128)}, u32[]{:S(2)}) copy-start(f32[1024,512]{1,0:T(8,128)} %fusion.55) | copy-start | bytes 6291460
  240.6 7.8 %copy-start.49 = (f32[1024,256]{1,0:T(8,128)S(1)}, f32[1024,256]{1,0:T(8,128)}, u32[]{:S(2)}) copy-start(f32[1024,256]{1,0:T(8,128)} %fusion.45) | copy-start | bytes 3145732
  245.6 4.7 copy-start.48
  245.6 6.4 %copy-start.47 = (bf16[1024,768]{1,0:T(8,128)(2,1)S(1)}, bf16[1024,768]{1,0:T(8,128)(2,1)}, u32[]{:S(2)}) copy-start(bf16[1024,768]{1,0:T(8,128)(2,1)} %pad_maximum_fusion.6) | copy-start | bytes 4718596
  250.3 51.1 %copy-start.28 = (bf16[1024,768]{1,0:T(8,128)(2,1)}, bf16[1024,768]{1,0:T(8,128)(2,1)S(1)}, u32[]{:S(2)}) copy-start(bf16[1024,768]{1,0:T(8,128)(2,1)S(1)} %fusion.3.refs_0_) | copy-start | bytes 4718596
  250.3 48.1 %copy-start.66 = (bf16[1024,256]{0,1:T(8,128)(2,1)S(1)}, bf16[1024,256]{0,1:T(8,128)(2,1)}, u32[]{:S(2)}) copy-start(bf16[1024,256]{0,1:T(8,128)(2,1)} %copy-done.65) | copy-start | bytes 1572868
  250.3 56.6 %collective-permute-start.6 = (bf16[1024,768]{1,0:T(8,128)(2,1)S(1)}, bf16[1024,768]{1,0:T(8,128)(2,1)S(1)}, u32[]{:S(2)}, u32[]{:S(2)}) collective-permute-start(bf16[1024,768]{1,0:T(8,128)(2,1)S(1)} %copy-done.48), channel_id=1, source_target_pairs={{0,16},{16,0},{1,17},{17,1},{2,18},{18,2},{3,19},{19,3},{4,20},{20... | collective-permute-start | bytes 4718600 | tf_op jit(solution)/shard_map/ppermute | solution.py:991
  251.9 55.0 %collective-permute-start.7 = (bf16[1024,768]{1,0:T(8,128)(2,1)S(1)}, bf16[1024,768]{1,0:T(8,128)(2,1)S(1)}, u32[]{:S(2)}, u32[]{:S(2)}) collective-permute-start(bf16[1024,768]{1,0:T(8,128)(2,1)S(1)} %fusion.3.refs_0_), channel_id=1, source_target_pairs={{0,4},{4,0},{8,12},{12,8},{1,5},{5,1},{9,13},{13,9},{2,6},{6,2},{1... | collective-permute-start | bytes 4718600 | tf_op jit(solution)/shard_map/ppermute | solution.py:1115
  251.9 80.5 %collective-permute-start.8 = (bf16[1024,768]{1,0:T(8,128)(2,1)S(1)}, bf16[1024,768]{1,0:T(8,128)(2,1)S(1)}, u32[]{:S(2)}, u32[]{:S(2)}) collective-permute-start(bf16[1024,768]{1,0:T(8,128)(2,1)S(1)} %copy-done.47), channel_id=1, source_target_pairs={{0,16},{16,0},{1,17},{17,1},{2,18},{18,2},{3,19},{19,3},{4,20},{20... | collective-permute-start | bytes 4718600 | tf_op jit(solution)/shard_map/ppermute | solution.py:991
  298.4 3.0 copy-start.20
  298.4 21.7 %copy-start.17 = (bf16[256,2048]{1,0:T(8,128)(2,1)}, bf16[256,2048]{1,0:T(8,128)(2,1)S(1)}, u32[]{:S(2)}) copy-start(bf16[256,2048]{1,0:T(8,128)(2,1)S(1)} %get-tuple-element.120) | copy-start | bytes 3145732
  298.4 3.0 copy-start.54
  298.4 3.0 copy-start.56
  306.9 3.7 copy-start.46
  307.0 5.4 %copy-start.30 = (bf16[1024,768]{1,0:T(8,128)(2,1)}, bf16[1024,768]{1,0:T(8,128)(2,1)S(1)}, u32[]{:S(2)}) copy-start(bf16[1024,768]{1,0:T(8,128)(2,1)S(1)} %collective-permute-done.7.refs_3_) | copy-start | bytes 4718596
  316.5 3.5 copy-start.4
  316.5 37.6 %collective-permute-start.9 = (bf16[1024,768]{1,0:T(8,128)(2,1)}, bf16[1024,768]{1,0:T(8,128)(2,1)}, u32[]{:S(2)}, u32[]{:S(2)}) collective-permute-start(bf16[1024,768]{1,0:T(8,128)(2,1)} %fusion.4.refs_1_), channel_id=1, source_target_pairs={{0,4},{4,0},{8,12},{12,8},{1,5},{5,1},{9,13},{13,9},{2,6},{6,2},{1... | collective-permute-start | bytes 4718600 | tf_op jit(solution)/shard_map/ppermute | solution.py:1115
  317.1 37.0 %collective-permute-start.10 = (bf16[1024,768]{1,0:T(8,128)(2,1)}, bf16[1024,768]{1,0:T(8,128)(2,1)}, u32[]{:S(2)}, u32[]{:S(2)}) collective-permute-start(bf16[1024,768]{1,0:T(8,128)(2,1)} %pad_maximum_fusion.4), channel_id=1, source_target_pairs={{0,16},{16,0},{1,17},{17,1},{2,18},{18,2},{3,19},{19,3},{4,20},{20... | collective-permute-start | bytes 4718600 | tf_op jit(solution)/shard_map/ppermute | solution.py:991
  343.6 6.7 %copy-start.7 = (bf16[8,64,256]{2,1,0:T(8,128)(2,1)S(1)}, bf16[8,64,256]{2,1,0:T(8,128)(2,1)}, u32[]{:S(2)}) copy-start(bf16[8,64,256]{2,1,0:T(8,128)(2,1)} %copy-done.6) | copy-start | bytes 786436
  348.4 4.1 copy-start.23
  348.4 4.1 copy-start.51
  348.4 4.1 copy-start.62
  348.4 64.0 %collective-permute-start.11 = (bf16[1024,768]{1,0:T(8,128)(2,1)}, bf16[1024,768]{1,0:T(8,128)(2,1)S(1)}, u32[]{:S(2)}, u32[]{:S(2)}) collective-permute-start(bf16[1024,768]{1,0:T(8,128)(2,1)} %fusion.5.refs_2_), channel_id=1, source_target_pairs={{0,4},{4,0},{8,12},{12,8},{1,5},{5,1},{9,13},{13,9},{2,6},{6,2},{1... | collective-permute-start | bytes 4718600 | tf_op jit(solution)/shard_map/ppermute | solution.py:1115
  350.2 3.9 copy-start.52
  352.3 3.9 copy-start.27
  352.3 6.3 %slice-start.4 = ((s8[8388608]{0:T(1024)(128)(4,1)}), s8[4194304]{0:T(1024)(128)(4,1)S(1)}, s32[]{:S(2)}) async-start(s8[8388608]{0:T(1024)(128)(4,1)} %bitcast.78), calls=%async_computation.4 | async-start | bytes 8388608
  356.2 2.5 slice-start.5
  361.9 50.5 %collective-permute-start.12 = (bf16[512,1024]{1,0:T(8,128)(2,1)S(1)}, bf16[512,1024]{1,0:T(8,128)(2,1)S(1)}, u32[]{:S(2)}, u32[]{:S(2)}) collective-permute-start(bf16[512,1024]{1,0:T(8,128)(2,1)S(1)} %slice.405), channel_id=1, source_target_pairs={{0,16},{16,0},{1,17},{17,1},{2,18},{18,2},{3,19},{19,3},{4,20},{20... | collective-permute-start | bytes 3145736 | tf_op jit(solution)/shard_map/ppermute | solution.py:991
  367.8 3.8 copy-start.25
  370.7 43.0 %copy-start.71 = (bf16[2048,768]{1,0:T(8,128)(2,1)S(1)}, bf16[2048,768]{1,0:T(8,128)(2,1)}, u32[]{:S(2)}) copy-start(bf16[2048,768]{1,0:T(8,128)(2,1)} %get-tuple-element.88) | copy-start | bytes 9437188
  370.7 123.3 %collective-permute-start.13 = (bf16[1024,768]{1,0:T(8,128)(2,1)S(1)}, bf16[1024,768]{1,0:T(8,128)(2,1)S(1)}, u32[]{:S(2)}, u32[]{:S(2)}) collective-permute-start(bf16[1024,768]{1,0:T(8,128)(2,1)S(1)} %pad_maximum_fusion.7), channel_id=1, source_target_pairs={{0,16},{16,0},{1,17},{17,1},{2,18},{18,2},{3,19},{19,3},{4,20},{20... | collective-permute-start | bytes 4718600 | tf_op jit(solution)/shard_map/ppermute | solution.py:991
  (28 other events, 41.9 us)

commit v7 on v6

--- a/solution.py
+++ b/solution.py
@@ -889,34 +889,42 @@
     )(cot_rows, *weights, gains, *hidden_weights)
 
 
-def place_blocks(table, pieces, wide, blocks, base=None):
+def place_blocks(table, pieces, wide, blocks, bases=None):
     count = len(pieces)
-    depth = pieces[0][0].shape[0]
-    tile = min(depth, 1024)
+    depth, width = pieces[0].shape
+    outs = width // wide
 
     def kernel(table_ref, *refs):
-        out_ref = refs[-1]
-        step = pl.program_id(1)
-        for k in range(count):
-            @pl.when(step == k)
-            def _(k=k):
-                out_ref[...] = refs[k][...].astype(F32)
-
+        which, step = pl.program_id(0), pl.program_id(1)
+        for o in range(outs):
+            for k in range(count):
+                @pl.when(jnp.logical_and(which == o, step == k))
+                def _(o=o, k=k):
+                    refs[len(refs) - outs + o][...] = refs[k][...].astype(F32)
+
+    def target(o):
+        def index(which, step, table_ref):
+            now = jnp.where(which < o, 0, jnp.where(which > o, count - 1, step))
+            return 0, table_ref[now]
+
+        return index
+
+    shape = jax.ShapeDtypeStruct((depth, blocks * wide), F32)
     return pl.pallas_call(
         kernel,
         grid_spec=pltpu.PrefetchScalarGridSpec(
             num_scalar_prefetch=1,
-            grid=(depth // tile, count),
+            grid=(outs, count),
             in_specs=[
-                pl.BlockSpec((tile, wide), lambda i, step, table_ref, at=at: (i, at))
-                for _, at in pieces
-            ]
-            + ([] if base is None else [HBM_SPEC]),
-            out_specs=pl.BlockSpec((tile, wide), lambda i, step, table_ref: (i, table_ref[step])),
+                pl.BlockSpec((depth, wide), lambda which, step, table_ref: (0, which))
+            ] * count
+            + [HBM_SPEC] * (0 if bases is None else outs),
+            out_specs=tuple(pl.BlockSpec((depth, wide), target(o)) for o in range(outs)),
         ),
-        out_shape=jax.ShapeDtypeStruct((depth, blocks * wide), F32),
-        input_output_aliases={} if base is None else {1 + count: 0},
-    )(table, *(array for array, _ in pieces), *(() if base is None else (base,)))
+        out_shape=(shape,) * outs,
+        input_output_aliases={} if bases is None else {1 + count + o: o for o in range(outs)},
+        compiler_params=pltpu.CompilerParams(vmem_limit_bytes=32 << 20),
+    )(table, *pieces, *(() if bases is None else bases))
 
 
 def transposed_grads(columns, widths, last):
@@ -1155,13 +1163,9 @@
         grad_kv, totals[3] = lax.optimization_barrier((grad_kv, totals[3]))
         swapped[3] = swap_ctx(totals[3])
         early = [totals[0], totals[2], totals[3], swapped[0]]
-        placed = [
-            place_blocks(
-                jnp.stack([table[0], table[2], table[3], table[5]]),
-                [(piece, block) for piece in early], unit, 8,
-            )
-            for block in range(3)
-        ]
+        placed = place_blocks(
+            jnp.stack([table[0], table[2], table[3], table[5]]), early, unit, 8
+        )
         others[4], placed, swapped[2], received[1], grad_out_half = lax.optimization_barrier(
             (others[4], placed, swapped[2], received[1], grad_out_half)
         )
@@ -1205,10 +1209,10 @@
         )
         totals[4] = summed(4, near_four)
 
-        def result(block):
-            pieces = [(piece, block) for piece in (totals[1], totals[4], swapped[2], swapped[3])]
-            late = jnp.stack([table[1], table[4], table[6], table[7]])
-            return place_blocks(late, pieces, unit, 8, placed[block])
+        late = jnp.stack([table[1], table[4], table[6], table[7]])
+        result = place_blocks(
+            late, [totals[1], totals[4], swapped[2], swapped[3]], unit, 8, placed
+        )
 
         return (
             own_first(output_rows)[None],
@@ -1219,9 +1223,9 @@
             grad_value,
             grad_out,
             gain_grads[1],
-            result(0),
-            result(1),
-            result(2),
+            result[0],
+            result[1],
+            result[2],
         )
 
     return local

time: 521 us -> 515 us (0.988)
  Pallas kernels: 322 us -> 302 us
  matrix products: 82.5 us -> 91.2 us
  waiting for transfers between devices: 8.46 us -> 16.2 us
    pallas_call x6 -> x2, Pallas kernels: 28.4 us -> 16.8 us  [place_blocks(): pl.pallas_call(kernel, grid_spec=pltpu.PrefetchScalarGridSpec(num_scalar_...]
    pallas_call x4, Pallas kernels: 205 us -> 197 us  [reduce_gather(): pl.pallas_call(kernel, out_shape=(jax.ShapeDtypeStruct((reach * block_row...]
    ppermute x3, waiting for transfers between devices: 1.48 us -> 9.5 us  [swap_ctx(): return lax.ppermute(total, 'ctx', swap_z)]
    dot_general x32, matrix products: 52.4 us -> 60.3 us  [contract(): lax.dot_general(left, right, (((left_dim,), (right_dim,)), ((), ())), pre...]
    unnamed x161 -> x113, local copies, waits for them, and re-layouts: 18.4 us -> 15.1 us
  transfers between devices with their start and end apart: 14 -> 14, of which waited for: 3 -> 3; matrix products, arithmetic and copies ran while one was open for 26% -> 27% of each run, Pallas kernels for 46% -> 44%
where the time goes in v7:
time: 515 us; the launch traced here: 508 us
  Pallas kernels  302 us (59%)
  matrix products  91.2 us (18%)
  other arithmetic  33.8 us (7%)
  local copies, waits for them, and re-layouts  33 us (6%)
  waiting for transfers between devices  16.2 us (3%)
  blocking collectives  15.4 us (3%)
  starting transfers between devices  14.3 us (3%)
    pallas_call x4, Pallas kernels, reduce_gather(): pl.pallas_call(kernel, out_shape=(jax.ShapeDtypeStruct((reach * block_row...  197 us
    pallas_call x1, Pallas kernels, opening(): pl.pallas_call(kernel, out_shape=(jax.ShapeDtypeStruct((ctx_size * block_...  66.2 us
    dot_general x32, matrix products, contract(): lax.dot_general(left, right, (((left_dim,), (right_dim,)), ((), ())), pre...  60.3 us
    pallas_call x2, Pallas kernels, place_blocks(): pl.pallas_call(kernel, grid_spec=pltpu.PrefetchScalarGridSpec(num_scalar_...  16.8 us
    dot_general x5, matrix products, forward(): both = jnp.dot(normed_all, pair_w, preferred_element_type=F32)  16.6 us
    all_gather x1, blocking collectives, local(): lax.all_gather(kv_own.reshape(2 * key_width, row_count).T, 'ctx', axis=0,...  15.4 us
    unnamed x113, local copies, waits for them, and re-layouts  15.1 us
    dot_general x5, matrix products, forward(): grad_hidden = jnp.dot(cot_all, down_w, preferred_element_type=F32)  13.6 us
  transfers between devices with their start and end apart: 14, of which 3 were waited for; matrix products, arithmetic and copies ran while one was open for 27% of the time, Pallas kernels for 44%

profile of v7, /device:TPU:0, one launch (start us, length us, event | category | flops | bytes accessed | tf_op | source)
XLA Modules:
  0.0 508.2 jit_solution(4286729272241559482)
XLA Ops:
  3.1 1.7 dynamic-slice_bitcast_fusion.1
  5.8 1.5 pad_maximum_fusion.2.cot_ref
  7.8 66.2 %shard_map.203 = (bf16[1024,4096]{1,0:T(8,128)(2,1)}, f32[2,1024]{1,0:T(2,128)S(1)}, bf16[2048,768]{1,0:T(8,128)(2,1)}, bf16[2048,512]{1,0:T(8,128)(2,1)S(1)}, b...) custom-call(bf16[256,4096]{1,0:T(8,128)(2,1)} %pad_maximum_fusion.2., ...), custom_call_target="tpu_custom_call" | custom-call | tf_op jit(solution)/shard_map/pallas_call | solution.py:874
  74.7 1.5 collective-permute-start.1
  76.5 3.0 fusion.67
  81.3 15.4 %all_gather.3 = bf16[1024,256]{0,1:T(8,128)(2,1)S(1)} all-gather(bf16[256,256]{0,1:T(8,128)(2,1)S(1)} %bitcast.82), channel_id=1, replica_groups=mesh['fsdp'=2,'ctx'=4,'tp'=4] {'ctx'}, dimensions={0}, use_global_device_ids=true | all-gather | bytes 655360 | tf_op jit(solution)/shard_map/all_gather | solution.py:1052
  101.5 7.7 %shard_map.204 = (bf16[8,64,256]{2,1,0:T(8,128)(2,1)S(1)}, f32[8,1,256]{2,1,0:T(1,128)S(1)}) custom-call(s32[2]{0:T(128)S(1)} %pad_add_fusion.bounds_ref, bf16[8,64,256]{2,1,0:T(8,128)(2,1)S(1)} %pad_maximum_fusion.27.query_ref, bf16[2,1024,64]{2,1,0:T(8,128)(2,1)S(1)} %get-tuple-element.197.key_ref, bf16[2,64,1024]{2,1,0:T(8,128)(2,1)S(1)} %bitcast.69), custom_call_target="tpu_custom_call" | custom-call | tf_op jit(solution)/shard_map/pallas_call | solution.py:72
  109.2 1.6 constant_dynamic-update-slice_fusion.3
  110.9 1.6 constant_dynamic-update-slice_fusion.1
  117.7 1.5 constant_dynamic-update-slice_fusion
  119.3 43.5 %shard_map.205 = (bf16[1024,2048]{1,0:T(8,128)(2,1)S(1)}, f32[64,2048]{1,0:T(8,128)S(1)}) custom-call(bf16[256,2048]{1,0:T(8,128)(2,1)S(1)} %convolution_convert_fusion.term_ref, bf16[256,2048]{1,0:T(8,128)(2,1)S(1)} %pad_maximum_fusion.12.refs_0_.refs_1_, f32[1,2048]{1,0:T(1,128)S(1)} %get-tuple-element.212.refs_1_.refs_2_), custom_call_target="tpu_custom_call" | custom-call | tf_op jit(solution)/shard_map/pallas_call | solution.py:786
  162.8 2.4 fusion.35
  165.3 1.7 multiply_convert_fusion.13
  169.1 1.3 pad_maximum_fusion.3
  171.2 1.6 collective-permute-start.3
  172.8 1.7 fusion.45
  174.5 2.6 fusion.55
  177.2 1.5 constant_dynamic-update-slice_fusion.2
  178.7 2.4 fusion.31
  181.1 2.0 multiply_convert_fusion.10
  187.8 1.9 pad_maximum_fusion
  193.2 2.8 fusion.78
  197.9 3.3 fusion.29
  201.2 2.8 constant_dynamic-update-slice_fusion.4
  204.0 5.3 %fusion.27 = f32[1024,512]{0,1:T(8,128)} fusion(bf16[1024,2048]{1,0:T(8,128)(2,1)S(1)} %get-tuple-element.101, bf16[2048,768]{1,0:T(8,128)(2,1)} %constant_dynamic-update-slice_fusion.4), kind=kOutput, calls=%fused_computation.45 | convolution fusion | flops 2147483648 | bytes 8388608 | tf_op jit(solution)/shard_map/dot_general | solution.py:1094
  209.3 4.0 multiply_convert_fusion.7
  216.8 1.5 constant_dynamic-update-slice_fusion.6
  218.3 2.4 fusion.23
  220.7 1.7 multiply_convert_fusion.3
  226.0 2.6 fusion.53
  228.7 5.4 %fusion.25 = f32[512,2048]{1,0:T(8,128)} fusion(bf16[2048,768]{1,0:T(8,128)(2,1)} %constant_dynamic-update-slice_fusion.4, s32[]{:T(128)S(6)} %select_n.43, bf16[1024,256]{0,1:T(8,128)(2,1)} %copy-done.41, bf16[1024,256]{0,1:T(8,128)(2,1)} %copy-done.42), kind=kOutput, calls=%fused_computation.43 | convolution fusion | flops 1074790400 | bytes 7340036 | tf_op jit(solution)/shard_map/dot_general | solution.py:19
  234.1 4.6 add_convert_fusion.term_ref
  238.7 5.9 %collective-permute-done.5 = bf16[1024,768]{1,0:T(8,128)(2,1)} collective-permute-done((bf16[1024,768]{1,0:T(8,128)(2,1)}, bf16[1024,768]{1,0:T(8,128)(2,1)}, u32[]{:S(2)}, u32[]{:S(2)}) %collective-permute-start.5) | collective-permute-done | bytes 1572896 | tf_op jit(solution)/shard_map/ppermute | solution.py:999
  244.6 2.2 fusion.3.refs_0_
  247.4 1.6 collective-permute-start.7
  249.0 1.5 collective-permute-start.8
  250.5 44.4 %shard_map.206 = (bf16[256,2048]{1,0:T(8,128)(2,1)S(1)}, f32[64,2048]{1,0:T(8,128)S(1)}, f32[1,2048]{1,0:T(1,128)S(1)}) custom-call(bf16[512,2048]{1,0:T(8,128)(2,1)S(1)} %add_convert_fusion.term_ref, f32[64,2048]{1,0:T(8,128)S(1)} %get-tuple-element.113.refs_0_, bf16[256,2048]{1,0:T(8,128)(2,1)S(1)} %pad_maximum_fusion.13.refs_1_, ...), custom_call_target="tpu_custom_call" | custom-call | tf_op jit(solution)/shard_map/pallas_call | solution.py:786
  294.9 2.4 fusion.43
  297.3 2.6 fusion.49
  299.9 2.1 fusion.75
  302.5 2.4 add_convert_fusion.1.term_ref
  305.0 3.2 fusion
  308.2 1.9 fusion.4.refs_1_
  310.2 3.0 fusion.2.refs_4_
  313.2 1.6 collective-permute-start.9
  314.8 1.5 collective-permute-start.10
  316.3 2.4 fusion.39
  319.5 9.6 %shard_map.207 = (f32[8,64,256]{2,1,0:T(8,128)S(1)}, bf16[4,64,1024]{2,1,0:T(8,128)(2,1)S(1)}) custom-call(s32[2]{0:T(128)S(1)} %pad_add_fusion.bounds_ref, bf16[8,64,256]{2,1,0:T(8,128)(2,1)S(1)} %pad_maximum_fusion.27.query_ref, bf16[2,1024,64]{2,1,0:T(8,128)(2,1)S(1)} %get-tuple-element.197.key_ref, bf16[2,64,1024]{2,1,0:T(8,128)(2,1)S(1)} %bitcast.68, ...), custom_call_target="tpu_custom_call" | custom-call | tf_op jit(solution)/shard_map/pallas_call | solution.py:112
  329.1 1.9 fusion.5.refs_2_
  332.4 8.5 %shard_map.208 = (f32[1024,2048]{1,0:T(8,128)}, f32[1024,2048]{1,0:T(8,128)}, f32[1024,2048]{1,0:T(8,128)}) custom-call(s32[4]{0:T(128)S(1)} %get-tuple-element.219.table_ref, bf16[1024,768]{1,0:T(8,128)(2,1)S(1)} %fusion.3.refs_0_, bf16[1024,768]{1,0:T(8,128)(2,1)S(1)} %fusion.4.refs_1_, bf16[1024,768]{1,0:T(8,128)(2,1)S(1)} %fusion.5.refs_2_, ...), custom_call_target="tpu_custom_call" | custom-call | tf_op jit(solution)/shard_map/pallas_call | solution.py:913
  341.0 9.5 %collective-permute-done.9.refs_2_ = bf16[1024,768]{1,0:T(8,128)(2,1)S(1)} collective-permute-done((bf16[1024,768]{1,0:T(8,128)(2,1)S(1)}, bf16[1024,768]{1,0:T(8,128)(2,1)S(1)}, u32[]{:S(2)}, u32[]{:S(2)}) %collective-permute-start.9) | collective-permute-done | bytes 1572896 | tf_op jit(solution)/shard_map/ppermute | solution.py:1123
  351.3 2.7 constant_dynamic-update-slice_fusion.8
  354.0 4.0 fusion.20
  358.0 4.2 multiply_convert_fusion.2
  362.2 2.4 fusion.37
  364.6 2.4 convolution_convert_fusion.7
  367.0 1.6 collective-permute-start.12
  371.3 1.9 pad_maximum_fusion.1
  374.3 1.8 add_convert_fusion.3.refs_0_
  376.7 32.5 %shard_map.209 = (bf16[256,2048]{1,0:T(8,128)(2,1)S(1)}, f32[256,256]{1,0:T(8,128)S(1)}) custom-call(bf16[512,2048]{1,0:T(8,128)(2,1)S(1)} %add_convert_fusion.1.term_ref, f32[64,2048]{1,0:T(8,128)S(1)} %get-tuple-element.113.refs_0_, bf16[256,1024]{1,0:T(8,128)(2,1)S(1)} %bitcast.70), custom_call_target="tpu_custom_call" | custom-call | tf_op jit(solution)/shard_map/pallas_call | solution.py:786
  411.7 76.1 %shard_map.210 = (bf16[256,2048]{1,0:T(8,128)(2,1)S(1)}, f32[1,2048]{1,0:T(1,128)}, bf16[768,1024]{1,0:T(8,128)(2,1)S(1)}, bf16[512,1024]{1,0:T(8,128)(2,1)S(1)}, f32[2,1024]{1,0:T(2,128)S(1)}) custom-call(bf16[256,2048]{1,0:T(8,128)(2,1)S(1)} %convolution_convert_fusion.1.term_ref, f32[64,2048]{1,0:T(8,128)S(1)} %get-tuple-element.152.refs_0_, ...), custom_call_target="tpu_custom_call" | custom-call | tf_op jit(solution)/shard_map/pallas_call | solution.py:786
  492.1 4.7 shard_map.211
  496.8 2.8 add_convert_fusion.2.refs_1_
  499.6 8.3 %shard_map.212 = (f32[1024,2048]{1,0:T(8,128)}, f32[1024,2048]{1,0:T(8,128)}, f32[1024,2048]{1,0:T(8,128)}) custom-call(s32[4]{0:T(128)S(1)} %get-tuple-element.220.table_ref, bf16[1024,768]{1,0:T(8,128)(2,1)S(1)} %add_convert_fusion.3.refs_0_, ...), custom_call_target="tpu_custom_call", output_to_operand_aliasing={{0}: (5, {}), {1}: (6, {}), {2}: (7, {})} | custom-call | tf_op jit(solution)/shard_map/pallas_call | solution.py:913
  (192 shorter events, 50.9 us)
Async XLA Ops:
  4.8 1.0 copy-start.29
  4.9 71.6 %copy-start.17 = (bf16[256,1024]{1,0:T(8,128)(2,1)}, bf16[256,1024]{1,0:T(8,128)(2,1)S(1)}, u32[]{:S(2)}) copy-start(bf16[256,1024]{1,0:T(8,128)(2,1)S(1)} %get-tuple-element.200) | copy-start | bytes 1572868
  4.9 71.6 %copy-start.19 = (bf16[256,1024]{1,0:T(8,128)(2,1)}, bf16[256,1024]{1,0:T(8,128)(2,1)S(1)}, u32[]{:S(2)}) copy-start(bf16[256,1024]{1,0:T(8,128)(2,1)S(1)} %get-tuple-element.201) | copy-start | bytes 1572868
  4.9 2.4 copy-start.12
  4.9 2.9 copy-start.13
  74.0 5.5 %copy-start.4 = (bf16[1024,768]{1,0:T(8,128)(2,1)}, bf16[1024,768]{1,0:T(8,128)(2,1)S(1)}, u32[]{:S(2)}) copy-start(bf16[1024,768]{1,0:T(8,128)(2,1)S(1)} %get-tuple-element.110) | copy-start | bytes 4718596
  74.0 5.5 %copy-start.6 = (bf16[1024,768]{1,0:T(8,128)(2,1)}, bf16[1024,768]{1,0:T(8,128)(2,1)S(1)}, u32[]{:S(2)}) copy-start(bf16[1024,768]{1,0:T(8,128)(2,1)S(1)} %get-tuple-element.108) | copy-start | bytes 4718596
  74.1 5.5 %copy-start.8 = (bf16[1024,768]{1,0:T(8,128)(2,1)}, bf16[1024,768]{1,0:T(8,128)(2,1)S(1)}, u32[]{:S(2)}) copy-start(bf16[1024,768]{1,0:T(8,128)(2,1)S(1)} %get-tuple-element.133) | copy-start | bytes 4718596
  74.1 40.9 %collective-permute-start = (bf16[1024,768]{1,0:T(8,128)(2,1)}, bf16[1024,768]{1,0:T(8,128)(2,1)}, u32[]{:S(2)}, u32[]{:S(2)}) collective-permute-start(bf16[1024,768]{1,0:T(8,128)(2,1)} %get-tuple-element.99), channel_id=1, source_target_pairs={{0,16},{16,0},{1,17},{17,1},{2,18},{18,2},{3,19},{19,3},{4,20},{20... | collective-permute-start | bytes 4718600 | tf_op jit(solution)/shard_map/ppermute | solution.py:999
  74.7 95.8 %collective-permute-start.1 = (bf16[1024,768]{1,0:T(8,128)(2,1)}, bf16[1024,768]{1,0:T(8,128)(2,1)}, u32[]{:S(2)}, u32[]{:S(2)}) collective-permute-start(bf16[1024,768]{1,0:T(8,128)(2,1)} %get-tuple-element.103), channel_id=1, source_target_pairs={{0,16},{16,0},{1,17},{17,1},{2,18},{18,2},{3,19},{19,3},{4,20},{20... | collective-permute-start | bytes 4718600 | tf_op jit(solution)/shard_map/ppermute | solution.py:999
  96.7 1.3 copy-start.26
  109.2 3.3 copy-start.9
  110.9 2.9 copy-start.18
  110.9 2.9 copy-start.20
  112.5 1.4 copy-start.28
  112.5 1.6 copy-start.30
  114.1 5.2 %copy-start = (bf16[256,2048]{1,0:T(8,128)(2,1)}, bf16[256,2048]{1,0:T(8,128)(2,1)S(1)}, u32[]{:S(2)}) copy-start(bf16[256,2048]{1,0:T(8,128)(2,1)S(1)} %pad_maximum_fusion.12.refs_0_.refs_1_) | copy-start | bytes 3145732
  114.1 1.8 copy-start.7
  117.2 84.1 %collective-permute-start.2 = (bf16[1024,768]{1,0:T(8,128)(2,1)S(1)}, bf16[1024,768]{1,0:T(8,128)(2,1)}, u32[]{:S(2)}, u32[]{:S(2)}) collective-permute-start(bf16[1024,768]{1,0:T(8,128)(2,1)S(1)} %copy-done.7), channel_id=1, source_target_pairs={{0,16},{16,0},{1,17},{17,1},{2,18},{18,2},{3,19},{19,3},{4,20},{20... | collective-permute-start | bytes 4718600 | tf_op jit(solution)/shard_map/ppermute | solution.py:999
  119.2 46.0 %copy-start.24 = (bf16[2048,768]{1,0:T(8,128)(2,1)}, bf16[2048,768]{1,0:T(8,128)(2,1)S(1)}, u32[]{:S(2)}) copy-start(bf16[2048,768]{1,0:T(8,128)(2,1)S(1)} %constant_dynamic-update-slice_fusion) | copy-start | bytes 9437188
  119.3 46.0 %slice-start = ((s8[8388608]{0:T(1024)(128)(4,1)}), s8[4194304]{0:T(1024)(128)(4,1)S(1)}, s32[]{:S(2)}) async-start(s8[8388608]{0:T(1024)(128)(4,1)} %bitcast.74), calls=%async_computation | async-start | bytes 8388608
  162.8 2.5 slice-start.1
  167.0 5.8 %copy-start.47 = (bf16[1024,256]{0,1:T(8,128)(2,1)}, bf16[1024,256]{0,1:T(8,128)(2,1)S(1)}, u32[]{:S(2)}) copy-start(bf16[1024,256]{0,1:T(8,128)(2,1)S(1)} %get-tuple-element.191) | copy-start | bytes 1572868
  167.0 7.5 %copy-start.39 = (bf16[1024,256]{0,1:T(8,128)(2,1)}, bf16[1024,256]{0,1:T(8,128)(2,1)S(1)}, u32[]{:S(2)}) copy-start(bf16[1024,256]{0,1:T(8,128)(2,1)S(1)} %get-tuple-element.186) | copy-start | bytes 1572868
  169.1 2.0 copy-start.5
  171.2 45.6 %collective-permute-start.3 = (bf16[1024,768]{1,0:T(8,128)(2,1)S(1)}, bf16[1024,768]{1,0:T(8,128)(2,1)}, u32[]{:S(2)}, u32[]{:S(2)}) collective-permute-start(bf16[1024,768]{1,0:T(8,128)(2,1)S(1)} %copy-done.5), channel_id=1, source_target_pairs={{0,16},{16,0},{1,17},{17,1},{2,18},{18,2},{3,19},{19,3},{4,20},{20... | collective-permute-start | bytes 4718600 | tf_op jit(solution)/shard_map/ppermute | solution.py:999
  177.2 39.6 %collective-permute-start.4 = (bf16[1024,768]{1,0:T(8,128)(2,1)}, bf16[1024,768]{1,0:T(8,128)(2,1)}, u32[]{:S(2)}, u32[]{:S(2)}) collective-permute-start(bf16[1024,768]{1,0:T(8,128)(2,1)} %collective-permute-done.1), channel_id=1, source_target_pairs={{0,4},{4,0},{8,12},{12,8},{1,5},{5,1},{9,13},{13,9},{2,6},{6,2},{1... | collective-permute-start | bytes 4718600 | tf_op jit(solution)/shard_map/ppermute | solution.py:1115
  178.7 14.3 %copy-start.22 = (bf16[2048,768]{1,0:T(8,128)(2,1)}, bf16[2048,768]{1,0:T(8,128)(2,1)S(1)}, u32[]{:S(2)}) copy-start(bf16[2048,768]{1,0:T(8,128)(2,1)S(1)} %constant_dynamic-update-slice_fusion.2) | copy-start | bytes 9437188
  187.3 57.3 %collective-permute-start.5 = (bf16[1024,768]{1,0:T(8,128)(2,1)}, bf16[1024,768]{1,0:T(8,128)(2,1)}, u32[]{:S(2)}, u32[]{:S(2)}) collective-permute-start(bf16[1024,768]{1,0:T(8,128)(2,1)} %pad_maximum_fusion.3), channel_id=1, source_target_pairs={{0,16},{16,0},{1,17},{17,1},{2,18},{18,2},{3,19},{19,3},{4,20},{20... | collective-permute-start | bytes 4718600 | tf_op jit(solution)/shard_map/ppermute | solution.py:999
  187.8 3.1 copy-start.48
  189.7 2.5 copy-start.25
  192.2 1.0 copy-start.50
  193.2 2.8 copy-start.40
  196.0 1.9 copy-start.23
  213.4 12.6 %copy-start.41 = (bf16[1024,256]{0,1:T(8,128)(2,1)}, bf16[1024,256]{0,1:T(8,128)(2,1)S(1)}, u32[]{:S(2)}) copy-start(bf16[1024,256]{0,1:T(8,128)(2,1)S(1)} %get-tuple-element.181) | copy-start | bytes 1572868
  213.4 12.6 %copy-start.42 = (bf16[1024,256]{0,1:T(8,128)(2,1)}, bf16[1024,256]{0,1:T(8,128)(2,1)S(1)}, u32[]{:S(2)}) copy-start(bf16[1024,256]{0,1:T(8,128)(2,1)S(1)} %get-tuple-element.182) | copy-start | bytes 1572868
  218.3 2.4 copy-start.21
  222.5 1.0 copy-start.37
  228.7 5.4 %copy-start.15 = (f32[512,2048]{1,0:T(8,128)S(1)}, f32[512,2048]{1,0:T(8,128)}, u32[]{:S(2)}) copy-start(f32[512,2048]{1,0:T(8,128)} %fusion.29) | copy-start | bytes 12582916
  228.7 5.4 %copy-start.38 = (bf16[1024,256]{0,1:T(8,128)(2,1)S(1)}, bf16[1024,256]{0,1:T(8,128)(2,1)}, u32[]{:S(2)}) copy-start(bf16[1024,256]{0,1:T(8,128)(2,1)} %copy-done.37) | copy-start | bytes 1572868
  234.1 10.5 %copy-start.31 = (f32[1024,512]{1,0:T(8,128)S(1)}, f32[1024,512]{1,0:T(8,128)}, u32[]{:S(2)}) copy-start(f32[1024,512]{1,0:T(8,128)} %fusion.55) | copy-start | bytes 6291460
  238.7 8.1 %copy-start.35 = (bf16[1024,768]{1,0:T(8,128)(2,1)S(1)}, bf16[1024,768]{1,0:T(8,128)(2,1)}, u32[]{:S(2)}) copy-start(bf16[1024,768]{1,0:T(8,128)(2,1)} %pad_maximum_fusion.5) | copy-start | bytes 4718596
  246.8 48.1 %copy-start.46 = (bf16[1024,256]{0,1:T(8,128)(2,1)S(1)}, bf16[1024,256]{0,1:T(8,128)(2,1)}, u32[]{:S(2)}) copy-start(bf16[1024,256]{0,1:T(8,128)(2,1)} %copy-done.45) | copy-start | bytes 1572868
  246.8 58.1 %collective-permute-start.6 = (bf16[1024,768]{1,0:T(8,128)(2,1)S(1)}, bf16[1024,768]{1,0:T(8,128)(2,1)}, u32[]{:S(2)}, u32[]{:S(2)}) collective-permute-start(bf16[1024,768]{1,0:T(8,128)(2,1)S(1)} %copy-done.35), channel_id=1, source_target_pairs={{0,16},{16,0},{1,17},{17,1},{2,18},{18,2},{3,19},{19,3},{4,20},{20... | collective-permute-start | bytes 4718600 | tf_op jit(solution)/shard_map/ppermute | solution.py:999
  247.4 57.6 %collective-permute-start.7 = (bf16[1024,768]{1,0:T(8,128)(2,1)S(1)}, bf16[1024,768]{1,0:T(8,128)(2,1)S(1)}, u32[]{:S(2)}, u32[]{:S(2)}) collective-permute-start(bf16[1024,768]{1,0:T(8,128)(2,1)S(1)} %fusion.3.refs_0_), channel_id=1, source_target_pairs={{0,4},{4,0},{8,12},{12,8},{1,5},{5,1},{9,13},{13,9},{2,6},{6,2},{1... | collective-permute-start | bytes 4718600 | tf_op jit(solution)/shard_map/ppermute | solution.py:1123
  249.0 80.1 %collective-permute-start.8 = (bf16[1024,768]{1,0:T(8,128)(2,1)}, bf16[1024,768]{1,0:T(8,128)(2,1)}, u32[]{:S(2)}, u32[]{:S(2)}) collective-permute-start(bf16[1024,768]{1,0:T(8,128)(2,1)} %pad_maximum_fusion.6), channel_id=1, source_target_pairs={{0,16},{16,0},{1,17},{17,1},{2,18},{18,2},{3,19},{19,3},{4,20},{20... | collective-permute-start | bytes 4718600 | tf_op jit(solution)/shard_map/ppermute | solution.py:999
  299.9 2.5 copy-start.14
  299.9 2.6 copy-start.44
  304.9 3.3 copy-start.32
  310.1 4.7 copy-start.34
  313.2 37.3 %collective-permute-start.9 = (bf16[1024,768]{1,0:T(8,128)(2,1)S(1)}, bf16[1024,768]{1,0:T(8,128)(2,1)S(1)}, u32[]{:S(2)}, u32[]{:S(2)}) collective-permute-start(bf16[1024,768]{1,0:T(8,128)(2,1)S(1)} %fusion.4.refs_1_), channel_id=1, source_target_pairs={{0,4},{4,0},{8,12},{12,8},{1,5},{5,1},{9,13},{13,9},{2,6},{6,2},{1... | collective-permute-start | bytes 4718600 | tf_op jit(solution)/shard_map/ppermute | solution.py:1123
  314.8 36.5 %collective-permute-start.10 = (bf16[1024,768]{1,0:T(8,128)(2,1)S(1)}, bf16[1024,768]{1,0:T(8,128)(2,1)}, u32[]{:S(2)}, u32[]{:S(2)}) collective-permute-start(bf16[1024,768]{1,0:T(8,128)(2,1)S(1)} %copy-done.34), channel_id=1, source_target_pairs={{0,16},{16,0},{1,17},{17,1},{2,18},{18,2},{3,19},{19,3},{4,20},{20... | collective-permute-start | bytes 4718600 | tf_op jit(solution)/shard_map/ppermute | solution.py:999
  318.7 10.4 %copy-start.33 = (f32[1024,512]{1,0:T(8,128)S(1)}, f32[1024,512]{1,0:T(8,128)}, u32[]{:S(2)}) copy-start(f32[1024,512]{1,0:T(8,128)} %fusion.49) | copy-start | bytes 6291460
  331.9 77.4 %collective-permute-start.11 = (bf16[1024,768]{1,0:T(8,128)(2,1)S(1)}, bf16[1024,768]{1,0:T(8,128)(2,1)S(1)}, u32[]{:S(2)}, u32[]{:S(2)}) collective-permute-start(bf16[1024,768]{1,0:T(8,128)(2,1)S(1)} %fusion.5.refs_2_), channel_id=1, source_target_pairs={{0,4},{4,0},{8,12},{12,8},{1,5},{5,1},{9,13},{13,9},{2,6},{6,2},{1... | collective-permute-start | bytes 4718600 | tf_op jit(solution)/shard_map/ppermute | solution.py:1123
  350.5 7.5 %copy-start.2 = (bf16[1024,768]{1,0:T(8,128)(2,1)}, bf16[1024,768]{1,0:T(8,128)(2,1)S(1)}, u32[]{:S(2)}) copy-start(bf16[1024,768]{1,0:T(8,128)(2,1)S(1)} %collective-permute-done.9.refs_2_) | copy-start | bytes 4718596
  367.0 42.3 %collective-permute-start.12 = (bf16[512,1024]{1,0:T(8,128)(2,1)S(1)}, bf16[512,1024]{1,0:T(8,128)(2,1)S(1)}, u32[]{:S(2)}, u32[]{:S(2)}) collective-permute-start(bf16[512,1024]{1,0:T(8,128)(2,1)S(1)} %slice.405), channel_id=1, source_target_pairs={{0,16},{16,0},{1,17},{17,1},{2,18},{18,2},{3,19},{19,3},{4,20},{20... | collective-permute-start | bytes 3145736 | tf_op jit(solution)/shard_map/ppermute | solution.py:999
  371.3 3.0 copy-start.16
  376.1 33.3 %copy-start.51 = (bf16[2048,768]{1,0:T(8,128)(2,1)S(1)}, bf16[2048,768]{1,0:T(8,128)(2,1)}, u32[]{:S(2)}) copy-start(bf16[2048,768]{1,0:T(8,128)(2,1)} %get-tuple-element.94) | copy-start | bytes 9437188
  376.1 114.8 %collective-permute-start.13 = (bf16[1024,768]{1,0:T(8,128)(2,1)S(1)}, bf16[1024,768]{1,0:T(8,128)(2,1)S(1)}, u32[]{:S(2)}, u32[]{:S(2)}) collective-permute-start(bf16[1024,768]{1,0:T(8,128)(2,1)S(1)} %pad_maximum_fusion.7), channel_id=1, source_target_pairs={{0,16},{16,0},{1,17},{17,1},{2,18},{18,2},{3,19},{19,3},{4,20},{20... | collective-permute-start | bytes 4718600 | tf_op jit(solution)/shard_map/ppermute | solution.py:999
  410.5 1.2 copy-start.1
  487.8 2.1 copy-start.10
  487.8 2.1 copy-start.11
  490.9 1.1 copy-start.36
  496.8 2.8 copy-start.3
  (4 other events, 3.2 us)

commit v8 on v7

--- a/solution.py
+++ b/solution.py
@@ -955,6 +955,28 @@
     return jnp.mean(rows * rows, axis=-1, keepdims=True)
 
 
+def normalize_rows(rows, gain):
+    count, width = rows.shape[0], rows.shape[1] // 2
+    tile = min(count, 256)
+
+    def kernel(row_ref, gain_ref, out_ref):
+        values = row_ref[...].astype(F32)
+        out_ref[...] = (
+            values * lax.rsqrt(mean_square(values) + EPSILON) * gain_ref[...]
+        ).astype(BF16)
+
+    return pl.pallas_call(
+        kernel,
+        grid=(count // tile,),
+        in_specs=[
+            pl.BlockSpec((tile, width), lambda i: (i, 1)),
+            pl.BlockSpec((1, width), lambda i: (0, 0)),
+        ],
+        out_specs=pl.BlockSpec((tile, width), lambda i: (i, 0)),
+        out_shape=jax.ShapeDtypeStruct((count, width), BF16),
+    )(rows, gain)
+
+
 def finish_middle(total, start, resid_ref, gain_ref, middle_ref):
     rows = total.shape[0]
     middle = resid_ref[pl.ds(start, rows), :].astype(F32) + total
@@ -1141,11 +1163,8 @@
         received[1] = swap_rows(fars[1])
         totals[2] = summed(2)
         near_one = near_of(1)
-        residual_all = rows_all[:, model_width:].astype(F32)
-        rms_all = lax.rsqrt(jnp.mean(residual_all * residual_all, axis=-1, keepdims=True) + EPSILON)
-        norm_all = (residual_all * rms_all * gain_first).astype(BF16)
-        branch_low, totals[2], near_one, norm_all = lax.optimization_barrier(
-            (branch_low, totals[2], near_one, norm_all)
+        branch_low, totals[2], near_one = lax.optimization_barrier(
+            (branch_low, totals[2], near_one)
         )
         swapped[2] = swap_ctx(totals[2])
         grad_out = jnp.dot(attended_flat, branch_low, preferred_element_type=F32)
@@ -1166,6 +1185,9 @@
         placed = place_blocks(
             jnp.stack([table[0], table[2], table[3], table[5]]), early, unit, 8
         )
+        grad_kv, rows_all = lax.optimization_barrier((grad_kv, rows_all))
+        norm_all = normalize_rows(rows_all, gain_first[None])
+        placed, norm_all = lax.optimization_barrier((placed, norm_all))
         others[4], placed, swapped[2], received[1], grad_out_half = lax.optimization_barrier(
             (others[4], placed, swapped[2], received[1], grad_out_half)
         )

time: 515 us -> 510 us (level)
  Pallas kernels: 302 us -> 311 us
  waiting for transfers between devices: 16.2 us -> 8.53 us
  local copies, waits for them, and re-layouts: 33 us -> 39.6 us
  matrix products: 91.2 us -> 84.7 us
  other arithmetic: 33.8 us -> 27.6 us
    ppermute x3, waiting for transfers between devices: 9.5 us -> 0.01 us  [swap_ctx(): return lax.ppermute(total, 'ctx', swap_z)]
    unnamed x113 -> x149, local copies, waits for them, and re-layouts: 15.1 us -> 23.3 us
    dot_general x32, matrix products: 60.3 us -> 54.7 us  [contract(): lax.dot_general(left, right, (((left_dim,), (right_dim,)), ((), ())), pre...]
    pallas_call x0 -> x1, Pallas kernels: none -> 5.44 us  [normalize_rows(): pl.pallas_call(kernel, grid=(count // tile,), in_specs=[pl.BlockSpec((til...]
  transfers between devices with their start and end apart: 14 -> 14, of which waited for: 3 -> 3; matrix products, arithmetic and copies ran while one was open for 27% -> 25% of each run, Pallas kernels for 44% -> 46%
where the time goes in v8:
time: 510 us; the launch traced here: 503 us
  Pallas kernels  311 us (61%)
  matrix products  84.7 us (17%)
  local copies, waits for them, and re-layouts  39.6 us (8%)
  other arithmetic  27.6 us (5%)
  blocking collectives  15 us (3%)
  starting transfers between devices  14.1 us (3%)
  waiting for transfers between devices  8.53 us (2%)
    pallas_call x4, Pallas kernels, reduce_gather(): pl.pallas_call(kernel, out_shape=(jax.ShapeDtypeStruct((reach * block_row...  197 us
    pallas_call x1, Pallas kernels, opening(): pl.pallas_call(kernel, out_shape=(jax.ShapeDtypeStruct((ctx_size * block_...  66.2 us
    dot_general x32, matrix products, contract(): lax.dot_general(left, right, (((left_dim,), (right_dim,)), ((), ())), pre...  54.7 us
    unnamed x149, local copies, waits for them, and re-layouts  23.3 us
    pallas_call x2, Pallas kernels, place_blocks(): pl.pallas_call(kernel, grid_spec=pltpu.PrefetchScalarGridSpec(num_scalar_...  20.3 us
    all_gather x1, blocking collectives, local(): lax.all_gather(kv_own.reshape(2 * key_width, row_count).T, 'ctx', axis=0,...  15 us
    dot_general x5, matrix products, forward(): both = jnp.dot(normed_all, pair_w, preferred_element_type=F32)  14.8 us
    dot_general x5, matrix products, forward(): grad_hidden = jnp.dot(cot_all, down_w, preferred_element_type=F32)  14.4 us
  transfers between devices with their start and end apart: 14, of which 3 were waited for; matrix products, arithmetic and copies ran while one was open for 25% of the time, Pallas kernels for 46%

profile of v8, /device:TPU:0, one launch (start us, length us, event | category | flops | bytes accessed | tf_op | source)
XLA Modules:
  0.0 503.4 jit_solution(1072559258214015139)
XLA Ops:
  3.1 1.7 dynamic-slice_bitcast_fusion.1
  4.9 1.5 pad_maximum_fusion.2.cot_ref
  7.7 66.2 %shard_map.203 = (bf16[1024,4096]{1,0:T(8,128)(2,1)}, f32[2,1024]{1,0:T(2,128)S(1)}, bf16[2048,768]{1,0:T(8,128)(2,1)}, bf16[2048,512]{1,0:T(8,128)(2,1)S(1)}, b...) custom-call(bf16[256,4096]{1,0:T(8,128)(2,1)} %pad_maximum_fusion.2., ...), custom_call_target="tpu_custom_call" | custom-call | tf_op jit(solution)/shard_map/pallas_call | solution.py:874
  74.6 1.5 collective-permute-start.1
  76.5 3.0 fusion.64
  81.3 15.0 %all_gather.3 = bf16[1024,256]{0,1:T(8,128)(2,1)S(1)} all-gather(bf16[256,256]{0,1:T(8,128)(2,1)S(1)} %bitcast.83), channel_id=1, replica_groups=mesh['fsdp'=2,'ctx'=4,'tp'=4] {'ctx'}, dimensions={0}, use_global_device_ids=true | all-gather | bytes 655360 | tf_op jit(solution)/shard_map/all_gather | solution.py:1074
  97.7 2.1 fusion.115
  101.9 7.6 %shard_map.204 = (bf16[8,64,256]{2,1,0:T(8,128)(2,1)S(1)}, f32[8,1,256]{2,1,0:T(1,128)S(1)}) custom-call(s32[2]{0:T(128)S(1)} %pad_add_fusion.bounds_ref, bf16[8,64,256]{2,1,0:T(8,128)(2,1)S(1)} %pad_maximum_fusion.27.query_ref, bf16[2,1024,64]{2,1,0:T(8,128)(2,1)S(1)} %get-tuple-element.207.key_ref, bf16[2,64,1024]{2,1,0:T(8,128)(2,1)S(1)} %bitcast.69), custom_call_target="tpu_custom_call" | custom-call | tf_op jit(solution)/shard_map/pallas_call | solution.py:72
  109.6 1.6 constant_dynamic-update-slice_fusion.3
  111.2 1.6 constant_dynamic-update-slice_fusion.1
  118.0 1.5 constant_dynamic-update-slice_fusion
  119.6 44.5 %shard_map.205 = (bf16[1024,2048]{1,0:T(8,128)(2,1)S(1)}, f32[64,2048]{1,0:T(8,128)S(1)}) custom-call(bf16[256,2048]{1,0:T(8,128)(2,1)S(1)} %convolution_convert_fusion.term_ref, bf16[256,2048]{1,0:T(8,128)(2,1)S(1)} %pad_maximum_fusion.12.refs_0_.refs_1_, f32[1,2048]{1,0:T(1,128)S(1)} %get-tuple-element.222.refs_1_.refs_2_), custom_call_target="tpu_custom_call" | custom-call | tf_op jit(solution)/shard_map/pallas_call | solution.py:786
  164.1 2.4 fusion.32
  167.8 1.7 multiply_convert_fusion.13
  173.7 1.6 collective-permute-start.3
  175.3 1.8 fusion.42
  177.1 2.6 fusion.52
  179.7 1.5 constant_dynamic-update-slice_fusion.2
  181.3 2.4 fusion.28
  183.7 1.9 multiply_convert_fusion.10
  190.4 1.9 pad_maximum_fusion
  198.9 1.5 constant_dynamic-update-slice_fusion.4
  200.5 3.8 fusion.24
  204.2 4.7 multiply_convert_fusion.7
  209.0 2.7 convolution_convert_fusion.9
  214.3 2.1 collective-permute-done.4
  216.4 1.5 constant_dynamic-update-slice_fusion.6
  218.0 3.8 fusion.20
  221.7 4.5 multiply_convert_fusion.3
  226.2 2.9 convolution_convert_fusion.8
  231.7 2.6 fusion.50
  234.4 3.8 fusion.22
  238.1 4.5 add_convert_fusion.term_ref
  242.7 1.8 collective-permute-done.5
  244.5 2.5 fusion.refs_0_
  247.1 1.4 collective-permute-start.6
  249.3 1.5 collective-permute-start.8
  250.7 44.4 %shard_map.206 = (bf16[256,2048]{1,0:T(8,128)(2,1)S(1)}, f32[64,2048]{1,0:T(8,128)S(1)}, f32[1,2048]{1,0:T(1,128)S(1)}) custom-call(bf16[512,2048]{1,0:T(8,128)(2,1)S(1)} %add_convert_fusion.term_ref, f32[64,2048]{1,0:T(8,128)S(1)} %get-tuple-element.118.refs_0_, bf16[256,2048]{1,0:T(8,128)(2,1)S(1)} %pad_maximum_fusion.13.refs_1_, ...), custom_call_target="tpu_custom_call" | custom-call | tf_op jit(solution)/shard_map/pallas_call | solution.py:786
  295.2 2.9 fusion.40
  299.5 2.0 fusion.72
  301.6 2.3 add_convert_fusion.1.term_ref
  303.9 1.7 fusion.1.refs_1_
  305.6 1.6 collective-permute-start.9
  307.2 1.5 collective-permute-start.10
  308.7 2.3 fusion.36
  312.1 9.6 %shard_map.207 = (f32[8,64,256]{2,1,0:T(8,128)S(1)}, bf16[4,64,1024]{2,1,0:T(8,128)(2,1)S(1)}) custom-call(s32[2]{0:T(128)S(1)} %pad_add_fusion.bounds_ref, bf16[8,64,256]{2,1,0:T(8,128)(2,1)S(1)} %pad_maximum_fusion.27.query_ref, bf16[2,1024,64]{2,1,0:T(8,128)(2,1)S(1)} %get-tuple-element.207.key_ref, bf16[2,64,1024]{2,1,0:T(8,128)(2,1)S(1)} %bitcast.68, ...), custom_call_target="tpu_custom_call" | custom-call | tf_op jit(solution)/shard_map/pallas_call | solution.py:112
  323.3 1.6 fusion.2.refs_2_
  324.9 5.4 %shard_map.209.refs_4_ = bf16[1024,2048]{1,0:T(8,128)(2,1)} custom-call(bf16[1024,4096]{1,0:T(8,128)(2,1)} %get-tuple-element.147.row_ref, f32[1,2048]{1,0:T(1,128)} %copy-done.34), custom_call_target="tpu_custom_call" | custom-call | tf_op jit(solution)/shard_map/pallas_call | solution.py:968
  330.8 1.4 copy-done.5
  332.2 1.4 copy-done.6
  333.6 1.4 copy-done.22
  335.0 10.2 %shard_map.208 = (f32[1024,2048]{1,0:T(8,128)}, f32[1024,2048]{1,0:T(8,128)}, f32[1024,2048]{1,0:T(8,128)}) custom-call(s32[4]{0:T(128)S(1)} %get-tuple-element.229.table_ref, bf16[1024,768]{1,0:T(8,128)(2,1)S(1)} %copy-done.5, bf16[1024,768]{1,0:T(8,128)(2,1)} %fusion.1.refs_1_, bf16[1024,768]{1,0:T(8,128)(2,1)S(1)} %copy-done.6, ...), custom_call_target="tpu_custom_call" | custom-call | tf_op jit(solution)/shard_map/pallas_call | solution.py:913
  346.4 4.6 collective-permute-done.10
  350.9 1.5 constant_dynamic-update-slice_fusion.8
  352.5 2.4 fusion.17
  354.9 1.7 multiply_convert_fusion.2
  362.0 1.9 pad_maximum_fusion.1
  365.0 3.1 add_convert_fusion.3.refs_0_
  369.1 32.6 %shard_map.210 = (bf16[256,2048]{1,0:T(8,128)(2,1)S(1)}, f32[256,256]{1,0:T(8,128)S(1)}) custom-call(bf16[512,2048]{1,0:T(8,128)(2,1)S(1)} %add_convert_fusion.1.term_ref, f32[64,2048]{1,0:T(8,128)S(1)} %get-tuple-element.118.refs_0_, bf16[256,1024]{1,0:T(8,128)(2,1)S(1)} %bitcast.70), custom_call_target="tpu_custom_call" | custom-call | tf_op jit(solution)/shard_map/pallas_call | solution.py:786
  404.3 1.8 copy-done
  406.1 75.6 %shard_map.211 = (bf16[256,2048]{1,0:T(8,128)(2,1)S(1)}, f32[1,2048]{1,0:T(1,128)}, bf16[768,1024]{1,0:T(8,128)(2,1)S(1)}, bf16[512,1024]{1,0:T(8,128)(2,1)S(1)}, f32[2,1024]{1,0:T(2,128)S(1)}) custom-call(bf16[256,2048]{1,0:T(8,128)(2,1)S(1)} %convolution_convert_fusion.1.term_ref, f32[64,2048]{1,0:T(8,128)S(1)} %copy-done.29, ...), custom_call_target="tpu_custom_call" | custom-call | tf_op jit(solution)/shard_map/pallas_call | solution.py:786
  486.0 4.7 shard_map.212
  490.8 1.9 add_convert_fusion.2.refs_1_
  493.1 10.1 %shard_map.213 = (f32[1024,2048]{1,0:T(8,128)}, f32[1024,2048]{1,0:T(8,128)}, f32[1024,2048]{1,0:T(8,128)}) custom-call(s32[4]{0:T(128)S(1)} %get-tuple-element.230.table_ref, bf16[1024,768]{1,0:T(8,128)(2,1)S(1)} %copy-done.3, bf16[1024,768]{1,0:T(8,128)(2,1)S(1)} %add_convert_fusion.2.refs_1_, ...), custom_call_target="tpu_custom_call", output_to_operand_aliasing={{0}: (5, {}), {1}: (6, {}), {2}: (7, {})} | custom-call | tf_op jit(solution)/shard_map/pallas_call | solution.py:913
  (227 shorter events, 57.5 us)
Async XLA Ops:
  4.8 69.1 %copy-start.48 = (bf16[256,1024]{1,0:T(8,128)(2,1)}, bf16[256,1024]{1,0:T(8,128)(2,1)S(1)}, u32[]{:S(2)}) copy-start(bf16[256,1024]{1,0:T(8,128)(2,1)S(1)} %get-tuple-element.231) | copy-start | bytes 1572868
  4.8 69.1 %copy-start.50 = (bf16[256,1024]{1,0:T(8,128)(2,1)}, bf16[256,1024]{1,0:T(8,128)(2,1)S(1)}, u32[]{:S(2)}) copy-start(bf16[256,1024]{1,0:T(8,128)(2,1)S(1)} %get-tuple-element.232) | copy-start | bytes 1572868
  4.9 71.6 %copy-start.40 = (bf16[256,1024]{1,0:T(8,128)(2,1)}, bf16[256,1024]{1,0:T(8,128)(2,1)S(1)}, u32[]{:S(2)}) copy-start(bf16[256,1024]{1,0:T(8,128)(2,1)S(1)} %get-tuple-element.211) | copy-start | bytes 1572868
  4.9 2.8 copy-start.27
  74.0 5.5 %copy-start.14 = (bf16[1024,768]{1,0:T(8,128)(2,1)}, bf16[1024,768]{1,0:T(8,128)(2,1)S(1)}, u32[]{:S(2)}) copy-start(bf16[1024,768]{1,0:T(8,128)(2,1)S(1)} %get-tuple-element.115) | copy-start | bytes 4718596
  74.0 5.5 %copy-start.16 = (bf16[1024,768]{1,0:T(8,128)(2,1)}, bf16[1024,768]{1,0:T(8,128)(2,1)S(1)}, u32[]{:S(2)}) copy-start(bf16[1024,768]{1,0:T(8,128)(2,1)S(1)} %get-tuple-element.113) | copy-start | bytes 4718596
  74.0 5.5 %copy-start.18 = (bf16[1024,768]{1,0:T(8,128)(2,1)}, bf16[1024,768]{1,0:T(8,128)(2,1)S(1)}, u32[]{:S(2)}) copy-start(bf16[1024,768]{1,0:T(8,128)(2,1)S(1)} %get-tuple-element.139) | copy-start | bytes 4718596
  74.0 40.5 %copy-start.7 = (bf16[2048,512]{1,0:T(8,128)(2,1)}, bf16[2048,512]{1,0:T(8,128)(2,1)S(1)}, u32[]{:S(2)}) copy-start(bf16[2048,512]{1,0:T(8,128)(2,1)S(1)} %get-tuple-element.102) | copy-start | bytes 6291460
  74.0 41.3 %collective-permute-start = (bf16[1024,768]{1,0:T(8,128)(2,1)}, bf16[1024,768]{1,0:T(8,128)(2,1)}, u32[]{:S(2)}, u32[]{:S(2)}) collective-permute-start(bf16[1024,768]{1,0:T(8,128)(2,1)} %get-tuple-element.104), channel_id=1, source_target_pairs={{0,16},{16,0},{1,17},{17,1},{2,18},{18,2},{3,19},{19,3},{4,20},{20... | collective-permute-start | bytes 4718600 | tf_op jit(solution)/shard_map/ppermute | solution.py:1021
  74.6 98.3 %collective-permute-start.1 = (bf16[1024,768]{1,0:T(8,128)(2,1)}, bf16[1024,768]{1,0:T(8,128)(2,1)}, u32[]{:S(2)}, u32[]{:S(2)}) collective-permute-start(bf16[1024,768]{1,0:T(8,128)(2,1)} %get-tuple-element.108), channel_id=1, source_target_pairs={{0,16},{16,0},{1,17},{17,1},{2,18},{18,2},{3,19},{19,3},{4,20},{20... | collective-permute-start | bytes 4718600 | tf_op jit(solution)/shard_map/ppermute | solution.py:1021
  76.4 3.1 copy-start.34
  109.5 5.0 %copy-start.10 = (bf16[8,64,256]{2,1,0:T(8,128)(2,1)}, bf16[8,64,256]{2,1,0:T(8,128)(2,1)S(1)}, u32[]{:S(2)}) copy-start(bf16[8,64,256]{2,1,0:T(8,128)(2,1)S(1)} %get-tuple-element.101) | copy-start | bytes 786436
  109.6 3.2 copy-start.19
  111.2 2.9 copy-start.41
  114.5 5.1 %copy-start.1 = (bf16[256,2048]{1,0:T(8,128)(2,1)}, bf16[256,2048]{1,0:T(8,128)(2,1)S(1)}, u32[]{:S(2)}) copy-start(bf16[256,2048]{1,0:T(8,128)(2,1)S(1)} %pad_maximum_fusion.12.refs_0_.refs_1_) | copy-start | bytes 3145732
  117.5 80.9 %collective-permute-start.2 = (bf16[1024,768]{1,0:T(8,128)(2,1)S(1)}, bf16[1024,768]{1,0:T(8,128)(2,1)}, u32[]{:S(2)}, u32[]{:S(2)}) collective-permute-start(bf16[1024,768]{1,0:T(8,128)(2,1)S(1)} %copy-done.17), channel_id=1, source_target_pairs={{0,16},{16,0},{1,17},{17,1},{2,18},{18,2},{3,19},{19,3},{4,20},{20... | collective-permute-start | bytes 4718600 | tf_op jit(solution)/shard_map/ppermute | solution.py:1021
  119.6 47.0 %slice-start = ((s8[8388608]{0:T(1024)(128)(4,1)}), s8[4194304]{0:T(1024)(128)(4,1)S(1)}, s32[]{:S(2)}) async-start(s8[8388608]{0:T(1024)(128)(4,1)} %bitcast.73), calls=%async_computation | async-start | bytes 8388608
  164.1 134.1 %copy-start.36 = (bf16[1024,2048]{1,0:T(8,128)(2,1)}, bf16[1024,2048]{1,0:T(8,128)(2,1)S(1)}, u32[]{:S(2)}) copy-start(bf16[1024,2048]{1,0:T(8,128)(2,1)S(1)} %get-tuple-element.106) | copy-start | bytes 12582916
  164.1 3.7 slice-start.1
  173.7 40.6 %collective-permute-start.3 = (bf16[1024,768]{1,0:T(8,128)(2,1)S(1)}, bf16[1024,768]{1,0:T(8,128)(2,1)}, u32[]{:S(2)}, u32[]{:S(2)}) collective-permute-start(bf16[1024,768]{1,0:T(8,128)(2,1)S(1)} %copy-done.15), channel_id=1, source_target_pairs={{0,16},{16,0},{1,17},{17,1},{2,18},{18,2},{3,19},{19,3},{4,20},{20... | collective-permute-start | bytes 4718600 | tf_op jit(solution)/shard_map/ppermute | solution.py:1021
  179.7 36.7 %collective-permute-start.4 = (bf16[1024,768]{1,0:T(8,128)(2,1)}, bf16[1024,768]{1,0:T(8,128)(2,1)}, u32[]{:S(2)}, u32[]{:S(2)}) collective-permute-start(bf16[1024,768]{1,0:T(8,128)(2,1)} %collective-permute-done.1), channel_id=1, source_target_pairs={{0,4},{4,0},{8,12},{12,8},{1,5},{5,1},{9,13},{13,9},{2,6},{6,2},{1... | collective-permute-start | bytes 4718600 | tf_op jit(solution)/shard_map/ppermute | solution.py:1137
  181.3 13.1 %copy-start.45 = (bf16[2048,768]{1,0:T(8,128)(2,1)}, bf16[2048,768]{1,0:T(8,128)(2,1)S(1)}, u32[]{:S(2)}) copy-start(bf16[2048,768]{1,0:T(8,128)(2,1)S(1)} %constant_dynamic-update-slice_fusion.2) | copy-start | bytes 9437188
  189.9 54.7 %collective-permute-start.5 = (bf16[1024,768]{1,0:T(8,128)(2,1)}, bf16[1024,768]{1,0:T(8,128)(2,1)}, u32[]{:S(2)}, u32[]{:S(2)}) collective-permute-start(bf16[1024,768]{1,0:T(8,128)(2,1)} %pad_maximum_fusion.3), channel_id=1, source_target_pairs={{0,16},{16,0},{1,17},{17,1},{2,18},{18,2},{3,19},{19,3},{4,20},{20... | collective-permute-start | bytes 4718600 | tf_op jit(solution)/shard_map/ppermute | solution.py:1021
  200.5 33.9 %copy-start.44 = (bf16[2048,768]{1,0:T(8,128)(2,1)}, bf16[2048,768]{1,0:T(8,128)(2,1)S(1)}, u32[]{:S(2)}) copy-start(bf16[2048,768]{1,0:T(8,128)(2,1)S(1)} %constant_dynamic-update-slice_fusion.4) | copy-start | bytes 9437188
  208.9 2.8 copy-start.65
  209.0 2.8 copy-start.61
  217.9 3.8 copy-start.42
  226.2 3.0 copy-start.63
  226.2 11.9 %copy-start.57 = (bf16[1024,256]{0,1:T(8,128)(2,1)}, bf16[1024,256]{0,1:T(8,128)(2,1)S(1)}, u32[]{:S(2)}) copy-start(bf16[1024,256]{0,1:T(8,128)(2,1)S(1)} %get-tuple-element.189) | copy-start | bytes 1572868
  226.2 11.9 %copy-start.59 = (bf16[1024,256]{0,1:T(8,128)(2,1)}, bf16[1024,256]{0,1:T(8,128)(2,1)S(1)}, u32[]{:S(2)}) copy-start(bf16[1024,256]{0,1:T(8,128)(2,1)S(1)} %get-tuple-element.190) | copy-start | bytes 1572868
  238.1 6.4 %copy-start.55 = (f32[1024,256]{1,0:T(8,128)S(1)}, f32[1024,256]{1,0:T(8,128)}, u32[]{:S(2)}) copy-start(f32[1024,256]{1,0:T(8,128)} %fusion.42) | copy-start | bytes 3145732
  242.7 6.6 %copy-start.53 = (bf16[1024,768]{1,0:T(8,128)(2,1)S(1)}, bf16[1024,768]{1,0:T(8,128)(2,1)}, u32[]{:S(2)}) copy-start(bf16[1024,768]{1,0:T(8,128)(2,1)} %pad_maximum_fusion.6) | copy-start | bytes 4718596
  247.1 51.1 %copy-start.4 = (bf16[1024,768]{1,0:T(8,128)(2,1)}, bf16[1024,768]{1,0:T(8,128)(2,1)S(1)}, u32[]{:S(2)}) copy-start(bf16[1024,768]{1,0:T(8,128)(2,1)S(1)} %fusion.refs_0_) | copy-start | bytes 4718596
  247.1 48.1 %copy-start.66 = (bf16[1024,256]{0,1:T(8,128)(2,1)S(1)}, bf16[1024,256]{0,1:T(8,128)(2,1)}, u32[]{:S(2)}) copy-start(bf16[1024,256]{0,1:T(8,128)(2,1)} %copy-done.65) | copy-start | bytes 1572868
  247.1 56.8 %collective-permute-start.6 = (bf16[1024,768]{1,0:T(8,128)(2,1)}, bf16[1024,768]{1,0:T(8,128)(2,1)S(1)}, u32[]{:S(2)}, u32[]{:S(2)}) collective-permute-start(bf16[1024,768]{1,0:T(8,128)(2,1)} %pad_maximum_fusion.5), channel_id=1, source_target_pairs={{0,16},{16,0},{1,17},{17,1},{2,18},{18,2},{3,19},{19,3},{4,20},{20... | collective-permute-start | bytes 4718600 | tf_op jit(solution)/shard_map/ppermute | solution.py:1021
  248.4 55.5 %collective-permute-start.7 = (bf16[1024,768]{1,0:T(8,128)(2,1)S(1)}, bf16[1024,768]{1,0:T(8,128)(2,1)S(1)}, u32[]{:S(2)}, u32[]{:S(2)}) collective-permute-start(bf16[1024,768]{1,0:T(8,128)(2,1)S(1)} %fusion.refs_0_), channel_id=1, source_target_pairs={{0,4},{4,0},{8,12},{12,8},{1,5},{5,1},{9,13},{13,9},{2,6},{6,2},{1... | collective-permute-start | bytes 4718600 | tf_op jit(solution)/shard_map/ppermute | solution.py:1145
  249.3 74.0 %collective-permute-start.8 = (bf16[1024,768]{1,0:T(8,128)(2,1)S(1)}, bf16[1024,768]{1,0:T(8,128)(2,1)S(1)}, u32[]{:S(2)}, u32[]{:S(2)}) collective-permute-start(bf16[1024,768]{1,0:T(8,128)(2,1)S(1)} %copy-done.53), channel_id=1, source_target_pairs={{0,16},{16,0},{1,17},{17,1},{2,18},{18,2},{3,19},{19,3},{4,20},{20... | collective-permute-start | bytes 4718600 | tf_op jit(solution)/shard_map/ppermute | solution.py:1021
  295.2 3.0 copy-start.28
  295.2 15.8 %copy-start.24 = (bf16[256,2048]{1,0:T(8,128)(2,1)}, bf16[256,2048]{1,0:T(8,128)(2,1)S(1)}, u32[]{:S(2)}) copy-start(bf16[256,2048]{1,0:T(8,128)(2,1)S(1)} %get-tuple-element.130) | copy-start | bytes 3145732
  295.2 3.0 copy-start.58
  295.2 3.0 copy-start.60
  299.5 2.1 copy-start.64
  301.6 2.3 copy-start.52
  305.6 5.4 %copy-start.8 = (bf16[2048,512]{1,0:T(8,128)(2,1)S(1)}, bf16[2048,512]{1,0:T(8,128)(2,1)}, u32[]{:S(2)}) copy-start(bf16[2048,512]{1,0:T(8,128)(2,1)} %copy-done.7) | copy-start | bytes 6291460
  305.6 40.8 %collective-permute-start.9 = (bf16[1024,768]{1,0:T(8,128)(2,1)}, bf16[1024,768]{1,0:T(8,128)(2,1)}, u32[]{:S(2)}, u32[]{:S(2)}) collective-permute-start(bf16[1024,768]{1,0:T(8,128)(2,1)} %fusion.1.refs_1_), channel_id=1, source_target_pairs={{0,4},{4,0},{8,12},{12,8},{1,5},{5,1},{9,13},{13,9},{2,6},{6,2},{1... | collective-permute-start | bytes 4718600 | tf_op jit(solution)/shard_map/ppermute | solution.py:1145
  307.2 43.8 %collective-permute-start.10 = (bf16[1024,768]{1,0:T(8,128)(2,1)}, bf16[1024,768]{1,0:T(8,128)(2,1)}, u32[]{:S(2)}, u32[]{:S(2)}) collective-permute-start(bf16[1024,768]{1,0:T(8,128)(2,1)} %pad_maximum_fusion.4), channel_id=1, source_target_pairs={{0,16},{16,0},{1,17},{17,1},{2,18},{18,2},{3,19},{19,3},{4,20},{20... | collective-permute-start | bytes 4718600 | tf_op jit(solution)/shard_map/ppermute | solution.py:1021
  330.3 71.4 %collective-permute-start.11 = (bf16[1024,768]{1,0:T(8,128)(2,1)}, bf16[1024,768]{1,0:T(8,128)(2,1)S(1)}, u32[]{:S(2)}, u32[]{:S(2)}) collective-permute-start(bf16[1024,768]{1,0:T(8,128)(2,1)} %fusion.2.refs_2_), channel_id=1, source_target_pairs={{0,4},{4,0},{8,12},{12,8},{1,5},{5,1},{9,13},{13,9},{2,6},{6,2},{1... | collective-permute-start | bytes 4718600 | tf_op jit(solution)/shard_map/ppermute | solution.py:1145
  335.0 10.2 %copy-start.11 = (bf16[8,64,256]{2,1,0:T(8,128)(2,1)S(1)}, bf16[8,64,256]{2,1,0:T(8,128)(2,1)}, u32[]{:S(2)}) copy-start(bf16[8,64,256]{2,1,0:T(8,128)(2,1)} %copy-done.10) | copy-start | bytes 786436
  335.0 10.2 %copy-start.25 = (bf16[256,2048]{1,0:T(8,128)(2,1)S(1)}, bf16[256,2048]{1,0:T(8,128)(2,1)}, u32[]{:S(2)}) copy-start(bf16[256,2048]{1,0:T(8,128)(2,1)} %copy-done.24) | copy-start | bytes 3145732
  345.2 5.7 %copy-start.56 = (bf16[2048,768]{1,0:T(8,128)(2,1)S(1)}, bf16[2048,768]{1,0:T(8,128)(2,1)}, u32[]{:S(2)}) copy-start(bf16[2048,768]{1,0:T(8,128)(2,1)} %constant_dynamic-update-slice_fusion.9) | copy-start | bytes 9437188
  346.0 6.5 %copy-start.37 = (bf16[1024,2048]{1,0:T(8,128)(2,1)S(1)}, bf16[1024,2048]{1,0:T(8,128)(2,1)}, u32[]{:S(2)}) copy-start(bf16[1024,2048]{1,0:T(8,128)(2,1)} %copy-done.36) | copy-start | bytes 12582916
  346.0 8.9 %slice-start.2 = ((s8[8388608]{0:T(1024)(128)(4,1)}), s8[4194304]{0:T(1024)(128)(4,1)S(1)}, s32[]{:S(2)}) async-start(s8[8388608]{0:T(1024)(128)(4,1)} %bitcast.75), calls=%async_computation.2 | async-start | bytes 8388608
  352.5 2.5 slice-start.3
  358.2 43.5 %collective-permute-start.12 = (bf16[512,1024]{1,0:T(8,128)(2,1)S(1)}, bf16[512,1024]{1,0:T(8,128)(2,1)S(1)}, u32[]{:S(2)}, u32[]{:S(2)}) collective-permute-start(bf16[512,1024]{1,0:T(8,128)(2,1)S(1)} %slice.399), channel_id=1, source_target_pairs={{0,16},{16,0},{1,17},{17,1},{2,18},{18,2},{3,19},{19,3},{4,20},{20... | collective-permute-start | bytes 3145736 | tf_op jit(solution)/shard_map/ppermute | solution.py:1021
  362.0 3.0 copy-start.38
  365.0 4.1 copy-start.33
  368.1 34.8 %copy-start.67 = (bf16[2048,768]{1,0:T(8,128)(2,1)S(1)}, bf16[2048,768]{1,0:T(8,128)(2,1)}, u32[]{:S(2)}) copy-start(bf16[2048,768]{1,0:T(8,128)(2,1)} %get-tuple-element.99) | copy-start | bytes 9437188
  368.1 116.7 %collective-permute-start.13 = (bf16[1024,768]{1,0:T(8,128)(2,1)S(1)}, bf16[1024,768]{1,0:T(8,128)(2,1)S(1)}, u32[]{:S(2)}, u32[]{:S(2)}) collective-permute-start(bf16[1024,768]{1,0:T(8,128)(2,1)S(1)} %pad_maximum_fusion.7), channel_id=1, source_target_pairs={{0,16},{16,0},{1,17},{17,1},{2,18},{18,2},{3,19},{19,3},{4,20},{20... | collective-permute-start | bytes 4718600 | tf_op jit(solution)/shard_map/ppermute | solution.py:1021
  401.8 2.5 copy-start.2
  401.8 2.4 copy-start.35
  403.9 2.2 copy-start
  481.7 2.1 copy-start.20
  482.7 8.0 %copy-start.39 = (f32[1024,768]{1,0:T(8,128)S(1)}, f32[1024,768]{1,0:T(8,128)}, u32[]{:S(2)}) copy-start(f32[1024,768]{1,0:T(8,128)} %pad_maximum_fusion.1) | copy-start | bytes 9437188
  490.8 2.3 copy-start.13
  (22 other events, 32.5 us)

commit v9 on v8

--- a/solution.py
+++ b/solution.py
@@ -1185,7 +1185,7 @@
         placed = place_blocks(
             jnp.stack([table[0], table[2], table[3], table[5]]), early, unit, 8
         )
-        grad_kv, rows_all = lax.optimization_barrier((grad_kv, rows_all))
+        placed, rows_all = lax.optimization_barrier((placed, rows_all))
         norm_all = normalize_rows(rows_all, gain_first[None])
         placed, norm_all = lax.optimization_barrier((placed, norm_all))
         others[4], placed, swapped[2], received[1], grad_out_half = lax.optimization_barrier(

time: 510 us -> 509 us (level)
    unnamed x149, local copies, waits for them, and re-layouts: 23.3 us -> 17.7 us
  transfers between devices with their start and end apart: 14 -> 14, of which waited for: 3 -> 3; matrix products, arithmetic and copies ran while one was open for 25% -> 26% of each run, Pallas kernels for 46% -> 46%
where the time goes in v9:
time: 509 us; the launch traced here: 502 us
  Pallas kernels  314 us (62%)
  matrix products  85.3 us (17%)
  local copies, waits for them, and re-layouts  35.6 us (7%)
  other arithmetic  28.5 us (6%)
  blocking collectives  15 us (3%)
  starting transfers between devices  13.2 us (3%)
  waiting for transfers between devices  7.56 us (1%)
    pallas_call x4, Pallas kernels, reduce_gather(): pl.pallas_call(kernel, out_shape=(jax.ShapeDtypeStruct((reach * block_row...  199 us
    pallas_call x1, Pallas kernels, opening(): pl.pallas_call(kernel, out_shape=(jax.ShapeDtypeStruct((ctx_size * block_...  66.4 us
    dot_general x32, matrix products, contract(): lax.dot_general(left, right, (((left_dim,), (right_dim,)), ((), ())), pre...  52.5 us
    pallas_call x2, Pallas kernels, place_blocks(): pl.pallas_call(kernel, grid_spec=pltpu.PrefetchScalarGridSpec(num_scalar_...  21.1 us
    dot_general x5, matrix products, forward(): both = jnp.dot(normed_all, pair_w, preferred_element_type=F32)  18.1 us
    unnamed x149, local copies, waits for them, and re-layouts  17.7 us
    all_gather x1, blocking collectives, local(): lax.all_gather(kv_own.reshape(2 * key_width, row_count).T, 'ctx', axis=0,...  15 us
    dot_general x5, matrix products, forward(): grad_hidden = jnp.dot(cot_all, down_w, preferred_element_type=F32)  12.6 us
  transfers between devices with their start and end apart: 14, of which 3 were waited for; matrix products, arithmetic and copies ran while one was open for 26% of the time, Pallas kernels for 46%

profile of v9, /device:TPU:0, one launch (start us, length us, event | category | flops | bytes accessed | tf_op | source)
XLA Modules:
  0.0 502.3 jit_solution(4103261750606309913)
XLA Ops:
  3.1 1.7 dynamic-slice_bitcast_fusion.1
  5.8 1.5 pad_maximum_fusion.2.cot_ref
  7.3 66.4 %shard_map.203 = (bf16[1024,4096]{1,0:T(8,128)(2,1)}, f32[2,1024]{1,0:T(2,128)S(1)}, bf16[2048,768]{1,0:T(8,128)(2,1)}, bf16[2048,512]{1,0:T(8,128)(2,1)S(1)}, b...) custom-call(bf16[256,4096]{1,0:T(8,128)(2,1)} %pad_maximum_fusion.2., ...), custom_call_target="tpu_custom_call" | custom-call | tf_op jit(solution)/shard_map/pallas_call | solution.py:874
  74.3 1.5 collective-permute-start.1
  76.2 3.0 fusion.64
  81.0 15.0 %all_gather.3 = bf16[1024,256]{0,1:T(8,128)(2,1)S(1)} all-gather(bf16[256,256]{0,1:T(8,128)(2,1)S(1)} %bitcast.85), channel_id=1, replica_groups=mesh['fsdp'=2,'ctx'=4,'tp'=4] {'ctx'}, dimensions={0}, use_global_device_ids=true | all-gather | bytes 655360 | tf_op jit(solution)/shard_map/all_gather | solution.py:1074
  96.0 1.3 copy.46
  97.3 2.1 fusion.115
  101.5 7.7 %shard_map.204 = (bf16[8,64,256]{2,1,0:T(8,128)(2,1)S(1)}, f32[8,1,256]{2,1,0:T(1,128)S(1)}) custom-call(s32[2]{0:T(128)S(1)} %pad_add_fusion.bounds_ref, bf16[8,64,256]{2,1,0:T(8,128)(2,1)S(1)} %pad_maximum_fusion.27.query_ref, bf16[2,1024,64]{2,1,0:T(8,128)(2,1)S(1)} %get-tuple-element.211.key_ref, bf16[2,64,1024]{2,1,0:T(8,128)(2,1)S(1)} %bitcast.69), custom_call_target="tpu_custom_call" | custom-call | tf_op jit(solution)/shard_map/pallas_call | solution.py:72
  109.3 1.6 constant_dynamic-update-slice_fusion.3
  111.0 1.6 constant_dynamic-update-slice_fusion.1
  117.7 1.5 constant_dynamic-update-slice_fusion
  119.3 44.5 %shard_map.205 = (bf16[1024,2048]{1,0:T(8,128)(2,1)S(1)}, f32[64,2048]{1,0:T(8,128)S(1)}) custom-call(bf16[256,2048]{1,0:T(8,128)(2,1)S(1)} %convolution_convert_fusion.term_ref, bf16[256,2048]{1,0:T(8,128)(2,1)S(1)} %pad_maximum_fusion.12.refs_0_.refs_1_, f32[1,2048]{1,0:T(1,128)S(1)} %get-tuple-element.226.refs_1_.refs_2_), custom_call_target="tpu_custom_call" | custom-call | tf_op jit(solution)/shard_map/pallas_call | solution.py:786
  163.8 2.4 fusion.32
  167.5 1.7 multiply_convert_fusion.13
  170.0 1.3 convolution_convert_fusion.6
  174.6 1.6 collective-permute-start.3
  176.1 1.7 fusion.42
  179.2 1.5 constant_dynamic-update-slice_fusion.2
  180.8 2.4 fusion.28
  183.2 1.9 multiply_convert_fusion.10
  186.7 1.3 convolution_convert_fusion.5
  188.0 1.3 fusion.48
  189.8 2.0 pad_maximum_fusion
  195.9 1.3 fusion.30
  197.2 3.3 fusion.26
  200.5 2.8 constant_dynamic-update-slice_fusion.4
  203.3 5.5 %fusion.24 = f32[1024,512]{0,1:T(8,128)} fusion(bf16[1024,2048]{1,0:T(8,128)(2,1)S(1)} %get-tuple-element.108, bf16[2048,768]{1,0:T(8,128)(2,1)} %constant_dynamic-update-slice_fusion.4), kind=kOutput, calls=%fused_computation.40 | convolution fusion | flops 2147483648 | bytes 8388608 | tf_op jit(solution)/shard_map/dot_general | solution.py:1116
  208.8 3.8 multiply_convert_fusion.7
  216.4 3.2 constant_dynamic-update-slice_fusion.6
  219.6 5.3 %fusion.20 = f32[1024,512]{0,1:T(8,128)} fusion(bf16[1024,2048]{1,0:T(8,128)(2,1)S(1)} %get-tuple-element.108, bf16[2048,768]{1,0:T(8,128)(2,1)} %constant_dynamic-update-slice_fusion.6), kind=kOutput, calls=%fused_computation.36 | convolution fusion | flops 2147483648 | bytes 8388608 | tf_op jit(solution)/shard_map/dot_general | solution.py:1116
  225.0 3.6 multiply_convert_fusion.3
  229.3 1.3 convolution_convert_fusion.3
  232.3 1.3 fusion.50
  233.6 5.3 %fusion.22 = f32[512,2048]{1,0:T(8,128)} fusion(bf16[2048,768]{1,0:T(8,128)(2,1)} %constant_dynamic-update-slice_fusion.4, s32[]{:T(128)S(6)} %select_n.43, bf16[1024,256]{0,1:T(8,128)(2,1)S(1)} %copy-done.55, bf16[1024,256]{0,1:T(8,128)(2,1)S(1)} %copy-done.57), kind=kOutput, calls=%fused_computation.38 | convolution fusion | flops 1074790400 | bytes 7340036 | tf_op jit(solution)/shard_map/dot_general | solution.py:19
  239.0 5.8 %add_convert_fusion.term_ref = bf16[512,2048]{1,0:T(8,128)(2,1)S(1)} fusion(f32[512,2048]{1,0:T(8,128)} %fusion.22, f32[512,2048]{1,0:T(8,128)S(1)} %fusion.30, f32[512,2048]{1,0:T(8,128)} %fusion.26, bf16[2048,768]{1,0:T(8,128)(2,1)} %constant_dynamic-update-slice_fusion.6, s32[]{:T(128)S(6)} %select_n.43, bf16[1024,256]{0,1:T(8,128)(2,1)S(1)} %get-tuple-element.194, ...), kind=kOutput, calls=%fused_computation | convolution fusion | flops 1078984704 | bytes 17825796 | tf_op jit(solution)/shard_map/dot_general | solution.py:19
  245.0 2.1 fusion.refs_0_
  247.1 1.6 collective-permute-start.6
  248.7 1.7 collective-permute-start.7
  250.9 44.8 %shard_map.206 = (bf16[256,2048]{1,0:T(8,128)(2,1)S(1)}, f32[64,2048]{1,0:T(8,128)S(1)}, f32[1,2048]{1,0:T(1,128)S(1)}) custom-call(bf16[512,2048]{1,0:T(8,128)(2,1)S(1)} %add_convert_fusion.term_ref, f32[64,2048]{1,0:T(8,128)S(1)} %get-tuple-element.120.refs_0_, bf16[256,2048]{1,0:T(8,128)(2,1)S(1)} %pad_maximum_fusion.13.refs_1_, ...), custom_call_target="tpu_custom_call" | custom-call | tf_op jit(solution)/shard_map/pallas_call | solution.py:786
  295.8 2.9 fusion.40
  298.8 1.3 fusion.46
  300.1 2.1 fusion.72
  302.2 2.1 add_convert_fusion.1.term_ref
  304.3 3.1 fusion.1.refs_1_
  309.2 2.4 fusion.36
  312.6 9.6 %shard_map.207 = (f32[8,64,256]{2,1,0:T(8,128)S(1)}, bf16[4,64,1024]{2,1,0:T(8,128)(2,1)S(1)}) custom-call(s32[2]{0:T(128)S(1)} %pad_add_fusion.bounds_ref, bf16[8,64,256]{2,1,0:T(8,128)(2,1)S(1)} %pad_maximum_fusion.27.query_ref, bf16[2,1024,64]{2,1,0:T(8,128)(2,1)S(1)} %get-tuple-element.211.key_ref, bf16[2,64,1024]{2,1,0:T(8,128)(2,1)S(1)} %bitcast.68, ...), custom_call_target="tpu_custom_call" | custom-call | tf_op jit(solution)/shard_map/pallas_call | solution.py:112
  322.3 1.7 fusion.2.refs_2_
  324.7 10.5 %shard_map.208 = (f32[1024,2048]{1,0:T(8,128)}, f32[1024,2048]{1,0:T(8,128)}, f32[1024,2048]{1,0:T(8,128)}) custom-call(s32[4]{0:T(128)S(1)} %get-tuple-element.233.table_ref, bf16[1024,768]{1,0:T(8,128)(2,1)S(1)} %fusion.refs_0_, bf16[1024,768]{1,0:T(8,128)(2,1)} %fusion.1.refs_1_, bf16[1024,768]{1,0:T(8,128)(2,1)} %fusion.2.refs_2_, ...), custom_call_target="tpu_custom_call" | custom-call | tf_op jit(solution)/shard_map/pallas_call | solution.py:913
  335.3 5.6 %shard_map.209.refs_4_ = bf16[1024,2048]{1,0:T(8,128)(2,1)} custom-call(bf16[1024,4096]{1,0:T(8,128)(2,1)} %get-tuple-element.151.row_ref, f32[1,2048]{1,0:T(1,128)} %copy-done.26), custom_call_target="tpu_custom_call" | custom-call | tf_op jit(solution)/shard_map/pallas_call | solution.py:968
  340.9 2.1 fusion.118
  343.3 1.7 collective-permute-done.9.refs_2_
  345.0 5.5 %collective-permute-done.10 = bf16[1024,768]{1,0:T(8,128)(2,1)} collective-permute-done((bf16[1024,768]{1,0:T(8,128)(2,1)}, bf16[1024,768]{1,0:T(8,128)(2,1)}, u32[]{:S(2)}, u32[]{:S(2)}) %collective-permute-start.10) | collective-permute-done | bytes 1572896 | tf_op jit(solution)/shard_map/ppermute | solution.py:1021
  350.7 2.4 fusion.17
  353.2 1.7 multiply_convert_fusion.2
  356.4 1.6 collective-permute-start.12
  360.8 1.9 pad_maximum_fusion.1
  363.8 3.0 add_convert_fusion.3.refs_0_
  367.2 35.6 %shard_map.210 = (bf16[256,2048]{1,0:T(8,128)(2,1)S(1)}, f32[256,256]{1,0:T(8,128)S(1)}) custom-call(bf16[512,2048]{1,0:T(8,128)(2,1)S(1)} %add_convert_fusion.1.term_ref, f32[64,2048]{1,0:T(8,128)S(1)} %get-tuple-element.120.refs_0_, bf16[256,1024]{1,0:T(8,128)(2,1)S(1)} %bitcast.70), custom_call_target="tpu_custom_call" | custom-call | tf_op jit(solution)/shard_map/pallas_call | solution.py:786
  404.4 1.9 copy-done
  406.3 74.1 %shard_map.211 = (bf16[256,2048]{1,0:T(8,128)(2,1)S(1)}, f32[1,2048]{1,0:T(1,128)}, bf16[768,1024]{1,0:T(8,128)(2,1)S(1)}, bf16[512,1024]{1,0:T(8,128)(2,1)S(1)}, f32[2,1024]{1,0:T(2,128)S(1)}) custom-call(bf16[256,2048]{1,0:T(8,128)(2,1)S(1)} %convolution_convert_fusion.1.term_ref, f32[64,2048]{1,0:T(8,128)S(1)} %copy-done.21, ...), custom_call_target="tpu_custom_call" | custom-call | tf_op jit(solution)/shard_map/pallas_call | solution.py:786
  484.8 4.7 shard_map.212
  489.6 1.9 add_convert_fusion.2.refs_1_
  491.4 10.6 %shard_map.213 = (f32[1024,2048]{1,0:T(8,128)}, f32[1024,2048]{1,0:T(8,128)}, f32[1024,2048]{1,0:T(8,128)}) custom-call(s32[4]{0:T(128)S(1)} %get-tuple-element.234.table_ref, bf16[1024,768]{1,0:T(8,128)(2,1)S(1)} %copy-done.3, bf16[1024,768]{1,0:T(8,128)(2,1)S(1)} %add_convert_fusion.2.refs_1_, ...), custom_call_target="tpu_custom_call", output_to_operand_aliasing={{0}: (5, {}), {1}: (6, {}), {2}: (7, {})} | custom-call | tf_op jit(solution)/shard_map/pallas_call | solution.py:913
  (228 shorter events, 48.1 us)
Async XLA Ops:
  4.9 71.3 %copy-start.32 = (bf16[256,1024]{1,0:T(8,128)(2,1)}, bf16[256,1024]{1,0:T(8,128)(2,1)S(1)}, u32[]{:S(2)}) copy-start(bf16[256,1024]{1,0:T(8,128)(2,1)S(1)} %get-tuple-element.215) | copy-start | bytes 1572868
  4.9 2.4 copy-start.18
  4.9 2.4 copy-start.19
  73.7 5.5 %copy-start.9 = (bf16[1024,768]{1,0:T(8,128)(2,1)}, bf16[1024,768]{1,0:T(8,128)(2,1)S(1)}, u32[]{:S(2)}) copy-start(bf16[1024,768]{1,0:T(8,128)(2,1)S(1)} %get-tuple-element.117) | copy-start | bytes 4718596
  73.7 5.5 %copy-start.11 = (bf16[1024,768]{1,0:T(8,128)(2,1)}, bf16[1024,768]{1,0:T(8,128)(2,1)S(1)}, u32[]{:S(2)}) copy-start(bf16[1024,768]{1,0:T(8,128)(2,1)S(1)} %get-tuple-element.115) | copy-start | bytes 4718596
  73.7 5.5 %copy-start.13 = (bf16[1024,768]{1,0:T(8,128)(2,1)}, bf16[1024,768]{1,0:T(8,128)(2,1)S(1)}, u32[]{:S(2)}) copy-start(bf16[1024,768]{1,0:T(8,128)(2,1)S(1)} %get-tuple-element.139) | copy-start | bytes 4718596
  73.7 40.5 %copy-start.4 = (bf16[2048,512]{1,0:T(8,128)(2,1)}, bf16[2048,512]{1,0:T(8,128)(2,1)S(1)}, u32[]{:S(2)}) copy-start(bf16[2048,512]{1,0:T(8,128)(2,1)S(1)} %get-tuple-element.104) | copy-start | bytes 6291460
  73.7 41.3 %collective-permute-start = (bf16[1024,768]{1,0:T(8,128)(2,1)}, bf16[1024,768]{1,0:T(8,128)(2,1)}, u32[]{:S(2)}, u32[]{:S(2)}) collective-permute-start(bf16[1024,768]{1,0:T(8,128)(2,1)} %get-tuple-element.106), channel_id=1, source_target_pairs={{0,16},{16,0},{1,17},{17,1},{2,18},{18,2},{3,19},{19,3},{4,20},{20... | collective-permute-start | bytes 4718600 | tf_op jit(solution)/shard_map/ppermute | solution.py:1021
  74.3 98.3 %collective-permute-start.1 = (bf16[1024,768]{1,0:T(8,128)(2,1)}, bf16[1024,768]{1,0:T(8,128)(2,1)}, u32[]{:S(2)}, u32[]{:S(2)}) collective-permute-start(bf16[1024,768]{1,0:T(8,128)(2,1)} %get-tuple-element.110), channel_id=1, source_target_pairs={{0,16},{16,0},{1,17},{17,1},{2,18},{18,2},{3,19},{19,3},{4,20},{20... | collective-permute-start | bytes 4718600 | tf_op jit(solution)/shard_map/ppermute | solution.py:1021
  76.1 3.1 copy-start.26
  109.2 5.0 %copy-start.7 = (bf16[8,64,256]{2,1,0:T(8,128)(2,1)}, bf16[8,64,256]{2,1,0:T(8,128)(2,1)S(1)}, u32[]{:S(2)}) copy-start(bf16[8,64,256]{2,1,0:T(8,128)(2,1)S(1)} %get-tuple-element.103) | copy-start | bytes 786436
  109.3 3.2 copy-start.14
  110.9 2.9 copy-start.33
  114.2 5.1 %copy-start.1 = (bf16[256,2048]{1,0:T(8,128)(2,1)}, bf16[256,2048]{1,0:T(8,128)(2,1)S(1)}, u32[]{:S(2)}) copy-start(bf16[256,2048]{1,0:T(8,128)(2,1)S(1)} %pad_maximum_fusion.12.refs_0_.refs_1_) | copy-start | bytes 3145732
  117.2 83.3 %collective-permute-start.2 = (bf16[1024,768]{1,0:T(8,128)(2,1)S(1)}, bf16[1024,768]{1,0:T(8,128)(2,1)}, u32[]{:S(2)}, u32[]{:S(2)}) collective-permute-start(bf16[1024,768]{1,0:T(8,128)(2,1)S(1)} %copy-done.12), channel_id=1, source_target_pairs={{0,16},{16,0},{1,17},{17,1},{2,18},{18,2},{3,19},{19,3},{4,20},{20... | collective-permute-start | bytes 4718600 | tf_op jit(solution)/shard_map/ppermute | solution.py:1021
  119.2 73.9 %copy-start.34 = (bf16[2048,768]{1,0:T(8,128)(2,1)}, bf16[2048,768]{1,0:T(8,128)(2,1)S(1)}, u32[]{:S(2)}) copy-start(bf16[2048,768]{1,0:T(8,128)(2,1)S(1)} %constant_dynamic-update-slice_fusion) | copy-start | bytes 9437188
  119.3 47.0 %slice-start = ((s8[8388608]{0:T(1024)(128)(4,1)}), s8[4194304]{0:T(1024)(128)(4,1)S(1)}, s32[]{:S(2)}) async-start(s8[8388608]{0:T(1024)(128)(4,1)} %bitcast.73), calls=%async_computation | async-start | bytes 8388608
  163.8 134.9 %copy-start.28 = (bf16[1024,2048]{1,0:T(8,128)(2,1)}, bf16[1024,2048]{1,0:T(8,128)(2,1)S(1)}, u32[]{:S(2)}) copy-start(bf16[1024,2048]{1,0:T(8,128)(2,1)S(1)} %get-tuple-element.108) | copy-start | bytes 12582916
  163.8 3.7 slice-start.1
  169.2 6.9 %copy-start.63 = (bf16[1024,256]{0,1:T(8,128)(2,1)}, bf16[1024,256]{0,1:T(8,128)(2,1)S(1)}, u32[]{:S(2)}) copy-start(bf16[1024,256]{0,1:T(8,128)(2,1)S(1)} %get-tuple-element.205) | copy-start | bytes 1572868
  169.2 8.6 %copy-start.52 = (bf16[1024,256]{0,1:T(8,128)(2,1)}, bf16[1024,256]{0,1:T(8,128)(2,1)S(1)}, u32[]{:S(2)}) copy-start(bf16[1024,256]{0,1:T(8,128)(2,1)S(1)} %get-tuple-element.200) | copy-start | bytes 1572868
  171.3 2.0 copy-start.10
  174.6 41.8 %collective-permute-start.3 = (bf16[1024,768]{1,0:T(8,128)(2,1)S(1)}, bf16[1024,768]{1,0:T(8,128)(2,1)}, u32[]{:S(2)}, u32[]{:S(2)}) collective-permute-start(bf16[1024,768]{1,0:T(8,128)(2,1)S(1)} %copy-done.10), channel_id=1, source_target_pairs={{0,16},{16,0},{1,17},{17,1},{2,18},{18,2},{3,19},{19,3},{4,20},{20... | collective-permute-start | bytes 4718600 | tf_op jit(solution)/shard_map/ppermute | solution.py:1021
  179.2 37.2 %collective-permute-start.4 = (bf16[1024,768]{1,0:T(8,128)(2,1)}, bf16[1024,768]{1,0:T(8,128)(2,1)S(1)}, u32[]{:S(2)}, u32[]{:S(2)}) collective-permute-start(bf16[1024,768]{1,0:T(8,128)(2,1)} %collective-permute-done.1), channel_id=1, source_target_pairs={{0,4},{4,0},{8,12},{12,8},{1,5},{5,1},{9,13},{13,9},{2,6},{6,2},{1... | collective-permute-start | bytes 4718600 | tf_op jit(solution)/shard_map/ppermute | solution.py:1137
  189.3 55.7 %collective-permute-start.5 = (bf16[1024,768]{1,0:T(8,128)(2,1)}, bf16[1024,768]{1,0:T(8,128)(2,1)}, u32[]{:S(2)}, u32[]{:S(2)}) collective-permute-start(bf16[1024,768]{1,0:T(8,128)(2,1)} %pad_maximum_fusion.3), channel_id=1, source_target_pairs={{0,16},{16,0},{1,17},{17,1},{2,18},{18,2},{3,19},{19,3},{4,20},{20... | collective-permute-start | bytes 4718600 | tf_op jit(solution)/shard_map/ppermute | solution.py:1021
  193.9 2.0 copy-start.53
  200.5 8.3 %slice-start.2 = ((s8[8388608]{0:T(1024)(128)(4,1)}), s8[4194304]{0:T(1024)(128)(4,1)S(1)}, s32[]{:S(2)}) async-start(s8[8388608]{0:T(1024)(128)(4,1)} %bitcast.75), calls=%async_computation.2 | async-start | bytes 8388608
  203.3 5.5 %slice-start.3 = ((s8[8388608]{0:T(1024)(128)(4,1)}), s8[4194304]{0:T(1024)(128)(4,1)S(1)}, s32[]{:S(2)}) async-start(s8[8388608]{0:T(1024)(128)(4,1)} %bitcast.75), calls=%async_computation.3 | async-start | bytes 8388608
  216.4 8.6 %copy-start.41 = (bf16[1024,768]{1,0:T(8,128)(2,1)}, bf16[1024,768]{1,0:T(8,128)(2,1)S(1)}, u32[]{:S(2)}) copy-start(bf16[1024,768]{1,0:T(8,128)(2,1)S(1)} %collective-permute-done.4) | copy-start | bytes 4718596
  228.5 10.4 %copy-start.48 = (bf16[1024,256]{0,1:T(8,128)(2,1)}, bf16[1024,256]{0,1:T(8,128)(2,1)S(1)}, u32[]{:S(2)}) copy-start(bf16[1024,256]{0,1:T(8,128)(2,1)S(1)} %get-tuple-element.193) | copy-start | bytes 1572868
  228.5 10.4 %copy-start.50 = (bf16[1024,256]{0,1:T(8,128)(2,1)}, bf16[1024,256]{0,1:T(8,128)(2,1)S(1)}, u32[]{:S(2)}) copy-start(bf16[1024,256]{0,1:T(8,128)(2,1)S(1)} %get-tuple-element.194) | copy-start | bytes 1572868
  239.0 6.1 %copy-start.46 = (f32[1024,256]{1,0:T(8,128)S(1)}, f32[1024,256]{1,0:T(8,128)}, u32[]{:S(2)}) copy-start(f32[1024,256]{1,0:T(8,128)} %fusion.42) | copy-start | bytes 3145732
  244.7 2.4 copy-start.44
  244.7 5.8 %copy-start.43 = (bf16[1024,768]{1,0:T(8,128)(2,1)S(1)}, bf16[1024,768]{1,0:T(8,128)(2,1)}, u32[]{:S(2)}) copy-start(bf16[1024,768]{1,0:T(8,128)(2,1)} %pad_maximum_fusion.6) | copy-start | bytes 4718596
  247.1 48.6 %copy-start.62 = (bf16[1024,256]{0,1:T(8,128)(2,1)S(1)}, bf16[1024,256]{0,1:T(8,128)(2,1)}, u32[]{:S(2)}) copy-start(bf16[1024,256]{0,1:T(8,128)(2,1)} %copy-done.61) | copy-start | bytes 1572868
  247.1 57.2 %collective-permute-start.6 = (bf16[1024,768]{1,0:T(8,128)(2,1)S(1)}, bf16[1024,768]{1,0:T(8,128)(2,1)}, u32[]{:S(2)}, u32[]{:S(2)}) collective-permute-start(bf16[1024,768]{1,0:T(8,128)(2,1)S(1)} %copy-done.44), channel_id=1, source_target_pairs={{0,16},{16,0},{1,17},{17,1},{2,18},{18,2},{3,19},{19,3},{4,20},{20... | collective-permute-start | bytes 4718600 | tf_op jit(solution)/shard_map/ppermute | solution.py:1021
  248.7 55.6 %collective-permute-start.7 = (bf16[1024,768]{1,0:T(8,128)(2,1)S(1)}, bf16[1024,768]{1,0:T(8,128)(2,1)S(1)}, u32[]{:S(2)}, u32[]{:S(2)}) collective-permute-start(bf16[1024,768]{1,0:T(8,128)(2,1)S(1)} %fusion.refs_0_), channel_id=1, source_target_pairs={{0,4},{4,0},{8,12},{12,8},{1,5},{5,1},{9,13},{13,9},{2,6},{6,2},{1... | collective-permute-start | bytes 4718600 | tf_op jit(solution)/shard_map/ppermute | solution.py:1145
  250.5 71.8 %collective-permute-start.8 = (bf16[1024,768]{1,0:T(8,128)(2,1)S(1)}, bf16[1024,768]{1,0:T(8,128)(2,1)S(1)}, u32[]{:S(2)}, u32[]{:S(2)}) collective-permute-start(bf16[1024,768]{1,0:T(8,128)(2,1)S(1)} %copy-done.43), channel_id=1, source_target_pairs={{0,16},{16,0},{1,17},{17,1},{2,18},{18,2},{3,19},{19,3},{4,20},{20... | collective-permute-start | bytes 4718600 | tf_op jit(solution)/shard_map/ppermute | solution.py:1021
  295.8 3.0 copy-start.20
  295.8 15.8 %copy-start.17 = (bf16[256,2048]{1,0:T(8,128)(2,1)}, bf16[256,2048]{1,0:T(8,128)(2,1)S(1)}, u32[]{:S(2)}) copy-start(bf16[256,2048]{1,0:T(8,128)(2,1)S(1)} %get-tuple-element.132) | copy-start | bytes 3145732
  295.8 3.0 copy-start.49
  295.8 3.0 copy-start.51
  300.1 2.1 copy-start.59
  304.3 4.8 copy-start.60
  307.4 4.1 copy-start.5
  307.4 37.6 %collective-permute-start.9 = (bf16[1024,768]{1,0:T(8,128)(2,1)}, bf16[1024,768]{1,0:T(8,128)(2,1)}, u32[]{:S(2)}, u32[]{:S(2)}) collective-permute-start(bf16[1024,768]{1,0:T(8,128)(2,1)} %fusion.1.refs_1_), channel_id=1, source_target_pairs={{0,4},{4,0},{8,12},{12,8},{1,5},{5,1},{9,13},{13,9},{2,6},{6,2},{1... | collective-permute-start | bytes 4718600 | tf_op jit(solution)/shard_map/ppermute | solution.py:1145
  308.4 42.1 %collective-permute-start.10 = (bf16[1024,768]{1,0:T(8,128)(2,1)}, bf16[1024,768]{1,0:T(8,128)(2,1)}, u32[]{:S(2)}, u32[]{:S(2)}) collective-permute-start(bf16[1024,768]{1,0:T(8,128)(2,1)} %pad_maximum_fusion.4), channel_id=1, source_target_pairs={{0,16},{16,0},{1,17},{17,1},{2,18},{18,2},{3,19},{19,3},{4,20},{20... | collective-permute-start | bytes 4718600 | tf_op jit(solution)/shard_map/ppermute | solution.py:1021
  323.9 78.9 %collective-permute-start.11 = (bf16[1024,768]{1,0:T(8,128)(2,1)}, bf16[1024,768]{1,0:T(8,128)(2,1)}, u32[]{:S(2)}, u32[]{:S(2)}) collective-permute-start(bf16[1024,768]{1,0:T(8,128)(2,1)} %fusion.2.refs_2_), channel_id=1, source_target_pairs={{0,4},{4,0},{8,12},{12,8},{1,5},{5,1},{9,13},{13,9},{2,6},{6,2},{1... | collective-permute-start | bytes 4718600 | tf_op jit(solution)/shard_map/ppermute | solution.py:1145
  335.3 5.6 %copy-start.8 = (bf16[8,64,256]{2,1,0:T(8,128)(2,1)S(1)}, bf16[8,64,256]{2,1,0:T(8,128)(2,1)}, u32[]{:S(2)}) copy-start(bf16[8,64,256]{2,1,0:T(8,128)(2,1)} %copy-done.7) | copy-start | bytes 786436
  340.9 2.3 copy-start.23
  340.9 9.6 %copy-start.42 = (bf16[1024,768]{1,0:T(8,128)(2,1)S(1)}, bf16[1024,768]{1,0:T(8,128)(2,1)}, u32[]{:S(2)}) copy-start(bf16[1024,768]{1,0:T(8,128)(2,1)} %copy-done.41) | copy-start | bytes 4718596
  340.9 9.6 %copy-start.47 = (bf16[2048,768]{1,0:T(8,128)(2,1)S(1)}, bf16[2048,768]{1,0:T(8,128)(2,1)}, u32[]{:S(2)}) copy-start(bf16[2048,768]{1,0:T(8,128)(2,1)} %constant_dynamic-update-slice_fusion.9) | copy-start | bytes 9437188
  343.0 7.7 %copy-start.29 = (bf16[1024,2048]{1,0:T(8,128)(2,1)S(1)}, bf16[1024,2048]{1,0:T(8,128)(2,1)}, u32[]{:S(2)}) copy-start(bf16[1024,2048]{1,0:T(8,128)(2,1)} %copy-done.28) | copy-start | bytes 12582916
  343.0 10.1 %slice-start.4 = ((s8[8388608]{0:T(1024)(128)(4,1)}), s8[4194304]{0:T(1024)(128)(4,1)S(1)}, s32[]{:S(2)}) async-start(s8[8388608]{0:T(1024)(128)(4,1)} %bitcast.77), calls=%async_computation.4 | async-start | bytes 8388608
  350.7 2.5 slice-start.5
  356.4 46.4 %collective-permute-start.12 = (bf16[512,1024]{1,0:T(8,128)(2,1)S(1)}, bf16[512,1024]{1,0:T(8,128)(2,1)S(1)}, u32[]{:S(2)}, u32[]{:S(2)}) collective-permute-start(bf16[512,1024]{1,0:T(8,128)(2,1)S(1)} %slice.399), channel_id=1, source_target_pairs={{0,16},{16,0},{1,17},{17,1},{2,18},{18,2},{3,19},{19,3},{4,20},{20... | collective-permute-start | bytes 3145736 | tf_op jit(solution)/shard_map/ppermute | solution.py:1021
  360.7 3.0 copy-start.30
  363.8 3.5 copy-start.25
  366.7 36.2 %copy-start.65 = (bf16[2048,768]{1,0:T(8,128)(2,1)S(1)}, bf16[2048,768]{1,0:T(8,128)(2,1)}, u32[]{:S(2)}) copy-start(bf16[2048,768]{1,0:T(8,128)(2,1)} %get-tuple-element.101) | copy-start | bytes 9437188
  366.8 116.8 %collective-permute-start.13 = (bf16[1024,768]{1,0:T(8,128)(2,1)S(1)}, bf16[1024,768]{1,0:T(8,128)(2,1)S(1)}, u32[]{:S(2)}, u32[]{:S(2)}) collective-permute-start(bf16[1024,768]{1,0:T(8,128)(2,1)S(1)} %pad_maximum_fusion.7), channel_id=1, source_target_pairs={{0,16},{16,0},{1,17},{17,1},{2,18},{18,2},{3,19},{19,3},{4,20},{20... | collective-permute-start | bytes 4718600 | tf_op jit(solution)/shard_map/ppermute | solution.py:1021
  404.0 2.3 copy-start
  480.4 2.1 copy-start.15
  480.4 2.1 copy-start.16
  481.4 8.1 %copy-start.31 = (f32[1024,768]{1,0:T(8,128)S(1)}, f32[1024,768]{1,0:T(8,128)}, u32[]{:S(2)}) copy-start(f32[1024,768]{1,0:T(8,128)} %pad_maximum_fusion.1) | copy-start | bytes 9437188
  (22 other events, 29.7 us)
